TPU v7x, 32 devices: a whole 2x2x4 slice. The times are simulated.
32 devices in a mesh: dp: 16 (over z, y, core), mp: 2 (over x).
Axes of the slice: x: 2, y: 2, z: 4, core: 2. Of those that a mesh axis runs over, the one named last changes fastest.
Arguments:
- tokens: bfloat16 [2048, 2048], P(('dp', 'mp')), may hold values from -6 to 6
- lengths: int32 [22], replicated, may hold values from 1 to 1024, 2048 in all
- w_in: bfloat16 [2048, 2048], P('dp'), may hold values from -0.125 to 0.125
- w_forget: bfloat16 [2048, 2048], P('dp'), may hold values from -0.125 to 0.125
- w_gate: bfloat16 [2048, 2048], P('dp'), may hold values from -0.125 to 0.125
- w_out: bfloat16 [2048, 2048], P('dp'), may hold values from -0.125 to 0.125
- attn_gain: bfloat16 [2048], P('dp'), may hold values from 0.5 to 1.5
- mix_gain: bfloat16 [2048], P('dp'), may hold values from 0.5 to 1.5
- bound_table: bfloat16 [24, 2048], P(None, 'dp'), may hold values from -14 to 3
- ff_gate: bfloat16 [2048, 5632], P('dp', 'mp'), may hold values from -0.125 to 0.125
- ff_up: bfloat16 [2048, 5632], P('dp', 'mp'), may hold values from -0.125 to 0.125
- ff_down: bfloat16 [5632, 2048], P('mp', 'dp'), may hold values from -0.078125 to 0.078125
- mlp_gain: bfloat16 [2048], P('dp'), may hold values from 0.5 to 1.5
- out_grad: bfloat16 [2048, 2048], P(('dp', 'mp')), may hold values from -6 to 6
Outputs:
- result: bfloat16 [2048, 2048], P(('dp', 'mp'))
- token_grad: float32 [2048, 2048], P(('dp', 'mp'))
- grad_w_in: float32 [2048, 2048], P('dp')
- grad_w_forget: float32 [2048, 2048], P('dp')
- grad_w_gate: float32 [2048, 2048], P('dp')
- grad_w_out: float32 [2048, 2048], P('dp')
- grad_attn_gain: float32 [2048], P('dp')
- grad_mix_gain: float32 [2048], P('dp')
- grad_bound_table: float32 [24, 2048], P(None, 'dp')
- grad_ff_gate: float32 [2048, 5632], P('dp', 'mp')
- grad_ff_up: float32 [2048, 5632], P('dp', 'mp')
- grad_ff_down: float32 [5632, 2048], P('mp', 'dp')
- grad_mlp_gain: float32 [2048], P('dp')
Inputs may be any that keep to these rules, and one draw needn't show every extreme that they name: lengths of 22 sequences packed end to end; they sum to 2048 and the longest is 1024.
All inputs are finite; a program needn't handle non-finite values.
Results may differ from a plain program's by a relative error of at most 0.0085.
Values may be sent and summed in bfloat16 or wider, within the bound.
No kernel may reach another device: no remote copies, remote signals or barrier semaphores. Data moves between devices by JAX's collectives and lax.ppermute only.
A program may use at most 384 MiB of HBM per device.

v0:
```python
import jax
import jax.numpy as jnp
from jax import lax
from jax.sharding import PartitionSpec as P

LAYER = 12


epsilon = 1e-06


def entering(value, axis, join, neutral, backward):
    count, mine = (lax.axis_size(axis), lax.axis_index(axis))
    pieces = jax.tree.map(lambda part: lax.all_gather(part, axis), value)
    if backward:
        pieces = jax.tree.map(lambda part: part[::-1], pieces)
        mine = count - 1 - mine
    running = jax.tree.map(
        lambda part, zero: jnp.full_like(part, 0) + jnp.asarray(zero, part.dtype), value, neutral
    )

    def turn(position, running):
        longer = join(running, jax.tree.map(lambda part: part[position], pieces))
        return jax.tree.map(lambda new, old: jnp.where(position < mine, new, old), longer, running)

    return lax.fori_loop(0, count - 1, turn, running)


def contract_rows(left, right):
    return lax.dot_general(
        left, right, (((0,), (0,)), ((), ())), preferred_element_type=jnp.float32
    )


def times_transposed(left, right):
    return lax.dot_general(
        left, right, (((1,), (1,)), ((), ())), preferred_element_type=jnp.float32
    )


def combine(earlier, later):
    return (earlier[0] * later[0], later[0] * earlier[1] + later[1])


def inverse_rms(value):
    return lax.rsqrt(jnp.mean(value * value, axis=-1, keepdims=True) + epsilon)


def sigmoid_slope(raw, sig):
    return sig * (1.0 + raw * (1.0 - sig))


def per_device(
    tokens,
    lengths,
    w_in,
    w_forget,
    w_gate,
    w_out,
    attn_gain,
    mix_gain,
    bound_table,
    ff_gate,
    ff_up,
    ff_down,
    mlp_gain,
    out_grad,
):
    whole = lax.all_gather(tokens, "mp", axis=0, tiled=True)
    mixer = (
        lax.all_gather(w_in, "dp", axis=0, tiled=True),
        lax.all_gather(w_forget, "dp", axis=0, tiled=True),
        lax.all_gather(w_gate, "dp", axis=0, tiled=True),
        lax.all_gather(w_out, "dp", axis=0, tiled=True),
        lax.all_gather(attn_gain, "dp", axis=0, tiled=True),
        lax.all_gather(mix_gain, "dp", axis=0, tiled=True),
        lax.all_gather(bound_table, "dp", axis=1, tiled=True),
    )
    dense = (
        lax.all_gather(ff_gate, "dp", axis=0, tiled=True),
        lax.all_gather(ff_up, "dp", axis=0, tiled=True),
        lax.all_gather(ff_down, "dp", axis=1, tiled=True),
        lax.all_gather(mlp_gain, "dp", axis=0, tiled=True),
    )
    row_count = whole.shape[0]
    half_rows = row_count // lax.axis_size("mp")
    width = whole.shape[1]
    layer_rows = bound_table.shape[0]
    mp_index = lax.axis_index("mp")
    starts = jnp.cumsum(lengths) - lengths
    position = lax.axis_index("dp") * row_count + jnp.arange(row_count, dtype=jnp.int32)
    opening = jnp.any(position[:, None] == starts[None, :], axis=1)
    keep = (1.0 - opening.astype(jnp.float32))[:, None]
    table_f = mixer[6].astype(jnp.float32)
    soft = jax.nn.softmax(table_f, axis=0)
    bound = jnp.sum(soft[1 : LAYER + 1], axis=0)
    attn_g = mixer[4].astype(jnp.float32)
    mix_g = mixer[5].astype(jnp.float32)
    mlp_g = dense[3].astype(jnp.float32)
    tokens_wide = whole.astype(jnp.float32)
    inv_tokens = inverse_rms(tokens_wide)
    tokens_hat = tokens_wide * inv_tokens
    normed = (tokens_hat * attn_g).astype(jnp.bfloat16)
    inner = jnp.dot(normed, mixer[0], preferred_element_type=jnp.float32)
    forget_raw = jnp.dot(normed, mixer[1], preferred_element_type=jnp.float32)
    gate_raw = jnp.dot(normed, mixer[2], preferred_element_type=jnp.float32)
    sig_forget = jax.nn.sigmoid(forget_raw)
    forget = bound + (1.0 - bound) * sig_forget
    sig_inner = jax.nn.sigmoid(inner)
    silu_inner = inner * sig_inner
    drive = silu_inner * (1.0 - forget)
    decay = forget * keep
    decay_all, state_all = lax.associative_scan(combine, (decay, drive), axis=0)
    ones_vec = jnp.ones((width,), jnp.float32)
    zeros_vec = jnp.zeros((width,), jnp.float32)
    carry_in = entering(
        (decay_all[-1], state_all[-1]), "dp", combine, (ones_vec, zeros_vec), False
    )[1]
    states = decay_all * carry_in[None, :] + state_all
    inv_states = inverse_rms(states)
    states_hat = states * inv_states
    sig_gate = jax.nn.sigmoid(gate_raw)
    silu_gate = gate_raw * sig_gate
    mixed_in = (states_hat * mix_g * silu_gate).astype(jnp.bfloat16)
    resid = tokens_wide + jnp.dot(mixed_in, mixer[3], preferred_element_type=jnp.float32)
    inv_resid = inverse_rms(resid)
    resid_hat = resid * inv_resid
    hidden_in = (resid_hat * mlp_g).astype(jnp.bfloat16)
    gate_ff = jnp.dot(hidden_in, dense[0], preferred_element_type=jnp.float32)
    up_ff = jnp.dot(hidden_in, dense[1], preferred_element_type=jnp.float32)
    sig_ff = jax.nn.sigmoid(gate_ff)
    silu_ff = gate_ff * sig_ff
    act = (silu_ff * up_ff).astype(jnp.bfloat16)
    partial_out = jnp.dot(act, dense[2], preferred_element_type=jnp.float32)
    glu_out = lax.psum_scatter(
        partial_out.astype(jnp.bfloat16), "mp", scatter_dimension=0, tiled=True
    ).astype(jnp.float32)
    own_resid = lax.dynamic_slice_in_dim(resid, mp_index * half_rows, half_rows, 0)
    result = (own_resid + glu_out).astype(jnp.bfloat16)
    grad_whole = lax.all_gather(out_grad, "mp", axis=0, tiled=True)
    grad_wide = grad_whole.astype(jnp.float32)
    d_act = times_transposed(grad_whole, dense[2])
    grad_down = contract_rows(act, grad_whole)
    d_gate_ff = (d_act * up_ff * sigmoid_slope(gate_ff, sig_ff)).astype(jnp.bfloat16)
    d_up_ff = (d_act * silu_ff).astype(jnp.bfloat16)
    grad_gate_ff = contract_rows(hidden_in, d_gate_ff)
    grad_up_ff = contract_rows(hidden_in, d_up_ff)
    d_hidden_part = times_transposed(d_gate_ff, dense[0]) + times_transposed(d_up_ff, dense[1])
    d_hidden = lax.psum(d_hidden_part, "mp")
    grad_mlp = jnp.sum(d_hidden * resid_hat, axis=0)
    glu_grads = (
        lax.psum_scatter(grad_gate_ff, "dp", scatter_dimension=0, tiled=True),
        lax.psum_scatter(grad_up_ff, "dp", scatter_dimension=0, tiled=True),
        lax.psum_scatter(grad_down, "dp", scatter_dimension=1, tiled=True),
        lax.psum_scatter(grad_mlp, "dp", scatter_dimension=0, tiled=True),
    )
    scaled_hidden = d_hidden * mlp_g
    d_resid = grad_wide + inv_resid * (
        scaled_hidden - resid_hat * jnp.mean(scaled_hidden * resid_hat, axis=-1, keepdims=True)
    )
    d_mixed = d_resid.astype(jnp.bfloat16)
    grad_out = contract_rows(mixed_in, d_mixed)
    d_mixin = times_transposed(d_mixed, mixer[3])
    grad_mix = jnp.sum(d_mixin * states_hat * silu_gate, axis=0)
    d_gate_raw = (d_mixin * states_hat * mix_g * sigmoid_slope(gate_raw, sig_gate)).astype(
        jnp.bfloat16
    )
    scaled_states = d_mixin * mix_g * silu_gate
    d_states = inv_states * (
        scaled_states - states_hat * jnp.mean(scaled_states * states_hat, axis=-1, keepdims=True)
    )
    decay_next = jnp.concatenate([decay[1:], jnp.ones((1, width), jnp.float32)], axis=0)
    tail_all, adjoint_local = lax.associative_scan(
        combine, (decay_next, d_states), reverse=True, axis=0
    )
    first_decay = decay[0]
    incoming = entering(
        (first_decay * tail_all[0], first_decay * adjoint_local[0]),
        "dp",
        combine,
        (ones_vec, zeros_vec),
        True,
    )[1]
    adjoint = adjoint_local + tail_all * incoming[None, :]
    prev_states = jnp.concatenate([carry_in[None, :], states[:-1]], axis=0)
    d_forget = adjoint * prev_states * keep - adjoint * silu_inner
    d_inner = (adjoint * (1.0 - forget) * sigmoid_slope(inner, sig_inner)).astype(jnp.bfloat16)
    d_forget_raw = (d_forget * (1.0 - bound) * sig_forget * (1.0 - sig_forget)).astype(jnp.bfloat16)
    d_bound = jnp.sum(d_forget * (1.0 - sig_forget), axis=0)
    row_ids = jnp.arange(layer_rows)[:, None]
    member = jnp.logical_and(row_ids >= 1, row_ids <= LAYER).astype(jnp.float32)
    grad_table = soft * (member - bound[None, :]) * d_bound[None, :]
    grad_in = contract_rows(normed, d_inner)
    grad_forget = contract_rows(normed, d_forget_raw)
    grad_gate = contract_rows(normed, d_gate_raw)
    d_normed = (
        times_transposed(d_inner, mixer[0])
        + times_transposed(d_forget_raw, mixer[1])
        + times_transposed(d_gate_raw, mixer[2])
    )
    grad_attn = jnp.sum(d_normed * tokens_hat, axis=0)
    scaled_normed = d_normed * attn_g
    d_tokens = d_resid + inv_tokens * (
        scaled_normed - tokens_hat * jnp.mean(scaled_normed * tokens_hat, axis=-1, keepdims=True)
    )
    token_grad = lax.dynamic_slice_in_dim(d_tokens, mp_index * half_rows, half_rows, 0)
    mixer_grads = (
        lax.psum_scatter(grad_in, "dp", scatter_dimension=0, tiled=True),
        lax.psum_scatter(grad_forget, "dp", scatter_dimension=0, tiled=True),
        lax.psum_scatter(grad_gate, "dp", scatter_dimension=0, tiled=True),
        lax.psum_scatter(grad_out, "dp", scatter_dimension=0, tiled=True),
        lax.psum_scatter(grad_attn, "dp", scatter_dimension=0, tiled=True),
        lax.psum_scatter(grad_mix, "dp", scatter_dimension=0, tiled=True),
        lax.psum_scatter(grad_table, "dp", scatter_dimension=1, tiled=True),
    )
    return (
        result,
        token_grad,
        mixer_grads[0],
        mixer_grads[1],
        mixer_grads[2],
        mixer_grads[3],
        mixer_grads[4],
        mixer_grads[5],
        mixer_grads[6],
        glu_grads[0],
        glu_grads[1],
        glu_grads[2],
        glu_grads[3],
    )


def solution(mesh):
    return jax.shard_map(
        per_device,
        mesh=mesh,
        in_specs=(
            P(("dp", "mp"), None),
            P(),
            P("dp", None),
            P("dp", None),
            P("dp", None),
            P("dp", None),
            P("dp"),
            P("dp"),
            P(None, "dp"),
            P("dp", "mp"),
            P("dp", "mp"),
            P("mp", "dp"),
            P("dp"),
            P(("dp", "mp"), None),
        ),
        out_specs=(
            P(("dp", "mp"), None),
            P(("dp", "mp"), None),
            P("dp", None),
            P("dp", None),
            P("dp", None),
            P("dp", None),
            P("dp"),
            P("dp"),
            P(None, "dp"),
            P("dp", "mp"),
            P("dp", "mp"),
            P("mp", "dp"),
            P("dp"),
        ),
        check_vma=False,
    )
```

profile of v0, /device:TPU:0, one launch (start us, length us, event | category | flops | bytes accessed | tf_op | source)
XLA Modules:
  0.0 2431.6 jit_solution(4686550156488616628)
XLA Ops:
  11.9 10.2 all_gather.53
  22.3 22.1 all-gather
  44.5 18.7 all_gather.54
  66.2 18.7 all-gather.3
  85.5 17.7 all-gather.4
  103.8 10.7 all_gather.67
  119.3 44.6 %all-gather.15.cloned.1.call-done = bf16[2048,2048]{1,0:T(8,128)(2,1)} async-done(((bf16[128,2048]{1,0:T(8,128)(2,1)}), bf16[2048,2048]{1,0:T(8,128)(2,1)}) %all-gather.15.cloned.1.call-update) | async-done | bytes 8388624 | tf_op jit(solution)/shard_map/all_gather | solution.py:72
  163.9 6.4 fusion.9
  241.0 19.5 all-gather.2
  270.6 18.4 all-gather.1
  298.7 16.7 all-gather.21.cloned.1.call-done
  320.3 90.0 %all-gather.23.cloned.1.call-done = bf16[2048,2816]{1,0:T(8,128)(2,1)} async-done(((bf16[128,2816]{1,0:T(8,128)(2,1)}), bf16[2048,2816]{1,0:T(8,128)(2,1)}) %all-gather.23.cloned.1.call-update) | async-done | bytes 11534352 | tf_op jit(solution)/shard_map/all_gather | solution.py:80
  410.4 7.0 fusion.58
  417.4 87.6 %all-gather.25.cloned.1.call-done = bf16[2048,2816]{1,0:T(8,128)(2,1)} async-done(((bf16[128,2816]{1,0:T(8,128)(2,1)}), bf16[2048,2816]{1,0:T(8,128)(2,1)}) %all-gather.25.cloned.1.call-update) | async-done | bytes 11534352 | tf_op jit(solution)/shard_map/all_gather | solution.py:81
  505.0 7.0 fusion.59
  512.1 90.7 %all-gather.27.cloned.1.call-done = bf16[2816,2048]{1,0:T(8,128)(2,1)} async-done(((bf16[2816,128]{1,0:T(8,128)(2,1)}), bf16[2816,2048]{1,0:T(8,128)(2,1)}) %all-gather.27.cloned.1.call-update) | async-done | bytes 11534352 | tf_op jit(solution)/shard_map/all_gather | solution.py:82
  602.8 10.3 multiply_convert_fusion
  613.9 8.2 fusion.60
  639.9 8.3 slice.514
  648.2 8.3 slice.521
  656.5 8.3 slice.512
  664.7 7.0 convolution_convert_fusion
  676.6 8.3 multiply_reduce_fusion.2
  692.8 8.2 slice.516
  701.1 8.2 slice.518
  837.1 8.3 slice.566
  867.1 19.5 all-gather.5
  891.4 18.2 all-gather.6
  914.5 13.9 while.29
  928.5 8.9 rev.15
  937.4 8.9 rev.14
  953.7 9.0 fusion.38
  963.8 8.4 fusion.39
  973.4 9.2 fusion.15
  982.7 9.2 fusion.37
  992.2 10.5 fusion.62
  1002.9 10.5 fusion.63
  1014.4 14.7 fusion.64
  1031.1 7.8 fusion.61
  1039.0 6.5 convolution_add_fusion.2
  1049.7 63.0 %all-reduce.61 = (f32[2048]{0:T(1024)S(1)}, f32[2048]{0:T(1024)S(1)}, f32[2048]{0:T(1024)S(1)}) all-reduce(f32[2048]{0:T(1024)S(1)} %get-tuple-element.243, f32[2048]{0:T(1024)S(1)} %copy-done.36, f32[2048]{0:T(1024)S(1)} %copy-done.28), channel_id=7, replica_groups=mesh['dp'=16,'mp'=2] {'dp'}, use_global_device_ids=true, to_apply=%region_22.23.clone | all-reduce | flops 6144 | bytes 49152
  1118.4 68.2 %reduce-scatter.14.cloned.1.call-done = f32[128,2048]{1,0:T(8,128)} async-done(((f32[2048,2048]{1,0:T(8,128)}), f32[128,2048]{1,0:T(8,128)}) %reduce-scatter.14.cloned.1.call-update) | async-done | bytes 1048592 | tf_op jit(solution)/shard_map/reduce_scatter | solution.py:209
  1186.6 182.1 %reduce-scatter.12.cloned.1.call-done = f32[128,2048]{1,0:T(8,128)} async-done(((f32[2048,2048]{1,0:T(8,128)}), f32[128,2048]{1,0:T(8,128)}) %reduce-scatter.12.cloned.1.call-update) | async-done | bytes 1048592 | tf_op jit(solution)/shard_map/reduce_scatter | solution.py:208
  1368.7 182.3 %reduce-scatter.18.cloned.1.call-done = f32[128,2048]{1,0:T(8,128)} async-done(((f32[2048,2048]{1,0:T(8,128)}), f32[128,2048]{1,0:T(8,128)}) %reduce-scatter.18.cloned.1.call-update) | async-done | bytes 1048592 | tf_op jit(solution)/shard_map/reduce_scatter | solution.py:211
  1551.0 182.1 %reduce-scatter.16.cloned.1.call-done = f32[128,2048]{1,0:T(8,128)} async-done(((f32[2048,2048]{1,0:T(8,128)}), f32[128,2048]{1,0:T(8,128)}) %reduce-scatter.16.cloned.1.call-update) | async-done | bytes 1048592 | tf_op jit(solution)/shard_map/reduce_scatter | solution.py:210
  1733.1 230.4 %reduce-scatter.22.cloned.1.call-done = f32[128,2816]{1,0:T(8,128)} async-done(((f32[2048,2816]{1,0:T(8,128)}), f32[128,2816]{1,0:T(8,128)}) %reduce-scatter.22.cloned.1.call-update) | async-done | bytes 1441808 | tf_op jit(solution)/shard_map/reduce_scatter | solution.py:152
  1963.5 230.6 %reduce-scatter.24.cloned.1.call-done = f32[128,2816]{1,0:T(8,128)} async-done(((f32[2048,2816]{1,0:T(8,128)}), f32[128,2816]{1,0:T(8,128)}) %reduce-scatter.24.cloned.1.call-update) | async-done | bytes 1441808 | tf_op jit(solution)/shard_map/reduce_scatter | solution.py:153
  2194.1 230.5 %reduce-scatter.26.cloned.1.call-done = f32[2816,128]{1,0:T(8,128)} async-done(((f32[2816,2048]{1,0:T(8,128)}), f32[2816,128]{1,0:T(8,128)}) %reduce-scatter.26.cloned.1.call-update) | async-done | bytes 1441808 | tf_op jit(solution)/shard_map/reduce_scatter | solution.py:154
  (457 shorter events, 335.5 us)
Async XLA Ops:
  7.2 107.3 %all-gather.17.cloned.1.call-start = ((), (), s32[]{:S(2)}) async-start(), calls=%async_computation.10 | async-start | bytes 8912896 | tf_op jit(solution)/shard_map/all_gather | solution.py:71
  7.9 156.0 %all-gather.15.cloned.1.call-start = ((), (), s32[]{:S(2)}) async-start(), calls=%async_computation.9 | async-start | bytes 8912896 | tf_op jit(solution)/shard_map/all_gather | solution.py:72
  8.7 284.0 %all-gather.19.cloned.1.call-start = ((), (), s32[]{:S(2)}) async-start(), calls=%async_computation.11 | async-start | bytes 8912896 | tf_op jit(solution)/shard_map/all_gather | solution.py:73
  9.4 306.0 %all-gather.21.cloned.1.call-start = ((), (), s32[]{:S(2)}) async-start(), calls=%async_computation.12 | async-start | bytes 8912896 | tf_op jit(solution)/shard_map/all_gather | solution.py:74
  10.0 400.4 %all-gather.23.cloned.1.call-start = ((), (), s32[]{:S(2)}) async-start(), calls=%async_computation.13 | async-start | bytes 12255232 | tf_op jit(solution)/shard_map/all_gather | solution.py:80
  10.6 494.5 %all-gather.25.cloned.1.call-start = ((), (), s32[]{:S(2)}) async-start(), calls=%async_computation.14 | async-start | bytes 12255232 | tf_op jit(solution)/shard_map/all_gather | solution.py:81
  11.1 591.6 %all-gather.27.cloned.1.call-start = ((), (), s32[]{:S(2)}) async-start(), calls=%async_computation.15 | async-start | bytes 12255232 | tf_op jit(solution)/shard_map/all_gather | solution.py:82
  11.9 659.9 %all-reduce.64.cloned.1.call-start = ((), (), s32[]{:S(2)}) async-start(), calls=%async_computation.17 | async-start | bytes 2097152 | tf_op jit(solution)/shard_map/psum | solution.py:149
  22.3 141.6 %copy-start.25 = (f32[128]{0:T(128)}, f32[128]{0:T(128)S(1)}, u32[]{:S(2)}) copy-start(f32[128]{0:T(128)S(1)} %add_rsqrt_fusion.2) | copy-start | bytes 1540
  64.5 99.4 %copy-start.18 = (f32[2048]{0:T(1024)}, f32[2048]{0:T(1024)S(1)}, u32[]{:S(2)}) copy-start(f32[2048]{0:T(1024)S(1)} %slice_reduce_fusion) | copy-start | bytes 24580
  64.5 99.4 %copy-start.22 = (f32[2048]{0:T(1024)}, f32[2048]{0:T(1024)S(1)}, u32[]{:S(2)}) copy-start(f32[2048]{0:T(1024)S(1)} %broadcast_subtract_fusion) | copy-start | bytes 24580
  66.2 97.7 %copy-start.37 = (f32[128]{0:T(128)}, f32[128]{0:T(128)S(1)}, u32[]{:S(2)}) copy-start(f32[128]{0:T(128)S(1)} %convert_subtract_fusion) | copy-start | bytes 1540
  119.3 51.0 %copy-start.10 = (f32[128,2048]{1,0:T(8,128)}, f32[128,2048]{1,0:T(8,128)S(1)}, u32[]{:S(2)}) copy-start(f32[128,2048]{1,0:T(8,128)S(1)} %fusion.41) | copy-start | bytes 3145732
  170.3 51.7 %copy-start = (f32[128,2048]{1,0:T(8,128)}, f32[128,2048]{1,0:T(8,128)S(1)}, u32[]{:S(2)}) copy-start(f32[128,2048]{1,0:T(8,128)S(1)} %get-tuple-element.282) | copy-start | bytes 3145732
  213.5 17.0 copy-start.35
  215.1 15.7 copy-start.16
  215.7 15.2 copy-start.32
  231.0 29.5 %copy-start.30 = (f32[1,2048]{1,0:T(1,128)S(1)}, f32[1,2048]{1,0:T(1,128)}, u32[]{:S(2)}) copy-start(f32[1,2048]{1,0:T(1,128)} %slice.583) | copy-start | bytes 24580
  234.9 57.8 %copy-start.26 = (f32[128]{0:T(128)S(1)}, f32[128]{0:T(128)}, u32[]{:S(2)}) copy-start(f32[128]{0:T(128)} %copy-done.25) | copy-start | bytes 1540
  234.9 57.8 %copy-start.29 = (f32[16,1,128]{2,1,0:T(1,128)S(1)}, f32[16,1,128]{2,1,0:T(1,128)}, u32[]{:S(2)}) copy-start(f32[16,1,128]{2,1,0:T(1,128)} %convert_element_type.94) | copy-start | bytes 24580
  237.1 53.3 %copy-start.8 = (f32[128,2048]{1,0:T(8,128)S(1)}, f32[128,2048]{1,0:T(8,128)}, u32[]{:S(2)}) copy-start(f32[128,2048]{1,0:T(8,128)} %pad.201) | copy-start | bytes 3145732
  240.0 50.4 %copy-start.9 = (f32[128,2048]{1,0:T(8,128)}, f32[128,2048]{1,0:T(8,128)S(1)}, u32[]{:S(2)}) copy-start(f32[128,2048]{1,0:T(8,128)S(1)} %pad.200) | copy-start | bytes 3145732
  298.7 21.5 copy-start.11
  298.7 21.5 copy-start.17
  602.8 19.4 slice-start
  602.8 19.4 slice-start.1
  613.1 9.1 copy-start.12
  613.9 8.2 slice-start.2
  627.1 487.4 %reduce-scatter.10.cloned.1.call-start = ((), (), s32[]{:S(2)}) async-start(), calls=%async_computation.16 | async-start | bytes 786432 | tf_op jit(solution)/shard_map/reduce_scatter | solution.py:135
  671.7 446.6 %reduce-scatter.20.cloned.1.call-start = ((), (), s32[]{:S(2)}) async-start(), calls=%async_computation.22 | async-start | bytes 208896 | tf_op jit(solution)/shard_map/reduce_scatter | solution.py:214
  675.7 9.2 copy-start.15
  777.4 36.8 %copy-start.34 = (f32[1,2048]{1,0:T(1,128)S(1)}, f32[1,2048]{1,0:T(1,128)}, u32[]{:S(2)}) copy-start(f32[1,2048]{1,0:T(1,128)} %slice.653) | copy-start | bytes 24580
  777.4 47.8 %copy-start.33 = (f32[1,2048]{1,0:T(1,128)S(1)}, f32[1,2048]{1,0:T(1,128)}, u32[]{:S(2)}) copy-start(f32[1,2048]{1,0:T(1,128)} %slice.631) | copy-start | bytes 24580
  849.1 97.1 %copy-start.19 = (f32[2048]{0:T(1024)S(1)}, f32[2048]{0:T(1024)}, u32[]{:S(2)}) copy-start(f32[2048]{0:T(1024)} %copy-done.18) | copy-start | bytes 24580
  849.1 97.1 %copy-start.23 = (f32[2048]{0:T(1024)S(1)}, f32[2048]{0:T(1024)}, u32[]{:S(2)}) copy-start(f32[2048]{0:T(1024)} %copy-done.22) | copy-start | bytes 24580
  862.8 87.6 %copy-start.21 = (f32[2048]{0:T(1024)S(1)}, f32[2048]{0:T(1024)}, u32[]{:S(2)}) copy-start(f32[2048]{0:T(1024)} %copy-done.20) | copy-start | bytes 24580
  953.7 9.1 copy-start.6
  953.7 232.9 %reduce-scatter.14.cloned.1.call-start = ((), (), s32[]{:S(2)}) async-start(), calls=%async_computation.19 | async-start | bytes 17825792 | tf_op jit(solution)/shard_map/reduce_scatter | solution.py:209
  962.8 405.9 %reduce-scatter.12.cloned.1.call-start = ((), (), s32[]{:S(2)}) async-start(), calls=%async_computation.18 | async-start | bytes 17825792 | tf_op jit(solution)/shard_map/reduce_scatter | solution.py:208
  972.2 578.8 %reduce-scatter.18.cloned.1.call-start = ((), (), s32[]{:S(2)}) async-start(), calls=%async_computation.21 | async-start | bytes 17825792 | tf_op jit(solution)/shard_map/reduce_scatter | solution.py:211
  982.6 750.5 %reduce-scatter.16.cloned.1.call-start = ((), (), s32[]{:S(2)}) async-start(), calls=%async_computation.20 | async-start | bytes 17825792 | tf_op jit(solution)/shard_map/reduce_scatter | solution.py:210
  991.9 971.6 %reduce-scatter.22.cloned.1.call-start = ((), (), s32[]{:S(2)}) async-start(), calls=%async_computation.23 | async-start | bytes 24510464 | tf_op jit(solution)/shard_map/reduce_scatter | solution.py:152
  1002.8 1191.3 %reduce-scatter.24.cloned.1.call-start = ((), (), s32[]{:S(2)}) async-start(), calls=%async_computation.24 | async-start | bytes 24510464 | tf_op jit(solution)/shard_map/reduce_scatter | solution.py:153
  1013.4 1411.2 %reduce-scatter.26.cloned.1.call-start = ((), (), s32[]{:S(2)}) async-start(), calls=%async_computation.25 | async-start | bytes 24510464 | tf_op jit(solution)/shard_map/reduce_scatter | solution.py:154
  1031.1 7.9 copy-start.7
  1031.1 14.3 slice-start.3
  1031.1 14.3 copy-start.14
  1039.0 6.5 slice-start.4
  (13 other events, 24.7 us)
Sparse Core Ops, SparseCore 0:
  10.2 77.9 all-gather.16
  90.3 73.4 all-gather.14
  166.0 73.1 all-gather.18
  241.2 74.0 all-gather.20
  317.5 92.8 all-gather.22
  412.5 92.4 all-gather.24
  507.2 95.5 all-gather.26
  627.2 38.2 all-reduce.63
  671.9 12.7 reduce-scatter.9
  953.8 51.4 reduce-scatter.19
  1010.0 176.5 reduce-scatter.13
  1191.1 177.5 reduce-scatter.11
  1373.4 177.5 reduce-scatter.17
  1555.5 177.5 reduce-scatter.15
  1737.6 225.8 reduce-scatter.21
  1968.1 225.9 reduce-scatter.23
  2198.6 225.9 reduce-scatter.25
where the time goes:
time: 2450 us; the launch traced here: 2430 us
  waiting for transfers between devices  1640 us (67%)
  local copies, waits for them, and re-layouts  276 us (11%)
  blocking collectives  237 us (10%)
  matrix products  165 us (7%)
  other arithmetic  95 us (4%)
    reduce_scatter x1, waiting for transfers between devices, per_device(): lax.psum_scatter(grad_up_ff, 'dp', scatter_dimension=0, tiled=True)  231 us
    reduce_scatter x1, waiting for transfers between devices, per_device(): lax.psum_scatter(grad_down, 'dp', scatter_dimension=1, tiled=True)  230 us
    reduce_scatter x1, waiting for transfers between devices, per_device(): lax.psum_scatter(grad_gate_ff, 'dp', scatter_dimension=0, tiled=True)  230 us
    reduce_scatter x1, waiting for transfers between devices, per_device(): lax.psum_scatter(grad_out, 'dp', scatter_dimension=0, tiled=True)  182 us
    reduce_scatter x1, waiting for transfers between devices, per_device(): lax.psum_scatter(grad_gate, 'dp', scatter_dimension=0, tiled=True)  182 us
    reduce_scatter x1, waiting for transfers between devices, per_device(): lax.psum_scatter(grad_in, 'dp', scatter_dimension=0, tiled=True)  182 us
    slice x49, local copies, waits for them, and re-layouts, per_device(): lax.associative_scan(combine, (decay_next, d_states), reverse=True, axis=0)  121 us
    all_gather x1, waiting for transfers between devices, per_device(): lax.all_gather(ff_down, 'dp', axis=1, tiled=True)  90.7 us
  transfers between devices with their start and end apart: 17, of which 12 were waited for; matrix products, arithmetic and copies ran while one was open for 21% of the time, Pallas kernels for 0%

commit v1 on v0

--- a/solution.py
+++ b/solution.py
@@ -87,7 +87,8 @@
     width = whole.shape[1]
     layer_rows = bound_table.shape[0]
     mp_index = lax.axis_index("mp")
-    starts = jnp.cumsum(lengths) - lengths
+    slot = jnp.arange(lengths.shape[0])
+    starts = jnp.sum(jnp.where(slot[None, :] < slot[:, None], lengths[None, :], 0), axis=1)
     position = lax.axis_index("dp") * row_count + jnp.arange(row_count, dtype=jnp.int32)
     opening = jnp.any(position[:, None] == starts[None, :], axis=1)
     keep = (1.0 - opening.astype(jnp.float32))[:, None]

time: 2450 us -> 2450 us (level)
  no operation moved by 1% of the time
where the time goes in v1:
time: 2450 us; the launch traced here: 2430 us
  waiting for transfers between devices  1640 us (67%)
  local copies, waits for them, and re-layouts  275 us (11%)
  blocking collectives  237 us (10%)
  matrix products  165 us (7%)
  other arithmetic  94.9 us (4%)
    reduce_scatter x1, waiting for transfers between devices, per_device(): lax.psum_scatter(grad_up_ff, 'dp', scatter_dimension=0, tiled=True)  231 us
    reduce_scatter x1, waiting for transfers between devices, per_device(): lax.psum_scatter(grad_down, 'dp', scatter_dimension=1, tiled=True)  231 us
    reduce_scatter x1, waiting for transfers between devices, per_device(): lax.psum_scatter(grad_gate_ff, 'dp', scatter_dimension=0, tiled=True)  230 us
    reduce_scatter x1, waiting for transfers between devices, per_device(): lax.psum_scatter(grad_out, 'dp', scatter_dimension=0, tiled=True)  182 us
    reduce_scatter x1, waiting for transfers between devices, per_device(): lax.psum_scatter(grad_in, 'dp', scatter_dimension=0, tiled=True)  182 us
    reduce_scatter x1, waiting for transfers between devices, per_device(): lax.psum_scatter(grad_gate, 'dp', scatter_dimension=0, tiled=True)  182 us
    slice x49, local copies, waits for them, and re-layouts, per_device(): lax.associative_scan(combine, (decay_next, d_states), reverse=True, axis=0)  121 us
    all_gather x1, waiting for transfers between devices, per_device(): lax.all_gather(ff_down, 'dp', axis=1, tiled=True)  90.7 us
  transfers between devices with their start and end apart: 17, of which 12 were waited for; matrix products, arithmetic and copies ran while one was open for 21% of the time, Pallas kernels for 0%

profile of v1, /device:TPU:0, one launch (start us, length us, event | category | flops | bytes accessed | tf_op | source)
XLA Modules:
  0.0 2431.7 jit_solution(10572672677253559393)
XLA Ops:
  11.9 10.2 all_gather.53
  22.3 22.1 all-gather
  44.5 18.7 all_gather.54
  65.4 18.7 all-gather.3
  84.7 17.8 all-gather.4
  103.1 10.5 all_gather.67
  118.4 45.5 %all-gather.15.cloned.1.call-done = bf16[2048,2048]{1,0:T(8,128)(2,1)} async-done(((bf16[128,2048]{1,0:T(8,128)(2,1)}), bf16[2048,2048]{1,0:T(8,128)(2,1)}) %all-gather.15.cloned.1.call-update) | async-done | bytes 8388624 | tf_op jit(solution)/shard_map/all_gather | solution.py:72
  163.9 6.4 fusion.9
  241.0 19.5 all-gather.2
  270.6 18.3 all-gather.1
  298.7 16.7 all-gather.21.cloned.1.call-done
  320.4 90.0 %all-gather.23.cloned.1.call-done = bf16[2048,2816]{1,0:T(8,128)(2,1)} async-done(((bf16[128,2816]{1,0:T(8,128)(2,1)}), bf16[2048,2816]{1,0:T(8,128)(2,1)}) %all-gather.23.cloned.1.call-update) | async-done | bytes 11534352 | tf_op jit(solution)/shard_map/all_gather | solution.py:80
  410.4 7.0 fusion.58
  417.4 87.6 %all-gather.25.cloned.1.call-done = bf16[2048,2816]{1,0:T(8,128)(2,1)} async-done(((bf16[128,2816]{1,0:T(8,128)(2,1)}), bf16[2048,2816]{1,0:T(8,128)(2,1)}) %all-gather.25.cloned.1.call-update) | async-done | bytes 11534352 | tf_op jit(solution)/shard_map/all_gather | solution.py:81
  505.0 7.0 fusion.59
  512.1 90.7 %all-gather.27.cloned.1.call-done = bf16[2816,2048]{1,0:T(8,128)(2,1)} async-done(((bf16[2816,128]{1,0:T(8,128)(2,1)}), bf16[2816,2048]{1,0:T(8,128)(2,1)}) %all-gather.27.cloned.1.call-update) | async-done | bytes 11534352 | tf_op jit(solution)/shard_map/all_gather | solution.py:82
  602.8 10.3 multiply_convert_fusion
  614.0 8.2 fusion.60
  640.0 8.3 slice.514
  648.2 8.3 slice.521
  656.5 8.3 slice.512
  664.8 7.0 convolution_convert_fusion
  676.7 8.2 multiply_reduce_fusion.2
  692.8 8.3 slice.516
  701.1 8.3 slice.518
  837.1 8.3 slice.566
  867.0 19.5 all-gather.5
  891.4 18.2 all-gather.6
  914.5 13.9 while.29
  928.4 8.9 rev.15
  937.3 8.9 rev.14
  953.7 9.0 fusion.38
  963.7 8.3 fusion.39
  973.3 9.2 fusion.15
  982.6 9.2 fusion.37
  992.2 10.5 fusion.62
  1002.8 10.5 fusion.63
  1014.3 14.7 fusion.64
  1031.0 7.8 fusion.61
  1038.9 6.5 convolution_add_fusion.2
  1049.6 63.2 %all-reduce.61 = (f32[2048]{0:T(1024)S(1)}, f32[2048]{0:T(1024)S(1)}, f32[2048]{0:T(1024)S(1)}) all-reduce(f32[2048]{0:T(1024)S(1)} %get-tuple-element.243, f32[2048]{0:T(1024)S(1)} %copy-done.36, f32[2048]{0:T(1024)S(1)} %copy-done.28), channel_id=7, replica_groups=mesh['dp'=16,'mp'=2] {'dp'}, use_global_device_ids=true, to_apply=%region_22.23.clone | all-reduce | flops 6144 | bytes 49152
  1118.5 68.1 %reduce-scatter.14.cloned.1.call-done = f32[128,2048]{1,0:T(8,128)} async-done(((f32[2048,2048]{1,0:T(8,128)}), f32[128,2048]{1,0:T(8,128)}) %reduce-scatter.14.cloned.1.call-update) | async-done | bytes 1048592 | tf_op jit(solution)/shard_map/reduce_scatter | solution.py:210
  1186.6 182.2 %reduce-scatter.12.cloned.1.call-done = f32[128,2048]{1,0:T(8,128)} async-done(((f32[2048,2048]{1,0:T(8,128)}), f32[128,2048]{1,0:T(8,128)}) %reduce-scatter.12.cloned.1.call-update) | async-done | bytes 1048592 | tf_op jit(solution)/shard_map/reduce_scatter | solution.py:209
  1368.8 182.3 %reduce-scatter.18.cloned.1.call-done = f32[128,2048]{1,0:T(8,128)} async-done(((f32[2048,2048]{1,0:T(8,128)}), f32[128,2048]{1,0:T(8,128)}) %reduce-scatter.18.cloned.1.call-update) | async-done | bytes 1048592 | tf_op jit(solution)/shard_map/reduce_scatter | solution.py:212
  1551.1 182.1 %reduce-scatter.16.cloned.1.call-done = f32[128,2048]{1,0:T(8,128)} async-done(((f32[2048,2048]{1,0:T(8,128)}), f32[128,2048]{1,0:T(8,128)}) %reduce-scatter.16.cloned.1.call-update) | async-done | bytes 1048592 | tf_op jit(solution)/shard_map/reduce_scatter | solution.py:211
  1733.2 230.4 %reduce-scatter.22.cloned.1.call-done = f32[128,2816]{1,0:T(8,128)} async-done(((f32[2048,2816]{1,0:T(8,128)}), f32[128,2816]{1,0:T(8,128)}) %reduce-scatter.22.cloned.1.call-update) | async-done | bytes 1441808 | tf_op jit(solution)/shard_map/reduce_scatter | solution.py:153
  1963.6 230.5 %reduce-scatter.24.cloned.1.call-done = f32[128,2816]{1,0:T(8,128)} async-done(((f32[2048,2816]{1,0:T(8,128)}), f32[128,2816]{1,0:T(8,128)}) %reduce-scatter.24.cloned.1.call-update) | async-done | bytes 1441808 | tf_op jit(solution)/shard_map/reduce_scatter | solution.py:154
  2194.2 230.5 %reduce-scatter.26.cloned.1.call-done = f32[2816,128]{1,0:T(8,128)} async-done(((f32[2816,2048]{1,0:T(8,128)}), f32[2816,128]{1,0:T(8,128)}) %reduce-scatter.26.cloned.1.call-update) | async-done | bytes 1441808 | tf_op jit(solution)/shard_map/reduce_scatter | solution.py:155
  (454 shorter events, 334.5 us)
Async XLA Ops:
  7.2 106.5 %all-gather.17.cloned.1.call-start = ((), (), s32[]{:S(2)}) async-start(), calls=%async_computation.10 | async-start | bytes 8912896 | tf_op jit(solution)/shard_map/all_gather | solution.py:71
  7.9 156.0 %all-gather.15.cloned.1.call-start = ((), (), s32[]{:S(2)}) async-start(), calls=%async_computation.9 | async-start | bytes 8912896 | tf_op jit(solution)/shard_map/all_gather | solution.py:72
  8.7 284.0 %all-gather.19.cloned.1.call-start = ((), (), s32[]{:S(2)}) async-start(), calls=%async_computation.11 | async-start | bytes 8912896 | tf_op jit(solution)/shard_map/all_gather | solution.py:73
  9.4 306.0 %all-gather.21.cloned.1.call-start = ((), (), s32[]{:S(2)}) async-start(), calls=%async_computation.12 | async-start | bytes 8912896 | tf_op jit(solution)/shard_map/all_gather | solution.py:74
  10.0 400.4 %all-gather.23.cloned.1.call-start = ((), (), s32[]{:S(2)}) async-start(), calls=%async_computation.13 | async-start | bytes 12255232 | tf_op jit(solution)/shard_map/all_gather | solution.py:80
  10.6 494.5 %all-gather.25.cloned.1.call-start = ((), (), s32[]{:S(2)}) async-start(), calls=%async_computation.14 | async-start | bytes 12255232 | tf_op jit(solution)/shard_map/all_gather | solution.py:81
  11.1 591.6 %all-gather.27.cloned.1.call-start = ((), (), s32[]{:S(2)}) async-start(), calls=%async_computation.15 | async-start | bytes 12255232 | tf_op jit(solution)/shard_map/all_gather | solution.py:82
  11.9 660.0 %all-reduce.64.cloned.1.call-start = ((), (), s32[]{:S(2)}) async-start(), calls=%async_computation.17 | async-start | bytes 2097152 | tf_op jit(solution)/shard_map/psum | solution.py:150
  22.3 141.6 %copy-start.25 = (f32[128]{0:T(128)}, f32[128]{0:T(128)S(1)}, u32[]{:S(2)}) copy-start(f32[128]{0:T(128)S(1)} %add_rsqrt_fusion.2) | copy-start | bytes 1540
  64.5 99.4 %copy-start.18 = (f32[2048]{0:T(1024)}, f32[2048]{0:T(1024)S(1)}, u32[]{:S(2)}) copy-start(f32[2048]{0:T(1024)S(1)} %slice_reduce_fusion) | copy-start | bytes 24580
  64.5 99.4 %copy-start.22 = (f32[2048]{0:T(1024)}, f32[2048]{0:T(1024)S(1)}, u32[]{:S(2)}) copy-start(f32[2048]{0:T(1024)S(1)} %broadcast_subtract_fusion) | copy-start | bytes 24580
  65.4 98.5 %copy-start.37 = (f32[128]{0:T(128)}, f32[128]{0:T(128)S(1)}, u32[]{:S(2)}) copy-start(f32[128]{0:T(128)S(1)} %convert_subtract_fusion) | copy-start | bytes 1540
  118.4 51.9 %copy-start.10 = (f32[128,2048]{1,0:T(8,128)}, f32[128,2048]{1,0:T(8,128)S(1)}, u32[]{:S(2)}) copy-start(f32[128,2048]{1,0:T(8,128)S(1)} %fusion.41) | copy-start | bytes 3145732
  170.3 51.7 %copy-start = (f32[128,2048]{1,0:T(8,128)}, f32[128,2048]{1,0:T(8,128)S(1)}, u32[]{:S(2)}) copy-start(f32[128,2048]{1,0:T(8,128)S(1)} %get-tuple-element.282) | copy-start | bytes 3145732
  213.5 17.0 copy-start.35
  215.2 15.7 copy-start.16
  215.8 15.2 copy-start.32
  231.0 29.5 %copy-start.30 = (f32[1,2048]{1,0:T(1,128)S(1)}, f32[1,2048]{1,0:T(1,128)}, u32[]{:S(2)}) copy-start(f32[1,2048]{1,0:T(1,128)} %slice.583) | copy-start | bytes 24580
  234.9 57.8 %copy-start.26 = (f32[128]{0:T(128)S(1)}, f32[128]{0:T(128)}, u32[]{:S(2)}) copy-start(f32[128]{0:T(128)} %copy-done.25) | copy-start | bytes 1540
  234.9 57.8 %copy-start.29 = (f32[16,1,128]{2,1,0:T(1,128)S(1)}, f32[16,1,128]{2,1,0:T(1,128)}, u32[]{:S(2)}) copy-start(f32[16,1,128]{2,1,0:T(1,128)} %convert_element_type.94) | copy-start | bytes 24580
  237.1 53.3 %copy-start.8 = (f32[128,2048]{1,0:T(8,128)S(1)}, f32[128,2048]{1,0:T(8,128)}, u32[]{:S(2)}) copy-start(f32[128,2048]{1,0:T(8,128)} %pad.201) | copy-start | bytes 3145732
  240.0 50.4 %copy-start.9 = (f32[128,2048]{1,0:T(8,128)}, f32[128,2048]{1,0:T(8,128)S(1)}, u32[]{:S(2)}) copy-start(f32[128,2048]{1,0:T(8,128)S(1)} %pad.200) | copy-start | bytes 3145732
  298.7 21.5 copy-start.11
  298.7 21.5 copy-start.17
  602.8 19.4 slice-start
  602.8 19.4 slice-start.1
  613.1 9.1 copy-start.12
  614.0 8.2 slice-start.2
  627.1 487.6 %reduce-scatter.10.cloned.1.call-start = ((), (), s32[]{:S(2)}) async-start(), calls=%async_computation.16 | async-start | bytes 786432 | tf_op jit(solution)/shard_map/reduce_scatter | solution.py:136
  671.8 446.8 %reduce-scatter.20.cloned.1.call-start = ((), (), s32[]{:S(2)}) async-start(), calls=%async_computation.22 | async-start | bytes 208896 | tf_op jit(solution)/shard_map/reduce_scatter | solution.py:215
  675.7 9.2 copy-start.15
  777.4 36.8 %copy-start.34 = (f32[1,2048]{1,0:T(1,128)S(1)}, f32[1,2048]{1,0:T(1,128)}, u32[]{:S(2)}) copy-start(f32[1,2048]{1,0:T(1,128)} %slice.653) | copy-start | bytes 24580
  777.4 47.7 %copy-start.33 = (f32[1,2048]{1,0:T(1,128)S(1)}, f32[1,2048]{1,0:T(1,128)}, u32[]{:S(2)}) copy-start(f32[1,2048]{1,0:T(1,128)} %slice.631) | copy-start | bytes 24580
  849.0 97.1 %copy-start.19 = (f32[2048]{0:T(1024)S(1)}, f32[2048]{0:T(1024)}, u32[]{:S(2)}) copy-start(f32[2048]{0:T(1024)} %copy-done.18) | copy-start | bytes 24580
  849.0 97.1 %copy-start.23 = (f32[2048]{0:T(1024)S(1)}, f32[2048]{0:T(1024)}, u32[]{:S(2)}) copy-start(f32[2048]{0:T(1024)} %copy-done.22) | copy-start | bytes 24580
  862.8 87.7 %copy-start.21 = (f32[2048]{0:T(1024)S(1)}, f32[2048]{0:T(1024)}, u32[]{:S(2)}) copy-start(f32[2048]{0:T(1024)} %copy-done.20) | copy-start | bytes 24580
  953.6 9.1 copy-start.6
  953.6 233.0 %reduce-scatter.14.cloned.1.call-start = ((), (), s32[]{:S(2)}) async-start(), calls=%async_computation.19 | async-start | bytes 17825792 | tf_op jit(solution)/shard_map/reduce_scatter | solution.py:210
  962.7 406.1 %reduce-scatter.12.cloned.1.call-start = ((), (), s32[]{:S(2)}) async-start(), calls=%async_computation.18 | async-start | bytes 17825792 | tf_op jit(solution)/shard_map/reduce_scatter | solution.py:209
  972.1 579.0 %reduce-scatter.18.cloned.1.call-start = ((), (), s32[]{:S(2)}) async-start(), calls=%async_computation.21 | async-start | bytes 17825792 | tf_op jit(solution)/shard_map/reduce_scatter | solution.py:212
  982.6 750.6 %reduce-scatter.16.cloned.1.call-start = ((), (), s32[]{:S(2)}) async-start(), calls=%async_computation.20 | async-start | bytes 17825792 | tf_op jit(solution)/shard_map/reduce_scatter | solution.py:211
  991.9 971.8 %reduce-scatter.22.cloned.1.call-start = ((), (), s32[]{:S(2)}) async-start(), calls=%async_computation.23 | async-start | bytes 24510464 | tf_op jit(solution)/shard_map/reduce_scatter | solution.py:153
  1002.7 1191.4 %reduce-scatter.24.cloned.1.call-start = ((), (), s32[]{:S(2)}) async-start(), calls=%async_computation.24 | async-start | bytes 24510464 | tf_op jit(solution)/shard_map/reduce_scatter | solution.py:154
  1013.3 1411.4 %reduce-scatter.26.cloned.1.call-start = ((), (), s32[]{:S(2)}) async-start(), calls=%async_computation.25 | async-start | bytes 24510464 | tf_op jit(solution)/shard_map/reduce_scatter | solution.py:155
  1031.0 7.9 copy-start.7
  1031.0 14.4 slice-start.3
  1031.0 14.4 copy-start.14
  1038.9 6.5 slice-start.4
  (13 other events, 24.7 us)
Sparse Core Ops, SparseCore 0:
  10.2 77.9 all-gather.16
  90.3 73.4 all-gather.14
  166.0 73.1 all-gather.18
  241.2 74.0 all-gather.20
  317.5 92.8 all-gather.22
  412.5 92.4 all-gather.24
  507.2 95.5 all-gather.26
  627.2 38.1 all-reduce.63
  671.9 12.7 reduce-scatter.9
  953.8 51.4 reduce-scatter.19
  1010.0 176.6 reduce-scatter.13
  1191.2 177.5 reduce-scatter.11
  1373.5 177.5 reduce-scatter.17
  1555.6 177.5 reduce-scatter.15
  1737.7 225.8 reduce-scatter.21
  1968.2 225.9 reduce-scatter.23
  2198.7 225.9 reduce-scatter.25

commit v2 on v0

v2 whole, which is shorter than its diff:
```python
import jax
import jax.numpy as jnp
from jax import lax
from jax.experimental import pallas as pl
from jax.experimental.pallas import tpu as pltpu
from jax.sharding import Mesh, PartitionSpec as P

LAYER = 12
Z, C, X = 4, 2, 2
epsilon = 1e-06
BF, F32 = jnp.bfloat16, jnp.float32


def swap(value, axis):
    return lax.ppermute(value, axis, [(0, 1), (1, 0)])


def across_z(value, step):
    return lax.ppermute(value, "z", [(i, i ^ step) for i in range(Z)])


def dot(left, right):
    return jnp.dot(left, right, preferred_element_type=F32)


def contract_rows(left, right):
    return lax.dot_general(left, right, (((0,), (0,)), ((), ())), preferred_element_type=F32)


def times_transposed(left, right):
    return lax.dot_general(left, right, (((1,), (1,)), ((), ())), preferred_element_type=F32)


def inverse_rms(value):
    return lax.rsqrt(jnp.mean(value * value, axis=-1, keepdims=True) + epsilon)


def sigmoid_slope(raw, sig):
    return sig * (1.0 + raw * (1.0 - sig))


def gather_rows(own):
    mine = jnp.concatenate([own] + [across_z(own, k) for k in range(1, Z)], axis=0)
    return jnp.concatenate([mine, swap(mine, "c")], axis=0)


def scatter_rows(partial):
    half = partial.shape[0] // C
    rows = half // Z
    both = partial[:half].astype(F32) + swap(partial[half:], "c").astype(F32)
    total = both[:rows]
    for k in range(1, Z):
        total = total + across_z(both[k * rows : (k + 1) * rows].astype(BF), k).astype(F32)
    return total


def forward_kernel(decay_ref, drive_ref, state_ref, through_ref):
    chunks = 8
    length = decay_ref.shape[0] // chunks

    def step(t, carry):
        state, through = carry
        at = pl.ds(t, chunks, stride=length)
        decay = decay_ref[at, :]
        state = decay * state + drive_ref[at, :]
        through = decay * through
        state_ref[at, :] = state
        through_ref[at, :] = through
        return state, through

    shape = (chunks, decay_ref.shape[1])
    lax.fori_loop(0, length, step, (jnp.zeros(shape, F32), jnp.ones(shape, F32)), unroll=8)


def backward_kernel(decay_ref, grad_ref, adjoint_ref, after_ref, first_ref):
    chunks = 8
    length = decay_ref.shape[0] // chunks

    def step(t, carry):
        coming, after = carry
        at = pl.ds(length - 1 - t, chunks, stride=length)
        decay = decay_ref[at, :]
        adjoint = grad_ref[at, :] + coming
        adjoint_ref[at, :] = adjoint
        after_ref[at, :] = after
        return decay * adjoint, decay * after

    shape = (chunks, decay_ref.shape[1])
    coming, _ = lax.fori_loop(
        0, length, step, (jnp.zeros(shape, F32), jnp.ones(shape, F32)), unroll=8
    )
    first_ref[...] = coming


LANES = 128


def scan_call(kernel, inputs, outputs):
    feats = inputs[0].shape[1]

    def spec(rows):
        return pl.BlockSpec((rows, LANES), lambda i: (0, i))

    return pl.pallas_call(
        kernel,
        grid=(feats // LANES,),
        in_specs=[spec(v.shape[0]) for v in inputs],
        out_specs=[spec(n) for n in outputs],
        out_shape=[jax.ShapeDtypeStruct((n, feats), F32) for n in outputs],
    )(*inputs)


def entry_kernel(order_ref, through_ref, last_ref, entry_ref):
    def step(n, running):
        row = pl.ds(order_ref[n], 1)
        entry_ref[row, :] = running
        return through_ref[row, :] * running + last_ref[row, :]

    lax.fori_loop(0, order_ref.shape[0], step, jnp.zeros((1, last_ref.shape[1]), F32))


def per_device(
    tokens, lengths, w_in, w_forget, w_gate, w_out, attn_gain, mix_gain, bound_table,
    ff_gate, ff_up, ff_down, mlp_gain, out_grad,
):
    Y = lax.axis_size("y")
    pair = Y == 2
    z, y, c, x = (lax.axis_index(a) for a in "zycx")
    rows, width = tokens.shape
    sub = w_in.shape[0]
    feats = Y * sub
    block = ff_gate.shape[1] // (Z * C)
    chunks = Z * C
    group = rows * chunks

    def y_first(value):
        parts = value.reshape(value.shape[0], Z, Y, C * sub)
        parts = [parts[:, :, k].reshape(value.shape[0], Z * C * sub) for k in range(Y)]
        if pair:
            first, second = parts
            return jnp.concatenate(
                [jnp.where(y == 0, first, second), jnp.where(y == 0, second, first)], axis=1
            )
        return jnp.concatenate(parts, axis=1)

    def z_first(value):
        parts = jnp.split(value, Y, axis=1)
        if pair:
            first, second = parts
            parts = [jnp.where(y == 0, first, second), jnp.where(y == 0, second, first)]
        parts = [p.reshape(-1, Z, C * sub) for p in parts]
        return jnp.stack(parts, axis=2).reshape(value.shape[0], width)

    def over_y(value):
        if pair:
            return [value, swap(value, "y")]
        return [lax.all_gather(value, "y", axis=0, tiled=True)]

    def y_sum(pieces):
        if pair:
            return pieces[0].astype(BF).astype(F32) + swap(pieces[1].astype(BF), "y").astype(F32)
        return lax.psum_scatter(pieces[0].astype(BF), "y", scatter_dimension=0, tiled=True).astype(F32)

    def in_order(value):
        if pair:
            other = swap(value, "y")
            return jnp.concatenate(
                [jnp.where(y == 0, value, other), jnp.where(y == 0, other, value)], axis=0
            )
        return lax.all_gather(value, "y", axis=0, tiled=True)

    def own_sum(value):
        if pair:
            first, second = jnp.split(value, 2, axis=0)
            mine = jnp.where(y == 0, first, second).astype(BF)
            sent = jnp.where(y == 0, second, first).astype(BF)
            return mine.astype(F32) + swap(sent, "y").astype(F32)
        return lax.psum_scatter(value.astype(BF), "y", scatter_dimension=0, tiled=True).astype(F32)

    def x_sum(value):
        value = value.astype(BF)
        return value.astype(F32) + swap(value, "x").astype(F32)

    def spread(value):
        return lax.all_to_all(value, ("z", "c"), 0, 0, tiled=True)

    tokens_rho = y_first(tokens)
    tokens_all = gather_rows(tokens_rho)
    grad_all = gather_rows(y_first(out_grad))

    def to_blocks(weight):
        return weight.reshape(sub, Z, Y, C, sub).transpose(1, 3, 0, 2, 4).reshape(chunks, sub, feats)

    mixer = jnp.concatenate([to_blocks(w) for w in (w_in, w_forget, w_gate)], axis=2)
    mixer = over_y(spread(mixer).reshape(chunks * sub, 3 * feats))
    out_rows = in_order(w_out)
    table_f = bound_table.astype(F32)
    soft = jax.nn.softmax(table_f, axis=0)
    own_bound = jnp.sum(soft[1 : LAYER + 1], axis=0)
    small = in_order(jnp.stack([own_bound, mix_gain.astype(F32)])[None])
    bound = small[:, 0].reshape(1, feats)
    mix_g = small[:, 1].reshape(1, feats)
    gains = lax.all_gather(
        jnp.stack([attn_gain, mlp_gain]), ("z", "y", "c"), axis=1, tiled=True
    ).astype(F32)
    attn_g, mlp_g = gains[:1], gains[1:]

    def columns(weight):
        return spread(weight.reshape(sub, chunks, block).transpose(1, 0, 2)).reshape(chunks * sub, block)

    def halves(own, x_last):
        if not pair:
            full = over_y(own)
            return [full, [swap(full[0], "x")]]
        if x_last:
            near = over_y(own)
            return [near, [swap(p, "x") for p in near]]
        side = swap(own, "x")
        return [over_y(own), over_y(side)]

    gate_w = halves(columns(ff_gate), True)
    up_w = halves(columns(ff_up), False)
    down_w = spread(ff_down.reshape(chunks, block, sub)).transpose(0, 2, 1).reshape(chunks * sub, block)
    down_w = halves(down_w, True)

    def k_parts(value):
        return jnp.split(value, 2, axis=1) if pair else [value]

    def into(value, weights):
        return sum(dot(v, w) for v, w in zip(k_parts(value), weights, strict=True))

    starts_slot = jnp.arange(lengths.shape[0])
    starts = jnp.sum(jnp.where(starts_slot[None, :] < starts_slot[:, None], lengths[None, :], 0), axis=1)
    slot = jnp.arange(chunks)
    chunk = ((z ^ (slot % Z)) * Y + y) * (C * X) + (c ^ (slot // Z)) * X + x
    position = (chunk[:, None] * rows + jnp.arange(rows)[None, :]).reshape(group)
    keep = 1.0 - jnp.any(position[:, None] == starts[None, :], axis=1).astype(F32)[:, None]
    count = Z * Y * C * X
    number = jnp.arange(count)
    xn, cn = number % X, number // X % C
    yn, zn = number // (X * C) % Y, number // (X * C * Y)
    party = (yn ^ y) * X + (xn ^ x) if pair else yn * X + xn
    order = (party * chunks + (cn ^ c) * Z + (zn ^ z)).astype(jnp.int32)

    def parties(value):
        if pair:
            side = swap(value, "x")
            return jnp.concatenate([value, side, swap(value, "y"), lax.ppermute(
                value, ("y", "x"), [(i, 3 - i) for i in range(4)])], axis=0)
        return lax.all_gather(value, ("y", "x"), axis=0, tiled=True)

    def entries(order, through, last):
        total = pl.pallas_call(
            entry_kernel,
            out_shape=jax.ShapeDtypeStruct(last.shape, F32),
            in_specs=[pl.BlockSpec(memory_space=pltpu.SMEM)] + [pl.BlockSpec(memory_space=pltpu.VMEM)] * 2,
            out_specs=pl.BlockSpec(memory_space=pltpu.VMEM),
        )(order, through, last)
        if pair:
            return total[:chunks]
        return lax.dynamic_slice_in_dim(total, (y * X + x) * chunks, chunks, 0)

    wide = tokens_all.astype(F32)
    normed = (wide * inverse_rms(wide) * y_first(attn_g)).astype(BF)
    projected = into(normed, mixer)
    inner, forget_raw, gate_raw = jnp.split(projected, 3, axis=1)
    sig_forget = jax.nn.sigmoid(forget_raw)
    forget = bound + (1.0 - bound) * sig_forget
    sig_inner = jax.nn.sigmoid(inner)
    silu_inner = inner * sig_inner
    drive = silu_inner * (1.0 - forget)
    decay = forget * keep
    local, through = scan_call(forward_kernel, [decay, drive], [group, group])

    def per_chunk(value):
        return value.reshape(chunks, rows, feats)

    def flat(value):
        return value.reshape(group, feats)

    all_edges = parties(jnp.stack([per_chunk(through)[:, -1], per_chunk(local)[:, -1]], axis=1))
    all_through = all_edges[:, 0]
    entry = entries(order, all_through, all_edges[:, 1])
    states3 = per_chunk(local) + per_chunk(through) * entry[:, None, :]
    states = flat(states3)
    previous = flat(jnp.concatenate([entry[:, None, :], states3[:, :-1]], axis=1))
    sig_gate = jax.nn.sigmoid(gate_raw)
    silu_gate = gate_raw * sig_gate
    raw_mix = states * (mix_g * silu_gate)
    squares = jnp.sum(states * states, axis=1, keepdims=True)

    def lanes(*columns):
        split = []
        for column in columns:
            high = lax.reduce_precision(column, 8, 7)
            split += [high, column - high]
        split.append(jnp.zeros((columns[0].shape[0], 128 - len(split)), F32))
        return jnp.concatenate(split, axis=1).astype(BF)

    def unlane(value, at):
        return value[:, 2 * at : 2 * at + 1].astype(F32) + value[:, 2 * at + 1 : 2 * at + 2].astype(F32)

    summed = scatter_rows(
        jnp.concatenate([dot(raw_mix.astype(BF), out_rows).astype(BF), lanes(squares)], axis=1)
    )
    own_q = lax.rsqrt(unlane(summed[:, width:], 0) * (1.0 / width) + epsilon)
    mixed = own_q * summed[:, :width]
    resid = tokens.astype(F32) + mixed
    inv_resid = inverse_rms(resid)
    resid_hat = resid * inv_resid
    hidden = gather_rows(y_first((resid_hat * mlp_g).astype(BF)))

    gate_ff = [into(hidden, w) for w in gate_w]
    up_ff = [into(hidden, w) for w in up_w]
    sig_ff = [jax.nn.sigmoid(g) for g in gate_ff]
    silu_ff = [g * s for g, s in zip(gate_ff, sig_ff)]
    act = [(s * u).astype(BF) for s, u in zip(silu_ff, up_ff)]

    def back(values, weights):
        parts = []
        for k in range(len(weights[0])):
            parts.append(sum(times_transposed(v, w[k]) for v, w in zip(values, weights)))
        return jnp.concatenate([p.astype(BF) for p in parts], axis=1)

    d_act = [into(grad_all, w) for w in down_w]
    d_gate_ff = [
        (d * u * sigmoid_slope(g, s)).astype(BF) for d, u, g, s in zip(d_act, up_ff, gate_ff, sig_ff)
    ]
    d_up_ff = [(d * s).astype(BF) for d, s in zip(d_act, silu_ff)]
    d_hidden = z_first(scatter_rows(back(d_gate_ff + d_up_ff, gate_w + up_w)))
    glu_out = z_first(scatter_rows(back(act, down_w)))
    result = (resid + glu_out).astype(BF)

    def glu_total(source, grads, x_first):
        pieces = [[contract_rows(s, g) for s in k_parts(source)] for g in grads]
        if x_first or not pair:
            near = [
                own.astype(BF).astype(F32) + swap(other.astype(BF), "x").astype(F32)
                for own, other in zip(*pieces)
            ]
            return y_sum(near)
        near = [y_sum(p) for p in pieces]
        return near[0].astype(BF).astype(F32) + swap(near[1].astype(BF), "x").astype(F32)

    def columns_back(value):
        value = spread(value.astype(BF).reshape(chunks, sub, block))
        return value.transpose(1, 0, 2).reshape(sub, chunks * block).astype(F32)

    grad_gate_ff = columns_back(glu_total(hidden, d_gate_ff, True))
    grad_up_ff = columns_back(glu_total(hidden, d_up_ff, False))
    grad_down = glu_total(grad_all, act, True)
    grad_down = spread(grad_down.astype(BF).reshape(chunks, sub, block).transpose(0, 2, 1))
    grad_down = grad_down.reshape(chunks * block, sub).astype(F32)

    scaled_hidden = d_hidden * mlp_g
    d_resid = out_grad.astype(F32) + inv_resid * (
        scaled_hidden - resid_hat * jnp.mean(scaled_hidden * resid_hat, axis=-1, keepdims=True)
    )
    own_d_mixed = d_resid.astype(BF)
    own_mean = jnp.mean(own_d_mixed.astype(F32) * mixed, axis=-1, keepdims=True)
    sent = gather_rows(jnp.concatenate([own_d_mixed, lanes(own_q, own_mean)], axis=1))
    d_mixed = sent[:, :width]
    inv_states, mean_states = unlane(sent[:, width:], 0), unlane(sent[:, width:], 1)
    states_hat = states * inv_states
    mixed_in = (states_hat * mix_g * silu_gate).astype(BF)
    grad_out = x_sum(own_sum(contract_rows(mixed_in, d_mixed)))
    d_mixin = times_transposed(d_mixed, out_rows)
    d_gate_raw = (d_mixin * states_hat * mix_g * sigmoid_slope(gate_raw, sig_gate)).astype(BF)
    d_states = inv_states * (d_mixin * mix_g * silu_gate - states_hat * mean_states)
    adjoint_local, after, first = scan_call(
        backward_kernel, [decay, d_states], [group, group, chunks]
    )
    coming = entries(order[::-1], all_through, parties(first))
    adjoint = flat(per_chunk(adjoint_local) + per_chunk(after) * coming[:, None, :])
    d_forget = adjoint * previous * keep - adjoint * silu_inner
    d_inner = (adjoint * (1.0 - forget) * sigmoid_slope(inner, sig_inner)).astype(BF)
    d_forget_raw = (d_forget * (1.0 - bound) * sig_forget * (1.0 - sig_forget)).astype(BF)
    d_raw = jnp.concatenate([d_inner, d_forget_raw, d_gate_raw], axis=1)
    d_normed = z_first(
        scatter_rows(
            jnp.concatenate([times_transposed(d_raw, w).astype(BF) for w in mixer], axis=1)
        )
    )

    part_bound = jnp.sum(d_forget * (1.0 - sig_forget), axis=0)
    if pair:
        first_half, second_half = jnp.split(part_bound, 2)
        d_bound = jnp.where(y == 0, first_half, second_half) + swap(
            jnp.where(y == 0, second_half, first_half), "y"
        )
    else:
        d_bound = lax.psum_scatter(part_bound, "y", scatter_dimension=0, tiled=True)
    d_bound = d_bound + swap(d_bound, "x")
    row_ids = jnp.arange(bound_table.shape[0])[:, None]
    member = jnp.logical_and(row_ids >= 1, row_ids <= LAYER).astype(F32)
    grad_table = soft * (member - own_bound[None, :]) * d_bound[None, :]

    grad_mixer = y_sum([contract_rows(s, d_raw) for s in k_parts(normed)])
    grad_mixer = spread(x_sum(grad_mixer).astype(BF).reshape(chunks, sub, 3 * feats))
    grad_mixer = grad_mixer.reshape(Z, C, sub, 3, Y, sub).transpose(3, 2, 0, 4, 1, 5)
    grad_mixer = grad_mixer.reshape(3, sub, width).astype(F32)
    grad_in, grad_forget, grad_gate = grad_mixer[0], grad_mixer[1], grad_mixer[2]

    def along(weight, grad):
        return jnp.sum(weight.astype(F32) * grad, axis=1)

    grad_attn = along(w_in, grad_in) + along(w_forget, grad_forget) + along(w_gate, grad_gate)
    grad_attn = grad_attn / attn_gain.astype(F32)
    grad_mix = along(w_out, grad_out) / mix_gain.astype(F32)
    grad_mlp = along(ff_gate, grad_gate_ff) + along(ff_up, grad_up_ff)
    grad_mlp = (grad_mlp + swap(grad_mlp, "x")) / mlp_gain.astype(F32)

    own_wide = tokens.astype(F32)
    inv_tokens = inverse_rms(own_wide)
    tokens_hat = own_wide * inv_tokens
    scaled_normed = d_normed * attn_g
    token_grad = d_resid + inv_tokens * (
        scaled_normed - tokens_hat * jnp.mean(scaled_normed * tokens_hat, axis=-1, keepdims=True)
    )
    return (
        result, token_grad, grad_in, grad_forget, grad_gate, grad_out, grad_attn, grad_mix,
        grad_table, grad_gate_ff, grad_up_ff, grad_down, grad_mlp,
    )


def solution(mesh):
    dp, mp = mesh.devices.shape
    grid = Mesh(mesh.devices.reshape(Z, dp // (Z * C), C, mp), ("z", "y", "c", "x"))
    dp_axes = ("z", "y", "c")
    every = ("z", "y", "c", "x")
    mat, row, gain = P(dp_axes, None), P(every, None), P(dp_axes)
    table, glu, glu_down = P(None, dp_axes), P(dp_axes, "x"), P("x", dp_axes)
    return jax.shard_map(
        per_device,
        mesh=grid,
        in_specs=(
            row, P(), mat, mat, mat, mat, gain, gain, table, glu, glu, glu_down, gain, row,
        ),
        out_specs=(
            row, row, mat, mat, mat, mat, gain, gain, table, glu, glu, glu_down, gain,
        ),
        check_vma=False,
    )
```

time: 2450 us -> 720 us (0.29)
  the two profiles are of different devices: /device:TPU:0 before, /device:TPU:10 now
where the time goes in v2:
time: 720 us; the launch traced here: 709 us
  waiting for transfers between devices  280 us (39%)
  starting transfers between devices  111 us (15%)
  local copies, waits for them, and re-layouts  100 us (14%)
  other arithmetic  80.5 us (11%)
  matrix products  74.8 us (10%)
  blocking collectives  49.4 us (7%)
  Pallas kernels  9.81 us (1%)
    ppermute x24, waiting for transfers between devices, across_z(): return lax.ppermute(value, 'z', [(i, i ^ step) for i in range(Z)])  148 us
    ppermute x40, waiting for transfers between devices, swap(): return lax.ppermute(value, axis, [(0, 1), (1, 0)])  132 us
    all_gather x1, blocking collectives, per_device(): lax.all_gather(jnp.stack([attn_gain, mlp_gain]), ('z', 'y', 'c'), axis=1,...  49.4 us
    all_to_all x8, starting transfers between devices, spread(): return lax.all_to_all(value, ('z', 'c'), 0, 0, tiled=True)  44.8 us
    ppermute x40, starting transfers between devices, swap(): return lax.ppermute(value, axis, [(0, 1), (1, 0)])  37 us
    unnamed x180, local copies, waits for them, and re-layouts  31.9 us
    dot_general x15, matrix products, dot(): return jnp.dot(left, right, preferred_element_type=F32)  27.4 us
    ppermute x24, starting transfers between devices, across_z(): return lax.ppermute(value, 'z', [(i, i ^ step) for i in range(Z)])  26.7 us
  transfers between devices with their start and end apart: 74, of which 25 were waited for; matrix products, arithmetic and copies ran while one was open for 31% of the time, Pallas kernels for 1%

profile of v2, /device:TPU:10, one launch (start us, length us, event | category | flops | bytes accessed | tf_op | source)
XLA Modules:
  0.0 708.6 jit_solution(4488511125733412083)
XLA Ops:
  13.4 6.4 all-to-all-start
  24.2 49.4 %all_gather.3 = bf16[2,2048]{1,0:T(2,128)(2,1)S(1)} all-gather(bf16[2,128]{1,0:T(2,128)(2,1)S(1)} %pad_maximum_fusion.20), channel_id=1, replica_groups=mesh['z'=4,'y'=2,'c'=2,'x'=2] {'z','y','c'}, dimensions={1}, use_global_device_ids=true | all-gather | bytes 8704 | tf_op jit(solution)/shard_map/all_gather | solution.py:203
  87.9 14.1 %collective-permute-done.32 = bf16[64,2048]{1,0:T(8,128)(2,1)S(1)} collective-permute-done((bf16[64,2048]{1,0:T(8,128)(2,1)}, bf16[64,2048]{1,0:T(8,128)(2,1)S(1)}, u32[]{:S(2)}, u32[]{:S(2)}) %collective-permute-start.32) | collective-permute-done | bytes 262176 | tf_op jit(solution)/shard_map/ppermute | solution.py:19
  102.0 5.6 collective-permute-done.33
  114.7 4.6 all-to-all-start.3
  128.0 30.6 %collective-permute-done.5 = bf16[1024,768]{1,0:T(8,128)(2,1)S(1)} collective-permute-done((bf16[1024,768]{1,0:T(8,128)(2,1)}, bf16[1024,768]{1,0:T(8,128)(2,1)S(1)}, u32[]{:S(2)}, u32[]{:S(2)}) %collective-permute-start.5) | collective-permute-done | bytes 1572896 | tf_op jit(solution)/shard_map/ppermute | solution.py:15
  162.0 5.1 all-to-all-start.1
  167.1 3.2 fusion.26
  172.8 3.2 shard_map.237
  183.9 6.9 all-to-all-start.2
  193.9 3.6 convolution_convert_fusion
  197.5 8.1 %concatenate.90 = bf16[512,2176]{0,1:T(8,128)(2,1)S(1)} concatenate(bf16[512,2048]{0,1:T(8,128)(2,1)} %convolution_convert_fusion, bf16[512,1]{0,1:T(2,128)(2,1)S(1)} %get-tuple-element.193, bf16[512,1]{0,1:T(2,128)(2,1)S(1)} %get-tuple-element.192, bf16[512,126]{0,1:T(8,128)(2,1)S(1)} %broadcast_in_dim.23), dimensions={1} | concatenate | bytes 4456448 | tf_op jit(solution)/shard_map/concatenate | solution.py:304
  220.6 2.9 fusion.120
  227.8 14.1 %collective-permute-done.24 = bf16[1024,352]{0,1:T(8,128)(2,1)} collective-permute-done((bf16[1024,352]{0,1:T(8,128)(2,1)}, bf16[1024,352]{0,1:T(8,128)(2,1)}, u32[]{:S(2)}, u32[]{:S(2)}) %collective-permute-start.24) | collective-permute-done | bytes 720928 | tf_op jit(solution)/shard_map/ppermute | solution.py:15
  243.4 2.9 fusion.41
  247.7 8.2 %collective-permute-done.13 = bf16[64,2176]{1,0:T(8,128)(2,1)S(1)} collective-permute-done((bf16[64,2176]{1,0:T(8,128)(2,1)S(1)}, bf16[64,2176]{1,0:T(8,128)(2,1)S(1)}, u32[]{:S(2)}, u32[]{:S(2)}) %collective-permute-start.13) | collective-permute-done | bytes 278560 | tf_op jit(solution)/shard_map/ppermute | solution.py:19
  264.0 2.9 collective-permute-start.15
  268.4 4.8 collective-permute-done.14
  273.7 11.2 %collective-permute-done.15 = bf16[64,2048]{1,0:T(8,128)(2,1)S(1)} collective-permute-done((bf16[64,2048]{1,0:T(8,128)(2,1)S(1)}, bf16[64,2048]{1,0:T(8,128)(2,1)S(1)}, u32[]{:S(2)}, u32[]{:S(2)}) %collective-permute-start.15) | collective-permute-done | bytes 262176 | tf_op jit(solution)/shard_map/ppermute | solution.py:19
  286.5 2.9 collective-permute-done.16
  296.3 15.3 %collective-permute-done.23 = bf16[1024,352]{0,1:T(8,128)(2,1)S(1)} collective-permute-done((bf16[1024,352]{0,1:T(8,128)(2,1)S(1)}, bf16[1024,352]{0,1:T(8,128)(2,1)S(1)}, u32[]{:S(2)}, u32[]{:S(2)}) %collective-permute-start.23) | collective-permute-done | bytes 720928 | tf_op jit(solution)/shard_map/ppermute | solution.py:15
  312.2 12.2 %collective-permute-done.21 = bf16[1024,352]{0,1:T(8,128)(2,1)S(1)} collective-permute-done((bf16[1024,352]{0,1:T(8,128)(2,1)}, bf16[1024,352]{0,1:T(8,128)(2,1)S(1)}, u32[]{:S(2)}, u32[]{:S(2)}) %collective-permute-start.21) | collective-permute-done | bytes 720928 | tf_op jit(solution)/shard_map/ppermute | solution.py:15
  371.9 3.5 collective-permute-done.57
  383.4 3.0 collective-permute-done.36
  386.8 10.2 %collective-permute-done.37 = bf16[64,2048]{1,0:T(8,128)(2,1)S(1)} collective-permute-done((bf16[64,2048]{1,0:T(8,128)(2,1)S(1)}, bf16[64,2048]{1,0:T(8,128)(2,1)S(1)}, u32[]{:S(2)}, u32[]{:S(2)}) %collective-permute-start.37) | collective-permute-done | bytes 262176 | tf_op jit(solution)/shard_map/ppermute | solution.py:19
  397.5 4.2 collective-permute-done.38
  418.8 7.2 %all-to-all-start.6 = ((bf16[8,128,352]{1,2,0:T(8,128)(2,1)}), bf16[8,128,352]{1,2,0:T(8,128)(2,1)S(1)}, u32[]{:S(2)}, u32[]{:S(2)}) async-start(bf16[8,128,352]{1,2,0:T(8,128)(2,1)} %copy_bitcast_fusion.4), calls=%async_computation.6 | async-start | bytes 1441792 | tf_op jit(solution)/shard_map/all_to_all | solution.py:185
  429.6 6.4 collective-permute-done.40
  438.8 7.3 %collective-permute-done.41 = bf16[64,2176]{1,0:T(8,128)(2,1)} collective-permute-done((bf16[64,2176]{1,0:T(8,128)(2,1)}, bf16[64,2176]{1,0:T(8,128)(2,1)}, u32[]{:S(2)}, u32[]{:S(2)}) %collective-permute-start.41) | collective-permute-done | bytes 278560 | tf_op jit(solution)/shard_map/ppermute | solution.py:19
  448.1 3.2 pad_maximum_fusion.1
  455.8 13.4 %collective-permute-done.29 = bf16[64,2048]{1,0:T(8,128)(2,1)} collective-permute-done((bf16[64,2048]{1,0:T(8,128)(2,1)}, bf16[64,2048]{1,0:T(8,128)(2,1)}, u32[]{:S(2)}, u32[]{:S(2)}) %collective-permute-start.29) | collective-permute-done | bytes 262176 | tf_op jit(solution)/shard_map/ppermute | solution.py:19
  469.7 4.2 collective-permute-done.30
  480.0 4.2 all-to-all-start.5
  484.2 5.7 collective-permute-done.64
  492.6 5.7 concatenate.101
  499.2 4.0 subtract_multiply_fusion
  503.2 3.3 shard_map.239
  510.0 3.6 fusion.3
  513.6 4.4 all-to-all-start.7
  539.1 2.9 copy.296
  553.7 16.9 %collective-permute-done.50 = bf16[1024,768]{1,0:T(8,128)(2,1)} collective-permute-done((bf16[1024,768]{1,0:T(8,128)(2,1)}, bf16[1024,768]{1,0:T(8,128)(2,1)}, u32[]{:S(2)}, u32[]{:S(2)}) %collective-permute-start.50) | collective-permute-done | bytes 1572896 | tf_op jit(solution)/shard_map/ppermute | solution.py:15
  575.9 30.9 %collective-permute-done.55 = f32[128]{0:T(128)S(1)} collective-permute-done((f32[128]{0:T(128)S(1)}, f32[128]{0:T(128)S(1)}, u32[]{:S(2)}, u32[]{:S(2)}) %collective-permute-start.55) | collective-permute-done | bytes 544 | tf_op jit(solution)/shard_map/ppermute | solution.py:15
  614.6 6.2 all-to-all-start.4
  621.1 2.9 collective-permute-start.48
  627.6 25.9 %collective-permute-done.47 = bf16[64,2048]{1,0:T(8,128)(2,1)S(1)} collective-permute-done((bf16[64,2048]{1,0:T(8,128)(2,1)S(1)}, bf16[64,2048]{1,0:T(8,128)(2,1)S(1)}, u32[]{:S(2)}, u32[]{:S(2)}) %collective-permute-start.47) | collective-permute-done | bytes 262176 | tf_op jit(solution)/shard_map/ppermute | solution.py:19
  653.5 18.5 %collective-permute-done.48 = bf16[64,2048]{1,0:T(8,128)(2,1)S(1)} collective-permute-done((bf16[64,2048]{1,0:T(8,128)(2,1)S(1)}, bf16[64,2048]{1,0:T(8,128)(2,1)S(1)}, u32[]{:S(2)}, u32[]{:S(2)}) %collective-permute-start.48) | collective-permute-done | bytes 262176 | tf_op jit(solution)/shard_map/ppermute | solution.py:19
  672.0 7.7 %collective-permute-done.49 = bf16[64,2048]{1,0:T(8,128)(2,1)S(1)} collective-permute-done((bf16[64,2048]{1,0:T(8,128)(2,1)S(1)}, bf16[64,2048]{1,0:T(8,128)(2,1)S(1)}, u32[]{:S(2)}, u32[]{:S(2)}) %collective-permute-start.49) | collective-permute-done | bytes 262176 | tf_op jit(solution)/shard_map/ppermute | solution.py:19
  692.4 3.3 reshape.372
  (490 shorter events, 279.1 us)
Async XLA Ops:
  3.8 80.0 %collective-permute-start.1 = (bf16[64,2048]{1,0:T(8,128)(2,1)}, bf16[64,2048]{1,0:T(8,128)(2,1)}, u32[]{:S(2)}, u32[]{:S(2)}) collective-permute-start(bf16[64,2048]{1,0:T(8,128)(2,1)} %get-tuple-element.180), channel_id=1, source_target_pairs={{0,8},{8,0},{16,24},{24,16},{1,9},{9,1},{17,25},{25,17},{2,10},{10... | collective-permute-start | bytes 786440 | tf_op jit(solution)/shard_map/ppermute | solution.py:19
  4.3 79.7 %collective-permute-start.2 = (bf16[64,2048]{1,0:T(8,128)(2,1)}, bf16[64,2048]{1,0:T(8,128)(2,1)}, u32[]{:S(2)}, u32[]{:S(2)}) collective-permute-start(bf16[64,2048]{1,0:T(8,128)(2,1)} %get-tuple-element.180), channel_id=1, source_target_pairs={{0,16},{8,24},{16,0},{24,8},{1,17},{9,25},{17,1},{25,9},{2,18},{10... | collective-permute-start | bytes 786440 | tf_op jit(solution)/shard_map/ppermute | solution.py:19
  6.8 78.8 %collective-permute-start.3 = (bf16[64,2048]{1,0:T(8,128)(2,1)}, bf16[64,2048]{1,0:T(8,128)(2,1)}, u32[]{:S(2)}, u32[]{:S(2)}) collective-permute-start(bf16[64,2048]{1,0:T(8,128)(2,1)} %get-tuple-element.180), channel_id=1, source_target_pairs={{0,24},{8,16},{16,8},{24,0},{1,25},{9,17},{17,9},{25,1},{2,26},{10... | collective-permute-start | bytes 786440 | tf_op jit(solution)/shard_map/ppermute | solution.py:19
  13.4 101.3 %all-to-all-start = ((bf16[8,128,768]{1,2,0:T(8,128)(2,1)}), bf16[8,128,768]{1,2,0:T(8,128)(2,1)}, u32[]{:S(2)}, u32[]{:S(2)}) async-start(bf16[8,128,768]{1,2,0:T(8,128)(2,1)} %pad_maximum_fusion), calls=%async_computation | async-start | bytes 3145728 | tf_op jit(solution)/shard_map/all_to_all | solution.py:185
  20.4 61.9 %collective-permute-start = (f32[1,2,128]{2,1,0:T(2,128)S(1)}, f32[1,2,128]{2,1,0:T(2,128)S(1)}, u32[]{:S(2)}, u32[]{:S(2)}) collective-permute-start(f32[1,2,128]{2,1,0:T(2,128)S(1)} %maximum_bitcast_fusion), channel_id=1, source_target_pairs={{0,4},{4,0},{1,5},{5,1},{2,6},{6,2},{3,7},{7,3},{8,12},{12,8},{9,1... | collective-permute-start | bytes 3080 | tf_op jit(solution)/shard_map/ppermute | solution.py:15
  24.2 63.7 %collective-permute-start.31 = (bf16[64,2048]{1,0:T(8,128)(2,1)}, bf16[64,2048]{1,0:T(8,128)(2,1)S(1)}, u32[]{:S(2)}, u32[]{:S(2)}) collective-permute-start(bf16[64,2048]{1,0:T(8,128)(2,1)} %get-tuple-element.172), channel_id=1, source_target_pairs={{0,8},{8,0},{16,24},{24,16},{1,9},{9,1},{17,25},{25,17},{2,10},{10... | collective-permute-start | bytes 786440 | tf_op jit(solution)/shard_map/ppermute | solution.py:19
  83.9 23.8 %collective-permute-start.33 = (bf16[64,2048]{1,0:T(8,128)(2,1)}, bf16[64,2048]{1,0:T(8,128)(2,1)S(1)}, u32[]{:S(2)}, u32[]{:S(2)}) collective-permute-start(bf16[64,2048]{1,0:T(8,128)(2,1)} %get-tuple-element.172), channel_id=1, source_target_pairs={{0,24},{8,16},{16,8},{24,0},{1,25},{9,17},{17,9},{25,1},{2,26},{10... | collective-permute-start | bytes 786440 | tf_op jit(solution)/shard_map/ppermute | solution.py:19
  84.0 39.5 %collective-permute-start.9 = (bf16[128,2048]{1,0:T(8,128)(2,1)S(1)}, bf16[128,2048]{1,0:T(8,128)(2,1)}, u32[]{:S(2)}, u32[]{:S(2)}) collective-permute-start(bf16[128,2048]{1,0:T(8,128)(2,1)S(1)} %copy-done.20), channel_id=1, source_target_pairs={{0,4},{4,0},{1,5},{5,1},{2,6},{6,2},{3,7},{7,3},{8,12},{12,8},{9,1... | collective-permute-start | bytes 1572872 | tf_op jit(solution)/shard_map/ppermute | solution.py:15
  87.9 37.7 %collective-permute-start.4 = (bf16[256,2048]{1,0:T(8,128)(2,1)}, bf16[256,2048]{1,0:T(8,128)(2,1)}, u32[]{:S(2)}, u32[]{:S(2)}) collective-permute-start(bf16[256,2048]{1,0:T(8,128)(2,1)} %pad_maximum_fusion.5), channel_id=1, source_target_pairs={{0,2},{2,0},{1,3},{3,1},{4,6},{6,4},{5,7},{7,5},{8,10},{10,8},{9,1... | collective-permute-start | bytes 3145736 | tf_op jit(solution)/shard_map/ppermute | solution.py:15
  109.6 102.5 %collective-permute-start.34 = (bf16[256,2048]{1,0:T(8,128)(2,1)}, bf16[256,2048]{1,0:T(8,128)(2,1)}, u32[]{:S(2)}, u32[]{:S(2)}) collective-permute-start(bf16[256,2048]{1,0:T(8,128)(2,1)} %pad_maximum_fusion.9), channel_id=1, source_target_pairs={{0,2},{2,0},{1,3},{3,1},{4,6},{6,4},{5,7},{7,5},{8,10},{10,8},{9,1... | collective-permute-start | bytes 3145736 | tf_op jit(solution)/shard_map/ppermute | solution.py:15
  114.7 47.2 %all-to-all-start.3 = ((bf16[8,352,128]{2,1,0:T(8,128)(2,1)}), bf16[8,352,128]{2,1,0:T(8,128)(2,1)S(1)}, u32[]{:S(2)}, u32[]{:S(2)}) async-start(bf16[8,352,128]{2,1,0:T(8,128)(2,1)} %bitcast.274), calls=%async_computation.3 | async-start | bytes 1441792 | tf_op jit(solution)/shard_map/all_to_all | solution.py:185
  121.9 36.7 %collective-permute-start.5 = (bf16[1024,768]{1,0:T(8,128)(2,1)}, bf16[1024,768]{1,0:T(8,128)(2,1)S(1)}, u32[]{:S(2)}, u32[]{:S(2)}) collective-permute-start(bf16[1024,768]{1,0:T(8,128)(2,1)} %bitcast.271), channel_id=1, source_target_pairs={{0,4},{4,0},{1,5},{5,1},{2,6},{6,2},{3,7},{7,3},{8,12},{12,8},{9,1... | collective-permute-start | bytes 4718600 | tf_op jit(solution)/shard_map/ppermute | solution.py:15
  182.3 33.7 %collective-permute-start.25 = (bf16[1024,352]{0,1:T(8,128)(2,1)}, bf16[1024,352]{0,1:T(8,128)(2,1)}, u32[]{:S(2)}, u32[]{:S(2)}) collective-permute-start(bf16[1024,352]{0,1:T(8,128)(2,1)} %copy_bitcast_fusion.1), channel_id=1, source_target_pairs={{0,4},{4,0},{1,5},{5,1},{2,6},{6,2},{3,7},{7,3},{8,12},{12,8},{9,1... | collective-permute-start | bytes 2162696 | tf_op jit(solution)/shard_map/ppermute | solution.py:15
  183.9 26.2 %all-to-all-start.2 = ((bf16[8,128,352]{1,2,0:T(8,128)(2,1)}), bf16[8,128,352]{1,2,0:T(8,128)(2,1)}, u32[]{:S(2)}, u32[]{:S(2)}) async-start(bf16[8,128,352]{1,2,0:T(8,128)(2,1)} %bitcast.32), calls=%async_computation.2 | async-start | bytes 1441792 | tf_op jit(solution)/shard_map/all_to_all | solution.py:185
  208.0 86.6 %collective-permute-start.20 = (bf16[1024,352]{0,1:T(8,128)(2,1)}, bf16[1024,352]{0,1:T(8,128)(2,1)}, u32[]{:S(2)}, u32[]{:S(2)}) collective-permute-start(bf16[1024,352]{0,1:T(8,128)(2,1)} %copy_bitcast_fusion.3), channel_id=1, source_target_pairs={{0,1},{1,0},{2,3},{3,2},{4,5},{5,4},{6,7},{7,6},{8,9},{9,8},{10,11... | collective-permute-start | bytes 2162696 | tf_op jit(solution)/shard_map/ppermute | solution.py:15
  208.5 82.3 %collective-permute-start.18 = (bf16[1024,352]{0,1:T(8,128)(2,1)}, bf16[1024,352]{0,1:T(8,128)(2,1)}, u32[]{:S(2)}, u32[]{:S(2)}) collective-permute-start(bf16[1024,352]{0,1:T(8,128)(2,1)} %copy_bitcast_fusion.3), channel_id=1, source_target_pairs={{0,4},{4,0},{1,5},{5,1},{2,6},{6,2},{3,7},{7,3},{8,12},{12,8},{9,1... | collective-permute-start | bytes 2162696 | tf_op jit(solution)/shard_map/ppermute | solution.py:15
  212.1 29.8 %collective-permute-start.24 = (bf16[1024,352]{0,1:T(8,128)(2,1)}, bf16[1024,352]{0,1:T(8,128)(2,1)}, u32[]{:S(2)}, u32[]{:S(2)}) collective-permute-start(bf16[1024,352]{0,1:T(8,128)(2,1)} %copy_bitcast_fusion.1), channel_id=1, source_target_pairs={{0,1},{1,0},{2,3},{3,2},{4,5},{5,4},{6,7},{7,6},{8,9},{9,8},{10,11... | collective-permute-start | bytes 2162696 | tf_op jit(solution)/shard_map/ppermute | solution.py:15
  224.2 22.1 %collective-permute-start.11 = (bf16[64,2176]{1,0:T(8,128)(2,1)S(1)}, bf16[64,2176]{1,0:T(8,128)(2,1)S(1)}, u32[]{:S(2)}, u32[]{:S(2)}) collective-permute-start(bf16[64,2176]{1,0:T(8,128)(2,1)S(1)} %copy.253), channel_id=1, source_target_pairs={{0,8},{8,0},{16,24},{24,16},{1,9},{9,1},{17,25},{25,17},{2,10},{10... | collective-permute-start | bytes 835592 | tf_op jit(solution)/shard_map/ppermute | solution.py:19
  266.9 22.5 %collective-permute-start.16 = (bf16[64,2048]{1,0:T(8,128)(2,1)S(1)}, bf16[64,2048]{1,0:T(8,128)(2,1)S(1)}, u32[]{:S(2)}, u32[]{:S(2)}) collective-permute-start(bf16[64,2048]{1,0:T(8,128)(2,1)S(1)} %get-tuple-element.176), channel_id=1, source_target_pairs={{0,24},{8,16},{16,8},{24,0},{1,25},{9,17},{17,9},{25,1},{2,26},{10... | collective-permute-start | bytes 786440 | tf_op jit(solution)/shard_map/ppermute | solution.py:19
  284.9 45.1 %collective-permute-start.19 = (bf16[1024,352]{0,1:T(8,128)(2,1)S(1)}, bf16[1024,352]{0,1:T(8,128)(2,1)S(1)}, u32[]{:S(2)}, u32[]{:S(2)}) collective-permute-start(bf16[1024,352]{0,1:T(8,128)(2,1)S(1)} %copy-done.31), channel_id=1, source_target_pairs={{0,4},{4,0},{1,5},{5,1},{2,6},{6,2},{3,7},{7,3},{8,12},{12,8},{9,1... | collective-permute-start | bytes 2162696 | tf_op jit(solution)/shard_map/ppermute | solution.py:15
  290.2 34.8 %collective-permute-start.26 = (bf16[1024,352]{0,1:T(8,128)(2,1)}, bf16[1024,352]{0,1:T(8,128)(2,1)S(1)}, u32[]{:S(2)}, u32[]{:S(2)}) collective-permute-start(bf16[1024,352]{0,1:T(8,128)(2,1)} %collective-permute-done.25), channel_id=1, source_target_pairs={{0,1},{1,0},{2,3},{3,2},{4,5},{5,4},{6,7},{7,6},{8,9},{9,8},{10,11... | collective-permute-start | bytes 2162696 | tf_op jit(solution)/shard_map/ppermute | solution.py:15
  292.4 32.1 %collective-permute-start.21 = (bf16[1024,352]{0,1:T(8,128)(2,1)}, bf16[1024,352]{0,1:T(8,128)(2,1)S(1)}, u32[]{:S(2)}, u32[]{:S(2)}) collective-permute-start(bf16[1024,352]{0,1:T(8,128)(2,1)} %collective-permute-done.18), channel_id=1, source_target_pairs={{0,1},{1,0},{2,3},{3,2},{4,5},{5,4},{6,7},{7,6},{8,9},{9,8},{10,11... | collective-permute-start | bytes 2162696 | tf_op jit(solution)/shard_map/ppermute | solution.py:15
  340.5 30.2 %collective-permute-start.60 = (bf16[1024,352]{0,1:T(8,128)(2,1)S(1)}, bf16[1024,352]{0,1:T(8,128)(2,1)S(1)}, u32[]{:S(2)}, u32[]{:S(2)}) collective-permute-start(bf16[1024,352]{0,1:T(8,128)(2,1)S(1)} %convolution_convert_fusion.9), channel_id=1, source_target_pairs={{0,4},{4,0},{1,5},{5,1},{2,6},{6,2},{3,7},{7,3},{8,12},{12,8},{9,1... | collective-permute-start | bytes 2162696 | tf_op jit(solution)/shard_map/ppermute | solution.py:15
  342.1 68.1 %collective-permute-start.59 = (bf16[1024,352]{0,1:T(8,128)(2,1)}, bf16[1024,352]{0,1:T(8,128)(2,1)}, u32[]{:S(2)}, u32[]{:S(2)}) collective-permute-start(bf16[1024,352]{0,1:T(8,128)(2,1)} %convolution_convert_fusion.11), channel_id=1, source_target_pairs={{0,4},{4,0},{1,5},{5,1},{2,6},{6,2},{3,7},{7,3},{8,12},{12,8},{9,1... | collective-permute-start | bytes 2162696 | tf_op jit(solution)/shard_map/ppermute | solution.py:15
  342.5 135.0 %collective-permute-start.56 = (bf16[1024,352]{0,1:T(8,128)(2,1)}, bf16[1024,352]{0,1:T(8,128)(2,1)}, u32[]{:S(2)}, u32[]{:S(2)}) collective-permute-start(bf16[1024,352]{0,1:T(8,128)(2,1)} %convolution_convert_fusion.15), channel_id=1, source_target_pairs={{0,1},{1,0},{2,3},{3,2},{4,5},{5,4},{6,7},{7,6},{8,9},{9,8},{10,11... | collective-permute-start | bytes 2162696 | tf_op jit(solution)/shard_map/ppermute | solution.py:15
  343.1 32.3 %collective-permute-start.57 = (bf16[1024,352]{0,1:T(8,128)(2,1)S(1)}, bf16[1024,352]{0,1:T(8,128)(2,1)S(1)}, u32[]{:S(2)}, u32[]{:S(2)}) collective-permute-start(bf16[1024,352]{0,1:T(8,128)(2,1)S(1)} %convolution_convert_fusion.13), channel_id=1, source_target_pairs={{0,1},{1,0},{2,3},{3,2},{4,5},{5,4},{6,7},{7,6},{8,9},{9,8},{10,11... | collective-permute-start | bytes 2162696 | tf_op jit(solution)/shard_map/ppermute | solution.py:15
  379.3 22.4 %collective-permute-start.38 = (bf16[64,2048]{1,0:T(8,128)(2,1)S(1)}, bf16[64,2048]{1,0:T(8,128)(2,1)S(1)}, u32[]{:S(2)}, u32[]{:S(2)}) collective-permute-start(bf16[64,2048]{1,0:T(8,128)(2,1)S(1)} %get-tuple-element.146), channel_id=1, source_target_pairs={{0,24},{8,16},{16,8},{24,0},{1,25},{9,17},{17,9},{25,1},{2,26},{10... | collective-permute-start | bytes 786440 | tf_op jit(solution)/shard_map/ppermute | solution.py:19
  386.3 64.9 %collective-permute-start.63 = (bf16[1024,352]{0,1:T(8,128)(2,1)}, bf16[1024,352]{0,1:T(8,128)(2,1)}, u32[]{:S(2)}, u32[]{:S(2)}) collective-permute-start(bf16[1024,352]{0,1:T(8,128)(2,1)} %convolution_convert_fusion.5), channel_id=1, source_target_pairs={{0,1},{1,0},{2,3},{3,2},{4,5},{5,4},{6,7},{7,6},{8,9},{9,8},{10,11... | collective-permute-start | bytes 2162696 | tf_op jit(solution)/shard_map/ppermute | solution.py:15
  410.2 25.8 %collective-permute-start.40 = (bf16[64,2176]{1,0:T(8,128)(2,1)}, bf16[64,2176]{1,0:T(8,128)(2,1)}, u32[]{:S(2)}, u32[]{:S(2)}) collective-permute-start(bf16[64,2176]{1,0:T(8,128)(2,1)} %copy.273), channel_id=1, source_target_pairs={{0,16},{8,24},{16,0},{24,8},{1,17},{9,25},{17,1},{25,9},{2,18},{10... | collective-permute-start | bytes 835592 | tf_op jit(solution)/shard_map/ppermute | solution.py:19
  415.1 31.0 %collective-permute-start.41 = (bf16[64,2176]{1,0:T(8,128)(2,1)}, bf16[64,2176]{1,0:T(8,128)(2,1)}, u32[]{:S(2)}, u32[]{:S(2)}) collective-permute-start(bf16[64,2176]{1,0:T(8,128)(2,1)} %copy.273), channel_id=1, source_target_pairs={{0,24},{8,16},{16,8},{24,0},{1,25},{9,17},{17,9},{25,1},{2,26},{10... | collective-permute-start | bytes 835592 | tf_op jit(solution)/shard_map/ppermute | solution.py:19
  418.8 61.2 %all-to-all-start.6 = ((bf16[8,128,352]{1,2,0:T(8,128)(2,1)}), bf16[8,128,352]{1,2,0:T(8,128)(2,1)S(1)}, u32[]{:S(2)}, u32[]{:S(2)}) async-start(bf16[8,128,352]{1,2,0:T(8,128)(2,1)} %copy_bitcast_fusion.4), calls=%async_computation.6 | async-start | bytes 1441792 | tf_op jit(solution)/shard_map/all_to_all | solution.py:185
  426.0 51.5 %collective-permute-start.58 = (bf16[1024,352]{0,1:T(8,128)(2,1)}, bf16[1024,352]{0,1:T(8,128)(2,1)}, u32[]{:S(2)}, u32[]{:S(2)}) collective-permute-start(bf16[1024,352]{0,1:T(8,128)(2,1)} %add_convert_fusion.13), channel_id=1, source_target_pairs={{0,4},{4,0},{1,5},{5,1},{2,6},{6,2},{3,7},{7,3},{8,12},{12,8},{9,1... | collective-permute-start | bytes 2162696 | tf_op jit(solution)/shard_map/ppermute | solution.py:15
  446.1 23.0 %collective-permute-start.29 = (bf16[64,2048]{1,0:T(8,128)(2,1)}, bf16[64,2048]{1,0:T(8,128)(2,1)}, u32[]{:S(2)}, u32[]{:S(2)}) collective-permute-start(bf16[64,2048]{1,0:T(8,128)(2,1)} %get-tuple-element.150), channel_id=1, source_target_pairs={{0,16},{8,24},{16,0},{24,8},{1,17},{9,25},{17,1},{25,9},{2,18},{10... | collective-permute-start | bytes 786440 | tf_op jit(solution)/shard_map/ppermute | solution.py:19
  451.3 22.5 %collective-permute-start.30 = (bf16[64,2048]{1,0:T(8,128)(2,1)S(1)}, bf16[64,2048]{1,0:T(8,128)(2,1)S(1)}, u32[]{:S(2)}, u32[]{:S(2)}) collective-permute-start(bf16[64,2048]{1,0:T(8,128)(2,1)S(1)} %copy-done.39), channel_id=1, source_target_pairs={{0,24},{8,16},{16,8},{24,0},{1,25},{9,17},{17,9},{25,1},{2,26},{10... | collective-permute-start | bytes 786440 | tf_op jit(solution)/shard_map/ppermute | solution.py:19
  453.5 39.1 %collective-permute-start.42 = (bf16[256,2176]{0,1:T(8,128)(2,1)}, bf16[256,2176]{0,1:T(8,128)(2,1)}, u32[]{:S(2)}, u32[]{:S(2)}) collective-permute-start(bf16[256,2176]{0,1:T(8,128)(2,1)} %pad_maximum_fusion.1), channel_id=1, source_target_pairs={{0,2},{2,0},{1,3},{3,1},{4,6},{6,4},{5,7},{7,5},{8,10},{10,8},{9,1... | collective-permute-start | bytes 3342344 | tf_op jit(solution)/shard_map/ppermute | solution.py:15
  480.0 33.6 %all-to-all-start.5 = ((bf16[8,128,352]{1,2,0:T(8,128)(2,1)}), bf16[8,128,352]{1,2,0:T(8,128)(2,1)}, u32[]{:S(2)}, u32[]{:S(2)}) async-start(bf16[8,128,352]{1,2,0:T(8,128)(2,1)} %copy_bitcast_fusion.5), calls=%async_computation.5 | async-start | bytes 1441792 | tf_op jit(solution)/shard_map/all_to_all | solution.py:185
  513.6 22.0 %all-to-all-start.7 = ((bf16[8,352,128]{2,1,0:T(8,128)(2,1)}), bf16[8,352,128]{2,1,0:T(8,128)(2,1)}, u32[]{:S(2)}, u32[]{:S(2)}) async-start(bf16[8,352,128]{2,1,0:T(8,128)(2,1)} %bitcast_bitcast_fusion), calls=%async_computation.7 | async-start | bytes 1441792 | tf_op jit(solution)/shard_map/all_to_all | solution.py:185
  520.2 87.3 %collective-permute-start.52 = (bf16[128,2048]{1,0:T(8,128)(2,1)}, bf16[128,2048]{1,0:T(8,128)(2,1)}, u32[]{:S(2)}, u32[]{:S(2)}) collective-permute-start(bf16[128,2048]{1,0:T(8,128)(2,1)} %select_convert_fusion), channel_id=1, source_target_pairs={{0,4},{4,0},{1,5},{5,1},{2,6},{6,2},{3,7},{7,3},{8,12},{12,8},{9,1... | collective-permute-start | bytes 1572872 | tf_op jit(solution)/shard_map/ppermute | solution.py:15
  525.6 49.1 %collective-permute-start.65 = (f32[128]{0:T(128)}, f32[128]{0:T(128)}, u32[]{:S(2)}, u32[]{:S(2)}) collective-permute-start(f32[128]{0:T(128)} %add.427), channel_id=1, source_target_pairs={{0,1},{1,0},{2,3},{3,2},{4,5},{5,4},{6,7},{7,6},{8,9},{9,8},{10,11... | collective-permute-start | bytes 1544 | tf_op jit(solution)/shard_map/ppermute | solution.py:15
  535.2 35.4 %collective-permute-start.50 = (bf16[1024,768]{1,0:T(8,128)(2,1)}, bf16[1024,768]{1,0:T(8,128)(2,1)}, u32[]{:S(2)}, u32[]{:S(2)}) collective-permute-start(bf16[1024,768]{1,0:T(8,128)(2,1)} %convolution_convert_fusion.1), channel_id=1, source_target_pairs={{0,4},{4,0},{1,5},{5,1},{2,6},{6,2},{3,7},{7,3},{8,12},{12,8},{9,1... | collective-permute-start | bytes 4718600 | tf_op jit(solution)/shard_map/ppermute | solution.py:15
  545.5 28.7 %collective-permute-start.54 = (f32[128]{0:T(128)S(1)}, f32[128]{0:T(128)S(1)}, u32[]{:S(2)}, u32[]{:S(2)}) collective-permute-start(f32[128]{0:T(128)S(1)} %broadcast_select_fusion.10), channel_id=1, source_target_pairs={{0,4},{4,0},{1,5},{5,1},{2,6},{6,2},{3,7},{7,3},{8,12},{12,8},{9,1... | collective-permute-start | bytes 1544 | tf_op jit(solution)/shard_map/ppermute | solution.py:15
  551.1 60.2 %collective-permute-start.46 = (bf16[256,2048]{1,0:T(8,128)(2,1)S(1)}, bf16[256,2048]{1,0:T(8,128)(2,1)S(1)}, u32[]{:S(2)}, u32[]{:S(2)}) collective-permute-start(bf16[256,2048]{1,0:T(8,128)(2,1)S(1)} %pad_maximum_fusion.2), channel_id=1, source_target_pairs={{0,2},{2,0},{1,3},{3,1},{4,6},{6,4},{5,7},{7,5},{8,10},{10,8},{9,1... | collective-permute-start | bytes 3145736 | tf_op jit(solution)/shard_map/ppermute | solution.py:15
  572.5 40.5 %collective-permute-start.51 = (bf16[1024,768]{1,0:T(8,128)(2,1)S(1)}, bf16[1024,768]{1,0:T(8,128)(2,1)S(1)}, u32[]{:S(2)}, u32[]{:S(2)}) collective-permute-start(bf16[1024,768]{1,0:T(8,128)(2,1)S(1)} %add_convert_fusion.1), channel_id=1, source_target_pairs={{0,1},{1,0},{2,3},{3,2},{4,5},{5,4},{6,7},{7,6},{8,9},{9,8},{10,11... | collective-permute-start | bytes 4718600 | tf_op jit(solution)/shard_map/ppermute | solution.py:15
  574.3 32.5 %collective-permute-start.55 = (f32[128]{0:T(128)S(1)}, f32[128]{0:T(128)S(1)}, u32[]{:S(2)}, u32[]{:S(2)}) collective-permute-start(f32[128]{0:T(128)S(1)} %fusion.91), channel_id=1, source_target_pairs={{0,1},{1,0},{2,3},{3,2},{4,5},{5,4},{6,7},{7,6},{8,9},{9,8},{10,11... | collective-permute-start | bytes 1544 | tf_op jit(solution)/shard_map/ppermute | solution.py:15
  614.6 77.8 %all-to-all-start.4 = ((bf16[8,128,768]{2,1,0:T(8,128)(2,1)}), bf16[8,128,768]{2,1,0:T(8,128)(2,1)}, u32[]{:S(2)}, u32[]{:S(2)}) async-start(bf16[8,128,768]{2,1,0:T(8,128)(2,1)} %bitcast.251), calls=%async_computation.4 | async-start | bytes 3145728 | tf_op jit(solution)/shard_map/all_to_all | solution.py:185
  621.0 32.5 %collective-permute-start.47 = (bf16[64,2048]{1,0:T(8,128)(2,1)S(1)}, bf16[64,2048]{1,0:T(8,128)(2,1)S(1)}, u32[]{:S(2)}, u32[]{:S(2)}) collective-permute-start(bf16[64,2048]{1,0:T(8,128)(2,1)S(1)} %get-tuple-element.142), channel_id=1, source_target_pairs={{0,8},{8,0},{16,24},{24,16},{1,9},{9,1},{17,25},{25,17},{2,10},{10... | collective-permute-start | bytes 786440 | tf_op jit(solution)/shard_map/ppermute | solution.py:19
  621.1 50.9 %collective-permute-start.48 = (bf16[64,2048]{1,0:T(8,128)(2,1)S(1)}, bf16[64,2048]{1,0:T(8,128)(2,1)S(1)}, u32[]{:S(2)}, u32[]{:S(2)}) collective-permute-start(bf16[64,2048]{1,0:T(8,128)(2,1)S(1)} %get-tuple-element.144), channel_id=1, source_target_pairs={{0,16},{8,24},{16,0},{24,8},{1,17},{9,25},{17,1},{25,9},{2,18},{10... | collective-permute-start | bytes 786440 | tf_op jit(solution)/shard_map/ppermute | solution.py:19
  624.0 55.7 %collective-permute-start.49 = (bf16[64,2048]{1,0:T(8,128)(2,1)S(1)}, bf16[64,2048]{1,0:T(8,128)(2,1)S(1)}, u32[]{:S(2)}, u32[]{:S(2)}) collective-permute-start(bf16[64,2048]{1,0:T(8,128)(2,1)S(1)} %get-tuple-element.143), channel_id=1, source_target_pairs={{0,24},{8,16},{16,8},{24,0},{1,25},{9,17},{17,9},{25,1},{2,26},{10... | collective-permute-start | bytes 786440 | tf_op jit(solution)/shard_map/ppermute | solution.py:19
  (100 other events, 1664.0 us)

commit v3 on v2

v3 whole, which is shorter than its diff:
```python
import functools

import jax
import jax.numpy as jnp
from jax import lax
from jax.experimental import pallas as pl
from jax.experimental.pallas import tpu as pltpu
from jax.sharding import Mesh, PartitionSpec as P

LAYER = 12
Z, C, X = 4, 2, 2
CHUNKS = Z * C
LANES = 128
epsilon = 1e-06
BF, F32 = jnp.bfloat16, jnp.float32


def swap(value, axis):
    return lax.ppermute(value, axis, [(0, 1), (1, 0)])


def across_z(value, step):
    return lax.ppermute(value, "z", [(i, i ^ step) for i in range(Z)])


def dot(left, right):
    return jnp.dot(left, right, preferred_element_type=F32)


def contract_rows(left, right):
    return lax.dot_general(left, right, (((0,), (0,)), ((), ())), preferred_element_type=F32)


def times_transposed(left, right):
    return lax.dot_general(left, right, (((1,), (1,)), ((), ())), preferred_element_type=F32)


def mean_last(value):
    return jnp.mean(value, axis=-1, keepdims=True)


def inverse_rms(value):
    return lax.rsqrt(mean_last(value * value) + epsilon)


def sigmoid_slope(raw, sig):
    return sig * (1.0 + raw * (1.0 - sig))


def call(kernel, outs, *ins, smem=0, scratch=(), flops=0):
    specs = [pl.BlockSpec(memory_space=pltpu.SMEM)] * smem
    specs += [pl.BlockSpec(memory_space=pltpu.VMEM)] * (len(ins) - smem)
    shapes = [jax.ShapeDtypeStruct(s, t) for s, t in outs]
    moved = sum(v.size * v.dtype.itemsize for v in list(ins) + shapes)
    return pl.pallas_call(
        kernel,
        out_shape=shapes,
        in_specs=specs,
        out_specs=[pl.BlockSpec(memory_space=pltpu.VMEM)] * len(outs),
        scratch_shapes=list(scratch),
        compiler_params=pltpu.CompilerParams(vmem_limit_bytes=40 << 20),
        cost_estimate=pl.CostEstimate(flops=flops, bytes_accessed=moved, transcendentals=0),
    )(*ins)


def stat_block(columns):
    rows = columns[0].shape[0]
    lane = lax.broadcasted_iota(jnp.int32, (rows, LANES), 1)
    block = jnp.zeros((rows, LANES), F32)
    for k, column in enumerate(columns):
        high = column.astype(BF).astype(F32)
        block = jnp.where(lane == 2 * k, high, block)
        block = jnp.where(lane == 2 * k + 1, column - high, block)
    return block


def stat(block, k):
    lane = lax.broadcasted_iota(jnp.int32, block.shape, 1)
    picked = jnp.where((lane == 2 * k) | (lane == 2 * k + 1), block.astype(F32), 0.0)
    return jnp.sum(picked, axis=1, keepdims=True)


def reorder_kernel(back, y_ref, *refs):
    y = y_ref[0]
    half = len(refs) // 2
    for in_ref, out_ref in zip(refs[:half], refs[half:]):
        width = in_ref.shape[1] // CHUNKS
        for k in range(2):
            there = k + y - 2 * k * y
            for z in range(Z):
                near = slice((k * Z + z) * width, (k * Z + z + 1) * width)
                far = pl.ds(pl.multiple_of((z * 2 + there) * width, width), width)
                if back:
                    out_ref[:, far] = in_ref[:, near]
                else:
                    out_ref[:, near] = in_ref[:, far]


def mixer_blocks_kernel(*refs):
    out_ref = refs[-1]
    for m, w_ref in enumerate(refs[:-1]):
        for z in range(Z):
            for y in range(2):
                for c in range(C):
                    at, to = ((z * 2 + y) * C + c) * LANES, (m * 2 + y) * LANES
                    out_ref[z * C + c, :, to : to + LANES] = w_ref[:, at : at + LANES]


def mixer_grads_kernel(blocks_ref, w_in, w_forget, w_gate, grad_in, grad_forget, grad_gate, along_ref):
    total = jnp.zeros((w_in.shape[0], 1), F32)
    for m, (w_ref, g_ref) in enumerate(((w_in, grad_in), (w_forget, grad_forget), (w_gate, grad_gate))):
        for z in range(Z):
            for y in range(2):
                for c in range(C):
                    to, at = ((z * 2 + y) * C + c) * LANES, (m * 2 + y) * LANES
                    piece = blocks_ref[z * C + c, :, at : at + LANES].astype(F32)
                    g_ref[:, to : to + LANES] = piece
                    weight = w_ref[:, to : to + LANES].astype(F32)
                    total = total + jnp.sum(piece * weight, axis=1, keepdims=True)
    along_ref[...] = jnp.broadcast_to(total, along_ref.shape)


def glu_blocks_kernel(gate_ref, up_ref, down_ref, out_ref):
    block = down_ref.shape[0] // CHUNKS
    for s in range(CHUNKS):
        at = slice(s * block, (s + 1) * block)
        out_ref[s, :block] = gate_ref[:, at].astype(F32).T.astype(BF)
        out_ref[s, block : 2 * block] = up_ref[:, at].astype(F32).T.astype(BF)
        out_ref[s, 2 * block :] = down_ref[at, :]


def glu_grads_kernel(blocks_ref, w_gate, w_up, grad_gate, grad_up, grad_down, along_ref):
    block = grad_down.shape[0] // CHUNKS
    total = jnp.zeros((w_gate.shape[0], 1), F32)
    for s in range(CHUNKS):
        at = slice(s * block, (s + 1) * block)
        for m, (w_ref, g_ref) in enumerate(((w_gate, grad_gate), (w_up, grad_up))):
            piece = blocks_ref[s, m * block : (m + 1) * block].astype(F32).T
            g_ref[:, at] = piece
            total = total + jnp.sum(piece * w_ref[:, at].astype(F32), axis=1, keepdims=True)
        grad_down[at, :] = blocks_ref[s, 2 * block :].astype(F32)
    along_ref[...] = jnp.broadcast_to(total, along_ref.shape)


def mixer_forward_kernel(parts, *refs):
    gain, near, far, bound, keep = refs[:5]
    weights = refs[5 : 5 + parts]
    normed, raw, decay, local, through, edge, drive = refs[5 + parts :]
    group, feats = raw.shape[0], bound.shape[1]
    rows = group // CHUNKS
    for k, source in enumerate((near, far)):

        @pl.loop(0, source.shape[0] // 32)
        def _(i, source=source, base=k * source.shape[0]):
            value = source[pl.ds(i * 32, 32), :].astype(F32)
            normed[pl.ds(base + i * 32, 32), :] = (value * inverse_rms(value) * gain[...]).astype(BF)

    @pl.loop(0, 4)
    def _(i):
        at = pl.ds(i * (group // 4), group // 4)
        total, begin = None, 0
        for w in weights:
            part = dot(normed[at, begin : begin + w.shape[0]], w[...])
            total = part if total is None else total + part
            begin += w.shape[0]
        raw[at, :] = total

    count = feats // LANES

    @pl.loop(0, CHUNKS)
    def _(i):
        at = pl.ds(i * rows, rows)
        for j in range(count):
            lanes = slice(j * LANES, (j + 1) * LANES)
            inner = raw[at, lanes]
            forget_raw = raw[at, feats + j * LANES : feats + (j + 1) * LANES]
            low = bound[:, lanes]
            forget = low + (1.0 - low) * jax.nn.sigmoid(forget_raw)
            drive[j, at, :] = inner * jax.nn.sigmoid(inner) * (1.0 - forget)
            decay[j, at, :] = forget * keep[at, :]

    def step(t, carry):
        out = []
        at = pl.ds(t, CHUNKS, stride=rows)
        for j in range(count):
            state, passed = carry[2 * j], carry[2 * j + 1]
            here = decay[j, at, :]
            state = here * state + drive[j, at, :]
            passed = here * passed
            local[j, at, :] = state
            through[j, at, :] = passed
            out += [state, passed]
        return tuple(out)

    zero, one = jnp.zeros((CHUNKS, LANES), F32), jnp.ones((CHUNKS, LANES), F32)
    last = lax.fori_loop(0, rows, step, (zero, one) * count, unroll=8)
    for j in range(count):
        edge[:CHUNKS, j * LANES : (j + 1) * LANES] = last[2 * j + 1]
        edge[CHUNKS:, j * LANES : (j + 1) * LANES] = last[2 * j]


def entries(order, backwards, count, passed, last, entry):
    def step(n, running):
        row = pl.ds(order[count - 1 - n if backwards else n], 1)
        entry[row, :] = running
        return passed[row, :] * running + last[row, :]

    lax.fori_loop(0, count, step, jnp.zeros((1, last.shape[1]), F32))


def collect(parties, at, to):
    base = 0
    for p in parties:
        for g in range(p.shape[0] // (at[1] * CHUNKS)):
            begin = (g * at[1] + at[0]) * CHUNKS
            to[base : base + CHUNKS, :] = p[begin : begin + CHUNKS, :]
            base += CHUNKS


def mixer_out_kernel(parties, count, order, *refs):
    edges = refs[:parties]
    local, through, raw, mix_gain, out_w = refs[parties : parties + 5]
    states, entry_own, keep, send, passed, last, entry, mixed, squares = refs[parties + 5 :]
    group, feats = raw.shape[0], mix_gain.shape[1]
    width = out_w.shape[1]
    rows = group // CHUNKS
    collect(edges, (0, 2), passed)
    collect(edges, (1, 2), last)
    entries(order, False, count, passed, last, entry)
    base = order[count]
    entry_own[...] = entry[pl.ds(pl.multiple_of(base, CHUNKS), CHUNKS), :]
    for s in range(CHUNKS):
        at = slice(s * rows, (s + 1) * rows)
        total = jnp.zeros((rows, LANES), F32)
        for j in range(feats // LANES):
            lanes = slice(j * LANES, (j + 1) * LANES)
            state = local[j, at, :] + through[j, at, :] * entry_own[s : s + 1, lanes]
            gate = raw[at, 2 * feats + j * LANES : 2 * feats + (j + 1) * LANES]
            mixed[at, lanes] = (state * (mix_gain[:, lanes] * (gate * jax.nn.sigmoid(gate)))).astype(BF)
            states[j, at, :] = state
            total = total + state * state
        squares[at, :] = stat_block([jnp.sum(total, axis=1, keepdims=True)])
    half = group // 2
    keep[:, width:] = squares[:half, :]
    send[:, width:] = squares[half:, :].astype(BF)

    for k in range(2):
        part = slice(k * half // 2, (k + 1) * half // 2)
        keep[part, :width] = dot(mixed[part, :], out_w[...])
        part2 = slice(half + k * half // 2, half + (k + 1) * half // 2)
        send[part, :width] = dot(mixed[part2, :], out_w[...]).astype(BF)


def shares_kernel(keep, got, own, *others):
    rows = own.shape[0]
    own[...] = keep[:rows, :] + got[:rows, :].astype(F32)
    for k, other in enumerate(others):
        at = slice((k + 1) * rows, (k + 2) * rows)
        other[...] = (keep[at, :] + got[at, :].astype(F32)).astype(BF)


def total_of(refs, at, lanes):
    total = refs[0][at, lanes]
    for r in refs[1:]:
        total = total + r[at, lanes].astype(F32)
    return total


STEP = 16


def resid_kernel(own, a, b, c, tokens, gain, resid, hidden, scale):
    width = tokens.shape[1]

    @pl.loop(0, tokens.shape[0] // STEP)
    def _(i):
        at = pl.ds(i * STEP, STEP)
        q = lax.rsqrt(stat(total_of((own, a, b, c), at, slice(width, None)), 0) / width + epsilon)
        value = tokens[at, :].astype(F32) + q * total_of((own, a, b, c), at, slice(0, width))
        resid[at, :] = value
        hidden[at, :] = (value * inverse_rms(value) * gain[...]).astype(BF)
        scale[at, :] = jnp.broadcast_to(q, (STEP, LANES))


def glu_kernel(first, *refs):
    h_near, h_far, d_near, d_far, weight = refs[:5]
    if first:
        d_gate, d_up, act, total = refs[5:]
    else:
        before, d_gate, d_up, act, keep, send = refs[5:]
    half, block = h_near.shape[0], d_gate.shape[1]
    rows = half // 2
    w_gate, w_up, w_down = (slice(k * block, (k + 1) * block) for k in range(3))
    for k, (h, d) in enumerate(((h_near, d_near), (h_far, d_far))):
        for i in range(half // rows):
            at, to = slice(i * rows, (i + 1) * rows), slice(k * half + i * rows, k * half + (i + 1) * rows)
            gate = times_transposed(h[at, :], weight[w_gate, :])
            up = times_transposed(h[at, :], weight[w_up, :])
            d_act = times_transposed(d[at, :], weight[w_down, :])
            sig = jax.nn.sigmoid(gate)
            silu = gate * sig
            act[to, :] = (silu * up).astype(BF)
            d_gate[to, :] = (d_act * up * sigmoid_slope(gate, sig)).astype(BF)
            d_up[to, :] = (d_act * silu).astype(BF)
            value = dot(d_gate[to, :], weight[w_gate, :]) + dot(d_up[to, :], weight[w_up, :])
            if first:
                total[to, :] = value
            elif k == 0:
                keep[at, :] = before[to, :] + value
            else:
                send[at, :] = (before[to, :] + value).astype(BF)


def glu_out_kernel(act0, act1, w0, w1, keep, send):
    half, block = keep.shape[0], act0.shape[1]
    down = slice(2 * block, 3 * block)
    rows = half // 2
    for k in range(4):
        at = slice(k * rows, (k + 1) * rows)
        to = slice(k % 2 * rows, (k % 2 + 1) * rows)
        value = dot(act0[at, :], w0[down, :]) + dot(act1[at, :], w1[down, :])
        if k < 2:
            keep[to, :] = value
        else:
            send[to, :] = value.astype(BF)


def glu_weights_kernel(parts, d_gate, d_up, act, h_near, h_far, d_near, d_far, *outs):
    half, block = h_near.shape[0], d_gate.shape[1]
    part = h_near.shape[1] // parts
    for m, (left, near, far) in enumerate(
        ((d_gate, h_near, h_far), (d_up, h_near, h_far), (act, d_near, d_far))
    ):
        for k in range(parts):
            cols = slice(k * part, (k + 1) * part)
            value = contract_rows(left[:half, :], near[:, cols])
            value = value + contract_rows(left[half:, :], far[:, cols])
            outs[k][m * block : (m + 1) * block, :] = value.astype(BF)


def d_resid_kernel(own, a, b, c, resid, tokens, grad, gain, scale, d_resid, piece):
    width = tokens.shape[1]

    @pl.loop(0, tokens.shape[0] // STEP)
    def _(i):
        at = pl.ds(i * STEP, STEP)
        d_hidden = total_of((own, a, b, c), at, slice(None)) * gain[...]
        value = resid[at, :]
        inv = inverse_rms(value)
        hat = value * inv
        d_value = grad[at, :].astype(F32) + inv * (d_hidden - hat * mean_last(d_hidden * hat))
        d_resid[at, :] = d_value
        low = d_value.astype(BF)
        piece[at, :width] = low
        mean = mean_last(low.astype(F32) * (value - tokens[at, :].astype(F32)))
        piece[at, width:] = stat_block([scale[at, :1], mean]).astype(BF)


def mixer_back_kernel(near, far, out_w, raw, states, mix_gain, decay, *refs):
    mixed, d_gate_raw, local, after, first, d_mixin, d_states = refs
    width = out_w.shape[1]
    group, feats = raw.shape[0], mix_gain.shape[1]
    rows, half = group // CHUNKS, group // 2
    count = feats // LANES
    for k, source in enumerate((near, far)):
        d_mixin[k * half : (k + 1) * half, :] = times_transposed(source[:, :width], out_w[...])
        for s in range(Z):
            part, at = slice(s * rows, (s + 1) * rows), slice(k * half + s * rows, k * half + (s + 1) * rows)
            stats = source[part, width:]
            q, mean = stat(stats, 0), stat(stats, 1)
            for j in range(count):
                lanes = slice(j * LANES, (j + 1) * LANES)
                hat = states[j, at, :] * q
                gate = raw[at, 2 * feats + j * LANES : 2 * feats + (j + 1) * LANES]
                sig = jax.nn.sigmoid(gate)
                silu = gate * sig
                gain = mix_gain[:, lanes]
                d = d_mixin[at, lanes] * gain
                mixed[at, lanes] = (hat * gain * silu).astype(BF)
                d_gate_raw[at, lanes] = (d * hat * sigmoid_slope(gate, sig)).astype(BF)
                d_states[j, at, :] = q * (d * silu - hat * mean)

    def step(t, carry):
        out = []
        at = pl.ds(rows - 1 - t, CHUNKS, stride=rows)
        for j in range(count):
            coming, passed = carry[2 * j], carry[2 * j + 1]
            here = decay[j, at, :]
            adjoint = d_states[j, at, :] + coming
            local[j, at, :] = adjoint
            after[j, at, :] = passed
            out += [here * adjoint, here * passed]
        return tuple(out)

    zero, one = jnp.zeros((CHUNKS, LANES), F32), jnp.ones((CHUNKS, LANES), F32)
    last = lax.fori_loop(0, rows, step, (zero, one) * count, unroll=8)
    for j in range(count):
        first[:, j * LANES : (j + 1) * LANES] = last[2 * j]


def d_mixer_kernel(parties, parts, count, order, *refs):
    edges, firsts = refs[:parties], refs[parties : 2 * parties]
    refs = refs[2 * parties :]
    local, after, states, entry_own, raw, keep_mask, bound, d_gate_raw = refs[:8]
    weights = refs[8 : 8 + parts]
    d_raw, d_bound, keep, send, passed, last, entry = refs[8 + parts :]
    group, feats = raw.shape[0], bound.shape[1]
    rows, half = group // CHUNKS, group // 2
    collect(edges, (0, 2), passed)
    collect(firsts, (0, 1), last)
    entries(order, True, count, passed, last, entry)
    base = pl.multiple_of(order[count], CHUNKS)
    top = lax.broadcasted_iota(jnp.int32, (rows, LANES), 0) == 0
    for j in range(feats // LANES):
        lanes = slice(j * LANES, (j + 1) * LANES)
        coming = entry[pl.ds(base, CHUNKS), lanes]
        low = bound[:, lanes]
        total = jnp.zeros((1, LANES), F32)
        for s in range(CHUNKS):
            at = slice(s * rows, (s + 1) * rows)
            adjoint = local[j, at, :] + after[j, at, :] * coming[s : s + 1, :]
            previous = jnp.where(top, entry_own[s : s + 1, lanes], pltpu.roll(states[j, at, :], 1, 0))
            inner = raw[at, lanes]
            sig_inner = jax.nn.sigmoid(inner)
            sig = jax.nn.sigmoid(raw[at, feats + j * LANES : feats + (j + 1) * LANES])
            open_part = (1.0 - low) * (1.0 - sig)
            d_forget = adjoint * (previous * keep_mask[at, :] - inner * sig_inner)
            d_inner = adjoint * open_part * sigmoid_slope(inner, sig_inner)
            d_raw[at, lanes] = d_inner.astype(BF)
            d_raw[at, feats + j * LANES : feats + (j + 1) * LANES] = (d_forget * open_part * sig).astype(BF)
            total = total + jnp.sum(d_forget * (1.0 - sig), axis=0, keepdims=True)
        d_bound[:, lanes] = total
    d_raw[:, 2 * feats :] = d_gate_raw[...]
    begin = 0
    for w in weights:
        cols = slice(begin, begin + w.shape[0])
        for k in range(2):
            part, part2 = slice(k * half // 2, (k + 1) * half // 2), slice(half + k * half // 2, half + (k + 1) * half // 2)
            keep[part, cols] = times_transposed(d_raw[part, :], w[...])
            send[part, cols] = times_transposed(d_raw[part2, :], w[...]).astype(BF)
        begin += w.shape[0]


def token_grad_kernel(own, a, b, c, tokens, d_resid, gain, out):
    @pl.loop(0, tokens.shape[0] // STEP)
    def _(i):
        at = pl.ds(i * STEP, STEP)
        value = tokens[at, :].astype(F32)
        inv = inverse_rms(value)
        hat = value * inv
        d = total_of((own, a, b, c), at, slice(None)) * gain[...]
        out[at, :] = d_resid[at, :] + inv * (d - hat * mean_last(d * hat))


def result_kernel(own, a, b, c, resid, out):
    @pl.loop(0, resid.shape[0] // STEP)
    def _(i):
        at = pl.ds(i * STEP, STEP)
        out[at, :] = (resid[at, :] + total_of((own, a, b, c), at, slice(None))).astype(BF)


def gather_rows(own):
    near = jnp.concatenate([own] + [across_z(own, k) for k in range(1, Z)], axis=0)
    return near, swap(near, "c")


def scatter_rows(keep, send):
    rows, width = keep.shape[0] // Z, keep.shape[1]
    shapes = [((rows, width), F32)] + [((rows, width), BF)] * (Z - 1)
    own, *others = call(shares_kernel, shapes, keep, swap(send, "c"))
    return [own] + [across_z(v, k + 1) for k, v in enumerate(others)]


def per_device(
    tokens, lengths, w_in, w_forget, w_gate, w_out, attn_gain, mix_gain, bound_table,
    ff_gate, ff_up, ff_down, mlp_gain, out_grad,
):
    Y = lax.axis_size("y")
    pair = Y == 2
    parts = 2 if pair else 1
    z, y, c, x = (lax.axis_index(a) for a in "zycx")
    rows, width = tokens.shape
    sub = w_in.shape[0]
    feats = Y * sub
    block = ff_gate.shape[1] // CHUNKS
    tall = 3 * block
    group = rows * CHUNKS
    half = group // 2
    near_y = y[None].astype(jnp.int32)

    def y_first(*values):
        if pair:
            return call(
                functools.partial(reorder_kernel, False),
                [(v.shape, v.dtype) for v in values], near_y, *values, smem=1,
            )
        return [
            v.reshape(v.shape[0], Z, Y, C * sub).transpose(0, 2, 1, 3).reshape(v.shape) for v in values
        ]

    def z_first(*values):
        if pair:
            return call(
                functools.partial(reorder_kernel, True),
                [(v.shape, v.dtype) for v in values], near_y, *values, smem=1,
            )
        return [
            v.reshape(v.shape[0], Y, Z, C * sub).transpose(0, 2, 1, 3).reshape(v.shape) for v in values
        ]

    def over_y(value):
        if pair:
            return [value, swap(value, "y")]
        return [lax.all_gather(value, "y", axis=0, tiled=True)]

    def in_order(value):
        if pair:
            other = swap(value, "y")
            return jnp.concatenate(
                [jnp.where(y == 0, value, other), jnp.where(y == 0, other, value)], axis=0
            )
        return lax.all_gather(value, "y", axis=0, tiled=True)

    def spread(value):
        return lax.all_to_all(value, ("z", "c"), 0, 0, tiled=True)

    def both(own, sent, axis):
        return own.astype(BF).astype(F32) + swap(sent.astype(BF), axis).astype(F32)

    gains = jnp.stack([attn_gain, mlp_gain])
    if pair:
        gains = jnp.stack([gains, swap(gains, "y")])
        gains = jnp.stack([gains] + [across_z(gains, k) for k in range(1, Z)])
        gains = jnp.stack([gains, swap(gains, "c")]).reshape(CHUNKS, 4 * sub)
        slot = jnp.arange(CHUNKS)
        source = (slot % C ^ c) * Z + (slot // C ^ z)
        pick = (source[:, None] == slot[None, :]).astype(BF)
        gains = dot(pick, gains).reshape(CHUNKS, 2, 2, sub)
        attn_g, mlp_g = (gains[:, :, k].transpose(1, 0, 2).reshape(1, width) for k in range(2))
    else:
        gains = lax.all_gather(gains, ("z", "y", "c"), axis=1, tiled=True).astype(F32)
        attn_g, mlp_g = y_first(gains[:1], gains[1:])

    tokens_y, grad_y = y_first(tokens, out_grad)
    tokens_near, tokens_far = gather_rows(tokens_y)

    if pair:
        (mixer,) = call(mixer_blocks_kernel, [((CHUNKS, sub, 3 * feats), BF)], w_in, w_forget, w_gate)
    else:
        mixer = jnp.concatenate(
            [
                w.reshape(sub, Z, Y, C, sub).transpose(1, 3, 0, 2, 4).reshape(CHUNKS, sub, feats)
                for w in (w_in, w_forget, w_gate)
            ],
            axis=2,
        )
    mixer = over_y(spread(mixer).reshape(CHUNKS * sub, 3 * feats))
    (out_rows,) = y_first(in_order(w_out))
    table_f = bound_table.astype(F32)
    soft = jax.nn.softmax(table_f, axis=0)
    own_bound = jnp.sum(soft[1 : LAYER + 1], axis=0)
    small = in_order(jnp.stack([own_bound, mix_gain.astype(F32)])[None])
    bound = small[:, 0].reshape(1, feats)
    mix_g = small[:, 1].reshape(1, feats)

    if pair:
        (glu,) = call(glu_blocks_kernel, [((CHUNKS, tall, sub), BF)], ff_gate, ff_up, ff_down)
    else:
        glu = jnp.concatenate(
            [w.T.reshape(CHUNKS, block, sub) for w in (ff_gate, ff_up)] + [ff_down.reshape(CHUNKS, block, sub)],
            axis=1,
        )
    glu = spread(glu)
    cut = tall // 2

    def assemble(pieces):
        return jnp.concatenate([p.transpose(1, 0, 2).reshape(p.shape[1], -1) for p in pieces], axis=1)

    if pair:
        side, up_y = swap(glu, "x"), swap(glu, "y")
        corner = jnp.concatenate([swap(up_y[:, :cut], "x"), swap(side[:, cut:], "y")], axis=1)
        glu_w = [assemble([glu, up_y]), assemble([side, corner])]
    else:
        every = assemble(over_y(glu))
        glu_w = [every, swap(every, "x")]

    slot = jnp.arange(lengths.shape[0])
    starts = jnp.sum(jnp.where(slot[None, :] < slot[:, None], lengths[None, :], 0), axis=1)
    slot = jnp.arange(CHUNKS)
    chunk = ((z ^ (slot % Z)) * Y + y) * (C * X) + (c ^ (slot // Z)) * X + x
    position = (chunk[:, None] * rows + jnp.arange(rows)[None, :]).reshape(group)
    keep = 1.0 - jnp.any(position[:, None] == starts[None, :], axis=1).astype(F32)[:, None]
    count = Z * Y * C * X
    number = jnp.arange(count)
    xn, cn = number % X, number // X % C
    yn, zn = number // (X * C) % Y, number // (X * C * Y)
    party = (yn ^ y) * X + (xn ^ x) if pair else yn * X + xn
    order = party * CHUNKS + (cn ^ c) * Z + (zn ^ z)
    base = 0 * y if pair else (y * X + x) * CHUNKS
    order = jnp.concatenate([order, base[None]]).astype(jnp.int32)

    def parties(value):
        if pair:
            corner = lax.ppermute(value, ("y", "x"), [(i, 3 - i) for i in range(4)])
            return [value, swap(value, "x"), swap(value, "y"), corner]
        return [lax.all_gather(value, ("y", "x"), axis=0, tiled=True)]

    crowd = 4 if pair else 1
    featured = ((feats // LANES, group, LANES), F32)
    normed, raw, decay, local, through, edge = call(
        functools.partial(mixer_forward_kernel, parts),
        [((group, width), BF), ((group, 3 * feats), F32)] + [featured] * 3 + [((2 * CHUNKS, feats), F32)],
        attn_g, tokens_near, tokens_far, bound, keep, *mixer,
        scratch=[pltpu.VMEM(*featured)], flops=2 * group * width * 3 * feats,
    )
    edges = parties(edge)
    carries = [pltpu.VMEM((Y * X * CHUNKS, feats), F32)] * 3
    states, entry, keep_rows, send_rows = call(
        functools.partial(mixer_out_kernel, crowd, count),
        [featured, ((CHUNKS, feats), F32), ((half, width + LANES), F32), ((half, width + LANES), BF)],
        order, *edges, local, through, raw, mix_g, out_rows,
        smem=1, scratch=carries + [pltpu.VMEM((group, feats), BF), pltpu.VMEM((group, LANES), F32)],
        flops=2 * group * width * feats,
    )
    resid, hidden, scale = call(
        resid_kernel,
        [((rows, width), F32), ((rows, width), BF), ((rows, LANES), F32)],
        *scatter_rows(keep_rows, send_rows), tokens_y, mlp_g,
    )
    hidden_near, hidden_far = gather_rows(hidden)
    grad_near, grad_far = gather_rows(grad_y)
    wide = [hidden_near, hidden_far, grad_near, grad_far]
    thin = ((group, block), BF)
    glu_flops = 2 * group * width * block
    d_gate0, d_up0, act0, d_hidden = call(
        functools.partial(glu_kernel, True), [thin] * 3 + [((group, width), F32)],
        *wide, glu_w[0], flops=5 * glu_flops,
    )
    d_gate1, d_up1, act1, keep_rows, send_rows = call(
        functools.partial(glu_kernel, False), [thin] * 3 + [((half, width), F32), ((half, width), BF)],
        *wide, glu_w[1], d_hidden, flops=5 * glu_flops,
    )
    d_resid, piece = call(
        d_resid_kernel, [((rows, width), F32), ((rows, width + LANES), BF)],
        *scatter_rows(keep_rows, send_rows), resid, tokens_y, grad_y, mlp_g, scale,
    )
    d_mixed_near, d_mixed_far = gather_rows(piece)

    grads = [
        call(
            functools.partial(glu_weights_kernel, parts), [((tall, width // parts), BF)] * parts,
            *left, *wide, flops=3 * glu_flops,
        )
        for left in ((d_gate0, d_up0, act0), (d_gate1, d_up1, act1))
    ]

    def to_blocks(value):
        return value.reshape(value.shape[0], -1, sub).transpose(1, 0, 2)

    if pair:
        upper = [both(grads[0][k][:cut], grads[1][k][:cut], "x") for k in range(2)]
        lower = [both(grads[k][0][cut:], grads[k][1][cut:], "y") for k in range(2)]
        glu_grad = jnp.concatenate([both(*upper, "y"), both(*lower, "x")], axis=0)
        glu_grad = to_blocks(glu_grad.astype(BF))
    else:
        glu_grad = to_blocks(both(grads[0][0], grads[1][0], "x").astype(BF))
        glu_grad = lax.psum_scatter(glu_grad, "y", scatter_dimension=0, tiled=True)
    glu_grad = spread(glu_grad)

    mixed_in, d_gate_raw, adjoint, after, first = call(
        mixer_back_kernel,
        [((group, feats), BF)] * 2 + [featured] * 2 + [((CHUNKS, feats), F32)],
        d_mixed_near, d_mixed_far, out_rows, raw, states, mix_g, decay,
        scratch=[pltpu.VMEM((group, feats), F32), pltpu.VMEM(*featured)],
        flops=2 * group * width * feats,
    )
    d_raw, part_bound, keep_rows, send_rows = call(
        functools.partial(d_mixer_kernel, crowd, parts, count),
        [((group, 3 * feats), BF), ((1, feats), F32), ((half, width), F32), ((half, width), BF)],
        order, *edges, *parties(first), adjoint, after, states, entry, raw, keep, bound, d_gate_raw, *mixer,
        smem=1, scratch=carries, flops=2 * group * width * 3 * feats,
    )

    act0, act1, _ = lax.optimization_barrier((act0, act1, d_mixed_far))
    keep_out, send_out = call(
        glu_out_kernel, [((half, width), F32), ((half, width), BF)],
        act0, act1, *glu_w, flops=2 * glu_flops,
    )
    (result_y,) = call(result_kernel, [((rows, width), BF)], *scatter_rows(keep_out, send_out), resid)

    (token_grad_y,) = call(
        token_grad_kernel, [((rows, width), F32)],
        *scatter_rows(keep_rows, send_rows), tokens_y, d_resid, attn_g,
    )
    result, token_grad = z_first(result_y, token_grad_y)

    grad_out = contract_rows(mixed_in[:half], d_mixed_near[:, :width])
    grad_out = grad_out + contract_rows(mixed_in[half:], d_mixed_far[:, :width])
    (grad_out,) = z_first(grad_out.astype(BF))
    if pair:
        top, bottom = jnp.split(grad_out, 2, axis=0)
        grad_out = both(jnp.where(y == 0, top, bottom), jnp.where(y == 0, bottom, top), "y")
    else:
        grad_out = lax.psum_scatter(grad_out, "y", scatter_dimension=0, tiled=True)
    grad_out = both(grad_out, grad_out, "x")

    part_bound = part_bound.reshape(feats)
    if pair:
        top, bottom = jnp.split(part_bound, 2)
        d_bound = jnp.where(y == 0, top, bottom) + swap(jnp.where(y == 0, bottom, top), "y")
    else:
        d_bound = lax.psum_scatter(part_bound, "y", scatter_dimension=0, tiled=True)
    d_bound = d_bound + swap(d_bound, "x")
    row_ids = jnp.arange(bound_table.shape[0])[:, None]
    member = jnp.logical_and(row_ids >= 1, row_ids <= LAYER).astype(F32)
    grad_table = soft * (member - own_bound[None, :]) * d_bound[None, :]

    if pair:
        span = width // 2
        mixer_grad = both(*(contract_rows(normed[:, k * span : (k + 1) * span], d_raw) for k in range(2)), "y")
    else:
        mixer_grad = lax.psum_scatter(
            contract_rows(normed, d_raw).astype(BF), "y", scatter_dimension=0, tiled=True
        )
    mixer_grad = both(mixer_grad, mixer_grad, "x").astype(BF)
    mixer_grad = spread(mixer_grad.reshape(CHUNKS, sub, 3 * feats))

    def along(weight, grad):
        return jnp.sum(weight.astype(F32) * grad, axis=1)

    square, glued = ((sub, width), F32), ((sub, CHUNKS * block), F32)
    if pair:
        grad_in, grad_forget, grad_gate, grad_attn = call(
            mixer_grads_kernel, [square] * 3 + [((sub, LANES), F32)], mixer_grad, w_in, w_forget, w_gate
        )
        grad_gate_ff, grad_up_ff, grad_down, grad_mlp = call(
            glu_grads_kernel, [glued] * 2 + [((CHUNKS * block, sub), F32), ((sub, LANES), F32)],
            glu_grad, ff_gate, ff_up,
        )
        grad_attn, grad_mlp = grad_attn[:, 0], grad_mlp[:, 0]
    else:
        mixer_grad = mixer_grad.reshape(Z, C, sub, 3, Y, sub).transpose(3, 2, 0, 4, 1, 5)
        grad_in, grad_forget, grad_gate = mixer_grad.reshape(3, sub, width).astype(F32)
        grad_attn = along(w_in, grad_in) + along(w_forget, grad_forget) + along(w_gate, grad_gate)
        pieces = jnp.split(glu_grad.astype(F32), 3, axis=1)
        grad_gate_ff, grad_up_ff = (p.reshape(CHUNKS * block, sub).T for p in pieces[:2])
        grad_down = pieces[2].reshape(CHUNKS * block, sub)
        grad_mlp = along(ff_gate, grad_gate_ff) + along(ff_up, grad_up_ff)
    grad_attn = grad_attn / attn_gain.astype(F32)
    grad_mix = along(w_out, grad_out) / mix_gain.astype(F32)
    grad_mlp = (grad_mlp + swap(grad_mlp, "x")) / mlp_gain.astype(F32)
    return (
        result, token_grad, grad_in, grad_forget, grad_gate, grad_out, grad_attn, grad_mix,
        grad_table, grad_gate_ff, grad_up_ff, grad_down, grad_mlp,
    )


def solution(mesh):
    dp, mp = mesh.devices.shape
    grid = Mesh(mesh.devices.reshape(Z, dp // CHUNKS, C, mp), ("z", "y", "c", "x"))
    dp_axes = ("z", "y", "c")
    every = ("z", "y", "c", "x")
    mat, row, gain = P(dp_axes, None), P(every, None), P(dp_axes)
    table, glu, glu_down = P(None, dp_axes), P(dp_axes, "x"), P("x", dp_axes)
    return jax.shard_map(
        per_device,
        mesh=grid,
        in_specs=(
            row, P(), mat, mat, mat, mat, gain, gain, table, glu, glu, glu_down, gain, row,
        ),
        out_specs=(
            row, row, mat, mat, mat, mat, gain, gain, table, glu, glu, glu_down, gain,
        ),
        check_vma=False,
    )
```

time: 720 us -> 574 us (0.80)
  the two profiles are of different devices: /device:TPU:10 before, /device:TPU:0 now
where the time goes in v3:
time: 574 us; the launch traced here: 565 us
  waiting for transfers between devices  345 us (60%)
  starting transfers between devices  98.8 us (17%)
  Pallas kernels  65.8 us (11%)
  local copies, waits for them, and re-layouts  32.3 us (6%)
  other arithmetic  15.7 us (3%)
    ppermute x27, waiting for transfers between devices, across_z(): return lax.ppermute(value, 'z', [(i, i ^ step) for i in range(Z)])  160 us
    ppermute x34, waiting for transfers between devices, swap(): return lax.ppermute(value, axis, [(0, 1), (1, 0)])  153 us
    pallas_call x25, Pallas kernels, call(): pl.pallas_call(kernel, out_shape=shapes, in_specs=specs, out_specs=[pl.Bl...  65.8 us
    ppermute x27, starting transfers between devices, across_z(): return lax.ppermute(value, 'z', [(i, i ^ step) for i in range(Z)])  49.9 us
    all_to_all x4, waiting for transfers between devices, spread(): return lax.all_to_all(value, ('z', 'c'), 0, 0, tiled=True)  31.3 us
    unnamed x122, local copies, waits for them, and re-layouts  26.9 us
    ppermute x34, starting transfers between devices, swap(): return lax.ppermute(value, axis, [(0, 1), (1, 0)])  26 us
    all_to_all x4, starting transfers between devices, spread(): return lax.all_to_all(value, ('z', 'c'), 0, 0, tiled=True)  18.9 us
  transfers between devices with their start and end apart: 67, of which 30 were waited for; matrix products, arithmetic and copies ran while one was open for 5% of the time, Pallas kernels for 6%

profile of v3, /device:TPU:0, one launch (start us, length us, event | category | flops | bytes accessed | tf_op | source)
XLA Modules:
  0.0 565.2 jit_solution(3909055241740876149)
XLA Ops:
  5.2 6.5 %all-to-all-start = ((bf16[8,128,768]{2,1,0:T(8,128)(2,1)}), bf16[8,128,768]{2,1,0:T(8,128)(2,1)S(1)}, u32[]{:S(2)}, u32[]{:S(2)}) async-start(bf16[8,128,768]{2,1,0:T(8,128)(2,1)} %shard_map.238), calls=%async_computation | async-start | bytes 3145728 | tf_op jit(solution)/shard_map/all_to_all | solution.py:525
  14.4 3.8 collective-permute-start.7
  24.4 31.3 %all-to-all-done = bf16[8,128,768]{2,1,0:T(8,128)(2,1)S(1)} async-done(((bf16[8,128,768]{2,1,0:T(8,128)(2,1)}), bf16[8,128,768]{2,1,0:T(8,128)(2,1)S(1)}, u32[]{:S(2)}, u32[]{:S(2)}) %all-to-all-start) | async-done | bytes 1572896 | tf_op jit(solution)/shard_map/all_to_all | solution.py:525
  55.6 4.3 all-to-all-start.1
  61.7 2.9 collective-permute-start.2
  66.2 44.3 %collective-permute-done.2 = bf16[2,2,128]{2,1,0:T(2,128)(2,1)S(1)} collective-permute-done((bf16[2,2,128]{2,1,0:T(2,128)(2,1)S(1)}, bf16[2,2,128]{2,1,0:T(2,128)(2,1)S(1)}, u32[]{:S(2)}, u32[]{:S(2)}) %collective-permute-start.2) | collective-permute-done | bytes 1056 | tf_op jit(solution)/shard_map/ppermute | solution.py:23
  114.4 9.5 %collective-permute-done.6 = bf16[64,2048]{1,0:T(8,128)(2,1)S(1)} collective-permute-done((bf16[64,2048]{1,0:T(8,128)(2,1)S(1)}, bf16[64,2048]{1,0:T(8,128)(2,1)S(1)}, u32[]{:S(2)}, u32[]{:S(2)}) %collective-permute-start.6) | collective-permute-done | bytes 262176 | tf_op jit(solution)/shard_map/ppermute | solution.py:23
  129.3 28.6 %collective-permute-done.10.refs_6_.refs_17_ = bf16[1024,768]{1,0:T(8,128)(2,1)S(1)} collective-permute-done((bf16[1024,768]{1,0:T(8,128)(2,1)S(1)}, bf16[1024,768]{1,0:T(8,128)(2,1)S(1)}, u32[]{:S(2)}, u32[]{:S(2)}) %collective-permute-start.10) | collective-permute-done | bytes 1572896 | tf_op jit(solution)/shard_map/ppermute | solution.py:19
  160.5 7.6 %shard_map.239 = (bf16[512,2048]{1,0:T(8,128)(2,1)S(1)}, f32[512,768]{1,0:T(8,128)S(1)}, f32[2,512,128]{2,1,0:T(8,128)S(1)}, f32[2,512,128]{2,1,0:T(8,128)S(1)},...) custom-call(f32[1,2048]{1,0:T(1,128)S(1)} %bitcast.98, bf16[256,2048]{1,0:T(8,128)(2,1)S(1)} %copy-done.44, ...), custom_call_target="tpu_custom_call" | custom-call | flops 1610612736 | bytes 10513408 | tf_op jit(solution)/shard_map/pallas_call | solution.py:55
  168.1 2.5 collective-permute-start.13
  174.9 2.6 shard_map.241
  185.0 4.9 collective-permute-done.23
  189.9 3.1 collective-permute-start.24
  199.3 9.8 %collective-permute-done.24 = bf16[64,2048]{1,0:T(8,128)(2,1)S(1)} collective-permute-done((bf16[64,2048]{1,0:T(8,128)(2,1)}, bf16[64,2048]{1,0:T(8,128)(2,1)S(1)}, u32[]{:S(2)}, u32[]{:S(2)}) %collective-permute-start.24) | collective-permute-done | bytes 262176 | tf_op jit(solution)/shard_map/ppermute | solution.py:23
  210.9 15.3 %collective-permute-done.17.b = bf16[64,2176]{1,0:T(8,128)(2,1)S(1)} collective-permute-done((bf16[64,2176]{1,0:T(8,128)(2,1)S(1)}, bf16[64,2176]{1,0:T(8,128)(2,1)S(1)}, u32[]{:S(2)}, u32[]{:S(2)}) %collective-permute-start.17) | collective-permute-done | bytes 278560 | tf_op jit(solution)/shard_map/ppermute | solution.py:23
  227.3 6.5 %collective-permute-start.19 = (bf16[64,2048]{1,0:T(8,128)(2,1)S(1)}, bf16[64,2048]{1,0:T(8,128)(2,1)S(1)}, u32[]{:S(2)}, u32[]{:S(2)}) collective-permute-start(bf16[64,2048]{1,0:T(8,128)(2,1)S(1)} %get-tuple-element.93), channel_id=1, source_target_pairs={{0,8},{8,0},{16,24},{24,16},{1,9},{9,1},{17,25},{25,17},{2,10},{10... | collective-permute-start | bytes 786440 | tf_op jit(solution)/shard_map/ppermute | solution.py:23
  239.1 3.9 collective-permute-done.19
  244.5 12.6 %collective-permute-done.20 = bf16[64,2048]{1,0:T(8,128)(2,1)S(1)} collective-permute-done((bf16[64,2048]{1,0:T(8,128)(2,1)S(1)}, bf16[64,2048]{1,0:T(8,128)(2,1)S(1)}, u32[]{:S(2)}, u32[]{:S(2)}) %collective-permute-start.20) | collective-permute-done | bytes 262176 | tf_op jit(solution)/shard_map/ppermute | solution.py:23
  259.3 4.4 collective-permute-done.30
  263.7 4.1 collective-permute-done.29
  269.6 8.5 %shard_map.245 = (bf16[512,352]{1,0:T(8,128)(2,1)S(1)}, bf16[512,352]{1,0:T(8,128)(2,1)S(1)}, bf16[512,352]{1,0:T(8,128)(2,1)S(1)}, f32[512,2048]{1,0:T(8,128)S(1)}) custom-call(bf16[256,2048]{1,0:T(8,128)(2,1)S(1)} %constant_dynamic-update-slice_fusion.4.refs_0_.h_near, bf16[256,2048]{1,0:T(8,128)(2,1)S(1)} %collective-permute-done.22.refs_1_.h_far, ...), custom_call_target="tpu_custom_call" | custom-call | flops 3690987520 | bytes 13795328 | tf_op jit(solution)/shard_map/pallas_call | solution.py:55
  278.1 11.1 %shard_map.246 = (bf16[512,352]{1,0:T(8,128)(2,1)S(1)}, bf16[512,352]{1,0:T(8,128)(2,1)S(1)}, bf16[512,352]{1,0:T(8,128)(2,1)S(1)}, f32[256,2048]{1,0:T(8,128)S(1)}, bf16[256,2048]{1,0:T(8,128)(2,1)S(1)}) custom-call(bf16[256,2048]{1,0:T(8,128)(2,1)S(1)} %constant_dynamic-update-slice_fusion.4.refs_0_.h_near, ...), custom_call_target="tpu_custom_call" | custom-call | flops 3690987520 | bytes 16941056 | tf_op jit(solution)/shard_map/pallas_call | solution.py:55
  289.2 2.4 shard_map.260
  294.7 2.4 shard_map.259
  298.6 2.7 collective-permute-start.33
  301.4 18.8 %collective-permute-done.57 = bf16[528,1024]{1,0:T(8,128)(2,1)S(1)} collective-permute-done((bf16[528,1024]{1,0:T(8,128)(2,1)}, bf16[528,1024]{1,0:T(8,128)(2,1)S(1)}, u32[]{:S(2)}, u32[]{:S(2)}) %collective-permute-start.57) | collective-permute-done | bytes 1081376 | tf_op jit(solution)/shard_map/ppermute | solution.py:19
  324.9 5.0 collective-permute-done.34.c
  332.2 9.1 %collective-permute-done.35 = bf16[64,2176]{1,0:T(8,128)(2,1)S(1)} collective-permute-done((bf16[64,2176]{1,0:T(8,128)(2,1)S(1)}, bf16[64,2176]{1,0:T(8,128)(2,1)S(1)}, u32[]{:S(2)}, u32[]{:S(2)}) %collective-permute-start.35) | collective-permute-done | bytes 278560 | tf_op jit(solution)/shard_map/ppermute | solution.py:23
  341.3 13.8 %collective-permute-done.36 = bf16[64,2176]{1,0:T(8,128)(2,1)S(1)} collective-permute-done((bf16[64,2176]{1,0:T(8,128)(2,1)S(1)}, bf16[64,2176]{1,0:T(8,128)(2,1)S(1)}, u32[]{:S(2)}, u32[]{:S(2)}) %collective-permute-start.36) | collective-permute-done | bytes 278560 | tf_op jit(solution)/shard_map/ppermute | solution.py:23
  356.3 7.1 %collective-permute-done.37 = bf16[64,2176]{1,0:T(8,128)(2,1)S(1)} collective-permute-done((bf16[64,2176]{1,0:T(8,128)(2,1)S(1)}, bf16[64,2176]{1,0:T(8,128)(2,1)S(1)}, u32[]{:S(2)}, u32[]{:S(2)}) %collective-permute-start.37) | collective-permute-done | bytes 278560 | tf_op jit(solution)/shard_map/ppermute | solution.py:23
  366.3 2.6 shard_map.252
  372.5 18.0 %collective-permute-done.61 = bf16[528,1024]{1,0:T(8,128)(2,1)S(1)} collective-permute-done((bf16[528,1024]{1,0:T(8,128)(2,1)S(1)}, bf16[528,1024]{1,0:T(8,128)(2,1)S(1)}, u32[]{:S(2)}, u32[]{:S(2)}) %collective-permute-start.61) | collective-permute-done | bytes 1081376 | tf_op jit(solution)/shard_map/ppermute | solution.py:19
  393.9 5.7 %shard_map.253 = (bf16[512,768]{1,0:T(8,128)(2,1)S(1)}, f32[1,256]{1,0:T(1,128)S(1)}, f32[256,2048]{1,0:T(8,128)S(1)}, bf16[256,2048]{1,0:T(8,128)(2,1)S(1)}) custom-call(s32[33]{0:T(128)S(1)} %pad_add_fusion.order, f32[16,256]{1,0:T(8,128)S(1)} %get-tuple-element.83.refs_0_, f32[16,256]{1,0:T(8,128)S(1)} %collective-permute-done.11.refs_1_, ...), custom_call_target="tpu_custom_call" | custom-call | flops 1610612736 | bytes 10596484 | tf_op jit(solution)/shard_map/pallas_call | solution.py:55
  403.8 3.6 all-to-all-start.3
  409.7 28.3 %collective-permute-done.50 = bf16[1024,768]{1,0:T(8,128)(2,1)} collective-permute-done((bf16[1024,768]{1,0:T(8,128)(2,1)}, bf16[1024,768]{1,0:T(8,128)(2,1)}, u32[]{:S(2)}, u32[]{:S(2)}) %collective-permute-start.50) | collective-permute-done | bytes 1572896 | tf_op jit(solution)/shard_map/ppermute | solution.py:19
  442.4 32.3 %collective-permute-done.51 = bf16[1024,768]{1,0:T(8,128)(2,1)S(1)} collective-permute-done((bf16[1024,768]{1,0:T(8,128)(2,1)S(1)}, bf16[1024,768]{1,0:T(8,128)(2,1)S(1)}, u32[]{:S(2)}, u32[]{:S(2)}) %collective-permute-start.51) | collective-permute-done | bytes 1572896 | tf_op jit(solution)/shard_map/ppermute | solution.py:19
  476.3 4.5 all-to-all-start.2
  485.6 4.6 shard_map.249
  492.1 3.1 collective-permute-done.52
  497.6 11.6 %collective-permute-done.55 = f32[128]{0:T(128)S(1)} collective-permute-done((f32[128]{0:T(128)S(1)}, f32[128]{0:T(128)S(1)}, u32[]{:S(2)}, u32[]{:S(2)}) %collective-permute-start.55) | collective-permute-done | bytes 544 | tf_op jit(solution)/shard_map/ppermute | solution.py:19
  511.4 2.4 collective-permute-start.41
  517.4 3.3 collective-permute-start.48
  520.7 5.9 %collective-permute-done.40.a = bf16[64,2048]{1,0:T(8,128)(2,1)S(1)} collective-permute-done((bf16[64,2048]{1,0:T(8,128)(2,1)S(1)}, bf16[64,2048]{1,0:T(8,128)(2,1)S(1)}, u32[]{:S(2)}, u32[]{:S(2)}) %collective-permute-start.40) | collective-permute-done | bytes 262176 | tf_op jit(solution)/shard_map/ppermute | solution.py:23
  526.6 7.9 %collective-permute-start.49 = (bf16[64,2048]{1,0:T(8,128)(2,1)S(1)}, bf16[64,2048]{1,0:T(8,128)(2,1)S(1)}, u32[]{:S(2)}, u32[]{:S(2)}) collective-permute-start(bf16[64,2048]{1,0:T(8,128)(2,1)S(1)} %get-tuple-element.127), channel_id=1, source_target_pairs={{0,24},{8,16},{16,8},{24,0},{1,25},{9,17},{17,9},{25,1},{2,26},{10... | collective-permute-start | bytes 786440 | tf_op jit(solution)/shard_map/ppermute | solution.py:23
  535.1 4.1 shard_map.261
  539.3 7.9 %collective-permute-done.41.b = bf16[64,2048]{1,0:T(8,128)(2,1)S(1)} collective-permute-done((bf16[64,2048]{1,0:T(8,128)(2,1)S(1)}, bf16[64,2048]{1,0:T(8,128)(2,1)S(1)}, u32[]{:S(2)}, u32[]{:S(2)}) %collective-permute-start.41) | collective-permute-done | bytes 262176 | tf_op jit(solution)/shard_map/ppermute | solution.py:23
  548.9 9.5 %collective-permute-done.48.b = bf16[64,2048]{1,0:T(8,128)(2,1)S(1)} collective-permute-done((bf16[64,2048]{1,0:T(8,128)(2,1)S(1)}, bf16[64,2048]{1,0:T(8,128)(2,1)S(1)}, u32[]{:S(2)}, u32[]{:S(2)}) %collective-permute-start.48) | collective-permute-done | bytes 262176 | tf_op jit(solution)/shard_map/ppermute | solution.py:23
  560.8 3.6 shard_map.257
  (299 shorter events, 114.8 us)
Async XLA Ops:
  5.2 50.4 %all-to-all-start = ((bf16[8,128,768]{2,1,0:T(8,128)(2,1)}), bf16[8,128,768]{2,1,0:T(8,128)(2,1)S(1)}, u32[]{:S(2)}, u32[]{:S(2)}) async-start(bf16[8,128,768]{2,1,0:T(8,128)(2,1)} %shard_map.238), calls=%async_computation | async-start | bytes 3145728 | tf_op jit(solution)/shard_map/all_to_all | solution.py:525
  14.4 110.2 %collective-permute-start.7 = (bf16[64,2048]{1,0:T(8,128)(2,1)S(1)}, bf16[64,2048]{1,0:T(8,128)(2,1)}, u32[]{:S(2)}, u32[]{:S(2)}) collective-permute-start(bf16[64,2048]{1,0:T(8,128)(2,1)S(1)} %get-tuple-element.82.tokens), channel_id=1, source_target_pairs={{0,24},{8,16},{16,8},{24,0},{1,25},{9,17},{17,9},{25,1},{2,26},{10... | collective-permute-start | bytes 786440 | tf_op jit(solution)/shard_map/ppermute | solution.py:23
  18.2 94.0 %collective-permute-start.5 = (bf16[64,2048]{1,0:T(8,128)(2,1)S(1)}, bf16[64,2048]{1,0:T(8,128)(2,1)}, u32[]{:S(2)}, u32[]{:S(2)}) collective-permute-start(bf16[64,2048]{1,0:T(8,128)(2,1)S(1)} %get-tuple-element.82.tokens), channel_id=1, source_target_pairs={{0,8},{8,0},{16,24},{24,16},{1,9},{9,1},{17,25},{25,17},{2,10},{10... | collective-permute-start | bytes 786440 | tf_op jit(solution)/shard_map/ppermute | solution.py:23
  18.2 43.4 %collective-permute-start = (bf16[2,128]{1,0:T(2,128)(2,1)S(1)}, bf16[2,128]{1,0:T(2,128)(2,1)S(1)}, u32[]{:S(2)}, u32[]{:S(2)}) collective-permute-start(bf16[2,128]{1,0:T(2,128)(2,1)S(1)} %pad_maximum_fusion.5), channel_id=1, source_target_pairs={{0,4},{4,0},{1,5},{5,1},{2,6},{6,2},{3,7},{7,3},{8,12},{12,8},{9,1... | collective-permute-start | bytes 1544 | tf_op jit(solution)/shard_map/ppermute | solution.py:19
  19.9 46.1 %collective-permute-start.9 = (f32[1,2,128]{2,1,0:T(2,128)S(1)}, f32[1,2,128]{2,1,0:T(2,128)S(1)}, u32[]{:S(2)}, u32[]{:S(2)}) collective-permute-start(f32[1,2,128]{2,1,0:T(2,128)S(1)} %maximum_bitcast_fusion.2), channel_id=1, source_target_pairs={{0,4},{4,0},{1,5},{5,1},{2,6},{6,2},{3,7},{7,3},{8,12},{12,8},{9,1... | collective-permute-start | bytes 3080 | tf_op jit(solution)/shard_map/ppermute | solution.py:19
  55.6 123.2 %all-to-all-start.1 = ((bf16[8,1056,128]{2,1,0:T(8,128)(2,1)}), bf16[8,1056,128]{2,1,0:T(8,128)(2,1)}, u32[]{:S(2)}, u32[]{:S(2)}) async-start(bf16[8,1056,128]{2,1,0:T(8,128)(2,1)} %shard_map.244), calls=%async_computation.1 | async-start | bytes 4325376 | tf_op jit(solution)/shard_map/all_to_all | solution.py:525
  61.7 48.8 %collective-permute-start.2 = (bf16[2,2,128]{2,1,0:T(2,128)(2,1)S(1)}, bf16[2,2,128]{2,1,0:T(2,128)(2,1)S(1)}, u32[]{:S(2)}, u32[]{:S(2)}) collective-permute-start(bf16[2,2,128]{2,1,0:T(2,128)(2,1)S(1)} %pad_maximum_fusion.4), channel_id=1, source_target_pairs={{0,16},{8,24},{16,0},{24,8},{1,17},{9,25},{17,1},{25,9},{2,18},{10... | collective-permute-start | bytes 3080 | tf_op jit(solution)/shard_map/ppermute | solution.py:23
  64.6 45.9 %collective-permute-start.1 = (bf16[2,2,128]{2,1,0:T(2,128)(2,1)S(1)}, bf16[2,2,128]{2,1,0:T(2,128)(2,1)S(1)}, u32[]{:S(2)}, u32[]{:S(2)}) collective-permute-start(bf16[2,2,128]{2,1,0:T(2,128)(2,1)S(1)} %pad_maximum_fusion.4), channel_id=1, source_target_pairs={{0,8},{8,0},{16,24},{24,16},{1,9},{9,1},{17,25},{25,17},{2,10},{10... | collective-permute-start | bytes 3080 | tf_op jit(solution)/shard_map/ppermute | solution.py:23
  66.0 46.0 %collective-permute-start.3 = (bf16[2,2,128]{2,1,0:T(2,128)(2,1)S(1)}, bf16[2,2,128]{2,1,0:T(2,128)(2,1)S(1)}, u32[]{:S(2)}, u32[]{:S(2)}) collective-permute-start(bf16[2,2,128]{2,1,0:T(2,128)(2,1)S(1)} %pad_maximum_fusion.4), channel_id=1, source_target_pairs={{0,24},{8,16},{16,8},{24,0},{1,25},{9,17},{17,9},{25,1},{2,26},{10... | collective-permute-start | bytes 3080 | tf_op jit(solution)/shard_map/ppermute | solution.py:23
  110.5 16.0 %collective-permute-start.14 = (bf16[128,2048]{1,0:T(8,128)(2,1)}, bf16[128,2048]{1,0:T(8,128)(2,1)}, u32[]{:S(2)}, u32[]{:S(2)}) collective-permute-start(bf16[128,2048]{1,0:T(8,128)(2,1)} %param.19), channel_id=1, source_target_pairs={{0,4},{4,0},{1,5},{5,1},{2,6},{6,2},{3,7},{7,3},{8,12},{12,8},{9,1... | collective-permute-start | bytes 1572872 | tf_op jit(solution)/shard_map/ppermute | solution.py:19
  112.2 45.7 %collective-permute-start.10 = (bf16[1024,768]{1,0:T(8,128)(2,1)S(1)}, bf16[1024,768]{1,0:T(8,128)(2,1)S(1)}, u32[]{:S(2)}, u32[]{:S(2)}) collective-permute-start(bf16[1024,768]{1,0:T(8,128)(2,1)S(1)} %bitcast.93), channel_id=1, source_target_pairs={{0,4},{4,0},{1,5},{5,1},{2,6},{6,2},{3,7},{7,3},{8,12},{12,8},{9,1... | collective-permute-start | bytes 4718600 | tf_op jit(solution)/shard_map/ppermute | solution.py:19
  178.8 15.1 %collective-permute-start.15 = (bf16[256,2176]{1,0:T(8,128)(2,1)}, bf16[256,2176]{1,0:T(8,128)(2,1)}, u32[]{:S(2)}, u32[]{:S(2)}) collective-permute-start(bf16[256,2176]{1,0:T(8,128)(2,1)} %get-tuple-element.88), channel_id=1, source_target_pairs={{0,2},{2,0},{1,3},{3,1},{4,6},{6,4},{5,7},{7,5},{8,10},{10,8},{9,1... | collective-permute-start | bytes 3342344 | tf_op jit(solution)/shard_map/ppermute | solution.py:19
  178.8 57.3 %collective-permute-start.28 = (bf16[8,1056,128]{2,1,0:T(8,128)(2,1)}, bf16[8,1056,128]{2,1,0:T(8,128)(2,1)S(1)}, u32[]{:S(2)}, u32[]{:S(2)}) collective-permute-start(bf16[8,1056,128]{2,1,0:T(8,128)(2,1)} %all-to-all-done.1), channel_id=1, source_target_pairs={{0,1},{1,0},{2,3},{3,2},{4,5},{5,4},{6,7},{7,6},{8,9},{9,8},{10,11... | collective-permute-start | bytes 6488072 | tf_op jit(solution)/shard_map/ppermute | solution.py:19
  179.4 59.0 %collective-permute-start.27 = (bf16[8,1056,128]{2,1,0:T(8,128)(2,1)}, bf16[8,1056,128]{2,1,0:T(8,128)(2,1)S(1)}, u32[]{:S(2)}, u32[]{:S(2)}) collective-permute-start(bf16[8,1056,128]{2,1,0:T(8,128)(2,1)} %all-to-all-done.1), channel_id=1, source_target_pairs={{0,4},{4,0},{1,5},{5,1},{2,6},{6,2},{3,7},{7,3},{8,12},{12,8},{9,1... | collective-permute-start | bytes 6488072 | tf_op jit(solution)/shard_map/ppermute | solution.py:19
  182.9 15.2 %collective-permute-start.25 = (bf16[64,2048]{1,0:T(8,128)(2,1)}, bf16[64,2048]{1,0:T(8,128)(2,1)S(1)}, u32[]{:S(2)}, u32[]{:S(2)}) collective-permute-start(bf16[64,2048]{1,0:T(8,128)(2,1)} %copy-done.29), channel_id=1, source_target_pairs={{0,24},{8,16},{16,8},{24,0},{1,25},{9,17},{17,9},{25,1},{2,26},{10... | collective-permute-start | bytes 786440 | tf_op jit(solution)/shard_map/ppermute | solution.py:23
  189.9 19.2 %collective-permute-start.24 = (bf16[64,2048]{1,0:T(8,128)(2,1)}, bf16[64,2048]{1,0:T(8,128)(2,1)S(1)}, u32[]{:S(2)}, u32[]{:S(2)}) collective-permute-start(bf16[64,2048]{1,0:T(8,128)(2,1)} %copy-done.29), channel_id=1, source_target_pairs={{0,16},{8,24},{16,0},{24,8},{1,17},{9,25},{17,1},{25,9},{2,18},{10... | collective-permute-start | bytes 786440 | tf_op jit(solution)/shard_map/ppermute | solution.py:23
  198.1 28.2 %collective-permute-start.17 = (bf16[64,2176]{1,0:T(8,128)(2,1)S(1)}, bf16[64,2176]{1,0:T(8,128)(2,1)S(1)}, u32[]{:S(2)}, u32[]{:S(2)}) collective-permute-start(bf16[64,2176]{1,0:T(8,128)(2,1)S(1)} %get-tuple-element.91), channel_id=1, source_target_pairs={{0,16},{8,24},{16,0},{24,8},{1,17},{9,25},{17,1},{25,9},{2,18},{10... | collective-permute-start | bytes 835592 | tf_op jit(solution)/shard_map/ppermute | solution.py:23
  209.1 17.1 %collective-permute-start.18 = (bf16[64,2176]{1,0:T(8,128)(2,1)S(1)}, bf16[64,2176]{1,0:T(8,128)(2,1)S(1)}, u32[]{:S(2)}, u32[]{:S(2)}) collective-permute-start(bf16[64,2176]{1,0:T(8,128)(2,1)S(1)} %get-tuple-element.92), channel_id=1, source_target_pairs={{0,24},{8,16},{16,8},{24,0},{1,25},{9,17},{17,9},{25,1},{2,26},{10... | collective-permute-start | bytes 835592 | tf_op jit(solution)/shard_map/ppermute | solution.py:23
  210.8 58.7 %collective-permute-start.26 = (bf16[256,2048]{1,0:T(8,128)(2,1)S(1)}, bf16[256,2048]{1,0:T(8,128)(2,1)S(1)}, u32[]{:S(2)}, u32[]{:S(2)}) collective-permute-start(bf16[256,2048]{1,0:T(8,128)(2,1)S(1)} %constant_dynamic-update-slice_fusion.8.refs_2_.d_near), channel_id=1, source_target_pairs={{0,2},{2,0},{1,3},{3,1},{4,6},{6,4},{5,7},{7,5},{8,10},{10,8},{9,1... | collective-permute-start | bytes 3145736 | tf_op jit(solution)/shard_map/ppermute | solution.py:19
  227.3 15.7 %collective-permute-start.19 = (bf16[64,2048]{1,0:T(8,128)(2,1)S(1)}, bf16[64,2048]{1,0:T(8,128)(2,1)S(1)}, u32[]{:S(2)}, u32[]{:S(2)}) collective-permute-start(bf16[64,2048]{1,0:T(8,128)(2,1)S(1)} %get-tuple-element.93), channel_id=1, source_target_pairs={{0,8},{8,0},{16,24},{24,16},{1,9},{9,1},{17,25},{25,17},{2,10},{10... | collective-permute-start | bytes 786440 | tf_op jit(solution)/shard_map/ppermute | solution.py:23
  235.7 21.4 %collective-permute-start.20 = (bf16[64,2048]{1,0:T(8,128)(2,1)S(1)}, bf16[64,2048]{1,0:T(8,128)(2,1)S(1)}, u32[]{:S(2)}, u32[]{:S(2)}) collective-permute-start(bf16[64,2048]{1,0:T(8,128)(2,1)S(1)} %get-tuple-element.93), channel_id=1, source_target_pairs={{0,16},{8,24},{16,0},{24,8},{1,17},{9,25},{17,1},{25,9},{2,18},{10... | collective-permute-start | bytes 786440 | tf_op jit(solution)/shard_map/ppermute | solution.py:23
  236.1 21.0 %collective-permute-start.21 = (bf16[64,2048]{1,0:T(8,128)(2,1)S(1)}, bf16[64,2048]{1,0:T(8,128)(2,1)S(1)}, u32[]{:S(2)}, u32[]{:S(2)}) collective-permute-start(bf16[64,2048]{1,0:T(8,128)(2,1)S(1)} %get-tuple-element.93), channel_id=1, source_target_pairs={{0,24},{8,16},{16,8},{24,0},{1,25},{9,17},{17,9},{25,1},{2,26},{10... | collective-permute-start | bytes 786440 | tf_op jit(solution)/shard_map/ppermute | solution.py:23
  238.4 25.3 %collective-permute-start.30 = (bf16[8,528,128]{2,1,0:T(8,128)(2,1)S(1)}, bf16[8,528,128]{2,1,0:T(8,128)(2,1)S(1)}, u32[]{:S(2)}, u32[]{:S(2)}) collective-permute-start(bf16[8,528,128]{2,1,0:T(8,128)(2,1)S(1)} %slice.100), channel_id=1, source_target_pairs={{0,4},{4,0},{1,5},{5,1},{2,6},{6,2},{3,7},{7,3},{8,12},{12,8},{9,1... | collective-permute-start | bytes 3244040 | tf_op jit(solution)/shard_map/ppermute | solution.py:19
  243.0 24.8 %collective-permute-start.29 = (bf16[8,528,128]{2,1,0:T(8,128)(2,1)S(1)}, bf16[8,528,128]{2,1,0:T(8,128)(2,1)S(1)}, u32[]{:S(2)}, u32[]{:S(2)}) collective-permute-start(bf16[8,528,128]{2,1,0:T(8,128)(2,1)S(1)} %slice.99), channel_id=1, source_target_pairs={{0,1},{1,0},{2,3},{3,2},{4,5},{5,4},{6,7},{7,6},{8,9},{9,8},{10,11... | collective-permute-start | bytes 3244040 | tf_op jit(solution)/shard_map/ppermute | solution.py:19
  293.2 27.0 %collective-permute-start.57 = (bf16[528,1024]{1,0:T(8,128)(2,1)}, bf16[528,1024]{1,0:T(8,128)(2,1)S(1)}, u32[]{:S(2)}, u32[]{:S(2)}) collective-permute-start(bf16[528,1024]{1,0:T(8,128)(2,1)} %get-tuple-element.155), channel_id=1, source_target_pairs={{0,1},{1,0},{2,3},{3,2},{4,5},{5,4},{6,7},{7,6},{8,9},{9,8},{10,11... | collective-permute-start | bytes 3244040 | tf_op jit(solution)/shard_map/ppermute | solution.py:19
  297.3 73.2 %collective-permute-start.56 = (bf16[528,1024]{1,0:T(8,128)(2,1)S(1)}, bf16[528,1024]{1,0:T(8,128)(2,1)S(1)}, u32[]{:S(2)}, u32[]{:S(2)}) collective-permute-start(bf16[528,1024]{1,0:T(8,128)(2,1)S(1)} %slice.86), channel_id=1, source_target_pairs={{0,1},{1,0},{2,3},{3,2},{4,5},{5,4},{6,7},{7,6},{8,9},{9,8},{10,11... | collective-permute-start | bytes 3244040 | tf_op jit(solution)/shard_map/ppermute | solution.py:19
  297.9 74.1 %collective-permute-start.59 = (bf16[528,1024]{1,0:T(8,128)(2,1)S(1)}, bf16[528,1024]{1,0:T(8,128)(2,1)S(1)}, u32[]{:S(2)}, u32[]{:S(2)}) collective-permute-start(bf16[528,1024]{1,0:T(8,128)(2,1)S(1)} %slice.90), channel_id=1, source_target_pairs={{0,4},{4,0},{1,5},{5,1},{2,6},{6,2},{3,7},{7,3},{8,12},{12,8},{9,1... | collective-permute-start | bytes 3244040 | tf_op jit(solution)/shard_map/ppermute | solution.py:19
  298.6 24.2 %collective-permute-start.32 = (bf16[64,2048]{1,0:T(8,128)(2,1)S(1)}, bf16[64,2048]{1,0:T(8,128)(2,1)S(1)}, u32[]{:S(2)}, u32[]{:S(2)}) collective-permute-start(bf16[64,2048]{1,0:T(8,128)(2,1)S(1)} %get-tuple-element.101), channel_id=1, source_target_pairs={{0,8},{8,0},{16,24},{24,16},{1,9},{9,1},{17,25},{25,17},{2,10},{10... | collective-permute-start | bytes 786440 | tf_op jit(solution)/shard_map/ppermute | solution.py:23
  298.6 24.7 %collective-permute-start.33 = (bf16[64,2048]{1,0:T(8,128)(2,1)S(1)}, bf16[64,2048]{1,0:T(8,128)(2,1)S(1)}, u32[]{:S(2)}, u32[]{:S(2)}) collective-permute-start(bf16[64,2048]{1,0:T(8,128)(2,1)S(1)} %get-tuple-element.102), channel_id=1, source_target_pairs={{0,16},{8,24},{16,0},{24,8},{1,17},{9,25},{17,1},{25,9},{2,18},{10... | collective-permute-start | bytes 786440 | tf_op jit(solution)/shard_map/ppermute | solution.py:23
  322.8 40.8 %collective-permute-start.60 = (bf16[528,1024]{1,0:T(8,128)(2,1)}, bf16[528,1024]{1,0:T(8,128)(2,1)S(1)}, u32[]{:S(2)}, u32[]{:S(2)}) collective-permute-start(bf16[528,1024]{1,0:T(8,128)(2,1)} %get-tuple-element.156), channel_id=1, source_target_pairs={{0,4},{4,0},{1,5},{5,1},{2,6},{6,2},{3,7},{7,3},{8,12},{12,8},{9,1... | collective-permute-start | bytes 3244040 | tf_op jit(solution)/shard_map/ppermute | solution.py:19
  323.4 49.2 %collective-permute-start.58 = (bf16[528,1024]{1,0:T(8,128)(2,1)S(1)}, bf16[528,1024]{1,0:T(8,128)(2,1)S(1)}, u32[]{:S(2)}, u32[]{:S(2)}) collective-permute-start(bf16[528,1024]{1,0:T(8,128)(2,1)S(1)} %add_convert_fusion.6), channel_id=1, source_target_pairs={{0,4},{4,0},{1,5},{5,1},{2,6},{6,2},{3,7},{7,3},{8,12},{12,8},{9,1... | collective-permute-start | bytes 3244040 | tf_op jit(solution)/shard_map/ppermute | solution.py:19
  364.0 26.5 %collective-permute-start.61 = (bf16[528,1024]{1,0:T(8,128)(2,1)S(1)}, bf16[528,1024]{1,0:T(8,128)(2,1)S(1)}, u32[]{:S(2)}, u32[]{:S(2)}) collective-permute-start(bf16[528,1024]{1,0:T(8,128)(2,1)S(1)} %add_convert_fusion.3), channel_id=1, source_target_pairs={{0,1},{1,0},{2,3},{3,2},{4,5},{5,4},{6,7},{7,6},{8,9},{9,8},{10,11... | collective-permute-start | bytes 3244040 | tf_op jit(solution)/shard_map/ppermute | solution.py:19
  368.9 23.5 %collective-permute-start.45 = (f32[8,256]{1,0:T(8,128)S(1)}, f32[8,256]{1,0:T(8,128)S(1)}, u32[]{:S(2)}, u32[]{:S(2)}) collective-permute-start(f32[8,256]{1,0:T(8,128)S(1)} %get-tuple-element.117.refs_4_), channel_id=1, source_target_pairs={{0,5},{1,4},{4,1},{5,0},{2,7},{3,6},{6,3},{7,2},{8,13},{9,12},{12,... | collective-permute-start | bytes 24584 | tf_op jit(solution)/shard_map/ppermute | solution.py:604
  370.4 22.0 %collective-permute-start.44 = (f32[8,256]{1,0:T(8,128)S(1)}, f32[8,256]{1,0:T(8,128)S(1)}, u32[]{:S(2)}, u32[]{:S(2)}) collective-permute-start(f32[8,256]{1,0:T(8,128)S(1)} %get-tuple-element.117.refs_4_), channel_id=1, source_target_pairs={{0,4},{4,0},{1,5},{5,1},{2,6},{6,2},{3,7},{7,3},{8,12},{12,8},{9,1... | collective-permute-start | bytes 24584 | tf_op jit(solution)/shard_map/ppermute | solution.py:19
  372.0 20.5 %collective-permute-start.43 = (f32[8,256]{1,0:T(8,128)S(1)}, f32[8,256]{1,0:T(8,128)S(1)}, u32[]{:S(2)}, u32[]{:S(2)}) collective-permute-start(f32[8,256]{1,0:T(8,128)S(1)} %get-tuple-element.117.refs_4_), channel_id=1, source_target_pairs={{0,1},{1,0},{2,3},{3,2},{4,5},{5,4},{6,7},{7,6},{8,9},{9,8},{10,11... | collective-permute-start | bytes 24584 | tf_op jit(solution)/shard_map/ppermute | solution.py:19
  401.8 36.1 %collective-permute-start.50 = (bf16[1024,768]{1,0:T(8,128)(2,1)}, bf16[1024,768]{1,0:T(8,128)(2,1)}, u32[]{:S(2)}, u32[]{:S(2)}) collective-permute-start(bf16[1024,768]{1,0:T(8,128)(2,1)} %convolution_convert_fusion), channel_id=1, source_target_pairs={{0,4},{4,0},{1,5},{5,1},{2,6},{6,2},{3,7},{7,3},{8,12},{12,8},{9,1... | collective-permute-start | bytes 4718600 | tf_op jit(solution)/shard_map/ppermute | solution.py:19
  403.8 72.5 %all-to-all-start.3 = ((bf16[8,1056,128]{2,1,0:T(8,128)(2,1)}), bf16[8,1056,128]{2,1,0:T(8,128)(2,1)S(1)}, u32[]{:S(2)}, u32[]{:S(2)}) async-start(bf16[8,1056,128]{2,1,0:T(8,128)(2,1)} %maximum_bitcast_fusion.1), calls=%async_computation.3 | async-start | bytes 4325376 | tf_op jit(solution)/shard_map/all_to_all | solution.py:525
  439.8 35.0 %collective-permute-start.51 = (bf16[1024,768]{1,0:T(8,128)(2,1)S(1)}, bf16[1024,768]{1,0:T(8,128)(2,1)S(1)}, u32[]{:S(2)}, u32[]{:S(2)}) collective-permute-start(bf16[1024,768]{1,0:T(8,128)(2,1)S(1)} %add_convert_fusion.1), channel_id=1, source_target_pairs={{0,1},{1,0},{2,3},{3,2},{4,5},{5,4},{6,7},{7,6},{8,9},{9,8},{10,11... | collective-permute-start | bytes 4718600 | tf_op jit(solution)/shard_map/ppermute | solution.py:19
  476.3 84.5 %all-to-all-start.2 = ((bf16[8,128,768]{2,1,0:T(8,128)(2,1)}), bf16[8,128,768]{2,1,0:T(8,128)(2,1)}, u32[]{:S(2)}, u32[]{:S(2)}) async-start(bf16[8,128,768]{2,1,0:T(8,128)(2,1)} %bitcast.100), calls=%async_computation.2 | async-start | bytes 3145728 | tf_op jit(solution)/shard_map/all_to_all | solution.py:525
  490.3 19.5 %collective-permute-start.39 = (bf16[256,2048]{1,0:T(8,128)(2,1)S(1)}, bf16[256,2048]{1,0:T(8,128)(2,1)S(1)}, u32[]{:S(2)}, u32[]{:S(2)}) collective-permute-start(bf16[256,2048]{1,0:T(8,128)(2,1)S(1)} %get-tuple-element.110), channel_id=1, source_target_pairs={{0,2},{2,0},{1,3},{3,1},{4,6},{6,4},{5,7},{7,5},{8,10},{10,8},{9,1... | collective-permute-start | bytes 3145736 | tf_op jit(solution)/shard_map/ppermute | solution.py:19
  492.1 24.7 %collective-permute-start.46 = (bf16[256,2048]{1,0:T(8,128)(2,1)S(1)}, bf16[256,2048]{1,0:T(8,128)(2,1)S(1)}, u32[]{:S(2)}, u32[]{:S(2)}) collective-permute-start(bf16[256,2048]{1,0:T(8,128)(2,1)S(1)} %copy-done.46), channel_id=1, source_target_pairs={{0,2},{2,0},{1,3},{3,1},{4,6},{6,4},{5,7},{7,5},{8,10},{10,8},{9,1... | collective-permute-start | bytes 3145736 | tf_op jit(solution)/shard_map/ppermute | solution.py:19
  495.5 19.0 %collective-permute-start.53 = (bf16[128,2048]{1,0:T(8,128)(2,1)S(1)}, bf16[128,2048]{1,0:T(8,128)(2,1)S(1)}, u32[]{:S(2)}, u32[]{:S(2)}) collective-permute-start(bf16[128,2048]{1,0:T(8,128)(2,1)S(1)} %add_convert_fusion.8), channel_id=1, source_target_pairs={{0,1},{1,0},{2,3},{3,2},{4,5},{5,4},{6,7},{7,6},{8,9},{9,8},{10,11... | collective-permute-start | bytes 1572872 | tf_op jit(solution)/shard_map/ppermute | solution.py:19
  510.0 16.6 %collective-permute-start.40 = (bf16[64,2048]{1,0:T(8,128)(2,1)S(1)}, bf16[64,2048]{1,0:T(8,128)(2,1)S(1)}, u32[]{:S(2)}, u32[]{:S(2)}) collective-permute-start(bf16[64,2048]{1,0:T(8,128)(2,1)S(1)} %get-tuple-element.112), channel_id=1, source_target_pairs={{0,8},{8,0},{16,24},{24,16},{1,9},{9,1},{17,25},{25,17},{2,10},{10... | collective-permute-start | bytes 786440 | tf_op jit(solution)/shard_map/ppermute | solution.py:23
  511.4 35.7 %collective-permute-start.41 = (bf16[64,2048]{1,0:T(8,128)(2,1)S(1)}, bf16[64,2048]{1,0:T(8,128)(2,1)S(1)}, u32[]{:S(2)}, u32[]{:S(2)}) collective-permute-start(bf16[64,2048]{1,0:T(8,128)(2,1)S(1)} %get-tuple-element.113), channel_id=1, source_target_pairs={{0,16},{8,24},{16,0},{24,8},{1,17},{9,25},{17,1},{25,9},{2,18},{10... | collective-permute-start | bytes 786440 | tf_op jit(solution)/shard_map/ppermute | solution.py:23
  513.8 34.8 %collective-permute-start.42 = (bf16[64,2048]{1,0:T(8,128)(2,1)S(1)}, bf16[64,2048]{1,0:T(8,128)(2,1)S(1)}, u32[]{:S(2)}, u32[]{:S(2)}) collective-permute-start(bf16[64,2048]{1,0:T(8,128)(2,1)S(1)} %get-tuple-element.114), channel_id=1, source_target_pairs={{0,24},{8,16},{16,8},{24,0},{1,25},{9,17},{17,9},{25,1},{2,26},{10... | collective-permute-start | bytes 786440 | tf_op jit(solution)/shard_map/ppermute | solution.py:23
  516.9 31.9 %collective-permute-start.47 = (bf16[64,2048]{1,0:T(8,128)(2,1)S(1)}, bf16[64,2048]{1,0:T(8,128)(2,1)S(1)}, u32[]{:S(2)}, u32[]{:S(2)}) collective-permute-start(bf16[64,2048]{1,0:T(8,128)(2,1)S(1)} %get-tuple-element.125), channel_id=1, source_target_pairs={{0,8},{8,0},{16,24},{24,16},{1,9},{9,1},{17,25},{25,17},{2,10},{10... | collective-permute-start | bytes 786440 | tf_op jit(solution)/shard_map/ppermute | solution.py:23
  517.4 41.0 %collective-permute-start.48 = (bf16[64,2048]{1,0:T(8,128)(2,1)S(1)}, bf16[64,2048]{1,0:T(8,128)(2,1)S(1)}, u32[]{:S(2)}, u32[]{:S(2)}) collective-permute-start(bf16[64,2048]{1,0:T(8,128)(2,1)S(1)} %get-tuple-element.126), channel_id=1, source_target_pairs={{0,16},{8,24},{16,0},{24,8},{1,17},{9,25},{17,1},{25,9},{2,18},{10... | collective-permute-start | bytes 786440 | tf_op jit(solution)/shard_map/ppermute | solution.py:23
  526.6 31.8 %collective-permute-start.49 = (bf16[64,2048]{1,0:T(8,128)(2,1)S(1)}, bf16[64,2048]{1,0:T(8,128)(2,1)S(1)}, u32[]{:S(2)}, u32[]{:S(2)}) collective-permute-start(bf16[64,2048]{1,0:T(8,128)(2,1)S(1)} %get-tuple-element.127), channel_id=1, source_target_pairs={{0,24},{8,16},{16,8},{24,0},{1,25},{9,17},{17,9},{25,1},{2,26},{10... | collective-permute-start | bytes 786440 | tf_op jit(solution)/shard_map/ppermute | solution.py:23
  (73 other events, 894.9 us)

commit v4 on v3

v4 whole, which is shorter than its diff:
```python
import functools

import jax
import jax.numpy as jnp
from jax import lax
from jax.experimental import pallas as pl
from jax.experimental.pallas import tpu as pltpu
from jax.sharding import Mesh, PartitionSpec as P

LAYER = 12
Z, C, X = 4, 2, 2
CHUNKS = Z * C
LANES = 128
epsilon = 1e-06
VMEM_LIMIT = 56 << 20
BF, F32 = jnp.bfloat16, jnp.float32


def swap(value, axis):
    return lax.ppermute(value, axis, [(0, 1), (1, 0)])


def dot(left, right):
    return jnp.dot(left, right, preferred_element_type=F32)


def contract_rows(left, right):
    return lax.dot_general(left, right, (((0,), (0,)), ((), ())), preferred_element_type=F32)


def times_transposed(left, right):
    return lax.dot_general(left, right, (((1,), (1,)), ((), ())), preferred_element_type=F32)


def mean_last(value):
    return jnp.mean(value, axis=-1, keepdims=True)


def inverse_rms(value):
    return lax.rsqrt(mean_last(value * value) + epsilon)


def sigmoid_slope(raw, sig):
    return sig * (1.0 + raw * (1.0 - sig))


class Copies:
    def __init__(self, inputs, outputs):
        self.inputs, self.outputs, self.waited, self.flushed = inputs, outputs, set(), set()
        for copy in inputs:
            copy.start()

    def wait(self, *numbers):
        for k in numbers:
            if k not in self.waited:
                self.waited.add(k)
                self.inputs[k].wait()

    def flush(self, *numbers):
        for k in numbers:
            if k not in self.flushed:
                self.flushed.add(k)
                self.outputs[k].start()


def call(kernel, outs, *ins, smem=0, scratch=(), late=None):
    n_in, n_out = len(ins) - smem, len(outs)

    def body(*refs):
        scalars, refs = refs[:smem], refs[smem:]
        far_in, far_out, refs = refs[:n_in], refs[n_in : n_in + n_out], refs[n_in + n_out :]
        near_in, near_out, refs = refs[:n_in], refs[n_in : n_in + n_out], refs[n_in + n_out :]
        *own, in_sems, out_sems = refs
        copies = Copies(
            [pltpu.make_async_copy(f, n, in_sems.at[k]) for k, (f, n) in enumerate(zip(far_in, near_in))],
            [pltpu.make_async_copy(n, f, out_sems.at[k]) for k, (f, n) in enumerate(zip(far_out, near_out))],
        )
        copies.wait(*range(n_in if late is None else late))
        kernel(*([] if late is None else [copies]), *scalars, *near_in, *near_out, *own)
        copies.wait(*range(n_in))
        copies.flush(*range(n_out))
        for copy in copies.outputs:
            copy.wait()

    shapes = [jax.ShapeDtypeStruct(s, t) for s, t in outs]
    near = [pltpu.VMEM(v.shape, v.dtype) for v in list(ins[smem:]) + shapes]
    return pl.pallas_call(
        body,
        out_shape=shapes,
        in_specs=[pl.BlockSpec(memory_space=pltpu.SMEM)] * smem + [pl.BlockSpec(memory_space=pl.ANY)] * n_in,
        out_specs=[pl.BlockSpec(memory_space=pl.ANY)] * n_out,
        scratch_shapes=near
        + list(scratch)
        + [pltpu.SemaphoreType.DMA((n_in,)), pltpu.SemaphoreType.DMA((n_out,))],
        compiler_params=pltpu.CompilerParams(vmem_limit_bytes=VMEM_LIMIT),
        cost_estimate=pl.CostEstimate(flops=0, bytes_accessed=1024, transcendentals=0),
    )(*ins)


def stat_block(columns, first=0):
    rows = columns[0].shape[0]
    lane = lax.broadcasted_iota(jnp.int32, (rows, LANES), 1) - first
    block = jnp.zeros((rows, LANES), F32)
    for k, column in enumerate(columns):
        high = column.astype(BF).astype(F32)
        block = jnp.where(lane == 2 * k, high, block)
        block = jnp.where(lane == 2 * k + 1, column - high, block)
    return block


def stat(block, k):
    lane = lax.broadcasted_iota(jnp.int32, block.shape, 1)
    picked = jnp.where((lane == 2 * k) | (lane == 2 * k + 1), block.astype(F32), 0.0)
    return jnp.sum(picked, axis=1, keepdims=True)


def reorder_kernel(back, y_ref, *refs):
    y = y_ref[0]
    half = len(refs) // 2
    for in_ref, out_ref in zip(refs[:half], refs[half:]):
        width = in_ref.shape[1] // CHUNKS
        for k in range(2):
            there = k + y - 2 * k * y
            for z in range(Z):
                near = slice((k * Z + z) * width, (k * Z + z + 1) * width)
                far = pl.ds(pl.multiple_of((z * 2 + there) * width, width), width)
                if back:
                    out_ref[:, far] = in_ref[:, near]
                else:
                    out_ref[:, near] = in_ref[:, far]


def token_piece_kernel(y_ref, tokens, gains, piece):
    width = tokens.shape[1]
    reorder_kernel(False, y_ref, tokens, piece.at[:, :width])
    row = lax.broadcasted_iota(jnp.int32, (tokens.shape[0], LANES), 0)
    block = jnp.zeros((tokens.shape[0], LANES), F32)
    for k in range(gains.shape[0]):
        block = jnp.where(row == k, gains[k : k + 1, :], block)
    piece[:, width:] = block.astype(BF)


def mixer_blocks_kernel(x_ref, *refs):
    *weights, out_ref = refs
    half = len(weights)
    x = x_ref[0]
    for z in range(Z):
        for c in range(C):
            for k in range(half):
                pieces = []
                for j in (k, half + k):
                    at = ((z * 2 + j % 2) * C + c) * LANES
                    pieces.append(weights[j // 2][:, at : at + LANES])
                out_ref[z * C + c, :, k * LANES : (k + 1) * LANES] = jnp.where(x == 0, *pieces)


def mixer_grads_kernel(
    x_ref, mine, theirs, w_in, w_forget, w_gate, grad_in, grad_forget, grad_gate, along_ref
):
    x = x_ref[0]
    total = jnp.zeros((w_in.shape[0], 1), F32)
    for m, (w_ref, g_ref) in enumerate(((w_in, grad_in), (w_forget, grad_forget), (w_gate, grad_gate))):
        for z in range(Z):
            for y in range(2):
                for c in range(C):
                    to, j = ((z * 2 + y) * C + c) * LANES, m * 2 + y
                    at = j % 3 * LANES
                    piece = jnp.where(
                        x == j // 3,
                        mine[z * C + c, :, at : at + LANES],
                        theirs[z * C + c, :, at : at + LANES],
                    ).astype(F32)
                    g_ref[:, to : to + LANES] = piece
                    weight = w_ref[:, to : to + LANES].astype(F32)
                    total = total + jnp.sum(piece * weight, axis=1, keepdims=True)
    along_ref[...] = jnp.broadcast_to(total, along_ref.shape)


def glu_blocks_kernel(gate_ref, up_ref, down_ref, out_ref):
    block = down_ref.shape[0] // CHUNKS
    for s in range(CHUNKS):
        at = slice(s * block, (s + 1) * block)
        out_ref[s, :block] = gate_ref[:, at].astype(F32).T.astype(BF)
        out_ref[s, block : 2 * block] = up_ref[:, at].astype(F32).T.astype(BF)
        out_ref[s, 2 * block :] = down_ref[at, :]


def glu_grads_kernel(blocks_ref, w_gate, w_up, grad_gate, grad_up, grad_down, along_ref):
    block = blocks_ref.shape[1] // 3
    total = jnp.zeros((w_gate.shape[0], 1), F32)
    for s in range(CHUNKS):
        at = slice(s * block, (s + 1) * block)
        for m, (w_ref, g_ref) in enumerate(((w_gate, grad_gate), (w_up, grad_up))):
            piece = blocks_ref[s, m * block : (m + 1) * block].astype(F32).T
            g_ref[:, at] = piece
            total = total + jnp.sum(piece * w_ref[:, at].astype(F32), axis=1, keepdims=True)
        grad_down[at, :] = blocks_ref[s, 2 * block :].astype(F32)
    along_ref[...] = jnp.broadcast_to(total, along_ref.shape)


def columns_of(x_ref, parts, k, span):
    if parts == 1:
        return slice(0, span)
    return pl.ds(pl.multiple_of((k + x_ref[0] - 2 * k * x_ref[0]) * span, LANES), span)


def mixer_forward_kernel(parts, copies, x_ref, *refs):
    gain, tokens, bound, keep = refs[:4]
    weights = refs[4 : 4 + parts * parts]
    normed, raw, decay, local, through, edge, drive = refs[4 + parts * parts :]
    group, feats = raw.shape[0], bound.shape[1]
    width = gain.shape[1]
    rows = group // CHUNKS

    @pl.loop(0, group // 32)
    def _(i):
        at = pl.ds(i * 32, 32)
        value = tokens[at, :width].astype(F32)
        normed[at, :] = (value * inverse_rms(value) * gain[...]).astype(BF)

    copies.flush(0)
    copies.wait(*range(2, 4 + parts * parts))

    @pl.loop(0, 4)
    def _(i):
        at = pl.ds(i * (group // 4), group // 4)
        deep, span = width // parts, 3 * feats // parts
        for k in range(parts):
            total = None
            for d in range(parts):
                part = dot(normed[at, d * deep : (d + 1) * deep], weights[d * parts + k][...])
                total = part if total is None else total + part
            raw[at, columns_of(x_ref, parts, k, span)] = total

    copies.flush(1)
    count = feats // LANES

    @pl.loop(0, CHUNKS)
    def _(i):
        at = pl.ds(i * rows, rows)
        for j in range(count):
            lanes = slice(j * LANES, (j + 1) * LANES)
            inner = raw[at, lanes]
            forget_raw = raw[at, feats + j * LANES : feats + (j + 1) * LANES]
            low = bound[:, lanes]
            forget = low + (1.0 - low) * jax.nn.sigmoid(forget_raw)
            drive[j, at, :] = inner * jax.nn.sigmoid(inner) * (1.0 - forget)
            decay[j, at, :] = forget * keep[at, :]

    copies.flush(2)

    def step(t, carry):
        out = []
        at = pl.ds(t, CHUNKS, stride=rows)
        for j in range(count):
            state, passed = carry[2 * j], carry[2 * j + 1]
            here = decay[j, at, :]
            state = here * state + drive[j, at, :]
            passed = here * passed
            local[j, at, :] = state
            through[j, at, :] = passed
            out += [state, passed]
        return tuple(out)

    zero, one = jnp.zeros((CHUNKS, LANES), F32), jnp.ones((CHUNKS, LANES), F32)
    last = lax.fori_loop(0, rows, step, (zero, one) * count, unroll=8)
    for j in range(count):
        edge[:CHUNKS, j * LANES : (j + 1) * LANES] = last[2 * j + 1]
        edge[CHUNKS:, j * LANES : (j + 1) * LANES] = last[2 * j]


def entries(order, backwards, count, passed, last, entry):
    def step(n, running):
        row = pl.ds(order[count - 1 - n if backwards else n], 1)
        entry[row, :] = running
        return passed[row, :] * running + last[row, :]

    lax.fori_loop(0, count, step, jnp.zeros((1, last.shape[1]), F32))


def collect(parties, at, to):
    base = 0
    for p in parties:
        for g in range(p.shape[0] // (at[1] * CHUNKS)):
            begin = (g * at[1] + at[0]) * CHUNKS
            to[base : base + CHUNKS, :] = p[begin : begin + CHUNKS, :]
            base += CHUNKS


def mixer_out_kernel(parties, count, copies, order, *refs):
    edges = refs[:parties]
    local, through, raw, mix_gain, out_w = refs[parties : parties + 5]
    states, entry_own, partial, passed, last, entry, mixed = refs[parties + 5 :]
    group, feats = raw.shape[0], mix_gain.shape[1]
    width = out_w.shape[1]
    rows = group // CHUNKS
    collect(edges, (0, 2), passed)
    collect(edges, (1, 2), last)
    entries(order, False, count, passed, last, entry)
    base = order[count]
    entry_own[...] = entry[pl.ds(pl.multiple_of(base, CHUNKS), CHUNKS), :]
    copies.wait(*range(parties, parties + 4))
    for s in range(CHUNKS):
        at = slice(s * rows, (s + 1) * rows)
        total = jnp.zeros((rows, LANES), F32)
        for j in range(feats // LANES):
            lanes = slice(j * LANES, (j + 1) * LANES)
            state = local[j, at, :] + through[j, at, :] * entry_own[s : s + 1, lanes]
            gate = raw[at, 2 * feats + j * LANES : 2 * feats + (j + 1) * LANES]
            mixed[at, lanes] = (state * (mix_gain[:, lanes] * (gate * jax.nn.sigmoid(gate)))).astype(BF)
            states[j, at, :] = state
            total = total + state * state
        squares = jnp.sum(total, axis=1, keepdims=True)
        partial[at, width:] = stat_block([squares], 2 * order[count + 1]).astype(BF)
    copies.flush(0)
    copies.wait(parties + 4)
    for k in range(4):
        at = slice(k * group // 4, (k + 1) * group // 4)
        partial[at, :width] = dot(mixed[at, :], out_w[...]).astype(BF)


STEP = 16


def resid_kernel(summed, tokens, gain, resid, hidden, scale):
    width = tokens.shape[1]

    @pl.loop(0, tokens.shape[0] // STEP)
    def _(i):
        at = pl.ds(i * STEP, STEP)
        squares = jnp.sum(summed[at, width:].astype(F32), axis=1, keepdims=True)
        q = lax.rsqrt(squares / width + epsilon)
        value = tokens[at, :].astype(F32) + q * summed[at, :width].astype(F32)
        resid[at, :] = value
        hidden[at, :] = (value * inverse_rms(value) * gain[...]).astype(BF)
        scale[at, :] = jnp.broadcast_to(q, (STEP, LANES))


def glu_kernel(copies, hidden, grad, *refs):
    weights, outs, total, partial = refs[:4], refs[4:10], refs[11], refs[10]
    group, block = outs[0].shape
    for k in range(2):
        gate_up, down = weights[k], weights[2 + k]
        act, d_gate, d_up = outs[3 * k : 3 * k + 3]
        w_gate, w_up = gate_up.at[:block, :], gate_up.at[block:, :]
        copies.wait(0, 2 + k)
        for i in range(4):
            at = slice(i * group // 4, (i + 1) * group // 4)
            gate = times_transposed(hidden[at, :], w_gate[...])
            up = times_transposed(hidden[at, :], w_up[...])
            copies.wait(1, 4 + k)
            d_act = times_transposed(grad[at, :], down[...])
            sig = jax.nn.sigmoid(gate)
            silu = gate * sig
            act[at, :] = (silu * up).astype(BF)
            d_gate[at, :] = (d_act * up * sigmoid_slope(gate, sig)).astype(BF)
            d_up[at, :] = (d_act * silu).astype(BF)
            value = dot(d_gate[at, :], w_gate[...]) + dot(d_up[at, :], w_up[...])
            if k == 0:
                total[at, :] = value
            else:
                partial[at, :] = (total[at, :] + value).astype(BF)
        copies.flush(3 * k, 3 * k + 1, 3 * k + 2)


def glu_out_kernel(act0, act1, w0, w1, partial):
    group = act0.shape[0]
    for k in range(4):
        at = slice(k * group // 4, (k + 1) * group // 4)
        partial[at, :] = (dot(act0[at, :], w0[...]) + dot(act1[at, :], w1[...])).astype(BF)


def glu_weights_kernel(parts, terms, *refs):
    count = len(terms)
    lefts, rights, outs = refs[: 2 * count], refs[2 * count : 2 * count + max(terms) + 1], None
    outs = refs[2 * count + max(terms) + 1 :]
    block = lefts[0].shape[1]
    part = rights[0].shape[1] // parts
    cut = count * block // 2
    for k in range(2):
        for m, right in enumerate(terms):
            begin, end = m * block, (m + 1) * block
            for d in range(parts):
                value = contract_rows(lefts[k * count + m][...], rights[right][:, d * part : (d + 1) * part])
                value = value.astype(BF)
                if parts == 1:
                    outs[k][begin:end, :] = value
                    continue
                upper, lower = outs[k], outs[2 + d]
                if begin < cut:
                    upper[d, begin : min(end, cut)] = value[: min(end, cut) - begin]
                if end > cut:
                    lower[k, max(begin, cut) - cut : end - cut] = value[max(begin, cut) - begin :]


def first_sums_kernel(upper, upper_got, lower, lower_got, upper_keep, upper_send, lower_keep, lower_send):
    for mine, got, keep, send in (
        (upper, upper_got, upper_keep, upper_send),
        (lower, lower_got, lower_keep, lower_send),
    ):
        keep[...] = mine[0].astype(F32) + got[0].astype(F32)
        send[...] = (mine[1].astype(F32) + got[1].astype(F32)).astype(BF)


def last_sums_kernel(*refs):
    *pieces, blocks = refs
    begin = 0
    for mine, got in zip(pieces[::2], pieces[1::2]):
        for s in range(CHUNKS):
            cols = slice(s * LANES, (s + 1) * LANES)
            blocks[s, begin : begin + mine.shape[0]] = (mine[:, cols] + got[:, cols].astype(F32)).astype(BF)
        begin += mine.shape[0]


def d_resid_kernel(summed, resid, tokens, grad, gain, scale, d_resid, piece):
    width = tokens.shape[1]

    @pl.loop(0, tokens.shape[0] // STEP)
    def _(i):
        at = pl.ds(i * STEP, STEP)
        d_hidden = summed[at, :].astype(F32) * gain[...]
        value = resid[at, :]
        inv = inverse_rms(value)
        hat = value * inv
        d_value = grad[at, :].astype(F32) + inv * (d_hidden - hat * mean_last(d_hidden * hat))
        d_resid[at, :] = d_value
        low = d_value.astype(BF)
        piece[at, :width] = low
        mean = mean_last(low.astype(F32) * (value - tokens[at, :].astype(F32)))
        piece[at, width:] = stat_block([scale[at, :1], mean]).astype(BF)


def mixer_back_kernel(copies, d_mixed, out_w, raw, states, mix_gain, decay, *refs):
    mixed, d_gate_raw, local, after, first, d_mixin, d_states = refs
    width = out_w.shape[1]
    group, feats = raw.shape[0], mix_gain.shape[1]
    rows = group // CHUNKS
    count = feats // LANES
    for k in range(2):
        at = slice(k * group // 2, (k + 1) * group // 2)
        d_mixin[at, :] = times_transposed(d_mixed[at, :width], out_w[...])
    copies.wait(2, 3, 4, 5)
    for s in range(CHUNKS):
        at = slice(s * rows, (s + 1) * rows)
        stats = d_mixed[at, width:]
        q, mean = stat(stats, 0), stat(stats, 1)
        for j in range(count):
            lanes = slice(j * LANES, (j + 1) * LANES)
            hat = states[j, at, :] * q
            gate = raw[at, 2 * feats + j * LANES : 2 * feats + (j + 1) * LANES]
            sig = jax.nn.sigmoid(gate)
            silu = gate * sig
            gain = mix_gain[:, lanes]
            d = d_mixin[at, lanes] * gain
            mixed[at, lanes] = (hat * gain * silu).astype(BF)
            d_gate_raw[at, lanes] = (d * hat * sigmoid_slope(gate, sig)).astype(BF)
            d_states[j, at, :] = q * (d * silu - hat * mean)
    copies.flush(0, 1)

    def step(t, carry):
        out = []
        at = pl.ds(rows - 1 - t, CHUNKS, stride=rows)
        for j in range(count):
            coming, passed = carry[2 * j], carry[2 * j + 1]
            here = decay[j, at, :]
            adjoint = d_states[j, at, :] + coming
            local[j, at, :] = adjoint
            after[j, at, :] = passed
            out += [here * adjoint, here * passed]
        return tuple(out)

    zero, one = jnp.zeros((CHUNKS, LANES), F32), jnp.ones((CHUNKS, LANES), F32)
    last = lax.fori_loop(0, rows, step, (zero, one) * count, unroll=8)
    for j in range(count):
        first[:, j * LANES : (j + 1) * LANES] = last[2 * j]


def mixer_weights_kernel(parts, normed, *refs):
    d_raw, outs = refs[:parts], refs[parts:]
    deep = normed.shape[1] // parts
    for d in range(parts):
        for k in range(parts):
            outs[d * parts + k][...] = contract_rows(normed[:, d * deep : (d + 1) * deep], d_raw[k][...]).astype(BF)


def d_mixer_kernel(parties, parts, count, copies, x_ref, order, *refs):
    edges, firsts = refs[:parties], refs[parties : 2 * parties]
    refs = refs[2 * parties :]
    local, after, states, entry_own, raw, keep_mask, bound, d_gate_raw = refs[:8]
    weights = refs[8 : 8 + parts * parts]
    refs = refs[8 + parts * parts :]
    d_parts, (d_bound, partial, passed, last, entry, d_raw) = refs[:parts], refs[parts:]
    group, feats = raw.shape[0], bound.shape[1]
    rows = group // CHUNKS
    collect(edges, (0, 2), passed)
    collect(firsts, (0, 1), last)
    entries(order, True, count, passed, last, entry)
    base = pl.multiple_of(order[count], CHUNKS)
    copies.wait(*range(2 * parties, 2 * parties + 8))
    top = lax.broadcasted_iota(jnp.int32, (rows, LANES), 0) == 0
    for j in range(feats // LANES):
        lanes = slice(j * LANES, (j + 1) * LANES)
        coming = entry[pl.ds(base, CHUNKS), lanes]
        low = bound[:, lanes]
        total = jnp.zeros((1, LANES), F32)
        for s in range(CHUNKS):
            at = slice(s * rows, (s + 1) * rows)
            adjoint = local[j, at, :] + after[j, at, :] * coming[s : s + 1, :]
            previous = jnp.where(top, entry_own[s : s + 1, lanes], pltpu.roll(states[j, at, :], 1, 0))
            inner = raw[at, lanes]
            sig_inner = jax.nn.sigmoid(inner)
            sig = jax.nn.sigmoid(raw[at, feats + j * LANES : feats + (j + 1) * LANES])
            open_part = (1.0 - low) * (1.0 - sig)
            d_forget = adjoint * (previous * keep_mask[at, :] - inner * sig_inner)
            d_inner = adjoint * open_part * sigmoid_slope(inner, sig_inner)
            d_raw[at, lanes] = d_inner.astype(BF)
            d_raw[at, feats + j * LANES : feats + (j + 1) * LANES] = (d_forget * open_part * sig).astype(BF)
            total = total + jnp.sum(d_forget * (1.0 - sig), axis=0, keepdims=True)
        d_bound[:, lanes] = total
    d_raw[:, 2 * feats :] = d_gate_raw[...]
    for k, d_part in enumerate(d_parts):
        d_part[...] = d_raw[:, columns_of(x_ref, parts, k, 3 * feats // parts)]
    copies.flush(*range(parts + 1))
    copies.wait(*range(2 * parties + 8, 2 * parties + 8 + parts * parts))
    deep = partial.shape[1] // parts
    for d in range(parts):
        for i in range(4):
            at = slice(i * group // 4, (i + 1) * group // 4)
            total = None
            for k, d_part in enumerate(d_parts):
                part = times_transposed(d_part[at, :], weights[d * parts + k][...])
                total = part if total is None else total + part
            partial[at, d * deep : (d + 1) * deep] = total.astype(BF)


def token_grad_kernel(summed, tokens, d_resid, gain, out):
    @pl.loop(0, tokens.shape[0] // STEP)
    def _(i):
        at = pl.ds(i * STEP, STEP)
        value = tokens[at, :].astype(F32)
        inv = inverse_rms(value)
        hat = value * inv
        d = summed[at, :].astype(F32) * gain[...]
        out[at, :] = d_resid[at, :] + inv * (d - hat * mean_last(d * hat))


def result_kernel(summed, resid, out):
    out[...] = (resid[...] + summed[...].astype(F32)).astype(BF)


def after(value, *others):
    return lax.optimization_barrier((value, *others))[0]


def gather_rows(own):
    return lax.all_gather(own, ("z", "c"), axis=0, tiled=True)


def scatter_rows(partial):
    return lax.psum_scatter(partial, ("z", "c"), scatter_dimension=0, tiled=True)


def per_device(
    tokens, lengths, w_in, w_forget, w_gate, w_out, attn_gain, mix_gain, bound_table,
    ff_gate, ff_up, ff_down, mlp_gain, out_grad,
):
    Y = lax.axis_size("y")
    pair = Y == 2
    parts = 2 if pair else 1
    z, y, c, x = (lax.axis_index(a) for a in "zycx")
    rows, width = tokens.shape
    sub = w_in.shape[0]
    feats = Y * sub
    block = ff_gate.shape[1] // CHUNKS
    tall = 3 * block
    group = rows * CHUNKS
    near_y = y[None].astype(jnp.int32)

    def y_first(*values):
        if pair:
            return call(
                functools.partial(reorder_kernel, False),
                [(v.shape, v.dtype) for v in values], near_y, *values, smem=1,
            )
        return [
            v.reshape(v.shape[0], Z, Y, C * sub).transpose(0, 2, 1, 3).reshape(v.shape) for v in values
        ]

    def z_first(*values):
        if pair:
            return call(
                functools.partial(reorder_kernel, True),
                [(v.shape, v.dtype) for v in values], near_y, *values, smem=1,
            )
        return [
            v.reshape(v.shape[0], Y, Z, C * sub).transpose(0, 2, 1, 3).reshape(v.shape) for v in values
        ]

    def over_y(value):
        if pair:
            return [value, swap(value, "y")]
        return [lax.all_gather(value, "y", axis=0, tiled=True)]

    def in_order(value):
        if pair:
            other = swap(value, "y")
            return jnp.concatenate(
                [jnp.where(y == 0, value, other), jnp.where(y == 0, other, value)], axis=0
            )
        return lax.all_gather(value, "y", axis=0, tiled=True)

    def spread(value):
        return lax.all_to_all(value, ("z", "c"), 0, 0, tiled=True)

    def both(own, sent, axis):
        return own.astype(BF).astype(F32) + swap(sent.astype(BF), axis).astype(F32)

    near_x = x[None].astype(jnp.int32)

    def own_and_neighbours(value):
        corner = lax.ppermute(value, ("y", "x"), [(i, 3 - i) for i in range(4)])
        return [value, swap(value, "x"), swap(value, "y"), corner]

    table_f = bound_table.astype(F32)
    soft = jax.nn.softmax(table_f, axis=0)
    own_bound = jnp.sum(soft[1 : LAYER + 1], axis=0)

    tokens_y, grad_y = y_first(tokens, out_grad)
    if pair:
        (blocks,) = call(
            mixer_blocks_kernel, [((CHUNKS, sub, 3 * feats // 2), BF)], near_x, w_in, w_forget, w_gate, smem=1
        )
        moved = spread(blocks)
        small = jnp.stack([attn_gain.astype(F32), mlp_gain.astype(F32), own_bound, mix_gain.astype(F32)])
        small = [small, swap(small, "y")]
        (piece,) = call(
            token_piece_kernel, [((rows, width + LANES), BF)],
            near_y, tokens, jnp.concatenate([v[:2] for v in small]), smem=1,
        )
        grad_all = gather_rows(grad_y)
        tokens_all = gather_rows(after(piece, moved))
        gains = tokens_all.reshape(CHUNKS, rows, -1)[:, :4, width:].astype(F32)
        attn_g, mlp_g = (
            jnp.concatenate([gains[:, k].reshape(1, -1), gains[:, 2 + k].reshape(1, -1)], axis=1) for k in range(2)
        )
        small = jnp.stack([v[2:] for v in small])
        small = jnp.where(y == 0, small, small[::-1])
        mixer = own_and_neighbours(moved.reshape(CHUNKS * sub, 3 * feats // 2))
    else:
        gains = lax.all_gather(jnp.stack([attn_gain, mlp_gain]), ("z", "y", "c"), axis=1, tiled=True)
        attn_g, mlp_g = y_first(gains[:1].astype(F32), gains[1:].astype(F32))
        tokens_all, grad_all = gather_rows(tokens_y), gather_rows(grad_y)
        small = in_order(jnp.stack([own_bound, mix_gain.astype(F32)])[None])
        mixer = [
            w.reshape(sub, Z, Y, C, sub).transpose(1, 3, 0, 2, 4).reshape(CHUNKS, sub, feats)
            for w in (w_in, w_forget, w_gate)
        ]
        moved = spread(jnp.concatenate(mixer, axis=2))
        mixer = over_y(moved.reshape(CHUNKS * sub, 3 * feats))
    (out_rows,) = y_first(in_order(w_out))
    bound = small[:, 0].reshape(1, feats)
    mix_g = small[:, 1].reshape(1, feats)

    if pair:
        (glu,) = call(glu_blocks_kernel, [((CHUNKS, tall, sub), BF)], ff_gate, ff_up, ff_down)
    else:
        glu = jnp.concatenate([w.T.reshape(CHUNKS, block, sub) for w in (ff_gate, ff_up)], axis=1)
        glu = jnp.concatenate([glu, ff_down.reshape(CHUNKS, block, sub)], axis=1)
    glu = spread(after(glu, moved))

    slot = jnp.arange(lengths.shape[0])
    starts = jnp.sum(jnp.where(slot[None, :] < slot[:, None], lengths[None, :], 0), axis=1)
    slot = jnp.arange(CHUNKS)
    chunk = (slot // C * Y + y) * (C * X) + slot % C * X + x
    position = (chunk[:, None] * rows + jnp.arange(rows)[None, :]).reshape(group)
    keep = 1.0 - jnp.any(position[:, None] == starts[None, :], axis=1).astype(F32)[:, None]
    count = Z * Y * C * X
    number = jnp.arange(count)
    xn, cn = number % X, number // X % C
    yn, zn = number // (X * C) % Y, number // (X * C * Y)
    party = (yn ^ y) * X + (xn ^ x) if pair else yn * X + xn
    order = party * CHUNKS + zn * C + cn
    base = 0 * y if pair else (y * X + x) * CHUNKS
    order = jnp.concatenate([order, jnp.stack([base, z * C + c])]).astype(jnp.int32)

    def parties(value):
        if pair:
            return own_and_neighbours(value)
        return [lax.all_gather(value, ("y", "x"), axis=0, tiled=True)]

    crowd = 4 if pair else 1
    featured = ((feats // LANES, group, LANES), F32)
    normed, raw, decay, local, through, edge = call(
        functools.partial(mixer_forward_kernel, parts),
        [((group, width), BF), ((group, 3 * feats), F32)] + [featured] * 3 + [((2 * CHUNKS, feats), F32)],
        near_x, attn_g, tokens_all, bound, keep, *mixer,
        smem=1, scratch=[pltpu.VMEM(*featured)], late=2,
    )
    edges = parties(edge)
    def assemble(pieces):
        return jnp.concatenate([p.transpose(1, 0, 2).reshape(p.shape[1], -1) for p in pieces], axis=1)

    def around(blocks):
        cut = blocks.shape[1] // 2
        side, up_y = swap(blocks, "x"), swap(blocks, "y")
        corner = [swap(up_y[:, :cut], "x"), swap(side[:, cut:], "y")]
        near, far = assemble([blocks, up_y]), assemble([side, jnp.concatenate(corner, axis=1)])
        return [near, far], (side, up_y), corner

    early, late, last = (), (), ()
    gate_up, down = glu[:, : 2 * block], glu[:, 2 * block :]
    if pair:
        gate_up_w, early, _ = around(after(gate_up, edges[0]))
        down_w, late, last = around(after(down, *early))
    else:
        gate_up_w, down_w = (assemble(over_y(v)) for v in (gate_up, down))
        gate_up_w, down_w = ([v, swap(v, "x")] for v in (gate_up_w, down_w))
    carries = [pltpu.VMEM((Y * X * CHUNKS, feats), F32)] * 3
    states, entry, partial = call(
        functools.partial(mixer_out_kernel, crowd, count),
        [featured, ((CHUNKS, feats), F32), ((group, width + LANES), BF)],
        order, *edges, local, through, raw, mix_g, out_rows,
        smem=1, scratch=carries + [pltpu.VMEM((group, feats), BF)], late=crowd,
    )
    summed = scatter_rows(after(partial, glu))
    resid, hidden, scale = call(
        resid_kernel,
        [((rows, width), F32), ((rows, width), BF), ((rows, LANES), F32)],
        after(summed, *early), tokens_y, mlp_g,
    )
    hidden_all = after(gather_rows(hidden), *late)
    thin = ((group, block), BF)
    act0, d_gate0, d_up0, act1, d_gate1, d_up1, partial = call(
        glu_kernel, [thin] * 6 + [((group, width), BF)],
        hidden_all, grad_all, *gate_up_w, *down_w, late=0, scratch=[pltpu.VMEM((group, width), F32)],
    )
    acts = [act0, act1]

    def weight_pieces(terms, lefts, *rights):
        height = len(terms) * block
        shapes = [((height, width), BF)] * 2
        if pair:
            shapes = [((2, height // 2, width // 2), BF)] * 4
        return call(
            functools.partial(glu_weights_kernel, parts, terms), shapes, *lefts, *rights,
        )

    def first_swaps(pieces):
        upper, upper_sent, lower, lower_sent = pieces
        return upper, swap(upper_sent, "x"), lower, swap(lower_sent, "y")

    def first_sums(pieces):
        height = pieces[0].shape[1]
        shapes = [((height, width // 2), F32), ((height, width // 2), BF)] * 2
        return call(first_sums_kernel, shapes, *pieces)

    def last_swaps(pieces):
        upper, upper_sent, lower, lower_sent = pieces
        return upper, swap(upper_sent, "y"), lower, swap(lower_sent, "x")

    def last_sums(*pieces):
        return call(last_sums_kernel, [((CHUNKS, tall, sub), BF)], *pieces)[0]

    def to_blocks(value):
        return value.reshape(value.shape[0], -1, sub).transpose(1, 0, 2)

    def total_blocks(pieces):
        blocks = to_blocks(both(*pieces, "x").astype(BF))
        return lax.psum_scatter(blocks, "y", scatter_dimension=0, tiled=True)

    summed = scatter_rows(partial)
    gate_up = weight_pieces((0, 0), [d_gate0, d_up0, d_gate1, d_up1], hidden_all)
    (partial_out,) = call(glu_out_kernel, [((group, width), BF)], *acts, *down_w)
    down = weight_pieces((0,), acts, grad_all)
    summed = after(summed, partial_out, *down)
    if pair:
        gate_up = first_swaps(gate_up)
        summed, *gate_up = lax.optimization_barrier((summed, *gate_up))
        gate_up = first_sums(gate_up)
    d_resid, piece = call(
        d_resid_kernel, [((rows, width), F32), ((rows, width + LANES), BF)],
        summed, resid, tokens_y, grad_y, mlp_g, scale,
    )
    d_mixed = gather_rows(piece)
    if pair:
        down = first_swaps(down)
        gate_up = last_swaps(gate_up)
        d_mixed, *gate_up = lax.optimization_barrier((d_mixed, *gate_up))
        d_mixed, *down = lax.optimization_barrier((d_mixed, *down))
        down = first_sums(down)

    mixed_in, d_gate_raw, adjoint, passed, first = call(
        mixer_back_kernel,
        [((group, feats), BF)] * 2 + [featured] * 2 + [((CHUNKS, feats), F32)],
        d_mixed, out_rows, raw, states, mix_g, decay,
        scratch=[pltpu.VMEM((group, feats), F32), pltpu.VMEM(*featured)], late=2,
    )
    firsts = parties(first)
    if pair:
        down = last_swaps(after(down, *firsts))
        glu_grad = last_sums(*gate_up, *down)
    else:
        glu_grad = jnp.concatenate([total_blocks(gate_up), total_blocks(down)], axis=1)
    glu_grad = spread(glu_grad)
    *d_raw, part_bound, partial = call(
        functools.partial(d_mixer_kernel, crowd, parts, count),
        [((group, 3 * feats // parts), BF)] * parts
        + [((1, feats), F32), ((group, width), BF)],
        near_x, order, *edges, *firsts, adjoint, passed, states, entry, raw, keep, bound, d_gate_raw, *mixer,
        smem=2, scratch=carries + [pltpu.VMEM((group, 3 * feats), BF)], late=2 * crowd,
    )

    result_sum = scatter_rows(after(partial_out, d_mixed))
    (token_grad_y,) = call(
        token_grad_kernel, [((rows, width), F32)],
        after(scatter_rows(partial), result_sum), tokens_y, d_resid, attn_g,
    )
    (result_y,) = call(result_kernel, [((rows, width), BF)], result_sum, resid)
    result, token_grad = z_first(result_y, token_grad_y)

    pieces = call(
        functools.partial(mixer_weights_kernel, parts),
        [((width // parts, 3 * feats // parts), BF)] * parts**2,
        normed, *d_raw,
    )
    part_bound = part_bound.reshape(feats)
    if pair:
        pieces = [
            pieces[0],
            swap(pieces[1], "x"),
            swap(pieces[2], "y"),
            lax.ppermute(pieces[3], ("y", "x"), [(i, 3 - i) for i in range(4)]),
        ]
        mixer_grad = sum(p.astype(F32) for p in pieces).astype(BF)
        mixed_in, part_bound = after((mixed_in, part_bound), mixer_grad)
        top, bottom = jnp.split(part_bound, 2)
        d_bound = jnp.where(y == 0, top, bottom) + swap(jnp.where(y == 0, bottom, top), "y")
    else:
        d_bound = lax.psum_scatter(part_bound, "y", scatter_dimension=0, tiled=True)
        mixer_grad = lax.psum_scatter(pieces[0], "y", scatter_dimension=0, tiled=True)
        mixer_grad = both(mixer_grad, mixer_grad, "x").astype(BF)
    d_bound = d_bound + swap(d_bound, "x")
    row_ids = jnp.arange(bound_table.shape[0])[:, None]
    member = jnp.logical_and(row_ids >= 1, row_ids <= LAYER).astype(F32)
    grad_table = soft * (member - own_bound[None, :]) * d_bound[None, :]
    mixer_grad = spread(after(mixer_grad, glu_grad).reshape(CHUNKS, sub, 3 * feats // parts))

    grad_out = contract_rows(mixed_in, d_mixed[:, :width])
    (grad_out,) = z_first(grad_out.astype(BF))
    if pair:
        top, bottom = jnp.split(grad_out, 2, axis=0)
        grad_out = both(jnp.where(y == 0, top, bottom), jnp.where(y == 0, bottom, top), "y")
    else:
        grad_out = lax.psum_scatter(grad_out, "y", scatter_dimension=0, tiled=True)
    grad_out = both(grad_out, grad_out, "x")
    if pair:
        mixer_grad = after(mixer_grad, grad_out, d_bound)
        mixer_grad = [mixer_grad, swap(mixer_grad, "x")]

    def along(weight, grad):
        return jnp.sum(weight.astype(F32) * grad, axis=1)

    square, glued = ((sub, width), F32), ((sub, CHUNKS * block), F32)
    if pair:
        grad_gate_ff, grad_up_ff, grad_down, grad_mlp = call(
            glu_grads_kernel, [glued] * 2 + [((CHUNKS * block, sub), F32), ((sub, LANES), F32)],
            glu_grad, ff_gate, ff_up,
        )
        grad_mlp = grad_mlp[:, 0]
        grad_mlp = grad_mlp + swap(grad_mlp, "x")
        grad_in, grad_forget, grad_gate, grad_attn = call(
            mixer_grads_kernel, [square] * 3 + [((sub, LANES), F32)],
            near_x, mixer_grad[0], after(mixer_grad[1], grad_mlp), w_in, w_forget, w_gate, smem=1,
        )
        grad_attn = grad_attn[:, 0]
    else:
        mixer_grad = mixer_grad.reshape(Z, C, sub, 3, Y, sub).transpose(3, 2, 0, 4, 1, 5)
        grad_in, grad_forget, grad_gate = mixer_grad.reshape(3, sub, width).astype(F32)
        grad_attn = along(w_in, grad_in) + along(w_forget, grad_forget) + along(w_gate, grad_gate)
        grad_gate_ff, grad_up_ff = (
            glu_grad[:, k * block : (k + 1) * block].astype(F32).reshape(CHUNKS * block, sub).T for k in range(2)
        )
        grad_down = glu_grad[:, 2 * block :].reshape(CHUNKS * block, sub).astype(F32)
        grad_mlp = along(ff_gate, grad_gate_ff) + along(ff_up, grad_up_ff)
        grad_mlp = grad_mlp + swap(grad_mlp, "x")
    grad_attn = grad_attn / attn_gain.astype(F32)
    grad_mix = along(w_out, grad_out) / mix_gain.astype(F32)
    grad_mlp = grad_mlp / mlp_gain.astype(F32)
    return (
        result, token_grad, grad_in, grad_forget, grad_gate, grad_out, grad_attn, grad_mix,
        grad_table, grad_gate_ff, grad_up_ff, grad_down, grad_mlp,
    )


def solution(mesh):
    dp, mp = mesh.devices.shape
    grid = Mesh(mesh.devices.reshape(Z, dp // CHUNKS, C, mp), ("z", "y", "c", "x"))
    dp_axes = ("z", "y", "c")
    every = ("z", "y", "c", "x")
    mat, row, gain = P(dp_axes, None), P(every, None), P(dp_axes)
    table, glu, glu_down = P(None, dp_axes), P(dp_axes, "x"), P("x", dp_axes)
    return jax.shard_map(
        per_device,
        mesh=grid,
        in_specs=(
            row, P(), mat, mat, mat, mat, gain, gain, table, glu, glu, glu_down, gain, row,
        ),
        out_specs=(
            row, row, mat, mat, mat, mat, gain, gain, table, glu, glu, glu_down, gain,
        ),
        check_vma=False,
    )
```

time: 574 us -> 489 us (0.85)
  waiting for transfers between devices: 345 us -> 246 us
  Pallas kernels: 65.8 us -> 127 us
  starting transfers between devices: 98.8 us -> 60 us
  local copies, waits for them, and re-layouts: 32.3 us -> 12.9 us
  between operations: 1.82 us -> 15.5 us
    ppermute x29 -> x4, waiting for transfers between devices: 161 us -> 0.89 us  [the longest x3 0.89 us: own_and_neighbours(): corner = lax.ppermute(value, ('y', 'x'), [(i, 3 - i) for i in range(4)])]
    pallas_call x25, Pallas kernels: 65.8 us -> 127 us  [call(): pl.pallas_call(body, out_shape=shapes, in_specs=[pl.BlockSpec(memory_spac...]
    ppermute x29 -> x4, starting transfers between devices: 53.9 us -> 5.35 us  [the longest x3 3.87 us: own_and_neighbours(): corner = lax.ppermute(value, ('y', 'x'), [(i, 3 - i) for i in range(4)])]
    all_gather x0 -> x4, waiting for transfers between devices: none -> 39.9 us  [gather_rows(): return lax.all_gather(own, ('z', 'c'), axis=0, tiled=True)]
    unnamed x122 -> x76, local copies, waits for them, and re-layouts: 26.9 us -> 5.31 us
    reduce_scatter x0 -> x4, waiting for transfers between devices: none -> 18.2 us  [scatter_rows(): lax.psum_scatter(partial, ('z', 'c'), scatter_dimension=0, tiled=True)]
    ppermute x34 -> x32, waiting for transfers between devices: 153 us -> 170 us  [swap(): return lax.ppermute(value, axis, [(0, 1), (1, 0)])]
    all_to_all x4, waiting for transfers between devices: 31.3 us -> 17 us  [spread(): return lax.all_to_all(value, ('z', 'c'), 0, 0, tiled=True)]
  transfers between devices with their start and end apart: 67 -> 48, of which waited for: 30 -> 31; matrix products, arithmetic and copies ran while one was open for 5% -> 6% of each run, Pallas kernels for 6% -> 19%
where the time goes in v4:
time: 489 us; the launch traced here: 483 us
  waiting for transfers between devices  246 us (50%)
  Pallas kernels  127 us (26%)
  starting transfers between devices  60 us (12%)
  other arithmetic  19.9 us (4%)
  between operations  15.5 us (3%)
  local copies, waits for them, and re-layouts  12.9 us (3%)
    ppermute x32, waiting for transfers between devices, swap(): return lax.ppermute(value, axis, [(0, 1), (1, 0)])  170 us
    pallas_call x25, Pallas kernels, call(): pl.pallas_call(body, out_shape=shapes, in_specs=[pl.BlockSpec(memory_spac...  127 us
    all_gather x4, waiting for transfers between devices, gather_rows(): return lax.all_gather(own, ('z', 'c'), axis=0, tiled=True)  39.9 us
    ppermute x32, starting transfers between devices, swap(): return lax.ppermute(value, axis, [(0, 1), (1, 0)])  35.6 us
    all_to_all x4, starting transfers between devices, spread(): return lax.all_to_all(value, ('z', 'c'), 0, 0, tiled=True)  18.2 us
    reduce_scatter x4, waiting for transfers between devices, scatter_rows(): lax.psum_scatter(partial, ('z', 'c'), scatter_dimension=0, tiled=True)  18.2 us
    all_to_all x4, waiting for transfers between devices, spread(): return lax.all_to_all(value, ('z', 'c'), 0, 0, tiled=True)  17 us
  transfers between devices with their start and end apart: 48, of which 31 were waited for; matrix products, arithmetic and copies ran while one was open for 6% of the time, Pallas kernels for 19%

profile of v4, /device:TPU:0, one launch (start us, length us, event | category | flops | bytes accessed | tf_op | source)
XLA Modules:
  0.0 483.0 jit_solution(11590294458075782478)
XLA Ops:
  7.2 2.5 shard_map.238
  9.7 6.3 %all-to-all-start = ((bf16[8,128,384]{2,1,0:T(8,128)(2,1)}), bf16[8,128,384]{2,1,0:T(8,128)(2,1)S(1)}, u32[]{:S(2)}, u32[]{:S(2)}) async-start(bf16[8,128,384]{2,1,0:T(8,128)(2,1)} %shard_map.238), calls=%async_computation | async-start | bytes 1572864 | tf_op jit(solution)/shard_map/all_to_all | solution.py:613
  22.3 14.8 %all-to-all-done = bf16[8,128,384]{2,1,0:T(8,128)(2,1)S(1)} async-done(((bf16[8,128,384]{2,1,0:T(8,128)(2,1)}), bf16[8,128,384]{2,1,0:T(8,128)(2,1)S(1)}, u32[]{:S(2)}, u32[]{:S(2)}) %all-to-all-start) | async-done | bytes 786464 | tf_op jit(solution)/shard_map/all_to_all | solution.py:613
  37.1 4.2 shard_map.242
  41.3 3.7 all-to-all-start.1
  52.7 7.4 %collective-permute-done.7 = bf16[128,2048]{1,0:T(8,128)(2,1)} collective-permute-done((bf16[128,2048]{1,0:T(8,128)(2,1)S(1)}, bf16[128,2048]{1,0:T(8,128)(2,1)}, u32[]{:S(2)}, u32[]{:S(2)}) %collective-permute-start.7) | collective-permute-done | bytes 524320 | tf_op jit(solution)/shard_map/ppermute | solution.py:20
  62.1 20.7 %all-gather.5.cloned.1.call-done.refs_2_ = bf16[512,2176]{1,0:T(8,128)(2,1)} async-done(((bf16[64,2176]{1,0:T(8,128)(2,1)}), bf16[512,2176]{1,0:T(8,128)(2,1)}) %all-gather.5.cloned.1.call-update) | async-done | bytes 2228240 | tf_op jit(solution)/shard_map/all_gather | solution.py:556
  84.2 9.0 %collective-permute-done.2.refs_7_.refs_20_ = bf16[1024,384]{1,0:T(8,128)(2,1)} collective-permute-done((bf16[1024,384]{1,0:T(8,128)(2,1)S(1)}, bf16[1024,384]{1,0:T(8,128)(2,1)}, u32[]{:S(2)}, u32[]{:S(2)}) %collective-permute-start.2) | collective-permute-done | bytes 786464 | tf_op jit(solution)/shard_map/ppermute | solution.py:20
  93.2 9.8 %shard_map.239 = (bf16[512,2048]{1,0:T(8,128)(2,1)}, f32[512,768]{1,0:T(8,128)}, f32[2,512,128]{2,1,0:T(8,128)}, f32[2,512,128]{2,1,0:T(8,128)}, f32[2,512,128]{2,1,0:T(8,128)}, /*index=5*/f32[16,256]{1,0:T(8,128)}) custom-call(s32[1]{0:T(128)} %bitcast.2.refs_0_, f32[1,2048]{1,0:T(1,128)} %pad_maximum_fusion.3.refs_1_.refs_3_, ...), custom_call_target="tpu_custom_call" | custom-call | bytes 1024 | tf_op jit(solution)/shard_map/pallas_call | solution.py:87
  107.7 2.4 shard_map.240.refs_9_.refs_1_
  111.6 4.9 %shard_map.241 = (f32[2,512,128]{2,1,0:T(8,128)}, f32[8,256]{1,0:T(8,128)}, bf16[512,2176]{1,0:T(8,128)(2,1)}) custom-call(s32[34]{0:T(128)} %pad_add_fusion.refs_0_.refs_1_, f32[16,256]{1,0:T(8,128)} %get-tuple-element.110.refs_1_.refs_2_, f32[16,256]{1,0:T(8,128)} %copy-done.26, f32[16,256]{1,0:T(8,128)} %copy-done.27, f32[16,256]{1,0:T(8,128)} %copy-done.28, ...), custom_call_target="tpu_custom_call" | custom-call | bytes 1024 | tf_op jit(solution)/shard_map/pallas_call | solution.py:87
  121.4 27.0 %collective-permute-done.8 = bf16[8,704,128]{2,1,0:T(8,128)(2,1)S(1)} collective-permute-done((bf16[8,704,128]{2,1,0:T(8,128)(2,1)S(1)}, bf16[8,704,128]{2,1,0:T(8,128)(2,1)S(1)}, u32[]{:S(2)}, u32[]{:S(2)}) %collective-permute-start.8) | collective-permute-done | bytes 1441824 | tf_op jit(solution)/shard_map/ppermute | solution.py:20
  149.6 3.4 reduce-scatter.5.cloned.1.call-done.refs_0_
  152.9 2.7 shard_map.244
  167.2 11.5 %collective-permute-done.11 = bf16[8,352,128]{2,1,0:T(8,128)(2,1)S(1)} collective-permute-done((bf16[8,352,128]{2,1,0:T(8,128)(2,1)S(1)}, bf16[8,352,128]{2,1,0:T(8,128)(2,1)S(1)}, u32[]{:S(2)}, u32[]{:S(2)}) %collective-permute-start.11) | collective-permute-done | bytes 720928 | tf_op jit(solution)/shard_map/ppermute | solution.py:20
  181.1 11.6 %collective-permute-done.12 = bf16[8,352,128]{2,1,0:T(8,128)(2,1)S(1)} collective-permute-done((bf16[8,352,128]{2,1,0:T(8,128)(2,1)S(1)}, bf16[8,352,128]{2,1,0:T(8,128)(2,1)S(1)}, u32[]{:S(2)}, u32[]{:S(2)}) %collective-permute-start.12) | collective-permute-done | bytes 720928 | tf_op jit(solution)/shard_map/ppermute | solution.py:20
  198.1 16.0 %all-gather.9.cloned.1.call-done.refs_1_.refs_2_ = bf16[512,2048]{1,0:T(8,128)(2,1)} async-done(((bf16[64,2048]{1,0:T(8,128)(2,1)}), bf16[512,2048]{1,0:T(8,128)(2,1)}) %all-gather.9.cloned.1.call-update) | async-done | bytes 2097168 | tf_op jit(solution)/shard_map/all_gather | solution.py:556
  214.1 22.2 %shard_map.245 = (bf16[512,352]{1,0:T(8,128)(2,1)}, bf16[512,352]{1,0:T(8,128)(2,1)}, bf16[512,352]{1,0:T(8,128)(2,1)}, bf16[512,352]{1,0:T(8,128)(2,1)}, bf16[5...) custom-call(bf16[512,2048]{1,0:T(8,128)(2,1)} %all-gather.7.cloned.1.call-done.refs_0_.refs_4_, ...), custom_call_target="tpu_custom_call" | custom-call | bytes 1024 | tf_op jit(solution)/shard_map/pallas_call | solution.py:87
  236.4 6.7 %shard_map.248 = (bf16[2,352,1024]{2,1,0:T(8,128)(2,1)}, bf16[2,352,1024]{2,1,0:T(8,128)(2,1)}, bf16[2,352,1024]{2,1,0:T(8,128)(2,1)}, bf16[2,352,1024]{2,1,0:T(8,128)(2,1)}) custom-call(bf16[512,352]{1,0:T(8,128)(2,1)} %get-tuple-element.132.refs_0_, bf16[512,352]{1,0:T(8,128)(2,1)} %get-tuple-element.133.refs_1_, ...), custom_call_target="tpu_custom_call" | custom-call | bytes 1024 | tf_op jit(solution)/shard_map/pallas_call | solution.py:87
  246.2 5.8 %shard_map.246 = bf16[512,2048]{1,0:T(8,128)(2,1)} custom-call(bf16[512,352]{1,0:T(8,128)(2,1)} %get-tuple-element.124.refs_0_, bf16[512,352]{1,0:T(8,128)(2,1)} %get-tuple-element.125.refs_1_, bf16[352,2048]{1,0:T(8,128)(2,1)} %copy-done.2, bf16[352,2048]{1,0:T(8,128)(2,1)} %copy-done.1), custom_call_target="tpu_custom_call" | custom-call | bytes 1024 | tf_op jit(solution)/shard_map/pallas_call | solution.py:87
  252.0 4.9 %shard_map.247 = (bf16[2,176,1024]{2,1,0:T(8,128)(2,1)}, bf16[2,176,1024]{2,1,0:T(8,128)(2,1)}, bf16[2,176,1024]{2,1,0:T(8,128)(2,1)}, bf16[2,176,1024]{2,1,0:T(8,128)(2,1)}) custom-call(bf16[512,352]{1,0:T(8,128)(2,1)} %get-tuple-element.124.refs_0_, bf16[512,352]{1,0:T(8,128)(2,1)} %get-tuple-element.125.refs_1_, ...), custom_call_target="tpu_custom_call" | custom-call | bytes 1024 | tf_op jit(solution)/shard_map/pallas_call | solution.py:87
  256.9 14.8 %reduce-scatter.7.cloned.1.call-done.refs_0_ = bf16[64,2048]{1,0:T(8,128)(2,1)} async-done(((bf16[512,2048]{1,0:T(8,128)(2,1)}), bf16[64,2048]{1,0:T(8,128)(2,1)}) %reduce-scatter.7.cloned.1.call-update) | async-done | bytes 262160 | tf_op jit(solution)/shard_map/reduce_scatter | solution.py:560
  271.7 5.5 %collective-permute-done.16.refs_1_ = bf16[2,352,1024]{2,1,0:T(8,128)(2,1)S(1)} collective-permute-done((bf16[2,352,1024]{2,1,0:T(8,128)(2,1)}, bf16[2,352,1024]{2,1,0:T(8,128)(2,1)S(1)}, u32[]{:S(2)}, u32[]{:S(2)}) %collective-permute-start.16) | collective-permute-done | bytes 1441824 | tf_op jit(solution)/shard_map/ppermute | solution.py:20
  278.3 4.0 shard_map.249
  282.7 4.9 %shard_map.250 = (f32[352,1024]{1,0:T(8,128)}, bf16[352,1024]{1,0:T(8,128)(2,1)}, f32[352,1024]{1,0:T(8,128)}, bf16[352,1024]{1,0:T(8,128)(2,1)}) custom-call(bf16[2,352,1024]{2,1,0:T(8,128)(2,1)} %get-tuple-element.144.refs_0_, bf16[2,352,1024]{2,1,0:T(8,128)(2,1)} %copy-done.14, bf16[2,352,1024]{2,1,0:T(8,128)(2,1)} %get-tuple-element.146.refs_2_, ...), custom_call_target="tpu_custom_call" | custom-call | bytes 1024 | tf_op jit(solution)/shard_map/pallas_call | solution.py:87
  291.8 15.2 %collective-permute-done.18.refs_1_ = bf16[352,1024]{1,0:T(8,128)(2,1)S(1)} collective-permute-done((bf16[352,1024]{1,0:T(8,128)(2,1)}, bf16[352,1024]{1,0:T(8,128)(2,1)S(1)}, u32[]{:S(2)}, u32[]{:S(2)}) %collective-permute-start.18) | collective-permute-done | bytes 720928 | tf_op jit(solution)/shard_map/ppermute | solution.py:20
  308.5 3.1 all-gather.11.cloned.1.call-done.refs_0_
  311.5 10.2 %collective-permute-done.20.refs_1_ = bf16[2,176,1024]{2,1,0:T(8,128)(2,1)S(1)} collective-permute-done((bf16[2,176,1024]{2,1,0:T(8,128)(2,1)}, bf16[2,176,1024]{2,1,0:T(8,128)(2,1)S(1)}, u32[]{:S(2)}, u32[]{:S(2)}) %collective-permute-start.20) | collective-permute-done | bytes 720928 | tf_op jit(solution)/shard_map/ppermute | solution.py:20
  321.7 6.2 %shard_map.252 = (bf16[512,256]{1,0:T(8,128)(2,1)}, bf16[512,256]{1,0:T(8,128)(2,1)}, f32[2,512,128]{2,1,0:T(8,128)}, f32[2,512,128]{2,1,0:T(8,128)}, f32[8,256]{1,0:T(8,128)}) custom-call(bf16[512,2176]{1,0:T(8,128)(2,1)} %all-gather.11.cloned.1.call-done.refs_0_, bf16[256,2048]{1,0:T(8,128)(2,1)} %shard_map.240.refs_9_.refs_1_, ...), custom_call_target="tpu_custom_call" | custom-call | bytes 1024 | tf_op jit(solution)/shard_map/pallas_call | solution.py:87
  331.6 3.3 shard_map.257
  337.0 5.6 %collective-permute-done.28.refs_5_ = bf16[176,1024]{1,0:T(8,128)(2,1)S(1)} collective-permute-done((bf16[176,1024]{1,0:T(8,128)(2,1)}, bf16[176,1024]{1,0:T(8,128)(2,1)S(1)}, u32[]{:S(2)}, u32[]{:S(2)}) %collective-permute-start.28) | collective-permute-done | bytes 360480 | tf_op jit(solution)/shard_map/ppermute | solution.py:20
  344.4 4.8 shard_map.258
  349.2 3.6 all-to-all-start.2
  352.9 9.3 %shard_map.253 = (bf16[512,384]{1,0:T(8,128)(2,1)}, bf16[512,384]{1,0:T(8,128)(2,1)}, f32[1,256]{1,0:T(1,128)}, bf16[512,2048]{1,0:T(8,128)(2,1)}) custom-call(s32[1]{0:T(128)} %bitcast.2.refs_0_, s32[34]{0:T(128)} %pad_add_fusion.refs_0_.refs_1_, f32[16,256]{1,0:T(8,128)} %get-tuple-element.110.refs_1_.refs_2_, f32[16,256]{1,0:T(8,128)} %copy-done.26, ...), custom_call_target="tpu_custom_call" | custom-call | bytes 1024 | tf_op jit(solution)/shard_map/pallas_call | solution.py:87
  362.2 5.1 %shard_map.256 = (bf16[1024,384]{1,0:T(8,128)(2,1)}, bf16[1024,384]{1,0:T(8,128)(2,1)}, bf16[1024,384]{1,0:T(8,128)(2,1)}, bf16[1024,384]{1,0:T(8,128)(2,1)}) custom-call(bf16[512,2048]{1,0:T(8,128)(2,1)} %get-tuple-element.167.refs_0_, bf16[512,384]{1,0:T(8,128)(2,1)} %get-tuple-element.168.refs_1_, bf16[512,384]{1,0:T(8,128)(2,1)} %get-tuple-element.169.refs_2_), custom_call_target="tpu_custom_call" | custom-call | bytes 1024 | tf_op jit(solution)/shard_map/pallas_call | solution.py:87
  370.9 17.2 %collective-permute-done.25 = bf16[1024,384]{1,0:T(8,128)(2,1)} collective-permute-done((bf16[1024,384]{1,0:T(8,128)(2,1)}, bf16[1024,384]{1,0:T(8,128)(2,1)}, u32[]{:S(2)}, u32[]{:S(2)}) %collective-permute-start.25) | collective-permute-done | bytes 786464 | tf_op jit(solution)/shard_map/ppermute | solution.py:20
  388.1 16.9 %collective-permute-done.26 = bf16[1024,384]{1,0:T(8,128)(2,1)} collective-permute-done((bf16[1024,384]{1,0:T(8,128)(2,1)}, bf16[1024,384]{1,0:T(8,128)(2,1)}, u32[]{:S(2)}, u32[]{:S(2)}) %collective-permute-start.26) | collective-permute-done | bytes 786464 | tf_op jit(solution)/shard_map/ppermute | solution.py:20
  405.0 3.0 add_convert_fusion
  409.7 2.3 shard_map.259
  412.1 2.1 broadcast_select_fusion
  417.1 4.5 all-to-all-start.3
  421.6 5.9 %collective-permute-done.30 = bf16[128,2048]{1,0:T(8,128)(2,1)} collective-permute-done((bf16[128,2048]{1,0:T(8,128)(2,1)}, bf16[128,2048]{1,0:T(8,128)(2,1)}, u32[]{:S(2)}, u32[]{:S(2)}) %collective-permute-start.30) | collective-permute-done | bytes 524320 | tf_op jit(solution)/shard_map/ppermute | solution.py:20
  431.0 2.5 collective-permute-done.32
  434.5 6.5 %collective-permute-done.33 = f32[128]{0:T(128)S(1)} collective-permute-done((f32[128]{0:T(128)S(1)}, f32[128]{0:T(128)S(1)}, u32[]{:S(2)}, u32[]{:S(2)}) %collective-permute-start.33) | collective-permute-done | bytes 544 | tf_op jit(solution)/shard_map/ppermute | solution.py:20
  444.2 6.2 %shard_map.260 = (f32[128,2816]{1,0:T(8,128)}, f32[128,2816]{1,0:T(8,128)}, f32[2816,128]{1,0:T(8,128)}, f32[128,128]{1,0:T(8,128)}) custom-call(bf16[8,1056,128]{2,1,0:T(8,128)(2,1)} %copy-done.3, bf16[128,2816]{1,0:T(8,128)(2,1)} %refs_1_.9, bf16[128,2816]{1,0:T(8,128)(2,1)} %refs_2_.7), custom_call_target="tpu_custom_call" | custom-call | bytes 1024 | tf_op jit(solution)/shard_map/pallas_call | solution.py:87
  453.0 9.0 %collective-permute-done.35 = f32[128]{0:T(128)S(1)} collective-permute-done((f32[128]{0:T(128)S(1)}, f32[128]{0:T(128)S(1)}, u32[]{:S(2)}, u32[]{:S(2)}) %collective-permute-start.35) | collective-permute-done | bytes 544 | tf_op jit(solution)/shard_map/ppermute | solution.py:20
  464.4 2.9 shard_map.254.refs_2_
  470.3 3.8 shard_map.261
  (216 shorter events, 91.5 us)
Async XLA Ops:
  9.7 27.3 %all-to-all-start = ((bf16[8,128,384]{2,1,0:T(8,128)(2,1)}), bf16[8,128,384]{2,1,0:T(8,128)(2,1)S(1)}, u32[]{:S(2)}, u32[]{:S(2)}) async-start(bf16[8,128,384]{2,1,0:T(8,128)(2,1)} %shard_map.238), calls=%async_computation | async-start | bytes 1572864 | tf_op jit(solution)/shard_map/all_to_all | solution.py:613
  16.1 66.8 %all-gather.5.cloned.1.call-start = ((), (), s32[]{:S(2)}) async-start(), calls=%async_computation.8 | async-start | bytes 2506752 | tf_op jit(solution)/shard_map/all_gather | solution.py:556
  16.3 3.7 collective-permute-start
  41.3 75.2 %all-to-all-start.1 = ((bf16[8,1056,128]{2,1,0:T(8,128)(2,1)}), bf16[8,1056,128]{2,1,0:T(8,128)(2,1)S(1)}, u32[]{:S(2)}, u32[]{:S(2)}) async-start(bf16[8,1056,128]{2,1,0:T(8,128)(2,1)} %shard_map.242), calls=%async_computation.1 | async-start | bytes 4325376 | tf_op jit(solution)/shard_map/all_to_all | solution.py:613
  45.1 107.9 %reduce-scatter.5.cloned.1.call-start = ((), (), s32[]{:S(2)}) async-start(), calls=%async_computation.9 | async-start | bytes 2506752 | tf_op jit(solution)/shard_map/reduce_scatter | solution.py:560
  45.1 14.9 %collective-permute-start.7 = (bf16[128,2048]{1,0:T(8,128)(2,1)S(1)}, bf16[128,2048]{1,0:T(8,128)(2,1)}, u32[]{:S(2)}, u32[]{:S(2)}) collective-permute-start(bf16[128,2048]{1,0:T(8,128)(2,1)S(1)} %copy-done.10), channel_id=1, source_target_pairs={{0,4},{4,0},{1,5},{5,1},{2,6},{6,2},{3,7},{7,3},{8,12},{12,8},{9,1... | collective-permute-start | bytes 1572872 | tf_op jit(solution)/shard_map/ppermute | solution.py:20
  49.2 35.0 %collective-permute-start.1 = (bf16[1024,384]{1,0:T(8,128)(2,1)S(1)}, bf16[1024,384]{1,0:T(8,128)(2,1)}, u32[]{:S(2)}, u32[]{:S(2)}) collective-permute-start(bf16[1024,384]{1,0:T(8,128)(2,1)S(1)} %bitcast.76), channel_id=1, source_target_pairs={{0,1},{1,0},{2,3},{3,2},{4,5},{5,4},{6,7},{7,6},{8,9},{9,8},{10,11... | collective-permute-start | bytes 2359304 | tf_op jit(solution)/shard_map/ppermute | solution.py:20
  50.7 42.5 %collective-permute-start.2 = (bf16[1024,384]{1,0:T(8,128)(2,1)S(1)}, bf16[1024,384]{1,0:T(8,128)(2,1)}, u32[]{:S(2)}, u32[]{:S(2)}) collective-permute-start(bf16[1024,384]{1,0:T(8,128)(2,1)S(1)} %bitcast.77), channel_id=1, source_target_pairs={{0,4},{4,0},{1,5},{5,1},{2,6},{6,2},{3,7},{7,3},{8,12},{12,8},{9,1... | collective-permute-start | bytes 2359304 | tf_op jit(solution)/shard_map/ppermute | solution.py:20
  51.2 42.0 %collective-permute-start.3 = (bf16[1024,384]{1,0:T(8,128)(2,1)S(1)}, bf16[1024,384]{1,0:T(8,128)(2,1)}, u32[]{:S(2)}, u32[]{:S(2)}) collective-permute-start(bf16[1024,384]{1,0:T(8,128)(2,1)S(1)} %bitcast.78), channel_id=1, source_target_pairs={{0,5},{1,4},{4,1},{5,0},{2,7},{3,6},{6,3},{7,2},{8,13},{9,12},{12,... | collective-permute-start | bytes 2359304 | tf_op jit(solution)/shard_map/ppermute | solution.py:621
  103.1 7.0 %collective-permute-start.4 = (f32[16,256]{1,0:T(8,128)}, f32[16,256]{1,0:T(8,128)S(1)}, u32[]{:S(2)}, u32[]{:S(2)}) collective-permute-start(f32[16,256]{1,0:T(8,128)} %get-tuple-element.110.refs_1_.refs_2_), channel_id=1, source_target_pairs={{0,1},{1,0},{2,3},{3,2},{4,5},{5,4},{6,7},{7,6},{8,9},{9,8},{10,11... | collective-permute-start | bytes 49160 | tf_op jit(solution)/shard_map/ppermute | solution.py:20
  104.6 5.5 %collective-permute-start.5 = (f32[16,256]{1,0:T(8,128)}, f32[16,256]{1,0:T(8,128)S(1)}, u32[]{:S(2)}, u32[]{:S(2)}) collective-permute-start(f32[16,256]{1,0:T(8,128)} %get-tuple-element.110.refs_1_.refs_2_), channel_id=1, source_target_pairs={{0,4},{4,0},{1,5},{5,1},{2,6},{6,2},{3,7},{7,3},{8,12},{12,8},{9,1... | collective-permute-start | bytes 49160 | tf_op jit(solution)/shard_map/ppermute | solution.py:20
  106.1 4.8 %collective-permute-start.6 = (f32[16,256]{1,0:T(8,128)}, f32[16,256]{1,0:T(8,128)S(1)}, u32[]{:S(2)}, u32[]{:S(2)}) collective-permute-start(f32[16,256]{1,0:T(8,128)} %get-tuple-element.110.refs_1_.refs_2_), channel_id=1, source_target_pairs={{0,5},{1,4},{4,1},{5,0},{2,7},{3,6},{6,3},{7,2},{8,13},{9,12},{12,... | collective-permute-start | bytes 49160 | tf_op jit(solution)/shard_map/ppermute | solution.py:621
  116.6 81.5 %all-gather.7.cloned.1.call-start = ((), (), s32[]{:S(2)}) async-start(), calls=%async_computation.10 | async-start | bytes 2359296 | tf_op jit(solution)/shard_map/all_gather | solution.py:556
  116.7 31.7 %collective-permute-start.8 = (bf16[8,704,128]{2,1,0:T(8,128)(2,1)S(1)}, bf16[8,704,128]{2,1,0:T(8,128)(2,1)S(1)}, u32[]{:S(2)}, u32[]{:S(2)}) collective-permute-start(bf16[8,704,128]{2,1,0:T(8,128)(2,1)S(1)} %slice.86), channel_id=1, source_target_pairs={{0,1},{1,0},{2,3},{3,2},{4,5},{5,4},{6,7},{7,6},{8,9},{9,8},{10,11... | collective-permute-start | bytes 4325384 | tf_op jit(solution)/shard_map/ppermute | solution.py:20
  117.8 31.7 %collective-permute-start.9 = (bf16[8,704,128]{2,1,0:T(8,128)(2,1)S(1)}, bf16[8,704,128]{2,1,0:T(8,128)(2,1)}, u32[]{:S(2)}, u32[]{:S(2)}) collective-permute-start(bf16[8,704,128]{2,1,0:T(8,128)(2,1)S(1)} %slice.86), channel_id=1, source_target_pairs={{0,4},{4,0},{1,5},{5,1},{2,6},{6,2},{3,7},{7,3},{8,12},{12,8},{9,1... | collective-permute-start | bytes 4325384 | tf_op jit(solution)/shard_map/ppermute | solution.py:20
  155.7 58.5 %all-gather.9.cloned.1.call-start = ((), (), s32[]{:S(2)}) async-start(), calls=%async_computation.11 | async-start | bytes 2359296 | tf_op jit(solution)/shard_map/all_gather | solution.py:556
  156.3 115.4 %reduce-scatter.7.cloned.1.call-start = ((), (), s32[]{:S(2)}) async-start(), calls=%async_computation.12 | async-start | bytes 2359296 | tf_op jit(solution)/shard_map/reduce_scatter | solution.py:560
  158.1 21.3 %collective-permute-start.10 = (bf16[8,352,128]{2,1,0:T(8,128)(2,1)S(1)}, bf16[8,352,128]{2,1,0:T(8,128)(2,1)S(1)}, u32[]{:S(2)}, u32[]{:S(2)}) collective-permute-start(bf16[8,352,128]{2,1,0:T(8,128)(2,1)S(1)} %slice.89), channel_id=1, source_target_pairs={{0,1},{1,0},{2,3},{3,2},{4,5},{5,4},{6,7},{7,6},{8,9},{9,8},{10,11... | collective-permute-start | bytes 2162696 | tf_op jit(solution)/shard_map/ppermute | solution.py:20
  159.6 19.1 %collective-permute-start.11 = (bf16[8,352,128]{2,1,0:T(8,128)(2,1)S(1)}, bf16[8,352,128]{2,1,0:T(8,128)(2,1)S(1)}, u32[]{:S(2)}, u32[]{:S(2)}) collective-permute-start(bf16[8,352,128]{2,1,0:T(8,128)(2,1)S(1)} %slice.89), channel_id=1, source_target_pairs={{0,4},{4,0},{1,5},{5,1},{2,6},{6,2},{3,7},{7,3},{8,12},{12,8},{9,1... | collective-permute-start | bytes 2162696 | tf_op jit(solution)/shard_map/ppermute | solution.py:20
  162.3 30.4 %collective-permute-start.12 = (bf16[8,352,128]{2,1,0:T(8,128)(2,1)S(1)}, bf16[8,352,128]{2,1,0:T(8,128)(2,1)S(1)}, u32[]{:S(2)}, u32[]{:S(2)}) collective-permute-start(bf16[8,352,128]{2,1,0:T(8,128)(2,1)S(1)} %slice.90), channel_id=1, source_target_pairs={{0,1},{1,0},{2,3},{3,2},{4,5},{5,4},{6,7},{7,6},{8,9},{9,8},{10,11... | collective-permute-start | bytes 2162696 | tf_op jit(solution)/shard_map/ppermute | solution.py:20
  162.9 31.2 %collective-permute-start.13 = (bf16[8,352,128]{2,1,0:T(8,128)(2,1)S(1)}, bf16[8,352,128]{2,1,0:T(8,128)(2,1)S(1)}, u32[]{:S(2)}, u32[]{:S(2)}) collective-permute-start(bf16[8,352,128]{2,1,0:T(8,128)(2,1)S(1)} %slice.91), channel_id=1, source_target_pairs={{0,4},{4,0},{1,5},{5,1},{2,6},{6,2},{3,7},{7,3},{8,12},{12,8},{9,1... | collective-permute-start | bytes 2162696 | tf_op jit(solution)/shard_map/ppermute | solution.py:20
  178.7 18.0 %collective-permute-start.14 = (bf16[8,176,128]{2,1,0:T(8,128)(2,1)S(1)}, bf16[8,176,128]{2,1,0:T(8,128)(2,1)S(1)}, u32[]{:S(2)}, u32[]{:S(2)}) collective-permute-start(bf16[8,176,128]{2,1,0:T(8,128)(2,1)S(1)} %slice.92), channel_id=1, source_target_pairs={{0,1},{1,0},{2,3},{3,2},{4,5},{5,4},{6,7},{7,6},{8,9},{9,8},{10,11... | collective-permute-start | bytes 1081352 | tf_op jit(solution)/shard_map/ppermute | solution.py:20
  179.4 18.6 %collective-permute-start.15 = (bf16[8,176,128]{2,1,0:T(8,128)(2,1)S(1)}, bf16[8,176,128]{2,1,0:T(8,128)(2,1)S(1)}, u32[]{:S(2)}, u32[]{:S(2)}) collective-permute-start(bf16[8,176,128]{2,1,0:T(8,128)(2,1)S(1)} %slice.93), channel_id=1, source_target_pairs={{0,4},{4,0},{1,5},{5,1},{2,6},{6,2},{3,7},{7,3},{8,12},{12,8},{9,1... | collective-permute-start | bytes 1081352 | tf_op jit(solution)/shard_map/ppermute | solution.py:20
  236.4 75.2 %all-gather.11.cloned.1.call-start = ((), (), s32[]{:S(2)}) async-start(), calls=%async_computation.13 | async-start | bytes 2506752 | tf_op jit(solution)/shard_map/all_gather | solution.py:556
  243.1 34.0 %collective-permute-start.16 = (bf16[2,352,1024]{2,1,0:T(8,128)(2,1)}, bf16[2,352,1024]{2,1,0:T(8,128)(2,1)S(1)}, u32[]{:S(2)}, u32[]{:S(2)}) collective-permute-start(bf16[2,352,1024]{2,1,0:T(8,128)(2,1)} %get-tuple-element.137), channel_id=1, source_target_pairs={{0,1},{1,0},{2,3},{3,2},{4,5},{5,4},{6,7},{7,6},{8,9},{9,8},{10,11... | collective-permute-start | bytes 4325384 | tf_op jit(solution)/shard_map/ppermute | solution.py:20
  244.7 33.7 %collective-permute-start.17 = (bf16[2,352,1024]{2,1,0:T(8,128)(2,1)}, bf16[2,352,1024]{2,1,0:T(8,128)(2,1)S(1)}, u32[]{:S(2)}, u32[]{:S(2)}) collective-permute-start(bf16[2,352,1024]{2,1,0:T(8,128)(2,1)} %get-tuple-element.139), channel_id=1, source_target_pairs={{0,4},{4,0},{1,5},{5,1},{2,6},{6,2},{3,7},{7,3},{8,12},{12,8},{9,1... | collective-permute-start | bytes 4325384 | tf_op jit(solution)/shard_map/ppermute | solution.py:20
  282.4 180.1 %reduce-scatter.9.cloned.1.call-start = ((), (), s32[]{:S(2)}) async-start(), calls=%async_computation.14 | async-start | bytes 2359296 | tf_op jit(solution)/shard_map/reduce_scatter | solution.py:560
  287.6 19.3 %collective-permute-start.18 = (bf16[352,1024]{1,0:T(8,128)(2,1)}, bf16[352,1024]{1,0:T(8,128)(2,1)S(1)}, u32[]{:S(2)}, u32[]{:S(2)}) collective-permute-start(bf16[352,1024]{1,0:T(8,128)(2,1)} %get-tuple-element.149), channel_id=1, source_target_pairs={{0,4},{4,0},{1,5},{5,1},{2,6},{6,2},{3,7},{7,3},{8,12},{12,8},{9,1... | collective-permute-start | bytes 2162696 | tf_op jit(solution)/shard_map/ppermute | solution.py:20
  289.2 19.3 %collective-permute-start.19 = (bf16[352,1024]{1,0:T(8,128)(2,1)}, bf16[352,1024]{1,0:T(8,128)(2,1)S(1)}, u32[]{:S(2)}, u32[]{:S(2)}) collective-permute-start(bf16[352,1024]{1,0:T(8,128)(2,1)} %get-tuple-element.151), channel_id=1, source_target_pairs={{0,1},{1,0},{2,3},{3,2},{4,5},{5,4},{6,7},{7,6},{8,9},{9,8},{10,11... | collective-permute-start | bytes 2162696 | tf_op jit(solution)/shard_map/ppermute | solution.py:20
  290.0 31.7 %collective-permute-start.20 = (bf16[2,176,1024]{2,1,0:T(8,128)(2,1)}, bf16[2,176,1024]{2,1,0:T(8,128)(2,1)S(1)}, u32[]{:S(2)}, u32[]{:S(2)}) collective-permute-start(bf16[2,176,1024]{2,1,0:T(8,128)(2,1)} %get-tuple-element.128), channel_id=1, source_target_pairs={{0,1},{1,0},{2,3},{3,2},{4,5},{5,4},{6,7},{7,6},{8,9},{9,8},{10,11... | collective-permute-start | bytes 2162696 | tf_op jit(solution)/shard_map/ppermute | solution.py:20
  291.2 30.5 %collective-permute-start.21 = (bf16[2,176,1024]{2,1,0:T(8,128)(2,1)}, bf16[2,176,1024]{2,1,0:T(8,128)(2,1)S(1)}, u32[]{:S(2)}, u32[]{:S(2)}) collective-permute-start(bf16[2,176,1024]{2,1,0:T(8,128)(2,1)} %get-tuple-element.130), channel_id=1, source_target_pairs={{0,4},{4,0},{1,5},{5,1},{2,6},{6,2},{3,7},{7,3},{8,12},{12,8},{9,1... | collective-permute-start | bytes 2162696 | tf_op jit(solution)/shard_map/ppermute | solution.py:20
  328.0 6.8 %collective-permute-start.22 = (f32[8,256]{1,0:T(8,128)}, f32[8,256]{1,0:T(8,128)S(1)}, u32[]{:S(2)}, u32[]{:S(2)}) collective-permute-start(f32[8,256]{1,0:T(8,128)} %get-tuple-element.157.refs_6_), channel_id=1, source_target_pairs={{0,1},{1,0},{2,3},{3,2},{4,5},{5,4},{6,7},{7,6},{8,9},{9,8},{10,11... | collective-permute-start | bytes 24584 | tf_op jit(solution)/shard_map/ppermute | solution.py:20
  329.1 5.8 %collective-permute-start.23 = (f32[8,256]{1,0:T(8,128)}, f32[8,256]{1,0:T(8,128)S(1)}, u32[]{:S(2)}, u32[]{:S(2)}) collective-permute-start(f32[8,256]{1,0:T(8,128)} %get-tuple-element.157.refs_6_), channel_id=1, source_target_pairs={{0,4},{4,0},{1,5},{5,1},{2,6},{6,2},{3,7},{7,3},{8,12},{12,8},{9,1... | collective-permute-start | bytes 24584 | tf_op jit(solution)/shard_map/ppermute | solution.py:20
  329.7 5.2 %collective-permute-start.24 = (f32[8,256]{1,0:T(8,128)}, f32[8,256]{1,0:T(8,128)S(1)}, u32[]{:S(2)}, u32[]{:S(2)}) collective-permute-start(f32[8,256]{1,0:T(8,128)} %get-tuple-element.157.refs_6_), channel_id=1, source_target_pairs={{0,5},{1,4},{4,1},{5,0},{2,7},{3,6},{6,3},{7,2},{8,13},{9,12},{12,... | collective-permute-start | bytes 24584 | tf_op jit(solution)/shard_map/ppermute | solution.py:621
  334.9 7.7 %collective-permute-start.28 = (bf16[176,1024]{1,0:T(8,128)(2,1)}, bf16[176,1024]{1,0:T(8,128)(2,1)S(1)}, u32[]{:S(2)}, u32[]{:S(2)}) collective-permute-start(bf16[176,1024]{1,0:T(8,128)(2,1)} %get-tuple-element.187), channel_id=1, source_target_pairs={{0,4},{4,0},{1,5},{5,1},{2,6},{6,2},{3,7},{7,3},{8,12},{12,8},{9,1... | collective-permute-start | bytes 1081352 | tf_op jit(solution)/shard_map/ppermute | solution.py:20
  336.0 7.6 %collective-permute-start.29 = (bf16[176,1024]{1,0:T(8,128)(2,1)}, bf16[176,1024]{1,0:T(8,128)(2,1)S(1)}, u32[]{:S(2)}, u32[]{:S(2)}) collective-permute-start(bf16[176,1024]{1,0:T(8,128)(2,1)} %get-tuple-element.189), channel_id=1, source_target_pairs={{0,1},{1,0},{2,3},{3,2},{4,5},{5,4},{6,7},{7,6},{8,9},{9,8},{10,11... | collective-permute-start | bytes 1081352 | tf_op jit(solution)/shard_map/ppermute | solution.py:20
  349.2 67.9 %all-to-all-start.2 = ((bf16[8,1056,128]{2,1,0:T(8,128)(2,1)}), bf16[8,1056,128]{2,1,0:T(8,128)(2,1)S(1)}, u32[]{:S(2)}, u32[]{:S(2)}) async-start(bf16[8,1056,128]{2,1,0:T(8,128)(2,1)} %shard_map.258), calls=%async_computation.6 | async-start | bytes 4325376 | tf_op jit(solution)/shard_map/all_to_all | solution.py:613
  352.8 111.6 %reduce-scatter.11.cloned.1.call-start = ((), (), s32[]{:S(2)}) async-start(), calls=%async_computation.15 | async-start | bytes 2359296 | tf_op jit(solution)/shard_map/reduce_scatter | solution.py:560
  367.3 20.7 %collective-permute-start.25 = (bf16[1024,384]{1,0:T(8,128)(2,1)}, bf16[1024,384]{1,0:T(8,128)(2,1)}, u32[]{:S(2)}, u32[]{:S(2)}) collective-permute-start(bf16[1024,384]{1,0:T(8,128)(2,1)} %get-tuple-element.171), channel_id=1, source_target_pairs={{0,1},{1,0},{2,3},{3,2},{4,5},{5,4},{6,7},{7,6},{8,9},{9,8},{10,11... | collective-permute-start | bytes 2359304 | tf_op jit(solution)/shard_map/ppermute | solution.py:20
  368.4 36.6 %collective-permute-start.26 = (bf16[1024,384]{1,0:T(8,128)(2,1)}, bf16[1024,384]{1,0:T(8,128)(2,1)}, u32[]{:S(2)}, u32[]{:S(2)}) collective-permute-start(bf16[1024,384]{1,0:T(8,128)(2,1)} %get-tuple-element.172), channel_id=1, source_target_pairs={{0,4},{4,0},{1,5},{5,1},{2,6},{6,2},{3,7},{7,3},{8,12},{12,8},{9,1... | collective-permute-start | bytes 2359304 | tf_op jit(solution)/shard_map/ppermute | solution.py:20
  369.4 35.6 %collective-permute-start.27 = (bf16[1024,384]{1,0:T(8,128)(2,1)}, bf16[1024,384]{1,0:T(8,128)(2,1)}, u32[]{:S(2)}, u32[]{:S(2)}) collective-permute-start(bf16[1024,384]{1,0:T(8,128)(2,1)} %get-tuple-element.173), channel_id=1, source_target_pairs={{0,5},{1,4},{4,1},{5,0},{2,7},{3,6},{6,3},{7,2},{8,13},{9,12},{12,... | collective-permute-start | bytes 2359304 | tf_op jit(solution)/shard_map/ppermute | solution.py:832
  414.2 13.3 %collective-permute-start.30 = (bf16[128,2048]{1,0:T(8,128)(2,1)}, bf16[128,2048]{1,0:T(8,128)(2,1)}, u32[]{:S(2)}, u32[]{:S(2)}) collective-permute-start(bf16[128,2048]{1,0:T(8,128)(2,1)} %broadcast_select_fusion), channel_id=1, source_target_pairs={{0,4},{4,0},{1,5},{5,1},{2,6},{6,2},{3,7},{7,3},{8,12},{12,8},{9,1... | collective-permute-start | bytes 1572872 | tf_op jit(solution)/shard_map/ppermute | solution.py:20
  417.1 25.5 %all-to-all-start.3 = ((bf16[8,128,384]{2,1,0:T(8,128)(2,1)}), bf16[8,128,384]{2,1,0:T(8,128)(2,1)}, u32[]{:S(2)}, u32[]{:S(2)}) async-start(bf16[8,128,384]{2,1,0:T(8,128)(2,1)} %bitcast.81), calls=%async_computation.7 | async-start | bytes 1572864 | tf_op jit(solution)/shard_map/all_to_all | solution.py:613
  428.8 12.2 %collective-permute-start.31 = (bf16[128,2048]{1,0:T(8,128)(2,1)S(1)}, bf16[128,2048]{1,0:T(8,128)(2,1)S(1)}, u32[]{:S(2)}, u32[]{:S(2)}) collective-permute-start(bf16[128,2048]{1,0:T(8,128)(2,1)S(1)} %add_convert_fusion.1), channel_id=1, source_target_pairs={{0,1},{1,0},{2,3},{3,2},{4,5},{5,4},{6,7},{7,6},{8,9},{9,8},{10,11... | collective-permute-start | bytes 1572872 | tf_op jit(solution)/shard_map/ppermute | solution.py:20
  430.0 3.5 collective-permute-start.32
  433.5 7.5 %collective-permute-start.33 = (f32[128]{0:T(128)S(1)}, f32[128]{0:T(128)S(1)}, u32[]{:S(2)}, u32[]{:S(2)}) collective-permute-start(f32[128]{0:T(128)S(1)} %fusion.8), channel_id=1, source_target_pairs={{0,1},{1,0},{2,3},{3,2},{4,5},{5,4},{6,7},{7,6},{8,9},{9,8},{10,11... | collective-permute-start | bytes 1544 | tf_op jit(solution)/shard_map/ppermute | solution.py:20
  442.6 26.9 %collective-permute-start.34 = (bf16[8,128,384]{2,1,0:T(8,128)(2,1)}, bf16[8,128,384]{2,1,0:T(8,128)(2,1)S(1)}, u32[]{:S(2)}, u32[]{:S(2)}) collective-permute-start(bf16[8,128,384]{2,1,0:T(8,128)(2,1)} %all-to-all-done.3.refs_1_), channel_id=1, source_target_pairs={{0,1},{1,0},{2,3},{3,2},{4,5},{5,4},{6,7},{7,6},{8,9},{9,8},{10,11... | collective-permute-start | bytes 2359304 | tf_op jit(solution)/shard_map/ppermute | solution.py:20
  451.3 10.6 %collective-permute-start.35 = (f32[128]{0:T(128)S(1)}, f32[128]{0:T(128)S(1)}, u32[]{:S(2)}, u32[]{:S(2)}) collective-permute-start(f32[128]{0:T(128)S(1)} %slice_reduce_fusion.1), channel_id=1, source_target_pairs={{0,1},{1,0},{2,3},{3,2},{4,5},{5,4},{6,7},{7,6},{8,9},{9,8},{10,11... | collective-permute-start | bytes 1544 | tf_op jit(solution)/shard_map/ppermute | solution.py:20
  (37 other events, 333.8 us)
Sparse Core Ops, SparseCore 0:
  37.2 45.6 all-gather.4
  116.7 36.2 reduce-scatter.4
  155.8 28.1 all-gather.6
  185.5 28.5 all-gather.8
  236.5 35.1 reduce-scatter.6
  282.5 28.9 all-gather.10
  321.9 33.8 reduce-scatter.8
  371.0 51.9 reduce-scatter.10

commit v5 on v4

--- a/solution.py
+++ b/solution.py
@@ -154,24 +154,46 @@
                 out_ref[z * C + c, :, k * LANES : (k + 1) * LANES] = jnp.where(x == 0, *pieces)
 
 
+def mixer_sums_kernel(at_ref, *refs):
+    pieces, theirs, mine = refs[:4], refs[4], refs[5:]
+    z, c = at_ref[0], at_ref[1]
+    sub = theirs.shape[1]
+    for k in range(Z):
+        bits = [(z // 2 + k // 2) % 2, (z + k) % 2]
+        for other in range(2):
+            core = c + other - 2 * c * other
+            row = pl.ds(pl.multiple_of(((bits[0] * 2 + bits[1]) * 2 + core) * sub, sub), sub)
+            total = pieces[0][row, :].astype(F32)
+            for p in pieces[1:]:
+                total = total + p[row, :].astype(F32)
+            if other:
+                theirs[k] = total.astype(BF)
+            else:
+                mine[k][0] = total.astype(BF)
+                mine[k][1] = jnp.zeros(theirs.shape[1:], BF)
+
+
 def mixer_grads_kernel(
-    x_ref, mine, theirs, w_in, w_forget, w_gate, grad_in, grad_forget, grad_gate, along_ref
+    at_ref, mine, theirs, w_in, w_forget, w_gate, grad_in, grad_forget, grad_gate, along_ref
 ):
-    x = x_ref[0]
+    x, z, c = at_ref[0], at_ref[1], at_ref[2]
     total = jnp.zeros((w_in.shape[0], 1), F32)
     for m, (w_ref, g_ref) in enumerate(((w_in, grad_in), (w_forget, grad_forget), (w_gate, grad_gate))):
-        for z in range(Z):
+        for k in range(Z):
+            there = (z // 2 + k // 2) % 2 * 2 + (z + k) % 2
             for y in range(2):
-                for c in range(C):
-                    to, j = ((z * 2 + y) * C + c) * LANES, m * 2 + y
+                for other in range(2):
+                    core = c + other - 2 * c * other
+                    j = m * 2 + y
+                    to = pl.ds(pl.multiple_of(((there * 2 + y) * C + core) * LANES, LANES), LANES)
                     at = j % 3 * LANES
                     piece = jnp.where(
                         x == j // 3,
-                        mine[z * C + c, :, at : at + LANES],
-                        theirs[z * C + c, :, at : at + LANES],
+                        mine[k * 2 + other, :, at : at + LANES],
+                        theirs[k * 2 + other, :, at : at + LANES],
                     ).astype(F32)
-                    g_ref[:, to : to + LANES] = piece
-                    weight = w_ref[:, to : to + LANES].astype(F32)
+                    g_ref[:, to] = piece
+                    weight = w_ref[:, to].astype(F32)
                     total = total + jnp.sum(piece * weight, axis=1, keepdims=True)
     along_ref[...] = jnp.broadcast_to(total, along_ref.shape)
 
@@ -221,9 +243,9 @@
     copies.flush(0)
     copies.wait(*range(2, 4 + parts * parts))
 
-    @pl.loop(0, 4)
+    @pl.loop(0, 2)
     def _(i):
-        at = pl.ds(i * (group // 4), group // 4)
+        at = pl.ds(i * (group // 2), group // 2)
         deep, span = width // parts, 3 * feats // parts
         for k in range(parts):
             total = None
@@ -314,8 +336,8 @@
         partial[at, width:] = stat_block([squares], 2 * order[count + 1]).astype(BF)
     copies.flush(0)
     copies.wait(parties + 4)
-    for k in range(4):
-        at = slice(k * group // 4, (k + 1) * group // 4)
+    for k in range(2):
+        at = slice(k * group // 2, (k + 1) * group // 2)
         partial[at, :width] = dot(mixed[at, :], out_w[...]).astype(BF)
 
 
@@ -337,15 +359,16 @@
 
 
 def glu_kernel(copies, hidden, grad, *refs):
-    weights, outs, total, partial = refs[:4], refs[4:10], refs[11], refs[10]
+    weights, outs, partial, total = refs[:4], refs[4:10], refs[10], refs[11]
     group, block = outs[0].shape
+    width = hidden.shape[1]
     for k in range(2):
         gate_up, down = weights[k], weights[2 + k]
         act, d_gate, d_up = outs[3 * k : 3 * k + 3]
         w_gate, w_up = gate_up.at[:block, :], gate_up.at[block:, :]
         copies.wait(0, 2 + k)
-        for i in range(4):
-            at = slice(i * group // 4, (i + 1) * group // 4)
+        for i in range(2):
+            at = slice(i * group // 2, (i + 1) * group // 2)
             gate = times_transposed(hidden[at, :], w_gate[...])
             up = times_transposed(hidden[at, :], w_up[...])
             copies.wait(1, 4 + k)
@@ -355,19 +378,13 @@
             act[at, :] = (silu * up).astype(BF)
             d_gate[at, :] = (d_act * up * sigmoid_slope(gate, sig)).astype(BF)
             d_up[at, :] = (d_act * silu).astype(BF)
-            value = dot(d_gate[at, :], w_gate[...]) + dot(d_up[at, :], w_up[...])
-            if k == 0:
-                total[at, :] = value
-            else:
-                partial[at, :] = (total[at, :] + value).astype(BF)
+            back = dot(d_gate[at, :], w_gate[...]) + dot(d_up[at, :], w_up[...])
+            for cols, value in ((slice(0, width), back), (slice(width, None), dot(act[at, :], down[...]))):
+                if k == 0:
+                    total[at, cols] = value
+                else:
+                    partial[at, cols] = (total[at, cols] + value).astype(BF)
         copies.flush(3 * k, 3 * k + 1, 3 * k + 2)
-
-
-def glu_out_kernel(act0, act1, w0, w1, partial):
-    group = act0.shape[0]
-    for k in range(4):
-        at = slice(k * group // 4, (k + 1) * group // 4)
-        partial[at, :] = (dot(act0[at, :], w0[...]) + dot(act1[at, :], w1[...])).astype(BF)
 
 
 def glu_weights_kernel(parts, terms, *refs):
@@ -412,18 +429,19 @@
         begin += mine.shape[0]
 
 
-def d_resid_kernel(summed, resid, tokens, grad, gain, scale, d_resid, piece):
+def d_resid_kernel(summed, resid, tokens, grad, gain, scale, d_resid, piece, result):
     width = tokens.shape[1]
 
     @pl.loop(0, tokens.shape[0] // STEP)
     def _(i):
         at = pl.ds(i * STEP, STEP)
-        d_hidden = summed[at, :].astype(F32) * gain[...]
+        d_hidden = summed[at, :width].astype(F32) * gain[...]
         value = resid[at, :]
         inv = inverse_rms(value)
         hat = value * inv
         d_value = grad[at, :].astype(F32) + inv * (d_hidden - hat * mean_last(d_hidden * hat))
         d_resid[at, :] = d_value
+        result[at, :] = (value + summed[at, width:].astype(F32)).astype(BF)
         low = d_value.astype(BF)
         piece[at, :width] = low
         mean = mean_last(low.astype(F32) * (value - tokens[at, :].astype(F32)))
@@ -481,6 +499,24 @@
     for d in range(parts):
         for k in range(parts):
             outs[d * parts + k][...] = contract_rows(normed[:, d * deep : (d + 1) * deep], d_raw[k][...]).astype(BF)
+
+
+def out_weights_kernel(y_ref, x_ref, mixed, d_mixed, *refs):
+    *outs, full = refs
+    y, x = y_ref[0], x_ref[0]
+    width = full.shape[1]
+    sub, part = mixed.shape[1] // 2, width // CHUNKS
+    for k in range(2):
+        row = pl.multiple_of((k + y - 2 * k * y) * sub, sub)
+        full[...] = contract_rows(mixed[:, pl.ds(row, sub)], d_mixed[:, :width])
+        for m in range(2):
+            half = m + x - 2 * m * x
+            for z in range(Z // 2):
+                for there in range(2):
+                    near = (there + y - 2 * there * y) * Z + half * (Z // 2) + z
+                    at = pl.ds(pl.multiple_of(near * part, part), part)
+                    to = (z * 2 + there) * part
+                    outs[k * 2 + m][:, to : to + part] = full[:, at].astype(BF)
 
 
 def d_mixer_kernel(parties, parts, count, copies, x_ref, order, *refs):
@@ -524,8 +560,8 @@
     copies.wait(*range(2 * parties + 8, 2 * parties + 8 + parts * parts))
     deep = partial.shape[1] // parts
     for d in range(parts):
-        for i in range(4):
-            at = slice(i * group // 4, (i + 1) * group // 4)
+        for i in range(2):
+            at = slice(i * group // 2, (i + 1) * group // 2)
             total = None
             for k, d_part in enumerate(d_parts):
                 part = times_transposed(d_part[at, :], weights[d * parts + k][...])
@@ -542,10 +578,6 @@
         hat = value * inv
         d = summed[at, :].astype(F32) * gain[...]
         out[at, :] = d_resid[at, :] + inv * (d - hat * mean_last(d * hat))
-
-
-def result_kernel(summed, resid, out):
-    out[...] = (resid[...] + summed[...].astype(F32)).astype(BF)
 
 
 def after(value, *others):
@@ -616,6 +648,7 @@
         return own.astype(BF).astype(F32) + swap(sent.astype(BF), axis).astype(F32)
 
     near_x = x[None].astype(jnp.int32)
+    z_c = jnp.stack([z, c]).astype(jnp.int32)
 
     def own_and_neighbours(value):
         corner = lax.ppermute(value, ("y", "x"), [(i, 3 - i) for i in range(4)])
@@ -624,20 +657,26 @@
     table_f = bound_table.astype(F32)
     soft = jax.nn.softmax(table_f, axis=0)
     own_bound = jnp.sum(soft[1 : LAYER + 1], axis=0)
+
+    if pair:
+        (glu,) = call(glu_blocks_kernel, [((CHUNKS, tall, sub), BF)], ff_gate, ff_up, ff_down)
+    else:
+        glu = jnp.concatenate([w.T.reshape(CHUNKS, block, sub) for w in (ff_gate, ff_up)], axis=1)
+        glu = jnp.concatenate([glu, ff_down.reshape(CHUNKS, block, sub)], axis=1)
+    (out_rows,) = y_first(in_order(w_out))
 
     tokens_y, grad_y = y_first(tokens, out_grad)
     if pair:
         (blocks,) = call(
             mixer_blocks_kernel, [((CHUNKS, sub, 3 * feats // 2), BF)], near_x, w_in, w_forget, w_gate, smem=1
         )
-        moved = spread(blocks)
+        moved = after(spread(blocks), glu, out_rows)
         small = jnp.stack([attn_gain.astype(F32), mlp_gain.astype(F32), own_bound, mix_gain.astype(F32)])
         small = [small, swap(small, "y")]
         (piece,) = call(
             token_piece_kernel, [((rows, width + LANES), BF)],
             near_y, tokens, jnp.concatenate([v[:2] for v in small]), smem=1,
         )
-        grad_all = gather_rows(grad_y)
         tokens_all = gather_rows(after(piece, moved))
         gains = tokens_all.reshape(CHUNKS, rows, -1)[:, :4, width:].astype(F32)
         attn_g, mlp_g = (
@@ -649,7 +688,7 @@
     else:
         gains = lax.all_gather(jnp.stack([attn_gain, mlp_gain]), ("z", "y", "c"), axis=1, tiled=True)
         attn_g, mlp_g = y_first(gains[:1].astype(F32), gains[1:].astype(F32))
-        tokens_all, grad_all = gather_rows(tokens_y), gather_rows(grad_y)
+        tokens_all = gather_rows(tokens_y)
         small = in_order(jnp.stack([own_bound, mix_gain.astype(F32)])[None])
         mixer = [
             w.reshape(sub, Z, Y, C, sub).transpose(1, 3, 0, 2, 4).reshape(CHUNKS, sub, feats)
@@ -657,16 +696,9 @@
         ]
         moved = spread(jnp.concatenate(mixer, axis=2))
         mixer = over_y(moved.reshape(CHUNKS * sub, 3 * feats))
-    (out_rows,) = y_first(in_order(w_out))
+    glu = spread(after(glu, moved))
     bound = small[:, 0].reshape(1, feats)
     mix_g = small[:, 1].reshape(1, feats)
-
-    if pair:
-        (glu,) = call(glu_blocks_kernel, [((CHUNKS, tall, sub), BF)], ff_gate, ff_up, ff_down)
-    else:
-        glu = jnp.concatenate([w.T.reshape(CHUNKS, block, sub) for w in (ff_gate, ff_up)], axis=1)
-        glu = jnp.concatenate([glu, ff_down.reshape(CHUNKS, block, sub)], axis=1)
-    glu = spread(after(glu, moved))
 
     slot = jnp.arange(lengths.shape[0])
     starts = jnp.sum(jnp.where(slot[None, :] < slot[:, None], lengths[None, :], 0), axis=1)
@@ -723,16 +755,21 @@
         smem=1, scratch=carries + [pltpu.VMEM((group, feats), BF)], late=crowd,
     )
     summed = scatter_rows(after(partial, glu))
+    own_grad = lax.all_to_all(jnp.broadcast_to(after(grad_y, glu)[None], (Z, rows, width)), "z", 0, 0, tiled=False)
+    other_grad = swap(own_grad, "c")
+    grad_all = jnp.where(
+        c == 0, jnp.stack([own_grad, other_grad], axis=1), jnp.stack([other_grad, own_grad], axis=1)
+    ).reshape(group, width)
     resid, hidden, scale = call(
         resid_kernel,
         [((rows, width), F32), ((rows, width), BF), ((rows, LANES), F32)],
-        after(summed, *early), tokens_y, mlp_g,
-    )
-    hidden_all = after(gather_rows(hidden), *late)
+        after(summed, own_grad, *early, *late), tokens_y, mlp_g,
+    )
+    hidden_all = after(gather_rows(hidden), grad_all)
     thin = ((group, block), BF)
     act0, d_gate0, d_up0, act1, d_gate1, d_up1, partial = call(
-        glu_kernel, [thin] * 6 + [((group, width), BF)],
-        hidden_all, grad_all, *gate_up_w, *down_w, late=0, scratch=[pltpu.VMEM((group, width), F32)],
+        glu_kernel, [thin] * 6 + [((group, 2 * width), BF)],
+        hidden_all, grad_all, *gate_up_w, *down_w, late=0, scratch=[pltpu.VMEM((group, 2 * width), F32)],
     )
     acts = [act0, act1]
 
@@ -759,7 +796,8 @@
         return upper, swap(upper_sent, "y"), lower, swap(lower_sent, "x")
 
     def last_sums(*pieces):
-        return call(last_sums_kernel, [((CHUNKS, tall, sub), BF)], *pieces)[0]
+        height = sum(p.shape[0] for p in pieces[::2])
+        return call(last_sums_kernel, [((CHUNKS, height, sub), BF)], *pieces)[0]
 
     def to_blocks(value):
         return value.reshape(value.shape[0], -1, sub).transpose(1, 0, 2)
@@ -770,24 +808,22 @@
 
     summed = scatter_rows(partial)
     gate_up = weight_pieces((0, 0), [d_gate0, d_up0, d_gate1, d_up1], hidden_all)
-    (partial_out,) = call(glu_out_kernel, [((group, width), BF)], *acts, *down_w)
     down = weight_pieces((0,), acts, grad_all)
-    summed = after(summed, partial_out, *down)
     if pair:
-        gate_up = first_swaps(gate_up)
+        gate_up = first_sums(first_swaps(gate_up))
+        down = first_swaps(down)
         summed, *gate_up = lax.optimization_barrier((summed, *gate_up))
-        gate_up = first_sums(gate_up)
-    d_resid, piece = call(
-        d_resid_kernel, [((rows, width), F32), ((rows, width + LANES), BF)],
+        summed, *down = lax.optimization_barrier((summed, *down))
+    d_resid, piece, result_y = call(
+        d_resid_kernel, [((rows, width), F32), ((rows, width + LANES), BF), ((rows, width), BF)],
         summed, resid, tokens_y, grad_y, mlp_g, scale,
     )
     d_mixed = gather_rows(piece)
     if pair:
-        down = first_swaps(down)
         gate_up = last_swaps(gate_up)
+        down = last_swaps(first_sums(down))
         d_mixed, *gate_up = lax.optimization_barrier((d_mixed, *gate_up))
         d_mixed, *down = lax.optimization_barrier((d_mixed, *down))
-        down = first_sums(down)
 
     mixed_in, d_gate_raw, adjoint, passed, first = call(
         mixer_back_kernel,
@@ -797,10 +833,10 @@
     )
     firsts = parties(first)
     if pair:
-        down = last_swaps(after(down, *firsts))
-        glu_grad = last_sums(*gate_up, *down)
+        glu_grad = last_sums(*after((*gate_up, *down), first))
     else:
         glu_grad = jnp.concatenate([total_blocks(gate_up), total_blocks(down)], axis=1)
+    raw = after(raw, glu_grad)
     glu_grad = spread(glu_grad)
     *d_raw, part_bound, partial = call(
         functools.partial(d_mixer_kernel, crowd, parts, count),
@@ -810,12 +846,10 @@
         smem=2, scratch=carries + [pltpu.VMEM((group, 3 * feats), BF)], late=2 * crowd,
     )
 
-    result_sum = scatter_rows(after(partial_out, d_mixed))
     (token_grad_y,) = call(
         token_grad_kernel, [((rows, width), F32)],
-        after(scatter_rows(partial), result_sum), tokens_y, d_resid, attn_g,
-    )
-    (result_y,) = call(result_kernel, [((rows, width), BF)], result_sum, resid)
+        scatter_rows(partial), tokens_y, d_resid, attn_g,
+    )
     result, token_grad = z_first(result_y, token_grad_y)
 
     pieces = call(
@@ -831,46 +865,68 @@
             swap(pieces[2], "y"),
             lax.ppermute(pieces[3], ("y", "x"), [(i, 3 - i) for i in range(4)]),
         ]
-        mixer_grad = sum(p.astype(F32) for p in pieces).astype(BF)
-        mixed_in, part_bound = after((mixed_in, part_bound), mixer_grad)
         top, bottom = jnp.split(part_bound, 2)
         d_bound = jnp.where(y == 0, top, bottom) + swap(jnp.where(y == 0, bottom, top), "y")
+        out_pieces = call(
+            out_weights_kernel, [((sub, width // 2), BF)] * 4,
+            near_y, near_x, after(mixed_in, *d_raw), d_mixed, smem=2, scratch=[pltpu.VMEM((sub, width), F32)],
+        )
+        pieces = after(pieces, *out_pieces, d_bound)
+        shape = (2, sub, 3 * feats // 2)
+        theirs, *mine = call(
+            mixer_sums_kernel, [((Z, *shape[1:]), BF)] + [(shape, BF)] * Z, z_c, *pieces, smem=1
+        )
+        out_pieces = after(out_pieces, theirs)
+        got = swap(theirs, "c")
+        mine = [v.at[1].set(got[k]) for k, v in enumerate(mine)]
+        mixer_grad = [mine[0]] + [lax.ppermute(mine[k], "z", [(i, i ^ k) for i in range(Z)]) for k in range(1, Z)]
+        mixer_grad = jnp.concatenate(mixer_grad, axis=0)
     else:
         d_bound = lax.psum_scatter(part_bound, "y", scatter_dimension=0, tiled=True)
         mixer_grad = lax.psum_scatter(pieces[0], "y", scatter_dimension=0, tiled=True)
         mixer_grad = both(mixer_grad, mixer_grad, "x").astype(BF)
+        mixer_grad = spread(mixer_grad.reshape(CHUNKS, sub, 3 * feats))
     d_bound = d_bound + swap(d_bound, "x")
     row_ids = jnp.arange(bound_table.shape[0])[:, None]
     member = jnp.logical_and(row_ids >= 1, row_ids <= LAYER).astype(F32)
     grad_table = soft * (member - own_bound[None, :]) * d_bound[None, :]
-    mixer_grad = spread(after(mixer_grad, glu_grad).reshape(CHUNKS, sub, 3 * feats // parts))
-
-    grad_out = contract_rows(mixed_in, d_mixed[:, :width])
-    (grad_out,) = z_first(grad_out.astype(BF))
+
     if pair:
-        top, bottom = jnp.split(grad_out, 2, axis=0)
-        grad_out = both(jnp.where(y == 0, top, bottom), jnp.where(y == 0, bottom, top), "y")
+        grad_out = sum(
+            p.astype(F32)
+            for p in (
+                out_pieces[0],
+                swap(out_pieces[1], "x"),
+                swap(out_pieces[2], "y"),
+                lax.ppermute(out_pieces[3], ("y", "x"), [(i, 3 - i) for i in range(4)]),
+            )
+        ).astype(BF)
+        grad_gate_ff, grad_up_ff, grad_down, along_ff = call(
+            glu_grads_kernel,
+            [((sub, CHUNKS * block), F32)] * 2 + [((CHUNKS * block, sub), F32), ((sub, LANES), F32)],
+            glu_grad, ff_gate, ff_up,
+        )
+        grad_mlp = along_ff[:, 0]
+        grad_mlp = grad_mlp + swap(grad_mlp, "x")
+        mixer_grad = after(mixer_grad, grad_out, d_bound, grad_mlp)
+        mixer_grad = [mixer_grad, swap(mixer_grad, "x")]
+        other = swap(grad_out, "x")
+        grad_out = jnp.concatenate(
+            [jnp.where(x == 0, grad_out, other), jnp.where(x == 0, other, grad_out)], axis=1
+        ).astype(F32)
     else:
+        (grad_out,) = z_first(contract_rows(mixed_in, d_mixed[:, :width]).astype(BF))
         grad_out = lax.psum_scatter(grad_out, "y", scatter_dimension=0, tiled=True)
-    grad_out = both(grad_out, grad_out, "x")
-    if pair:
-        mixer_grad = after(mixer_grad, grad_out, d_bound)
-        mixer_grad = [mixer_grad, swap(mixer_grad, "x")]
+        grad_out = both(grad_out, grad_out, "x")
 
     def along(weight, grad):
         return jnp.sum(weight.astype(F32) * grad, axis=1)
 
-    square, glued = ((sub, width), F32), ((sub, CHUNKS * block), F32)
+    square = ((sub, width), F32)
     if pair:
-        grad_gate_ff, grad_up_ff, grad_down, grad_mlp = call(
-            glu_grads_kernel, [glued] * 2 + [((CHUNKS * block, sub), F32), ((sub, LANES), F32)],
-            glu_grad, ff_gate, ff_up,
-        )
-        grad_mlp = grad_mlp[:, 0]
-        grad_mlp = grad_mlp + swap(grad_mlp, "x")
         grad_in, grad_forget, grad_gate, grad_attn = call(
             mixer_grads_kernel, [square] * 3 + [((sub, LANES), F32)],
-            near_x, mixer_grad[0], after(mixer_grad[1], grad_mlp), w_in, w_forget, w_gate, smem=1,
+            jnp.concatenate([near_x, z_c]), *mixer_grad, w_in, w_forget, w_gate, smem=1,
         )
         grad_attn = grad_attn[:, 0]
     else:

time: 489 us -> 457 us (0.935)
  waiting for transfers between devices: 246 us -> 203 us
  local copies, waits for them, and re-layouts: 12.9 us -> 24.1 us
  starting transfers between devices: 60 us -> 69.1 us
  Pallas kernels: 127 us -> 120 us
    ppermute x32 -> x35, waiting for transfers between devices: 170 us -> 125 us  [swap(): return lax.ppermute(value, axis, [(0, 1), (1, 0)])]
    reduce_scatter x4 -> x3, waiting for transfers between devices: 18.2 us -> 1.24 us  [scatter_rows(): lax.psum_scatter(partial, ('z', 'c'), scatter_dimension=0, tiled=True)]
    all_to_all x0 -> x1, waiting for transfers between devices: none -> 13.4 us  [per_device(): lax.all_to_all(jnp.broadcast_to(after(grad_y, glu)[None], (Z, rows, width...]
    ppermute x0 -> x4, starting transfers between devices: none -> 9.91 us  [the longest x3 7.56 us: per_device(): lax.ppermute(mine[k], 'z', [(i, i ^ k) for i in range(Z)])]
    all_gather x4 -> x3, waiting for transfers between devices: 39.9 us -> 46.7 us  [gather_rows(): return lax.all_gather(own, ('z', 'c'), axis=0, tiled=True)]
    pallas_call x25 -> x24, Pallas kernels: 127 us -> 120 us  [call(): pl.pallas_call(body, out_shape=shapes, in_specs=[pl.BlockSpec(memory_spac...]
    all_to_all x4 -> x3, starting transfers between devices: 18.2 us -> 12.3 us  [spread(): return lax.all_to_all(value, ('z', 'c'), 0, 0, tiled=True)]
    all_to_all x4 -> x3, waiting for transfers between devices: 17 us -> 11.2 us  [spread(): return lax.all_to_all(value, ('z', 'c'), 0, 0, tiled=True)]
  transfers between devices with their start and end apart: 48 -> 53, of which waited for: 31 -> 29; matrix products, arithmetic and copies ran while one was open for 6% -> 8% of each run, Pallas kernels for 19% -> 17%
where the time goes in v5:
time: 457 us; the launch traced here: 451 us
  waiting for transfers between devices  203 us (44%)
  Pallas kernels  120 us (26%)
  starting transfers between devices  69.1 us (15%)
  local copies, waits for them, and re-layouts  24.1 us (5%)
  other arithmetic  19.9 us (4%)
  between operations  15.3 us (3%)
    ppermute x35, waiting for transfers between devices, swap(): return lax.ppermute(value, axis, [(0, 1), (1, 0)])  125 us
    pallas_call x24, Pallas kernels, call(): pl.pallas_call(body, out_shape=shapes, in_specs=[pl.BlockSpec(memory_spac...  120 us
    all_gather x3, waiting for transfers between devices, gather_rows(): return lax.all_gather(own, ('z', 'c'), axis=0, tiled=True)  46.7 us
    ppermute x35, starting transfers between devices, swap(): return lax.ppermute(value, axis, [(0, 1), (1, 0)])  36.1 us
    all_to_all x1, waiting for transfers between devices, per_device(): lax.all_to_all(jnp.broadcast_to(after(grad_y, glu)[None], (Z, rows, width...  13.4 us
    all_to_all x3, starting transfers between devices, spread(): return lax.all_to_all(value, ('z', 'c'), 0, 0, tiled=True)  12.3 us
    all_to_all x3, waiting for transfers between devices, spread(): return lax.all_to_all(value, ('z', 'c'), 0, 0, tiled=True)  11.2 us
  transfers between devices with their start and end apart: 53, of which 29 were waited for; matrix products, arithmetic and copies ran while one was open for 8% of the time, Pallas kernels for 17%

profile of v5, /device:TPU:0, one launch (start us, length us, event | category | flops | bytes accessed | tf_op | source)
XLA Modules:
  0.0 450.9 jit_solution(18190378179692432741)
XLA Ops:
  7.2 3.0 collective-permute-start.1
  10.2 2.5 shard_map.238
  12.8 4.9 %all-to-all-start = ((bf16[8,128,384]{2,1,0:T(8,128)(2,1)}), bf16[8,128,384]{2,1,0:T(8,128)(2,1)S(1)}, u32[]{:S(2)}, u32[]{:S(2)}) async-start(bf16[8,128,384]{2,1,0:T(8,128)(2,1)} %shard_map.238), calls=%async_computation | async-start | bytes 1572864 | tf_op jit(solution)/shard_map/all_to_all | solution.py:645
  18.9 4.0 shard_map.239
  26.4 2.4 shard_map.240.refs_9_.refs_1_
  28.7 9.9 %all-to-all-done = bf16[8,128,384]{2,1,0:T(8,128)(2,1)S(1)} async-done(((bf16[8,128,384]{2,1,0:T(8,128)(2,1)}), bf16[8,128,384]{2,1,0:T(8,128)(2,1)S(1)}, u32[]{:S(2)}, u32[]{:S(2)}) %all-to-all-start) | async-done | bytes 786464 | tf_op jit(solution)/shard_map/all_to_all | solution.py:645
  38.7 3.7 all-to-all-start.1
  47.9 37.1 %all-gather.4.cloned.1.call-done.refs_2_ = bf16[512,2176]{1,0:T(8,128)(2,1)} async-done(((bf16[64,2176]{1,0:T(8,128)(2,1)}), bf16[512,2176]{1,0:T(8,128)(2,1)}) %all-gather.4.cloned.1.call-update) | async-done | bytes 2228240 | tf_op jit(solution)/shard_map/all_gather | solution.py:588
  86.4 9.4 %shard_map.241 = (bf16[512,2048]{1,0:T(8,128)(2,1)}, f32[512,768]{1,0:T(8,128)}, f32[2,512,128]{2,1,0:T(8,128)}, f32[2,512,128]{2,1,0:T(8,128)}, f32[2,512,128]{2,1,0:T(8,128)}, /*index=5*/f32[16,256]{1,0:T(8,128)}) custom-call(s32[1]{0:T(128)} %bitcast.2.refs_0_.refs_1_, f32[1,2048]{1,0:T(1,128)} %pad_maximum_fusion.6.refs_1_.refs_3_, ...), custom_call_target="tpu_custom_call" | custom-call | bytes 1024 | tf_op jit(solution)/shard_map/pallas_call | solution.py:87
  101.3 2.6 collective-permute-done.7.refs_4_.refs_5_
  104.5 4.9 %shard_map.242 = (f32[2,512,128]{2,1,0:T(8,128)}, f32[8,256]{1,0:T(8,128)}, bf16[512,2176]{1,0:T(8,128)(2,1)}) custom-call(s32[34]{0:T(128)} %pad_add_fusion.refs_0_.refs_1_, f32[16,256]{1,0:T(8,128)} %get-tuple-element.183.refs_1_.refs_2_, f32[16,256]{1,0:T(8,128)} %copy-done.20, f32[16,256]{1,0:T(8,128)} %copy-done.21, f32[16,256]{1,0:T(8,128)} %copy-done.22, ...), custom_call_target="tpu_custom_call" | custom-call | bytes 1024 | tf_op jit(solution)/shard_map/pallas_call | solution.py:87
  115.8 2.0 broadcast_in_dim.22
  117.9 5.4 %all-to-all-start.2 = ((bf16[4,64,2048]{2,1,0:T(8,128)(2,1)}), bf16[4,64,2048]{2,1,0:T(8,128)(2,1)S(1)}, u32[]{:S(2)}, u32[]{:S(2)}) async-start(bf16[4,64,2048]{2,1,0:T(8,128)(2,1)} %broadcast_in_dim.22), calls=%async_computation.3 | async-start | bytes 2097152 | tf_op jit(solution)/shard_map/all_to_all | solution.py:758
  124.2 21.2 %collective-permute-done.8 = bf16[8,704,128]{2,1,0:T(8,128)(2,1)} collective-permute-done((bf16[8,704,128]{2,1,0:T(8,128)(2,1)}, bf16[8,704,128]{2,1,0:T(8,128)(2,1)}, u32[]{:S(2)}, u32[]{:S(2)}) %collective-permute-start.8) | collective-permute-done | bytes 1441824 | tf_op jit(solution)/shard_map/ppermute | solution.py:20
  148.2 13.4 %all-to-all-done.2 = bf16[4,64,2048]{2,1,0:T(8,128)(2,1)S(1)} async-done(((bf16[4,64,2048]{2,1,0:T(8,128)(2,1)}), bf16[4,64,2048]{2,1,0:T(8,128)(2,1)S(1)}, u32[]{:S(2)}, u32[]{:S(2)}) %all-to-all-start.2) | async-done | bytes 1048608 | tf_op jit(solution)/shard_map/all_to_all | solution.py:758
  163.5 2.7 shard_map.244
  178.8 2.2 collective-permute-start.12
  182.3 5.2 %collective-permute-done.13 = bf16[8,352,128]{2,1,0:T(8,128)(2,1)S(1)} collective-permute-done((bf16[8,352,128]{2,1,0:T(8,128)(2,1)S(1)}, bf16[8,352,128]{2,1,0:T(8,128)(2,1)S(1)}, u32[]{:S(2)}, u32[]{:S(2)}) %collective-permute-start.13) | collective-permute-done | bytes 720928 | tf_op jit(solution)/shard_map/ppermute | solution.py:20
  198.0 19.7 %shard_map.245 = (bf16[512,352]{1,0:T(8,128)(2,1)}, bf16[512,352]{1,0:T(8,128)(2,1)}, bf16[512,352]{1,0:T(8,128)(2,1)}, bf16[512,352]{1,0:T(8,128)(2,1)}, bf16[5...) custom-call(bf16[512,2048]{1,0:T(8,128)(2,1)} %all-gather.6.cloned.1.call-done.refs_0_.refs_4_, ...), custom_call_target="tpu_custom_call" | custom-call | bytes 1024 | tf_op jit(solution)/shard_map/pallas_call | solution.py:87
  217.8 6.7 %shard_map.246 = (bf16[2,352,1024]{2,1,0:T(8,128)(2,1)}, bf16[2,352,1024]{2,1,0:T(8,128)(2,1)}, bf16[2,352,1024]{2,1,0:T(8,128)(2,1)}, bf16[2,352,1024]{2,1,0:T(8,128)(2,1)}) custom-call(bf16[512,352]{1,0:T(8,128)(2,1)} %get-tuple-element.199.refs_0_, bf16[512,352]{1,0:T(8,128)(2,1)} %get-tuple-element.200.refs_1_, ...), custom_call_target="tpu_custom_call" | custom-call | bytes 1024 | tf_op jit(solution)/shard_map/pallas_call | solution.py:87
  224.5 2.1 collective-permute-start.17
  228.3 4.9 %shard_map.248 = (bf16[2,176,1024]{2,1,0:T(8,128)(2,1)}, bf16[2,176,1024]{2,1,0:T(8,128)(2,1)}, bf16[2,176,1024]{2,1,0:T(8,128)(2,1)}, bf16[2,176,1024]{2,1,0:T(8,128)(2,1)}) custom-call(bf16[512,352]{1,0:T(8,128)(2,1)} %get-tuple-element.212.refs_0_, bf16[512,352]{1,0:T(8,128)(2,1)} %get-tuple-element.213.refs_1_, bf16[512,2048]{1,0:T(8,128)(2,1)} %bitcast.85), custom_call_target="tpu_custom_call" | custom-call | bytes 1024 | tf_op jit(solution)/shard_map/pallas_call | solution.py:87
  233.8 25.5 %collective-permute-done.17.refs_1_ = bf16[2,352,1024]{2,1,0:T(8,128)(2,1)S(1)} collective-permute-done((bf16[2,352,1024]{2,1,0:T(8,128)(2,1)}, bf16[2,352,1024]{2,1,0:T(8,128)(2,1)S(1)}, u32[]{:S(2)}, u32[]{:S(2)}) %collective-permute-start.17) | collective-permute-done | bytes 1441824 | tf_op jit(solution)/shard_map/ppermute | solution.py:20
  259.3 2.0 collective-permute-done.18.refs_3_
  262.4 5.0 %shard_map.247 = (f32[352,1024]{1,0:T(8,128)}, bf16[352,1024]{1,0:T(8,128)(2,1)}, f32[352,1024]{1,0:T(8,128)}, bf16[352,1024]{1,0:T(8,128)(2,1)}) custom-call(bf16[2,352,1024]{2,1,0:T(8,128)(2,1)} %get-tuple-element.203.refs_0_, bf16[2,352,1024]{2,1,0:T(8,128)(2,1)} %copy-done.5, bf16[2,352,1024]{2,1,0:T(8,128)(2,1)} %get-tuple-element.205.refs_2_, ...), custom_call_target="tpu_custom_call" | custom-call | bytes 1024 | tf_op jit(solution)/shard_map/pallas_call | solution.py:87
  268.6 6.0 %collective-permute-done.19.refs_1_ = bf16[2,176,1024]{2,1,0:T(8,128)(2,1)S(1)} collective-permute-done((bf16[2,176,1024]{2,1,0:T(8,128)(2,1)}, bf16[2,176,1024]{2,1,0:T(8,128)(2,1)S(1)}, u32[]{:S(2)}, u32[]{:S(2)}) %collective-permute-start.19) | collective-permute-done | bytes 720928 | tf_op jit(solution)/shard_map/ppermute | solution.py:20
  275.8 4.0 shard_map.249
  282.0 3.2 shard_map.250
  287.2 11.9 %collective-permute-done.21.refs_1_ = bf16[352,1024]{1,0:T(8,128)(2,1)S(1)} collective-permute-done((bf16[352,1024]{1,0:T(8,128)(2,1)}, bf16[352,1024]{1,0:T(8,128)(2,1)S(1)}, u32[]{:S(2)}, u32[]{:S(2)}) %collective-permute-start.21) | collective-permute-done | bytes 720928 | tf_op jit(solution)/shard_map/ppermute | solution.py:20
  300.7 9.6 %all-gather.8.cloned.1.call-done.refs_0_.refs_3_ = bf16[512,2176]{1,0:T(8,128)(2,1)} async-done(((bf16[64,2176]{1,0:T(8,128)(2,1)}), bf16[512,2176]{1,0:T(8,128)(2,1)}) %all-gather.8.cloned.1.call-update) | async-done | bytes 2228240 | tf_op jit(solution)/shard_map/all_gather | solution.py:588
  310.3 6.0 %shard_map.251 = (bf16[512,256]{1,0:T(8,128)(2,1)}, bf16[512,256]{1,0:T(8,128)(2,1)}, f32[2,512,128]{2,1,0:T(8,128)}, f32[2,512,128]{2,1,0:T(8,128)}, f32[8,256]{1,0:T(8,128)}) custom-call(bf16[512,2176]{1,0:T(8,128)(2,1)} %all-gather.8.cloned.1.call-done.refs_0_.refs_3_, bf16[256,2048]{1,0:T(8,128)(2,1)} %shard_map.240.refs_9_.refs_1_, ...), custom_call_target="tpu_custom_call" | custom-call | bytes 1024 | tf_op jit(solution)/shard_map/pallas_call | solution.py:87
  316.3 4.8 %shard_map.252 = bf16[8,1056,128]{2,1,0:T(8,128)(2,1)} custom-call(f32[352,1024]{1,0:T(8,128)} %get-tuple-element.251.refs_0_, bf16[352,1024]{1,0:T(8,128)(2,1)} %copy-done.13, f32[352,1024]{1,0:T(8,128)} %get-tuple-element.253.refs_2_, bf16[352,1024]{1,0:T(8,128)(2,1)} %copy-done.14, f32[176,1024]{1,0:T(8,128)} %get-tuple-element.255.refs_4_, ...), custom_call_target="tpu_custom_call" | custom-call | bytes 1024 | tf_op jit(solution)/shard_map/pallas_call | solution.py:87
  321.1 3.6 all-to-all-start.3
  330.2 2.4 collective-permute-done.27.refs_9_
  333.2 7.6 %shard_map.253 = (bf16[512,384]{1,0:T(8,128)(2,1)}, bf16[512,384]{1,0:T(8,128)(2,1)}, f32[1,256]{1,0:T(1,128)}, bf16[512,2048]{1,0:T(8,128)(2,1)}) custom-call(s32[1]{0:T(128)} %bitcast.2.refs_0_.refs_1_, s32[34]{0:T(128)} %pad_add_fusion.refs_0_.refs_1_, f32[16,256]{1,0:T(8,128)} %get-tuple-element.183.refs_1_.refs_2_, f32[16,256]{1,0:T(8,128)} %copy-done.20, ...), custom_call_target="tpu_custom_call" | custom-call | bytes 1024 | tf_op jit(solution)/shard_map/pallas_call | solution.py:87
  340.8 5.1 %shard_map.256 = (bf16[1024,384]{1,0:T(8,128)(2,1)}, bf16[1024,384]{1,0:T(8,128)(2,1)}, bf16[1024,384]{1,0:T(8,128)(2,1)}, bf16[1024,384]{1,0:T(8,128)(2,1)}) custom-call(bf16[512,2048]{1,0:T(8,128)(2,1)} %get-tuple-element.265.refs_0_, bf16[512,384]{1,0:T(8,128)(2,1)} %get-tuple-element.266.refs_1_, bf16[512,384]{1,0:T(8,128)(2,1)} %get-tuple-element.267.refs_2_), custom_call_target="tpu_custom_call" | custom-call | bytes 1024 | tf_op jit(solution)/shard_map/pallas_call | solution.py:87
  347.1 2.4 collective-permute-start.30
  350.6 3.4 shard_map.257
  354.0 27.7 %collective-permute-done.31 = f32[128]{0:T(128)S(1)} collective-permute-done((f32[128]{0:T(128)S(1)}, f32[128]{0:T(128)S(1)}, u32[]{:S(2)}, u32[]{:S(2)}) %collective-permute-start.31) | collective-permute-done | bytes 544 | tf_op jit(solution)/shard_map/ppermute | solution.py:20
  383.2 3.9 shard_map.258
  390.4 2.4 collective-permute-start.38
  396.2 2.4 collective-permute-start.34
  398.6 3.5 collective-permute-start.35
  407.8 6.2 %shard_map.259 = (f32[128,2816]{1,0:T(8,128)}, f32[128,2816]{1,0:T(8,128)}, f32[2816,128]{1,0:T(8,128)}, f32[128,128]{1,0:T(8,128)}) custom-call(bf16[8,1056,128]{2,1,0:T(8,128)(2,1)} %copy-done, bf16[128,2816]{1,0:T(8,128)(2,1)} %refs_1_.9, bf16[128,2816]{1,0:T(8,128)(2,1)} %refs_2_.7), custom_call_target="tpu_custom_call" | custom-call | bytes 1024 | tf_op jit(solution)/shard_map/pallas_call | solution.py:87
  422.1 2.9 shard_map.254.refs_2_
  425.0 2.1 shard_map.255
  427.1 9.2 %collective-permute-done.41.refs_2_ = bf16[8,128,384]{2,1,0:T(8,128)(2,1)S(1)} collective-permute-done((bf16[8,128,384]{2,1,0:T(8,128)(2,1)S(1)}, bf16[8,128,384]{2,1,0:T(8,128)(2,1)S(1)}, u32[]{:S(2)}, u32[]{:S(2)}) %collective-permute-start.41) | collective-permute-done | bytes 786464 | tf_op jit(solution)/shard_map/ppermute | solution.py:20
  437.2 4.9 %shard_map.260 = (f32[128,2048]{1,0:T(8,128)}, f32[128,2048]{1,0:T(8,128)}, f32[128,2048]{1,0:T(8,128)}, f32[128,128]{1,0:T(8,128)}) custom-call(s32[3]{0:T(128)} %pad_add_fusion.1.refs_0_, bf16[8,128,384]{2,1,0:T(8,128)(2,1)} %copy-done.2, bf16[8,128,384]{2,1,0:T(8,128)(2,1)} %copy-done.9, bf16[128,2048]{1,0:T(8,128)(2,1)} %refs_3_.3, ...), custom_call_target="tpu_custom_call" | custom-call | bytes 1024 | tf_op jit(solution)/shard_map/pallas_call | solution.py:87
  (233 shorter events, 98.0 us)
Async XLA Ops:
  7.2 18.0 %collective-permute-start.1 = (bf16[128,2048]{1,0:T(8,128)(2,1)}, bf16[128,2048]{1,0:T(8,128)(2,1)S(1)}, u32[]{:S(2)}, u32[]{:S(2)}) collective-permute-start(bf16[128,2048]{1,0:T(8,128)(2,1)} %param.27), channel_id=1, source_target_pairs={{0,4},{4,0},{1,5},{5,1},{2,6},{6,2},{3,7},{7,3},{8,12},{12,8},{9,1... | collective-permute-start | bytes 1572872 | tf_op jit(solution)/shard_map/ppermute | solution.py:20
  12.8 25.9 %all-to-all-start = ((bf16[8,128,384]{2,1,0:T(8,128)(2,1)}), bf16[8,128,384]{2,1,0:T(8,128)(2,1)S(1)}, u32[]{:S(2)}, u32[]{:S(2)}) async-start(bf16[8,128,384]{2,1,0:T(8,128)(2,1)} %shard_map.238), calls=%async_computation | async-start | bytes 1572864 | tf_op jit(solution)/shard_map/all_to_all | solution.py:645
  17.6 67.4 %all-gather.4.cloned.1.call-start = ((), (), s32[]{:S(2)}) async-start(), calls=%async_computation.7 | async-start | bytes 2506752 | tf_op jit(solution)/shard_map/all_gather | solution.py:588
  18.3 4.6 %collective-permute-start = (f32[4,128]{1,0:T(4,128)S(1)}, f32[4,128]{1,0:T(4,128)S(1)}, u32[]{:S(2)}, u32[]{:S(2)}) collective-permute-start(f32[4,128]{1,0:T(4,128)S(1)} %pad_maximum_fusion.8), channel_id=1, source_target_pairs={{0,4},{4,0},{1,5},{5,1},{2,6},{6,2},{3,7},{7,3},{8,12},{12,8},{9,1... | collective-permute-start | bytes 6152 | tf_op jit(solution)/shard_map/ppermute | solution.py:20
  38.7 72.1 %all-to-all-start.1 = ((bf16[8,1056,128]{2,1,0:T(8,128)(2,1)}), bf16[8,1056,128]{2,1,0:T(8,128)(2,1)S(1)}, u32[]{:S(2)}, u32[]{:S(2)}) async-start(bf16[8,1056,128]{2,1,0:T(8,128)(2,1)} %shard_map.239), calls=%async_computation.1 | async-start | bytes 4325376 | tf_op jit(solution)/shard_map/all_to_all | solution.py:645
  42.4 121.1 %reduce-scatter.4.cloned.1.call-start = ((), (), s32[]{:S(2)}) async-start(), calls=%async_computation.8 | async-start | bytes 2506752 | tf_op jit(solution)/shard_map/reduce_scatter | solution.py:592
  43.8 42.6 %collective-permute-start.2 = (bf16[1024,384]{1,0:T(8,128)(2,1)S(1)}, bf16[1024,384]{1,0:T(8,128)(2,1)}, u32[]{:S(2)}, u32[]{:S(2)}) collective-permute-start(bf16[1024,384]{1,0:T(8,128)(2,1)S(1)} %bitcast.86), channel_id=1, source_target_pairs={{0,1},{1,0},{2,3},{3,2},{4,5},{5,4},{6,7},{7,6},{8,9},{9,8},{10,11... | collective-permute-start | bytes 2359304 | tf_op jit(solution)/shard_map/ppermute | solution.py:20
  45.3 41.1 %collective-permute-start.3 = (bf16[1024,384]{1,0:T(8,128)(2,1)S(1)}, bf16[1024,384]{1,0:T(8,128)(2,1)}, u32[]{:S(2)}, u32[]{:S(2)}) collective-permute-start(bf16[1024,384]{1,0:T(8,128)(2,1)S(1)} %bitcast.87), channel_id=1, source_target_pairs={{0,4},{4,0},{1,5},{5,1},{2,6},{6,2},{3,7},{7,3},{8,12},{12,8},{9,1... | collective-permute-start | bytes 2359304 | tf_op jit(solution)/shard_map/ppermute | solution.py:20
  45.8 40.5 %collective-permute-start.4 = (bf16[1024,384]{1,0:T(8,128)(2,1)S(1)}, bf16[1024,384]{1,0:T(8,128)(2,1)}, u32[]{:S(2)}, u32[]{:S(2)}) collective-permute-start(bf16[1024,384]{1,0:T(8,128)(2,1)S(1)} %bitcast.88), channel_id=1, source_target_pairs={{0,5},{1,4},{4,1},{5,0},{2,7},{3,6},{6,3},{7,2},{8,13},{9,12},{12,... | collective-permute-start | bytes 2359304 | tf_op jit(solution)/shard_map/ppermute | solution.py:654
  99.0 4.8 %collective-permute-start.7 = (f32[16,256]{1,0:T(8,128)}, f32[16,256]{1,0:T(8,128)S(1)}, u32[]{:S(2)}, u32[]{:S(2)}) collective-permute-start(f32[16,256]{1,0:T(8,128)} %get-tuple-element.183.refs_1_.refs_2_), channel_id=1, source_target_pairs={{0,5},{1,4},{4,1},{5,0},{2,7},{3,6},{6,3},{7,2},{8,13},{9,12},{12,... | collective-permute-start | bytes 49160 | tf_op jit(solution)/shard_map/ppermute | solution.py:654
  111.9 33.4 %collective-permute-start.8 = (bf16[8,704,128]{2,1,0:T(8,128)(2,1)}, bf16[8,704,128]{2,1,0:T(8,128)(2,1)}, u32[]{:S(2)}, u32[]{:S(2)}) collective-permute-start(bf16[8,704,128]{2,1,0:T(8,128)(2,1)} %slice.180), channel_id=1, source_target_pairs={{0,1},{1,0},{2,3},{3,2},{4,5},{5,4},{6,7},{7,6},{8,9},{9,8},{10,11... | collective-permute-start | bytes 4325384 | tf_op jit(solution)/shard_map/ppermute | solution.py:20
  113.4 33.2 %collective-permute-start.9 = (bf16[8,704,128]{2,1,0:T(8,128)(2,1)}, bf16[8,704,128]{2,1,0:T(8,128)(2,1)}, u32[]{:S(2)}, u32[]{:S(2)}) collective-permute-start(bf16[8,704,128]{2,1,0:T(8,128)(2,1)} %slice.180), channel_id=1, source_target_pairs={{0,4},{4,0},{1,5},{5,1},{2,6},{6,2},{3,7},{7,3},{8,12},{12,8},{9,1... | collective-permute-start | bytes 4325384 | tf_op jit(solution)/shard_map/ppermute | solution.py:20
  117.9 43.8 %all-to-all-start.2 = ((bf16[4,64,2048]{2,1,0:T(8,128)(2,1)}), bf16[4,64,2048]{2,1,0:T(8,128)(2,1)S(1)}, u32[]{:S(2)}, u32[]{:S(2)}) async-start(bf16[4,64,2048]{2,1,0:T(8,128)(2,1)} %broadcast_in_dim.22), calls=%async_computation.3 | async-start | bytes 2097152 | tf_op jit(solution)/shard_map/all_to_all | solution.py:758
  123.3 74.7 %all-gather.6.cloned.1.call-start = ((), (), s32[]{:S(2)}) async-start(), calls=%async_computation.9 | async-start | bytes 2359296 | tf_op jit(solution)/shard_map/all_gather | solution.py:588
  146.6 16.7 %collective-permute-start.11 = (bf16[8,352,128]{2,1,0:T(8,128)(2,1)}, bf16[8,352,128]{2,1,0:T(8,128)(2,1)S(1)}, u32[]{:S(2)}, u32[]{:S(2)}) collective-permute-start(bf16[8,352,128]{2,1,0:T(8,128)(2,1)} %slice.181), channel_id=1, source_target_pairs={{0,4},{4,0},{1,5},{5,1},{2,6},{6,2},{3,7},{7,3},{8,12},{12,8},{9,1... | collective-permute-start | bytes 2162696 | tf_op jit(solution)/shard_map/ppermute | solution.py:20
  147.1 16.4 %collective-permute-start.10 = (bf16[8,352,128]{2,1,0:T(8,128)(2,1)}, bf16[8,352,128]{2,1,0:T(8,128)(2,1)S(1)}, u32[]{:S(2)}, u32[]{:S(2)}) collective-permute-start(bf16[8,352,128]{2,1,0:T(8,128)(2,1)} %slice.181), channel_id=1, source_target_pairs={{0,1},{1,0},{2,3},{3,2},{4,5},{5,4},{6,7},{7,6},{8,9},{9,8},{10,11... | collective-permute-start | bytes 2162696 | tf_op jit(solution)/shard_map/ppermute | solution.py:20
  166.2 102.4 %reduce-scatter.6.cloned.1.call-start = ((), (), s32[]{:S(2)}) async-start(), calls=%async_computation.10 | async-start | bytes 4718592 | tf_op jit(solution)/shard_map/reduce_scatter | solution.py:592
  169.2 18.3 %collective-permute-start.13 = (bf16[8,352,128]{2,1,0:T(8,128)(2,1)S(1)}, bf16[8,352,128]{2,1,0:T(8,128)(2,1)S(1)}, u32[]{:S(2)}, u32[]{:S(2)}) collective-permute-start(bf16[8,352,128]{2,1,0:T(8,128)(2,1)S(1)} %slice.184), channel_id=1, source_target_pairs={{0,1},{1,0},{2,3},{3,2},{4,5},{5,4},{6,7},{7,6},{8,9},{9,8},{10,11... | collective-permute-start | bytes 2162696 | tf_op jit(solution)/shard_map/ppermute | solution.py:20
  171.0 18.0 %collective-permute-start.14 = (bf16[8,352,128]{2,1,0:T(8,128)(2,1)S(1)}, bf16[8,352,128]{2,1,0:T(8,128)(2,1)S(1)}, u32[]{:S(2)}, u32[]{:S(2)}) collective-permute-start(bf16[8,352,128]{2,1,0:T(8,128)(2,1)S(1)} %slice.185), channel_id=1, source_target_pairs={{0,4},{4,0},{1,5},{5,1},{2,6},{6,2},{3,7},{7,3},{8,12},{12,8},{9,1... | collective-permute-start | bytes 2162696 | tf_op jit(solution)/shard_map/ppermute | solution.py:20
  178.8 13.7 %collective-permute-start.12 = (bf16[4,64,2048]{2,1,0:T(8,128)(2,1)S(1)}, bf16[4,64,2048]{2,1,0:T(8,128)(2,1)S(1)}, u32[]{:S(2)}, u32[]{:S(2)}) collective-permute-start(bf16[4,64,2048]{2,1,0:T(8,128)(2,1)S(1)} %all-to-all-done.2), channel_id=1, source_target_pairs={{0,2},{2,0},{1,3},{3,1},{4,6},{6,4},{5,7},{7,5},{8,10},{10,8},{9,1... | collective-permute-start | bytes 3145736 | tf_op jit(solution)/shard_map/ppermute | solution.py:20
  181.1 14.1 %collective-permute-start.15 = (bf16[8,176,128]{2,1,0:T(8,128)(2,1)S(1)}, bf16[8,176,128]{2,1,0:T(8,128)(2,1)S(1)}, u32[]{:S(2)}, u32[]{:S(2)}) collective-permute-start(bf16[8,176,128]{2,1,0:T(8,128)(2,1)S(1)} %slice.186), channel_id=1, source_target_pairs={{0,1},{1,0},{2,3},{3,2},{4,5},{5,4},{6,7},{7,6},{8,9},{9,8},{10,11... | collective-permute-start | bytes 1081352 | tf_op jit(solution)/shard_map/ppermute | solution.py:20
  181.6 15.1 %collective-permute-start.16 = (bf16[8,176,128]{2,1,0:T(8,128)(2,1)S(1)}, bf16[8,176,128]{2,1,0:T(8,128)(2,1)S(1)}, u32[]{:S(2)}, u32[]{:S(2)}) collective-permute-start(bf16[8,176,128]{2,1,0:T(8,128)(2,1)S(1)} %slice.187), channel_id=1, source_target_pairs={{0,4},{4,0},{1,5},{5,1},{2,6},{6,2},{3,7},{7,3},{8,12},{12,8},{9,1... | collective-permute-start | bytes 1081352 | tf_op jit(solution)/shard_map/ppermute | solution.py:20
  217.8 92.5 %all-gather.8.cloned.1.call-start = ((), (), s32[]{:S(2)}) async-start(), calls=%async_computation.11 | async-start | bytes 2506752 | tf_op jit(solution)/shard_map/all_gather | solution.py:588
  224.5 34.8 %collective-permute-start.17 = (bf16[2,352,1024]{2,1,0:T(8,128)(2,1)}, bf16[2,352,1024]{2,1,0:T(8,128)(2,1)S(1)}, u32[]{:S(2)}, u32[]{:S(2)}) collective-permute-start(bf16[2,352,1024]{2,1,0:T(8,128)(2,1)} %get-tuple-element.204), channel_id=1, source_target_pairs={{0,1},{1,0},{2,3},{3,2},{4,5},{5,4},{6,7},{7,6},{8,9},{9,8},{10,11... | collective-permute-start | bytes 4325384 | tf_op jit(solution)/shard_map/ppermute | solution.py:20
  226.6 34.7 %collective-permute-start.18 = (bf16[2,352,1024]{2,1,0:T(8,128)(2,1)}, bf16[2,352,1024]{2,1,0:T(8,128)(2,1)S(1)}, u32[]{:S(2)}, u32[]{:S(2)}) collective-permute-start(bf16[2,352,1024]{2,1,0:T(8,128)(2,1)} %get-tuple-element.206), channel_id=1, source_target_pairs={{0,4},{4,0},{1,5},{5,1},{2,6},{6,2},{3,7},{7,3},{8,12},{12,8},{9,1... | collective-permute-start | bytes 4325384 | tf_op jit(solution)/shard_map/ppermute | solution.py:20
  233.3 41.4 %collective-permute-start.19 = (bf16[2,176,1024]{2,1,0:T(8,128)(2,1)}, bf16[2,176,1024]{2,1,0:T(8,128)(2,1)S(1)}, u32[]{:S(2)}, u32[]{:S(2)}) collective-permute-start(bf16[2,176,1024]{2,1,0:T(8,128)(2,1)} %get-tuple-element.215), channel_id=1, source_target_pairs={{0,1},{1,0},{2,3},{3,2},{4,5},{5,4},{6,7},{7,6},{8,9},{9,8},{10,11... | collective-permute-start | bytes 2162696 | tf_op jit(solution)/shard_map/ppermute | solution.py:20
  233.4 42.4 %collective-permute-start.20 = (bf16[2,176,1024]{2,1,0:T(8,128)(2,1)}, bf16[2,176,1024]{2,1,0:T(8,128)(2,1)S(1)}, u32[]{:S(2)}, u32[]{:S(2)}) collective-permute-start(bf16[2,176,1024]{2,1,0:T(8,128)(2,1)} %get-tuple-element.217), channel_id=1, source_target_pairs={{0,4},{4,0},{1,5},{5,1},{2,6},{6,2},{3,7},{7,3},{8,12},{12,8},{9,1... | collective-permute-start | bytes 2162696 | tf_op jit(solution)/shard_map/ppermute | solution.py:20
  279.8 19.3 %collective-permute-start.21 = (bf16[352,1024]{1,0:T(8,128)(2,1)}, bf16[352,1024]{1,0:T(8,128)(2,1)S(1)}, u32[]{:S(2)}, u32[]{:S(2)}) collective-permute-start(bf16[352,1024]{1,0:T(8,128)(2,1)} %get-tuple-element.224), channel_id=1, source_target_pairs={{0,4},{4,0},{1,5},{5,1},{2,6},{6,2},{3,7},{7,3},{8,12},{12,8},{9,1... | collective-permute-start | bytes 2162696 | tf_op jit(solution)/shard_map/ppermute | solution.py:20
  281.4 19.3 %collective-permute-start.22 = (bf16[352,1024]{1,0:T(8,128)(2,1)}, bf16[352,1024]{1,0:T(8,128)(2,1)S(1)}, u32[]{:S(2)}, u32[]{:S(2)}) collective-permute-start(bf16[352,1024]{1,0:T(8,128)(2,1)} %get-tuple-element.226), channel_id=1, source_target_pairs={{0,1},{1,0},{2,3},{3,2},{4,5},{5,4},{6,7},{7,6},{8,9},{9,8},{10,11... | collective-permute-start | bytes 2162696 | tf_op jit(solution)/shard_map/ppermute | solution.py:20
  285.2 25.0 %collective-permute-start.23 = (bf16[176,1024]{1,0:T(8,128)(2,1)}, bf16[176,1024]{1,0:T(8,128)(2,1)S(1)}, u32[]{:S(2)}, u32[]{:S(2)}) collective-permute-start(bf16[176,1024]{1,0:T(8,128)(2,1)} %get-tuple-element.233), channel_id=1, source_target_pairs={{0,4},{4,0},{1,5},{5,1},{2,6},{6,2},{3,7},{7,3},{8,12},{12,8},{9,1... | collective-permute-start | bytes 1081352 | tf_op jit(solution)/shard_map/ppermute | solution.py:20
  285.8 24.5 %collective-permute-start.24 = (bf16[176,1024]{1,0:T(8,128)(2,1)}, bf16[176,1024]{1,0:T(8,128)(2,1)S(1)}, u32[]{:S(2)}, u32[]{:S(2)}) collective-permute-start(bf16[176,1024]{1,0:T(8,128)(2,1)} %get-tuple-element.235), channel_id=1, source_target_pairs={{0,1},{1,0},{2,3},{3,2},{4,5},{5,4},{6,7},{7,6},{8,9},{9,8},{10,11... | collective-permute-start | bytes 1081352 | tf_op jit(solution)/shard_map/ppermute | solution.py:20
  321.1 85.4 %all-to-all-start.3 = ((bf16[8,1056,128]{2,1,0:T(8,128)(2,1)}), bf16[8,1056,128]{2,1,0:T(8,128)(2,1)S(1)}, u32[]{:S(2)}, u32[]{:S(2)}) async-start(bf16[8,1056,128]{2,1,0:T(8,128)(2,1)} %shard_map.252), calls=%async_computation.6 | async-start | bytes 4325376 | tf_op jit(solution)/shard_map/all_to_all | solution.py:645
  324.7 97.4 %reduce-scatter.8.cloned.1.call-start = ((), (), s32[]{:S(2)}) async-start(), calls=%async_computation.12 | async-start | bytes 2359296 | tf_op jit(solution)/shard_map/reduce_scatter | solution.py:592
  328.0 4.5 %collective-permute-start.27 = (f32[8,256]{1,0:T(8,128)S(1)}, f32[8,256]{1,0:T(8,128)S(1)}, u32[]{:S(2)}, u32[]{:S(2)}) collective-permute-start(f32[8,256]{1,0:T(8,128)S(1)} %copy-done.23), channel_id=1, source_target_pairs={{0,5},{1,4},{4,1},{5,0},{2,7},{3,6},{6,3},{7,2},{8,13},{9,12},{12,... | collective-permute-start | bytes 24584 | tf_op jit(solution)/shard_map/ppermute | solution.py:654
  345.9 35.9 %collective-permute-start.28 = (bf16[1024,384]{1,0:T(8,128)(2,1)}, bf16[1024,384]{1,0:T(8,128)(2,1)S(1)}, u32[]{:S(2)}, u32[]{:S(2)}) collective-permute-start(bf16[1024,384]{1,0:T(8,128)(2,1)} %get-tuple-element.269), channel_id=1, source_target_pairs={{0,1},{1,0},{2,3},{3,2},{4,5},{5,4},{6,7},{7,6},{8,9},{9,8},{10,11... | collective-permute-start | bytes 2359304 | tf_op jit(solution)/shard_map/ppermute | solution.py:20
  346.5 35.2 %collective-permute-start.29 = (bf16[1024,384]{1,0:T(8,128)(2,1)}, bf16[1024,384]{1,0:T(8,128)(2,1)S(1)}, u32[]{:S(2)}, u32[]{:S(2)}) collective-permute-start(bf16[1024,384]{1,0:T(8,128)(2,1)} %get-tuple-element.270), channel_id=1, source_target_pairs={{0,4},{4,0},{1,5},{5,1},{2,6},{6,2},{3,7},{7,3},{8,12},{12,8},{9,1... | collective-permute-start | bytes 2359304 | tf_op jit(solution)/shard_map/ppermute | solution.py:20
  347.1 34.7 %collective-permute-start.30 = (bf16[1024,384]{1,0:T(8,128)(2,1)}, bf16[1024,384]{1,0:T(8,128)(2,1)S(1)}, u32[]{:S(2)}, u32[]{:S(2)}) collective-permute-start(bf16[1024,384]{1,0:T(8,128)(2,1)} %get-tuple-element.271), channel_id=1, source_target_pairs={{0,5},{1,4},{4,1},{5,0},{2,7},{3,6},{6,3},{7,2},{8,13},{9,12},{12,... | collective-permute-start | bytes 2359304 | tf_op jit(solution)/shard_map/ppermute | solution.py:866
  349.5 32.3 %collective-permute-start.31 = (f32[128]{0:T(128)S(1)}, f32[128]{0:T(128)S(1)}, u32[]{:S(2)}, u32[]{:S(2)}) collective-permute-start(f32[128]{0:T(128)S(1)} %fusion.9), channel_id=1, source_target_pairs={{0,4},{4,0},{1,5},{5,1},{2,6},{6,2},{3,7},{7,3},{8,12},{12,8},{9,1... | collective-permute-start | bytes 1544 | tf_op jit(solution)/shard_map/ppermute | solution.py:20
  387.1 6.7 %collective-permute-start.32 = (bf16[4,128,384]{2,1,0:T(8,128)(2,1)}, bf16[4,128,384]{2,1,0:T(8,128)(2,1)S(1)}, u32[]{:S(2)}, u32[]{:S(2)}) collective-permute-start(bf16[4,128,384]{2,1,0:T(8,128)(2,1)} %get-tuple-element.284), channel_id=1, source_target_pairs={{0,2},{2,0},{1,3},{3,1},{4,6},{6,4},{5,7},{7,5},{8,10},{10,8},{9,1... | collective-permute-start | bytes 1179656 | tf_op jit(solution)/shard_map/ppermute | solution.py:20
  387.8 5.5 %collective-permute-start.39 = (f32[128]{0:T(128)S(1)}, f32[128]{0:T(128)S(1)}, u32[]{:S(2)}, u32[]{:S(2)}) collective-permute-start(f32[128]{0:T(128)S(1)} %fusion.8), channel_id=1, source_target_pairs={{0,1},{1,0},{2,3},{3,2},{4,5},{5,4},{6,7},{7,6},{8,9},{9,8},{10,11... | collective-permute-start | bytes 1544 | tf_op jit(solution)/shard_map/ppermute | solution.py:20
  389.2 9.4 %collective-permute-start.36 = (bf16[128,1024]{1,0:T(8,128)(2,1)}, bf16[128,1024]{1,0:T(8,128)(2,1)S(1)}, u32[]{:S(2)}, u32[]{:S(2)}) collective-permute-start(bf16[128,1024]{1,0:T(8,128)(2,1)} %get-tuple-element.289), channel_id=1, source_target_pairs={{0,1},{1,0},{2,3},{3,2},{4,5},{5,4},{6,7},{7,6},{8,9},{9,8},{10,11... | collective-permute-start | bytes 786440 | tf_op jit(solution)/shard_map/ppermute | solution.py:20
  389.8 14.0 %collective-permute-start.37 = (bf16[128,1024]{1,0:T(8,128)(2,1)}, bf16[128,1024]{1,0:T(8,128)(2,1)S(1)}, u32[]{:S(2)}, u32[]{:S(2)}) collective-permute-start(bf16[128,1024]{1,0:T(8,128)(2,1)} %get-tuple-element.290), channel_id=1, source_target_pairs={{0,4},{4,0},{1,5},{5,1},{2,6},{6,2},{3,7},{7,3},{8,12},{12,8},{9,1... | collective-permute-start | bytes 786440 | tf_op jit(solution)/shard_map/ppermute | solution.py:20
  390.4 13.4 %collective-permute-start.38 = (bf16[128,1024]{1,0:T(8,128)(2,1)}, bf16[128,1024]{1,0:T(8,128)(2,1)}, u32[]{:S(2)}, u32[]{:S(2)}) collective-permute-start(bf16[128,1024]{1,0:T(8,128)(2,1)} %get-tuple-element.291), channel_id=1, source_target_pairs={{0,5},{1,4},{4,1},{5,0},{2,7},{3,6},{6,3},{7,2},{8,13},{9,12},{12,... | collective-permute-start | bytes 786440 | tf_op jit(solution)/shard_map/ppermute | solution.py:901
  394.5 21.1 %collective-permute-start.33 = (bf16[2,128,384]{2,1,0:T(8,128)(2,1)}, bf16[2,128,384]{2,1,0:T(8,128)(2,1)S(1)}, u32[]{:S(2)}, u32[]{:S(2)}) collective-permute-start(bf16[2,128,384]{2,1,0:T(8,128)(2,1)} %get-tuple-element.312), channel_id=1, source_target_pairs={{0,8},{8,0},{16,24},{24,16},{1,9},{9,1},{17,25},{25,17},{2,10},{10... | collective-permute-start | bytes 589832 | tf_op jit(solution)/shard_map/ppermute | solution.py:882
  396.2 19.4 %collective-permute-start.34 = (bf16[2,128,384]{2,1,0:T(8,128)(2,1)}, bf16[2,128,384]{2,1,0:T(8,128)(2,1)}, u32[]{:S(2)}, u32[]{:S(2)}) collective-permute-start(bf16[2,128,384]{2,1,0:T(8,128)(2,1)} %get-tuple-element.311), channel_id=1, source_target_pairs={{0,16},{8,24},{16,0},{24,8},{1,17},{9,25},{17,1},{25,9},{2,18},{10... | collective-permute-start | bytes 589832 | tf_op jit(solution)/shard_map/ppermute | solution.py:882
  398.6 17.0 %collective-permute-start.35 = (bf16[2,128,384]{2,1,0:T(8,128)(2,1)}, bf16[2,128,384]{2,1,0:T(8,128)(2,1)}, u32[]{:S(2)}, u32[]{:S(2)}) collective-permute-start(bf16[2,128,384]{2,1,0:T(8,128)(2,1)} %get-tuple-element.310), channel_id=1, source_target_pairs={{0,24},{8,16},{16,8},{24,0},{1,25},{9,17},{17,9},{25,1},{2,26},{10... | collective-permute-start | bytes 589832 | tf_op jit(solution)/shard_map/ppermute | solution.py:882
  404.9 15.5 %collective-permute-start.42 = (bf16[128,1024]{1,0:T(8,128)(2,1)S(1)}, bf16[128,1024]{1,0:T(8,128)(2,1)S(1)}, u32[]{:S(2)}, u32[]{:S(2)}) collective-permute-start(bf16[128,1024]{1,0:T(8,128)(2,1)S(1)} %add_convert_fusion), channel_id=1, source_target_pairs={{0,1},{1,0},{2,3},{3,2},{4,5},{5,4},{6,7},{7,6},{8,9},{9,8},{10,11... | collective-permute-start | bytes 786440 | tf_op jit(solution)/shard_map/ppermute | solution.py:20
  419.1 17.2 %collective-permute-start.41 = (bf16[8,128,384]{2,1,0:T(8,128)(2,1)S(1)}, bf16[8,128,384]{2,1,0:T(8,128)(2,1)S(1)}, u32[]{:S(2)}, u32[]{:S(2)}) collective-permute-start(bf16[8,128,384]{2,1,0:T(8,128)(2,1)S(1)} %pad_maximum_fusion.5.refs_1_), channel_id=1, source_target_pairs={{0,1},{1,0},{2,3},{3,2},{4,5},{5,4},{6,7},{7,6},{8,9},{9,8},{10,11... | collective-permute-start | bytes 2359304 | tf_op jit(solution)/shard_map/ppermute | solution.py:20
  (44 other events, 242.9 us)
Sparse Core Ops, SparseCore 0:
  38.8 46.2 all-gather.3
  110.9 49.1 reduce-scatter.3
  166.4 31.2 all-gather.5
  217.9 50.7 reduce-scatter.5
  279.9 30.2 all-gather.7
  340.9 52.6 reduce-scatter.7

commit v6 on v5

--- a/solution.py
+++ b/solution.py
@@ -173,9 +173,9 @@
                 mine[k][1] = jnp.zeros(theirs.shape[1:], BF)
 
 
-def mixer_grads_kernel(
-    at_ref, mine, theirs, w_in, w_forget, w_gate, grad_in, grad_forget, grad_gate, along_ref
-):
+def mixer_grads_kernel(at_ref, *refs):
+    mine, theirs, refs = refs[:Z], refs[Z : 2 * Z], refs[2 * Z :]
+    w_in, w_forget, w_gate, grad_in, grad_forget, grad_gate, along_ref = refs
     x, z, c = at_ref[0], at_ref[1], at_ref[2]
     total = jnp.zeros((w_in.shape[0], 1), F32)
     for m, (w_ref, g_ref) in enumerate(((w_in, grad_in), (w_forget, grad_forget), (w_gate, grad_gate))):
@@ -189,8 +189,8 @@
                     at = j % 3 * LANES
                     piece = jnp.where(
                         x == j // 3,
-                        mine[k * 2 + other, :, at : at + LANES],
-                        theirs[k * 2 + other, :, at : at + LANES],
+                        mine[k][other, :, at : at + LANES],
+                        theirs[k][other, :, at : at + LANES],
                     ).astype(F32)
                     g_ref[:, to] = piece
                     weight = w_ref[:, to].astype(F32)
@@ -523,9 +523,8 @@
     edges, firsts = refs[:parties], refs[parties : 2 * parties]
     refs = refs[2 * parties :]
     local, after, states, entry_own, raw, keep_mask, bound, d_gate_raw = refs[:8]
-    weights = refs[8 : 8 + parts * parts]
-    refs = refs[8 + parts * parts :]
-    d_parts, (d_bound, partial, passed, last, entry, d_raw) = refs[:parts], refs[parts:]
+    refs = refs[8:]
+    d_parts, (d_bound, passed, last, entry, d_raw) = refs[:parts], refs[parts:]
     group, feats = raw.shape[0], bound.shape[1]
     rows = group // CHUNKS
     collect(edges, (0, 2), passed)
@@ -556,10 +555,13 @@
     d_raw[:, 2 * feats :] = d_gate_raw[...]
     for k, d_part in enumerate(d_parts):
         d_part[...] = d_raw[:, columns_of(x_ref, parts, k, 3 * feats // parts)]
-    copies.flush(*range(parts + 1))
-    copies.wait(*range(2 * parties + 8, 2 * parties + 8 + parts * parts))
-    deep = partial.shape[1] // parts
+
+
+def d_normed_kernel(parts, copies, *refs):
+    d_parts, weights, partial = refs[:parts], refs[parts:-1], refs[-1]
+    group, deep = partial.shape[0], partial.shape[1] // parts
     for d in range(parts):
+        copies.wait(*range(parts + d * parts, parts + (d + 1) * parts))
         for i in range(2):
             at = slice(i * group // 2, (i + 1) * group // 2)
             total = None
@@ -813,11 +815,12 @@
         gate_up = first_sums(first_swaps(gate_up))
         down = first_swaps(down)
         summed, *gate_up = lax.optimization_barrier((summed, *gate_up))
-        summed, *down = lax.optimization_barrier((summed, *down))
     d_resid, piece, result_y = call(
         d_resid_kernel, [((rows, width), F32), ((rows, width + LANES), BF), ((rows, width), BF)],
         summed, resid, tokens_y, grad_y, mlp_g, scale,
     )
+    if pair:
+        piece, *down = lax.optimization_barrier((piece, *down))
     d_mixed = gather_rows(piece)
     if pair:
         gate_up = last_swaps(gate_up)
@@ -832,66 +835,13 @@
         scratch=[pltpu.VMEM((group, feats), F32), pltpu.VMEM(*featured)], late=2,
     )
     firsts = parties(first)
-    if pair:
-        glu_grad = last_sums(*after((*gate_up, *down), first))
-    else:
-        glu_grad = jnp.concatenate([total_blocks(gate_up), total_blocks(down)], axis=1)
-    raw = after(raw, glu_grad)
-    glu_grad = spread(glu_grad)
-    *d_raw, part_bound, partial = call(
-        functools.partial(d_mixer_kernel, crowd, parts, count),
-        [((group, 3 * feats // parts), BF)] * parts
-        + [((1, feats), F32), ((group, width), BF)],
-        near_x, order, *edges, *firsts, adjoint, passed, states, entry, raw, keep, bound, d_gate_raw, *mixer,
-        smem=2, scratch=carries + [pltpu.VMEM((group, 3 * feats), BF)], late=2 * crowd,
-    )
-
-    (token_grad_y,) = call(
-        token_grad_kernel, [((rows, width), F32)],
-        scatter_rows(partial), tokens_y, d_resid, attn_g,
-    )
-    result, token_grad = z_first(result_y, token_grad_y)
-
-    pieces = call(
-        functools.partial(mixer_weights_kernel, parts),
-        [((width // parts, 3 * feats // parts), BF)] * parts**2,
-        normed, *d_raw,
-    )
-    part_bound = part_bound.reshape(feats)
-    if pair:
-        pieces = [
-            pieces[0],
-            swap(pieces[1], "x"),
-            swap(pieces[2], "y"),
-            lax.ppermute(pieces[3], ("y", "x"), [(i, 3 - i) for i in range(4)]),
-        ]
-        top, bottom = jnp.split(part_bound, 2)
-        d_bound = jnp.where(y == 0, top, bottom) + swap(jnp.where(y == 0, bottom, top), "y")
+    grad_out = mixed_in
+    if pair:
         out_pieces = call(
             out_weights_kernel, [((sub, width // 2), BF)] * 4,
-            near_y, near_x, after(mixed_in, *d_raw), d_mixed, smem=2, scratch=[pltpu.VMEM((sub, width), F32)],
+            near_y, near_x, mixed_in, d_mixed, smem=2, scratch=[pltpu.VMEM((sub, width), F32)],
         )
-        pieces = after(pieces, *out_pieces, d_bound)
-        shape = (2, sub, 3 * feats // 2)
-        theirs, *mine = call(
-            mixer_sums_kernel, [((Z, *shape[1:]), BF)] + [(shape, BF)] * Z, z_c, *pieces, smem=1
-        )
-        out_pieces = after(out_pieces, theirs)
-        got = swap(theirs, "c")
-        mine = [v.at[1].set(got[k]) for k, v in enumerate(mine)]
-        mixer_grad = [mine[0]] + [lax.ppermute(mine[k], "z", [(i, i ^ k) for i in range(Z)]) for k in range(1, Z)]
-        mixer_grad = jnp.concatenate(mixer_grad, axis=0)
-    else:
-        d_bound = lax.psum_scatter(part_bound, "y", scatter_dimension=0, tiled=True)
-        mixer_grad = lax.psum_scatter(pieces[0], "y", scatter_dimension=0, tiled=True)
-        mixer_grad = both(mixer_grad, mixer_grad, "x").astype(BF)
-        mixer_grad = spread(mixer_grad.reshape(CHUNKS, sub, 3 * feats))
-    d_bound = d_bound + swap(d_bound, "x")
-    row_ids = jnp.arange(bound_table.shape[0])[:, None]
-    member = jnp.logical_and(row_ids >= 1, row_ids <= LAYER).astype(F32)
-    grad_table = soft * (member - own_bound[None, :]) * d_bound[None, :]
-
-    if pair:
+        out_pieces = after(out_pieces, *firsts)
         grad_out = sum(
             p.astype(F32)
             for p in (
@@ -901,6 +851,60 @@
                 lax.ppermute(out_pieces[3], ("y", "x"), [(i, 3 - i) for i in range(4)]),
             )
         ).astype(BF)
+    if pair:
+        glu_grad = last_sums(*after((*gate_up, *down), first))
+    else:
+        glu_grad = jnp.concatenate([total_blocks(gate_up), total_blocks(down)], axis=1)
+    raw = after(raw, glu_grad)
+    glu_grad = spread(glu_grad)
+    *d_raw, part_bound = call(
+        functools.partial(d_mixer_kernel, crowd, parts, count),
+        [((group, 3 * feats // parts), BF)] * parts
+        + [((1, feats), F32)],
+        near_x, order, *edges, *firsts, adjoint, passed, states, entry, raw, keep, bound, d_gate_raw,
+        smem=2, scratch=carries + [pltpu.VMEM((group, 3 * feats), BF)], late=2 * crowd,
+    )
+
+    pieces = call(
+        functools.partial(mixer_weights_kernel, parts),
+        [((width // parts, 3 * feats // parts), BF)] * parts**2,
+        normed, *d_raw,
+    )
+    (partial,) = call(
+        functools.partial(d_normed_kernel, parts), [((group, width), BF)],
+        *after(d_raw, grad_out, *pieces), *mixer, late=parts,
+    )
+    (token_grad_y,) = call(
+        token_grad_kernel, [((rows, width), F32)],
+        scatter_rows(partial), tokens_y, d_resid, attn_g,
+    )
+    result, token_grad = z_first(result_y, token_grad_y)
+
+    part_bound = part_bound.reshape(feats)
+    if pair:
+        pieces = [
+            pieces[0],
+            swap(pieces[1], "x"),
+            swap(pieces[2], "y"),
+            lax.ppermute(pieces[3], ("y", "x"), [(i, 3 - i) for i in range(4)]),
+        ]
+        top, bottom = jnp.split(part_bound, 2)
+        d_bound = jnp.where(y == 0, top, bottom) + swap(jnp.where(y == 0, bottom, top), "y")
+        pieces = after(pieces, d_bound)
+        shape = (2, sub, 3 * feats // 2)
+        theirs, *mine = call(
+            mixer_sums_kernel, [((Z, *shape[1:]), BF)] + [(shape, BF)] * Z, z_c, *pieces, smem=1
+        )
+        got = swap(theirs, "c")
+        d_bound = after(d_bound, got)
+        mine = [v.at[1].set(got[k]) for k, v in enumerate(mine)]
+        mixer_grad = [mine[0]] + [lax.ppermute(mine[k], "z", [(i, i ^ k) for i in range(Z)]) for k in range(1, Z)]
+    else:
+        d_bound = lax.psum_scatter(part_bound, "y", scatter_dimension=0, tiled=True)
+        mixer_grad = lax.psum_scatter(pieces[0], "y", scatter_dimension=0, tiled=True)
+        mixer_grad = both(mixer_grad, mixer_grad, "x").astype(BF)
+        mixer_grad = spread(mixer_grad.reshape(CHUNKS, sub, 3 * feats))
+    if pair:
         grad_gate_ff, grad_up_ff, grad_down, along_ff = call(
             glu_grads_kernel,
             [((sub, CHUNKS * block), F32)] * 2 + [((CHUNKS * block, sub), F32), ((sub, LANES), F32)],
@@ -908,8 +912,9 @@
         )
         grad_mlp = along_ff[:, 0]
         grad_mlp = grad_mlp + swap(grad_mlp, "x")
-        mixer_grad = after(mixer_grad, grad_out, d_bound, grad_mlp)
-        mixer_grad = [mixer_grad, swap(mixer_grad, "x")]
+        d_bound = d_bound + swap(d_bound, "x")
+        mixer_grad[-1] = after(mixer_grad[-1], grad_out, d_bound, grad_mlp)
+        mixer_grad = mixer_grad + [swap(v, "x") for v in mixer_grad]
         other = swap(grad_out, "x")
         grad_out = jnp.concatenate(
             [jnp.where(x == 0, grad_out, other), jnp.where(x == 0, other, grad_out)], axis=1
@@ -918,6 +923,10 @@
         (grad_out,) = z_first(contract_rows(mixed_in, d_mixed[:, :width]).astype(BF))
         grad_out = lax.psum_scatter(grad_out, "y", scatter_dimension=0, tiled=True)
         grad_out = both(grad_out, grad_out, "x")
+        d_bound = d_bound + swap(d_bound, "x")
+    row_ids = jnp.arange(bound_table.shape[0])[:, None]
+    member = jnp.logical_and(row_ids >= 1, row_ids <= LAYER).astype(F32)
+    grad_table = soft * (member - own_bound[None, :]) * d_bound[None, :]
 
     def along(weight, grad):
         return jnp.sum(weight.astype(F32) * grad, axis=1)

time: 457 us -> 451 us (0.987)
    ppermute x35 -> x38, starting transfers between devices: 36.1 us -> 42.9 us  [swap(): return lax.ppermute(value, axis, [(0, 1), (1, 0)])]
    ppermute x35 -> x38, waiting for transfers between devices: 125 us -> 119 us  [swap(): return lax.ppermute(value, axis, [(0, 1), (1, 0)])]
    pallas_call x24 -> x25, Pallas kernels: 120 us -> 122 us  [call(): pl.pallas_call(body, out_shape=shapes, in_specs=[pl.BlockSpec(memory_spac...]
  transfers between devices with their start and end apart: 53 -> 56, of which waited for: 29 -> 31; matrix products, arithmetic and copies ran while one was open for 8% -> 8% of each run, Pallas kernels for 17% -> 20%
where the time goes in v6:
time: 451 us; the launch traced here: 445 us
  waiting for transfers between devices  200 us (44%)
  Pallas kernels  122 us (27%)
  starting transfers between devices  70.4 us (16%)
  local copies, waits for them, and re-layouts  20.9 us (5%)
  other arithmetic  16.8 us (4%)
  between operations  15.4 us (3%)
    pallas_call x25, Pallas kernels, call(): pl.pallas_call(body, out_shape=shapes, in_specs=[pl.BlockSpec(memory_spac...  122 us
    ppermute x38, waiting for transfers between devices, swap(): return lax.ppermute(value, axis, [(0, 1), (1, 0)])  119 us
    all_gather x3, waiting for transfers between devices, gather_rows(): return lax.all_gather(own, ('z', 'c'), axis=0, tiled=True)  46.7 us
    ppermute x38, starting transfers between devices, swap(): return lax.ppermute(value, axis, [(0, 1), (1, 0)])  42.9 us
    all_to_all x1, waiting for transfers between devices, per_device(): lax.all_to_all(jnp.broadcast_to(after(grad_y, glu)[None], (Z, rows, width...  13.4 us
    all_to_all x3, starting transfers between devices, spread(): return lax.all_to_all(value, ('z', 'c'), 0, 0, tiled=True)  12.3 us
    all_to_all x3, waiting for transfers between devices, spread(): return lax.all_to_all(value, ('z', 'c'), 0, 0, tiled=True)  11.7 us
  transfers between devices with their start and end apart: 56, of which 31 were waited for; matrix products, arithmetic and copies ran while one was open for 8% of the time, Pallas kernels for 20%

profile of v6, /device:TPU:0, one launch (start us, length us, event | category | flops | bytes accessed | tf_op | source)
XLA Modules:
  0.0 445.0 jit_solution(15870268348220310979)
XLA Ops:
  7.2 3.0 collective-permute-start.1
  10.2 2.5 shard_map.238
  12.8 4.9 %all-to-all-start = ((bf16[8,128,384]{2,1,0:T(8,128)(2,1)}), bf16[8,128,384]{2,1,0:T(8,128)(2,1)S(1)}, u32[]{:S(2)}, u32[]{:S(2)}) async-start(bf16[8,128,384]{2,1,0:T(8,128)(2,1)} %shard_map.238), calls=%async_computation | async-start | bytes 1572864 | tf_op jit(solution)/shard_map/all_to_all | solution.py:647
  18.4 4.0 shard_map.239
  25.9 2.4 shard_map.240.refs_9_.refs_1_
  28.3 10.4 %all-to-all-done = bf16[8,128,384]{2,1,0:T(8,128)(2,1)S(1)} async-done(((bf16[8,128,384]{2,1,0:T(8,128)(2,1)}), bf16[8,128,384]{2,1,0:T(8,128)(2,1)S(1)}, u32[]{:S(2)}, u32[]{:S(2)}) %all-to-all-start) | async-done | bytes 786464 | tf_op jit(solution)/shard_map/all_to_all | solution.py:647
  38.7 3.7 all-to-all-start.1
  47.9 37.2 %all-gather.4.cloned.1.call-done.refs_2_ = bf16[512,2176]{1,0:T(8,128)(2,1)} async-done(((bf16[64,2176]{1,0:T(8,128)(2,1)}), bf16[512,2176]{1,0:T(8,128)(2,1)}) %all-gather.4.cloned.1.call-update) | async-done | bytes 2228240 | tf_op jit(solution)/shard_map/all_gather | solution.py:590
  86.4 9.4 %shard_map.241 = (bf16[512,2048]{1,0:T(8,128)(2,1)}, f32[512,768]{1,0:T(8,128)}, f32[2,512,128]{2,1,0:T(8,128)}, f32[2,512,128]{2,1,0:T(8,128)}, f32[2,512,128]{2,1,0:T(8,128)}, /*index=5*/f32[16,256]{1,0:T(8,128)}) custom-call(s32[1]{0:T(128)} %bitcast.2.refs_0_.refs_1_, f32[1,2048]{1,0:T(1,128)} %pad_maximum_fusion.5.refs_1_.refs_3_, ...), custom_call_target="tpu_custom_call" | custom-call | bytes 1024 | tf_op jit(solution)/shard_map/pallas_call | solution.py:87
  101.3 2.6 collective-permute-done.7.refs_4_.refs_5_
  104.5 4.9 %shard_map.242 = (f32[2,512,128]{2,1,0:T(8,128)}, f32[8,256]{1,0:T(8,128)}, bf16[512,2176]{1,0:T(8,128)(2,1)}) custom-call(s32[34]{0:T(128)} %pad_add_fusion.refs_0_.refs_1_, f32[16,256]{1,0:T(8,128)} %get-tuple-element.184.refs_1_.refs_2_, f32[16,256]{1,0:T(8,128)} %copy-done.24, f32[16,256]{1,0:T(8,128)} %copy-done.25, f32[16,256]{1,0:T(8,128)} %copy-done.26, ...), custom_call_target="tpu_custom_call" | custom-call | bytes 1024 | tf_op jit(solution)/shard_map/pallas_call | solution.py:87
  115.8 2.0 broadcast_in_dim.22
  117.9 5.4 %all-to-all-start.2 = ((bf16[4,64,2048]{2,1,0:T(8,128)(2,1)}), bf16[4,64,2048]{2,1,0:T(8,128)(2,1)S(1)}, u32[]{:S(2)}, u32[]{:S(2)}) async-start(bf16[4,64,2048]{2,1,0:T(8,128)(2,1)} %broadcast_in_dim.22), calls=%async_computation.3 | async-start | bytes 2097152 | tf_op jit(solution)/shard_map/all_to_all | solution.py:760
  124.2 21.2 %collective-permute-done.8 = bf16[8,704,128]{2,1,0:T(8,128)(2,1)} collective-permute-done((bf16[8,704,128]{2,1,0:T(8,128)(2,1)}, bf16[8,704,128]{2,1,0:T(8,128)(2,1)}, u32[]{:S(2)}, u32[]{:S(2)}) %collective-permute-start.8) | collective-permute-done | bytes 1441824 | tf_op jit(solution)/shard_map/ppermute | solution.py:20
  148.2 13.4 %all-to-all-done.2 = bf16[4,64,2048]{2,1,0:T(8,128)(2,1)S(1)} async-done(((bf16[4,64,2048]{2,1,0:T(8,128)(2,1)}), bf16[4,64,2048]{2,1,0:T(8,128)(2,1)S(1)}, u32[]{:S(2)}, u32[]{:S(2)}) %all-to-all-start.2) | async-done | bytes 1048608 | tf_op jit(solution)/shard_map/all_to_all | solution.py:760
  163.5 2.7 shard_map.244
  178.9 2.2 collective-permute-start.12
  182.2 5.3 %collective-permute-done.13 = bf16[8,352,128]{2,1,0:T(8,128)(2,1)S(1)} collective-permute-done((bf16[8,352,128]{2,1,0:T(8,128)(2,1)S(1)}, bf16[8,352,128]{2,1,0:T(8,128)(2,1)S(1)}, u32[]{:S(2)}, u32[]{:S(2)}) %collective-permute-start.13) | collective-permute-done | bytes 720928 | tf_op jit(solution)/shard_map/ppermute | solution.py:20
  198.0 19.7 %shard_map.245 = (bf16[512,352]{1,0:T(8,128)(2,1)}, bf16[512,352]{1,0:T(8,128)(2,1)}, bf16[512,352]{1,0:T(8,128)(2,1)}, bf16[512,352]{1,0:T(8,128)(2,1)}, bf16[5...) custom-call(bf16[512,2048]{1,0:T(8,128)(2,1)} %all-gather.6.cloned.1.call-done.refs_0_.refs_4_, ...), custom_call_target="tpu_custom_call" | custom-call | bytes 1024 | tf_op jit(solution)/shard_map/pallas_call | solution.py:87
  217.8 6.7 %shard_map.246 = (bf16[2,352,1024]{2,1,0:T(8,128)(2,1)}, bf16[2,352,1024]{2,1,0:T(8,128)(2,1)}, bf16[2,352,1024]{2,1,0:T(8,128)(2,1)}, bf16[2,352,1024]{2,1,0:T(8,128)(2,1)}) custom-call(bf16[512,352]{1,0:T(8,128)(2,1)} %get-tuple-element.200.refs_0_, bf16[512,352]{1,0:T(8,128)(2,1)} %get-tuple-element.201.refs_1_, ...), custom_call_target="tpu_custom_call" | custom-call | bytes 1024 | tf_op jit(solution)/shard_map/pallas_call | solution.py:87
  224.5 2.2 collective-permute-start.17
  228.3 4.9 %shard_map.249 = (bf16[2,176,1024]{2,1,0:T(8,128)(2,1)}, bf16[2,176,1024]{2,1,0:T(8,128)(2,1)}, bf16[2,176,1024]{2,1,0:T(8,128)(2,1)}, bf16[2,176,1024]{2,1,0:T(8,128)(2,1)}) custom-call(bf16[512,352]{1,0:T(8,128)(2,1)} %get-tuple-element.217.refs_0_, bf16[512,352]{1,0:T(8,128)(2,1)} %get-tuple-element.218.refs_1_, bf16[512,2048]{1,0:T(8,128)(2,1)} %bitcast.85), custom_call_target="tpu_custom_call" | custom-call | bytes 1024 | tf_op jit(solution)/shard_map/pallas_call | solution.py:87
  233.7 25.5 %collective-permute-done.17.refs_1_ = bf16[2,352,1024]{2,1,0:T(8,128)(2,1)S(1)} collective-permute-done((bf16[2,352,1024]{2,1,0:T(8,128)(2,1)}, bf16[2,352,1024]{2,1,0:T(8,128)(2,1)S(1)}, u32[]{:S(2)}, u32[]{:S(2)}) %collective-permute-start.17) | collective-permute-done | bytes 1441824 | tf_op jit(solution)/shard_map/ppermute | solution.py:20
  259.3 2.0 collective-permute-done.18.refs_3_
  262.5 5.0 %shard_map.247 = (f32[352,1024]{1,0:T(8,128)}, bf16[352,1024]{1,0:T(8,128)(2,1)}, f32[352,1024]{1,0:T(8,128)}, bf16[352,1024]{1,0:T(8,128)(2,1)}) custom-call(bf16[2,352,1024]{2,1,0:T(8,128)(2,1)} %get-tuple-element.204.refs_0_, bf16[2,352,1024]{2,1,0:T(8,128)(2,1)} %copy-done.4, bf16[2,352,1024]{2,1,0:T(8,128)(2,1)} %get-tuple-element.206.refs_2_, ...), custom_call_target="tpu_custom_call" | custom-call | bytes 1024 | tf_op jit(solution)/shard_map/pallas_call | solution.py:87
  268.6 3.7 shard_map.248
  272.3 2.4 collective-permute-done.19.refs_1_
  278.0 3.2 shard_map.250
  283.2 11.9 %collective-permute-done.21.refs_1_ = bf16[352,1024]{1,0:T(8,128)(2,1)S(1)} collective-permute-done((bf16[352,1024]{1,0:T(8,128)(2,1)}, bf16[352,1024]{1,0:T(8,128)(2,1)S(1)}, u32[]{:S(2)}, u32[]{:S(2)}) %collective-permute-start.21) | collective-permute-done | bytes 720928 | tf_op jit(solution)/shard_map/ppermute | solution.py:20
  296.7 9.6 %all-gather.8.cloned.1.call-done.refs_0_.refs_3_ = bf16[512,2176]{1,0:T(8,128)(2,1)} async-done(((bf16[64,2176]{1,0:T(8,128)(2,1)}), bf16[512,2176]{1,0:T(8,128)(2,1)}) %all-gather.8.cloned.1.call-update) | async-done | bytes 2228240 | tf_op jit(solution)/shard_map/all_gather | solution.py:590
  306.2 6.0 %shard_map.251 = (bf16[512,256]{1,0:T(8,128)(2,1)}, bf16[512,256]{1,0:T(8,128)(2,1)}, f32[2,512,128]{2,1,0:T(8,128)}, f32[2,512,128]{2,1,0:T(8,128)}, f32[8,256]{1,0:T(8,128)}) custom-call(bf16[512,2176]{1,0:T(8,128)(2,1)} %all-gather.8.cloned.1.call-done.refs_0_.refs_3_, bf16[256,2048]{1,0:T(8,128)(2,1)} %shard_map.240.refs_9_.refs_1_, ...), custom_call_target="tpu_custom_call" | custom-call | bytes 1024 | tf_op jit(solution)/shard_map/pallas_call | solution.py:87
  315.8 3.4 shard_map.254
  323.5 4.7 %shard_map.252 = bf16[8,1056,128]{2,1,0:T(8,128)(2,1)} custom-call(f32[352,1024]{1,0:T(8,128)} %get-tuple-element.252.refs_0_, bf16[352,1024]{1,0:T(8,128)(2,1)} %copy-done.7, f32[352,1024]{1,0:T(8,128)} %get-tuple-element.254.refs_2_, bf16[352,1024]{1,0:T(8,128)(2,1)} %copy-done.8, f32[176,1024]{1,0:T(8,128)} %get-tuple-element.256.refs_4_, ...), custom_call_target="tpu_custom_call" | custom-call | bytes 1024 | tf_op jit(solution)/shard_map/pallas_call | solution.py:87
  328.3 3.6 all-to-all-start.3
  332.2 4.4 shard_map.253
  336.6 5.1 %shard_map.255 = (bf16[1024,384]{1,0:T(8,128)(2,1)}, bf16[1024,384]{1,0:T(8,128)(2,1)}, bf16[1024,384]{1,0:T(8,128)(2,1)}, bf16[1024,384]{1,0:T(8,128)(2,1)}) custom-call(bf16[512,2048]{1,0:T(8,128)(2,1)} %get-tuple-element.273.refs_0_, bf16[512,384]{1,0:T(8,128)(2,1)} %get-tuple-element.278.refs_1_.refs_0_, bf16[512,384]{1,0:T(8,128)(2,1)} %get-tuple-element.279.refs_2_.refs_1_), custom_call_target="tpu_custom_call" | custom-call | bytes 1024 | tf_op jit(solution)/shard_map/pallas_call | solution.py:87
  341.9 5.6 %shard_map.256 = bf16[512,2048]{1,0:T(8,128)(2,1)} custom-call(bf16[512,384]{1,0:T(8,128)(2,1)} %get-tuple-element.278.refs_1_.refs_0_, bf16[512,384]{1,0:T(8,128)(2,1)} %get-tuple-element.279.refs_2_.refs_1_, bf16[1024,384]{1,0:T(8,128)(2,1)} %bitcast.90, bf16[1024,384]{1,0:T(8,128)(2,1)} %collective-permute-done.2.refs_6_.refs_3_, ...), custom_call_target="tpu_custom_call" | custom-call | bytes 1024 | tf_op jit(solution)/shard_map/pallas_call | solution.py:87
  354.6 30.2 %collective-permute-done.34 = f32[128]{0:T(128)S(1)} collective-permute-done((f32[128]{0:T(128)S(1)}, f32[128]{0:T(128)S(1)}, u32[]{:S(2)}, u32[]{:S(2)}) %collective-permute-start.34) | collective-permute-done | bytes 544 | tf_op jit(solution)/shard_map/ppermute | solution.py:20
  385.7 3.8 shard_map.259
  393.4 2.4 collective-permute-start.37
  399.1 6.2 %shard_map.260 = (f32[128,2816]{1,0:T(8,128)}, f32[128,2816]{1,0:T(8,128)}, f32[2816,128]{1,0:T(8,128)}, f32[128,128]{1,0:T(8,128)}) custom-call(bf16[8,1056,128]{2,1,0:T(8,128)(2,1)} %copy-done, bf16[128,2816]{1,0:T(8,128)(2,1)} %refs_1_.9, bf16[128,2816]{1,0:T(8,128)(2,1)} %refs_2_.7), custom_call_target="tpu_custom_call" | custom-call | bytes 1024 | tf_op jit(solution)/shard_map/pallas_call | solution.py:87
  411.1 3.5 collective-permute-done.38.refs_4_
  416.7 2.6 collective-permute-done.42.refs_6_
  419.3 4.0 collective-permute-done.43.refs_7_
  423.3 2.1 collective-permute-done.44.refs_8_
  426.1 5.1 %shard_map.261 = (f32[128,2048]{1,0:T(8,128)}, f32[128,2048]{1,0:T(8,128)}, f32[128,2048]{1,0:T(8,128)}, f32[128,128]{1,0:T(8,128)}) custom-call(s32[3]{0:T(128)} %pad_add_fusion.1.refs_0_, bf16[2,128,384]{2,1,0:T(8,128)(2,1)} %copy-done.21, bf16[2,128,384]{2,1,0:T(8,128)(2,1)} %copy-done.14, bf16[2,128,384]{2,1,0:T(8,128)(2,1)} %copy-done.15, ...), custom_call_target="tpu_custom_call" | custom-call | bytes 1024 | tf_op jit(solution)/shard_map/pallas_call | solution.py:87
  432.7 2.9 shard_map.257.refs_2_
  435.6 2.1 shard_map.258
  (241 shorter events, 98.0 us)
Async XLA Ops:
  7.2 17.6 %collective-permute-start.1 = (bf16[128,2048]{1,0:T(8,128)(2,1)}, bf16[128,2048]{1,0:T(8,128)(2,1)S(1)}, u32[]{:S(2)}, u32[]{:S(2)}) collective-permute-start(bf16[128,2048]{1,0:T(8,128)(2,1)} %param.27), channel_id=1, source_target_pairs={{0,4},{4,0},{1,5},{5,1},{2,6},{6,2},{3,7},{7,3},{8,12},{12,8},{9,1... | collective-permute-start | bytes 1572872 | tf_op jit(solution)/shard_map/ppermute | solution.py:20
  12.8 25.9 %all-to-all-start = ((bf16[8,128,384]{2,1,0:T(8,128)(2,1)}), bf16[8,128,384]{2,1,0:T(8,128)(2,1)S(1)}, u32[]{:S(2)}, u32[]{:S(2)}) async-start(bf16[8,128,384]{2,1,0:T(8,128)(2,1)} %shard_map.238), calls=%async_computation | async-start | bytes 1572864 | tf_op jit(solution)/shard_map/all_to_all | solution.py:647
  17.6 67.4 %all-gather.4.cloned.1.call-start = ((), (), s32[]{:S(2)}) async-start(), calls=%async_computation.7 | async-start | bytes 2506752 | tf_op jit(solution)/shard_map/all_gather | solution.py:590
  38.7 72.1 %all-to-all-start.1 = ((bf16[8,1056,128]{2,1,0:T(8,128)(2,1)}), bf16[8,1056,128]{2,1,0:T(8,128)(2,1)S(1)}, u32[]{:S(2)}, u32[]{:S(2)}) async-start(bf16[8,1056,128]{2,1,0:T(8,128)(2,1)} %shard_map.239), calls=%async_computation.1 | async-start | bytes 4325376 | tf_op jit(solution)/shard_map/all_to_all | solution.py:647
  42.4 121.1 %reduce-scatter.4.cloned.1.call-start = ((), (), s32[]{:S(2)}) async-start(), calls=%async_computation.8 | async-start | bytes 2506752 | tf_op jit(solution)/shard_map/reduce_scatter | solution.py:594
  43.8 42.6 %collective-permute-start.2 = (bf16[1024,384]{1,0:T(8,128)(2,1)S(1)}, bf16[1024,384]{1,0:T(8,128)(2,1)}, u32[]{:S(2)}, u32[]{:S(2)}) collective-permute-start(bf16[1024,384]{1,0:T(8,128)(2,1)S(1)} %bitcast.86), channel_id=1, source_target_pairs={{0,1},{1,0},{2,3},{3,2},{4,5},{5,4},{6,7},{7,6},{8,9},{9,8},{10,11... | collective-permute-start | bytes 2359304 | tf_op jit(solution)/shard_map/ppermute | solution.py:20
  45.3 41.1 %collective-permute-start.3 = (bf16[1024,384]{1,0:T(8,128)(2,1)S(1)}, bf16[1024,384]{1,0:T(8,128)(2,1)}, u32[]{:S(2)}, u32[]{:S(2)}) collective-permute-start(bf16[1024,384]{1,0:T(8,128)(2,1)S(1)} %bitcast.87), channel_id=1, source_target_pairs={{0,4},{4,0},{1,5},{5,1},{2,6},{6,2},{3,7},{7,3},{8,12},{12,8},{9,1... | collective-permute-start | bytes 2359304 | tf_op jit(solution)/shard_map/ppermute | solution.py:20
  45.8 40.5 %collective-permute-start.4 = (bf16[1024,384]{1,0:T(8,128)(2,1)S(1)}, bf16[1024,384]{1,0:T(8,128)(2,1)}, u32[]{:S(2)}, u32[]{:S(2)}) collective-permute-start(bf16[1024,384]{1,0:T(8,128)(2,1)S(1)} %bitcast.88), channel_id=1, source_target_pairs={{0,5},{1,4},{4,1},{5,0},{2,7},{3,6},{6,3},{7,2},{8,13},{9,12},{12,... | collective-permute-start | bytes 2359304 | tf_op jit(solution)/shard_map/ppermute | solution.py:656
  111.9 33.4 %collective-permute-start.8 = (bf16[8,704,128]{2,1,0:T(8,128)(2,1)}, bf16[8,704,128]{2,1,0:T(8,128)(2,1)}, u32[]{:S(2)}, u32[]{:S(2)}) collective-permute-start(bf16[8,704,128]{2,1,0:T(8,128)(2,1)} %slice.180), channel_id=1, source_target_pairs={{0,1},{1,0},{2,3},{3,2},{4,5},{5,4},{6,7},{7,6},{8,9},{9,8},{10,11... | collective-permute-start | bytes 4325384 | tf_op jit(solution)/shard_map/ppermute | solution.py:20
  113.4 33.2 %collective-permute-start.9 = (bf16[8,704,128]{2,1,0:T(8,128)(2,1)}, bf16[8,704,128]{2,1,0:T(8,128)(2,1)}, u32[]{:S(2)}, u32[]{:S(2)}) collective-permute-start(bf16[8,704,128]{2,1,0:T(8,128)(2,1)} %slice.180), channel_id=1, source_target_pairs={{0,4},{4,0},{1,5},{5,1},{2,6},{6,2},{3,7},{7,3},{8,12},{12,8},{9,1... | collective-permute-start | bytes 4325384 | tf_op jit(solution)/shard_map/ppermute | solution.py:20
  117.9 43.8 %all-to-all-start.2 = ((bf16[4,64,2048]{2,1,0:T(8,128)(2,1)}), bf16[4,64,2048]{2,1,0:T(8,128)(2,1)S(1)}, u32[]{:S(2)}, u32[]{:S(2)}) async-start(bf16[4,64,2048]{2,1,0:T(8,128)(2,1)} %broadcast_in_dim.22), calls=%async_computation.3 | async-start | bytes 2097152 | tf_op jit(solution)/shard_map/all_to_all | solution.py:760
  123.3 74.7 %all-gather.6.cloned.1.call-start = ((), (), s32[]{:S(2)}) async-start(), calls=%async_computation.9 | async-start | bytes 2359296 | tf_op jit(solution)/shard_map/all_gather | solution.py:590
  146.6 16.7 %collective-permute-start.11 = (bf16[8,352,128]{2,1,0:T(8,128)(2,1)}, bf16[8,352,128]{2,1,0:T(8,128)(2,1)S(1)}, u32[]{:S(2)}, u32[]{:S(2)}) collective-permute-start(bf16[8,352,128]{2,1,0:T(8,128)(2,1)} %slice.181), channel_id=1, source_target_pairs={{0,4},{4,0},{1,5},{5,1},{2,6},{6,2},{3,7},{7,3},{8,12},{12,8},{9,1... | collective-permute-start | bytes 2162696 | tf_op jit(solution)/shard_map/ppermute | solution.py:20
  147.1 16.4 %collective-permute-start.10 = (bf16[8,352,128]{2,1,0:T(8,128)(2,1)}, bf16[8,352,128]{2,1,0:T(8,128)(2,1)S(1)}, u32[]{:S(2)}, u32[]{:S(2)}) collective-permute-start(bf16[8,352,128]{2,1,0:T(8,128)(2,1)} %slice.181), channel_id=1, source_target_pairs={{0,1},{1,0},{2,3},{3,2},{4,5},{5,4},{6,7},{7,6},{8,9},{9,8},{10,11... | collective-permute-start | bytes 2162696 | tf_op jit(solution)/shard_map/ppermute | solution.py:20
  166.2 102.3 %reduce-scatter.6.cloned.1.call-start = ((), (), s32[]{:S(2)}) async-start(), calls=%async_computation.10 | async-start | bytes 4718592 | tf_op jit(solution)/shard_map/reduce_scatter | solution.py:594
  169.2 18.3 %collective-permute-start.13 = (bf16[8,352,128]{2,1,0:T(8,128)(2,1)S(1)}, bf16[8,352,128]{2,1,0:T(8,128)(2,1)S(1)}, u32[]{:S(2)}, u32[]{:S(2)}) collective-permute-start(bf16[8,352,128]{2,1,0:T(8,128)(2,1)S(1)} %slice.184), channel_id=1, source_target_pairs={{0,1},{1,0},{2,3},{3,2},{4,5},{5,4},{6,7},{7,6},{8,9},{9,8},{10,11... | collective-permute-start | bytes 2162696 | tf_op jit(solution)/shard_map/ppermute | solution.py:20
  171.0 18.0 %collective-permute-start.14 = (bf16[8,352,128]{2,1,0:T(8,128)(2,1)S(1)}, bf16[8,352,128]{2,1,0:T(8,128)(2,1)S(1)}, u32[]{:S(2)}, u32[]{:S(2)}) collective-permute-start(bf16[8,352,128]{2,1,0:T(8,128)(2,1)S(1)} %slice.185), channel_id=1, source_target_pairs={{0,4},{4,0},{1,5},{5,1},{2,6},{6,2},{3,7},{7,3},{8,12},{12,8},{9,1... | collective-permute-start | bytes 2162696 | tf_op jit(solution)/shard_map/ppermute | solution.py:20
  178.9 13.6 %collective-permute-start.12 = (bf16[4,64,2048]{2,1,0:T(8,128)(2,1)S(1)}, bf16[4,64,2048]{2,1,0:T(8,128)(2,1)S(1)}, u32[]{:S(2)}, u32[]{:S(2)}) collective-permute-start(bf16[4,64,2048]{2,1,0:T(8,128)(2,1)S(1)} %all-to-all-done.2), channel_id=1, source_target_pairs={{0,2},{2,0},{1,3},{3,1},{4,6},{6,4},{5,7},{7,5},{8,10},{10,8},{9,1... | collective-permute-start | bytes 3145736 | tf_op jit(solution)/shard_map/ppermute | solution.py:20
  181.1 14.1 %collective-permute-start.15 = (bf16[8,176,128]{2,1,0:T(8,128)(2,1)S(1)}, bf16[8,176,128]{2,1,0:T(8,128)(2,1)S(1)}, u32[]{:S(2)}, u32[]{:S(2)}) collective-permute-start(bf16[8,176,128]{2,1,0:T(8,128)(2,1)S(1)} %slice.186), channel_id=1, source_target_pairs={{0,1},{1,0},{2,3},{3,2},{4,5},{5,4},{6,7},{7,6},{8,9},{9,8},{10,11... | collective-permute-start | bytes 1081352 | tf_op jit(solution)/shard_map/ppermute | solution.py:20
  181.6 15.2 %collective-permute-start.16 = (bf16[8,176,128]{2,1,0:T(8,128)(2,1)S(1)}, bf16[8,176,128]{2,1,0:T(8,128)(2,1)S(1)}, u32[]{:S(2)}, u32[]{:S(2)}) collective-permute-start(bf16[8,176,128]{2,1,0:T(8,128)(2,1)S(1)} %slice.187), channel_id=1, source_target_pairs={{0,4},{4,0},{1,5},{5,1},{2,6},{6,2},{3,7},{7,3},{8,12},{12,8},{9,1... | collective-permute-start | bytes 1081352 | tf_op jit(solution)/shard_map/ppermute | solution.py:20
  217.7 88.5 %all-gather.8.cloned.1.call-start = ((), (), s32[]{:S(2)}) async-start(), calls=%async_computation.11 | async-start | bytes 2506752 | tf_op jit(solution)/shard_map/all_gather | solution.py:590
  224.5 34.8 %collective-permute-start.17 = (bf16[2,352,1024]{2,1,0:T(8,128)(2,1)}, bf16[2,352,1024]{2,1,0:T(8,128)(2,1)S(1)}, u32[]{:S(2)}, u32[]{:S(2)}) collective-permute-start(bf16[2,352,1024]{2,1,0:T(8,128)(2,1)} %get-tuple-element.205), channel_id=1, source_target_pairs={{0,1},{1,0},{2,3},{3,2},{4,5},{5,4},{6,7},{7,6},{8,9},{9,8},{10,11... | collective-permute-start | bytes 4325384 | tf_op jit(solution)/shard_map/ppermute | solution.py:20
  226.6 34.7 %collective-permute-start.18 = (bf16[2,352,1024]{2,1,0:T(8,128)(2,1)}, bf16[2,352,1024]{2,1,0:T(8,128)(2,1)S(1)}, u32[]{:S(2)}, u32[]{:S(2)}) collective-permute-start(bf16[2,352,1024]{2,1,0:T(8,128)(2,1)} %get-tuple-element.207), channel_id=1, source_target_pairs={{0,4},{4,0},{1,5},{5,1},{2,6},{6,2},{3,7},{7,3},{8,12},{12,8},{9,1... | collective-permute-start | bytes 4325384 | tf_op jit(solution)/shard_map/ppermute | solution.py:20
  233.2 41.4 %collective-permute-start.19 = (bf16[2,176,1024]{2,1,0:T(8,128)(2,1)}, bf16[2,176,1024]{2,1,0:T(8,128)(2,1)S(1)}, u32[]{:S(2)}, u32[]{:S(2)}) collective-permute-start(bf16[2,176,1024]{2,1,0:T(8,128)(2,1)} %get-tuple-element.220), channel_id=1, source_target_pairs={{0,1},{1,0},{2,3},{3,2},{4,5},{5,4},{6,7},{7,6},{8,9},{9,8},{10,11... | collective-permute-start | bytes 2162696 | tf_op jit(solution)/shard_map/ppermute | solution.py:20
  233.4 42.4 %collective-permute-start.20 = (bf16[2,176,1024]{2,1,0:T(8,128)(2,1)}, bf16[2,176,1024]{2,1,0:T(8,128)(2,1)S(1)}, u32[]{:S(2)}, u32[]{:S(2)}) collective-permute-start(bf16[2,176,1024]{2,1,0:T(8,128)(2,1)} %get-tuple-element.222), channel_id=1, source_target_pairs={{0,4},{4,0},{1,5},{5,1},{2,6},{6,2},{3,7},{7,3},{8,12},{12,8},{9,1... | collective-permute-start | bytes 2162696 | tf_op jit(solution)/shard_map/ppermute | solution.py:20
  275.8 19.3 %collective-permute-start.21 = (bf16[352,1024]{1,0:T(8,128)(2,1)}, bf16[352,1024]{1,0:T(8,128)(2,1)S(1)}, u32[]{:S(2)}, u32[]{:S(2)}) collective-permute-start(bf16[352,1024]{1,0:T(8,128)(2,1)} %get-tuple-element.225), channel_id=1, source_target_pairs={{0,4},{4,0},{1,5},{5,1},{2,6},{6,2},{3,7},{7,3},{8,12},{12,8},{9,1... | collective-permute-start | bytes 2162696 | tf_op jit(solution)/shard_map/ppermute | solution.py:20
  277.4 19.3 %collective-permute-start.22 = (bf16[352,1024]{1,0:T(8,128)(2,1)}, bf16[352,1024]{1,0:T(8,128)(2,1)S(1)}, u32[]{:S(2)}, u32[]{:S(2)}) collective-permute-start(bf16[352,1024]{1,0:T(8,128)(2,1)} %get-tuple-element.227), channel_id=1, source_target_pairs={{0,1},{1,0},{2,3},{3,2},{4,5},{5,4},{6,7},{7,6},{8,9},{9,8},{10,11... | collective-permute-start | bytes 2162696 | tf_op jit(solution)/shard_map/ppermute | solution.py:20
  281.2 25.0 %collective-permute-start.23 = (bf16[176,1024]{1,0:T(8,128)(2,1)}, bf16[176,1024]{1,0:T(8,128)(2,1)S(1)}, u32[]{:S(2)}, u32[]{:S(2)}) collective-permute-start(bf16[176,1024]{1,0:T(8,128)(2,1)} %get-tuple-element.234), channel_id=1, source_target_pairs={{0,4},{4,0},{1,5},{5,1},{2,6},{6,2},{3,7},{7,3},{8,12},{12,8},{9,1... | collective-permute-start | bytes 1081352 | tf_op jit(solution)/shard_map/ppermute | solution.py:20
  281.8 24.4 %collective-permute-start.24 = (bf16[176,1024]{1,0:T(8,128)(2,1)}, bf16[176,1024]{1,0:T(8,128)(2,1)S(1)}, u32[]{:S(2)}, u32[]{:S(2)}) collective-permute-start(bf16[176,1024]{1,0:T(8,128)(2,1)} %get-tuple-element.236), channel_id=1, source_target_pairs={{0,1},{1,0},{2,3},{3,2},{4,5},{5,4},{6,7},{7,6},{8,9},{9,8},{10,11... | collective-permute-start | bytes 1081352 | tf_op jit(solution)/shard_map/ppermute | solution.py:20
  312.3 7.0 %collective-permute-start.25 = (f32[8,256]{1,0:T(8,128)}, f32[8,256]{1,0:T(8,128)S(1)}, u32[]{:S(2)}, u32[]{:S(2)}) collective-permute-start(f32[8,256]{1,0:T(8,128)} %get-tuple-element.240.refs_6_), channel_id=1, source_target_pairs={{0,1},{1,0},{2,3},{3,2},{4,5},{5,4},{6,7},{7,6},{8,9},{9,8},{10,11... | collective-permute-start | bytes 24584 | tf_op jit(solution)/shard_map/ppermute | solution.py:20
  320.0 21.7 %collective-permute-start.28 = (bf16[128,1024]{1,0:T(8,128)(2,1)}, bf16[128,1024]{1,0:T(8,128)(2,1)S(1)}, u32[]{:S(2)}, u32[]{:S(2)}) collective-permute-start(bf16[128,1024]{1,0:T(8,128)(2,1)} %get-tuple-element.270), channel_id=1, source_target_pairs={{0,1},{1,0},{2,3},{3,2},{4,5},{5,4},{6,7},{7,6},{8,9},{9,8},{10,11... | collective-permute-start | bytes 786440 | tf_op jit(solution)/shard_map/ppermute | solution.py:20
  320.8 20.9 %collective-permute-start.29 = (bf16[128,1024]{1,0:T(8,128)(2,1)}, bf16[128,1024]{1,0:T(8,128)(2,1)S(1)}, u32[]{:S(2)}, u32[]{:S(2)}) collective-permute-start(bf16[128,1024]{1,0:T(8,128)(2,1)} %get-tuple-element.271), channel_id=1, source_target_pairs={{0,4},{4,0},{1,5},{5,1},{2,6},{6,2},{3,7},{7,3},{8,12},{12,8},{9,1... | collective-permute-start | bytes 786440 | tf_op jit(solution)/shard_map/ppermute | solution.py:20
  322.3 19.4 %collective-permute-start.30 = (bf16[128,1024]{1,0:T(8,128)(2,1)}, bf16[128,1024]{1,0:T(8,128)(2,1)S(1)}, u32[]{:S(2)}, u32[]{:S(2)}) collective-permute-start(bf16[128,1024]{1,0:T(8,128)(2,1)} %get-tuple-element.272), channel_id=1, source_target_pairs={{0,5},{1,4},{4,1},{5,0},{2,7},{3,6},{6,3},{7,2},{8,13},{9,12},{12,... | collective-permute-start | bytes 786440 | tf_op jit(solution)/shard_map/ppermute | solution.py:851
  328.3 69.5 %all-to-all-start.3 = ((bf16[8,1056,128]{2,1,0:T(8,128)(2,1)}), bf16[8,1056,128]{2,1,0:T(8,128)(2,1)S(1)}, u32[]{:S(2)}, u32[]{:S(2)}) async-start(bf16[8,1056,128]{2,1,0:T(8,128)(2,1)} %shard_map.252), calls=%async_computation.6 | async-start | bytes 4325376 | tf_op jit(solution)/shard_map/all_to_all | solution.py:647
  331.9 100.8 %reduce-scatter.8.cloned.1.call-start = ((), (), s32[]{:S(2)}) async-start(), calls=%async_computation.12 | async-start | bytes 2359296 | tf_op jit(solution)/shard_map/reduce_scatter | solution.py:594
  347.6 37.3 %collective-permute-start.31 = (bf16[1024,384]{1,0:T(8,128)(2,1)}, bf16[1024,384]{1,0:T(8,128)(2,1)S(1)}, u32[]{:S(2)}, u32[]{:S(2)}) collective-permute-start(bf16[1024,384]{1,0:T(8,128)(2,1)} %get-tuple-element.275), channel_id=1, source_target_pairs={{0,1},{1,0},{2,3},{3,2},{4,5},{5,4},{6,7},{7,6},{8,9},{9,8},{10,11... | collective-permute-start | bytes 2359304 | tf_op jit(solution)/shard_map/ppermute | solution.py:20
  348.5 36.4 %collective-permute-start.32 = (bf16[1024,384]{1,0:T(8,128)(2,1)}, bf16[1024,384]{1,0:T(8,128)(2,1)}, u32[]{:S(2)}, u32[]{:S(2)}) collective-permute-start(bf16[1024,384]{1,0:T(8,128)(2,1)} %get-tuple-element.276), channel_id=1, source_target_pairs={{0,4},{4,0},{1,5},{5,1},{2,6},{6,2},{3,7},{7,3},{8,12},{12,8},{9,1... | collective-permute-start | bytes 2359304 | tf_op jit(solution)/shard_map/ppermute | solution.py:20
  349.9 35.5 %collective-permute-start.33 = (bf16[1024,384]{1,0:T(8,128)(2,1)}, bf16[1024,384]{1,0:T(8,128)(2,1)}, u32[]{:S(2)}, u32[]{:S(2)}) collective-permute-start(bf16[1024,384]{1,0:T(8,128)(2,1)} %get-tuple-element.277), channel_id=1, source_target_pairs={{0,5},{1,4},{4,1},{5,0},{2,7},{3,6},{6,3},{7,2},{8,13},{9,12},{12,... | collective-permute-start | bytes 2359304 | tf_op jit(solution)/shard_map/ppermute | solution.py:889
  352.3 32.5 %collective-permute-start.34 = (f32[128]{0:T(128)S(1)}, f32[128]{0:T(128)S(1)}, u32[]{:S(2)}, u32[]{:S(2)}) collective-permute-start(f32[128]{0:T(128)S(1)} %fusion.9), channel_id=1, source_target_pairs={{0,4},{4,0},{1,5},{5,1},{2,6},{6,2},{3,7},{7,3},{8,12},{12,8},{9,1... | collective-permute-start | bytes 1544 | tf_op jit(solution)/shard_map/ppermute | solution.py:20
  353.1 37.0 %collective-permute-start.45 = (bf16[128,1024]{1,0:T(8,128)(2,1)S(1)}, bf16[128,1024]{1,0:T(8,128)(2,1)S(1)}, u32[]{:S(2)}, u32[]{:S(2)}) collective-permute-start(bf16[128,1024]{1,0:T(8,128)(2,1)S(1)} %add_convert_fusion), channel_id=1, source_target_pairs={{0,1},{1,0},{2,3},{3,2},{4,5},{5,4},{6,7},{7,6},{8,9},{9,8},{10,11... | collective-permute-start | bytes 786440 | tf_op jit(solution)/shard_map/ppermute | solution.py:20
  391.7 16.8 %collective-permute-start.36 = (bf16[2,128,384]{2,1,0:T(8,128)(2,1)S(1)}, bf16[2,128,384]{2,1,0:T(8,128)(2,1)S(1)}, u32[]{:S(2)}, u32[]{:S(2)}) collective-permute-start(bf16[2,128,384]{2,1,0:T(8,128)(2,1)S(1)} %get-tuple-element.313), channel_id=1, source_target_pairs={{0,8},{8,0},{16,24},{24,16},{1,9},{9,1},{17,25},{25,17},{2,10},{10... | collective-permute-start | bytes 589832 | tf_op jit(solution)/shard_map/ppermute | solution.py:901
  393.4 15.9 %collective-permute-start.37 = (bf16[2,128,384]{2,1,0:T(8,128)(2,1)S(1)}, bf16[2,128,384]{2,1,0:T(8,128)(2,1)S(1)}, u32[]{:S(2)}, u32[]{:S(2)}) collective-permute-start(bf16[2,128,384]{2,1,0:T(8,128)(2,1)S(1)} %get-tuple-element.312), channel_id=1, source_target_pairs={{0,16},{8,24},{16,0},{24,8},{1,17},{9,25},{17,1},{25,9},{2,18},{10... | collective-permute-start | bytes 589832 | tf_op jit(solution)/shard_map/ppermute | solution.py:901
  396.3 10.9 %collective-permute-start.39 = (f32[128]{0:T(128)S(1)}, f32[128]{0:T(128)S(1)}, u32[]{:S(2)}, u32[]{:S(2)}) collective-permute-start(f32[128]{0:T(128)S(1)} %fusion.8), channel_id=1, source_target_pairs={{0,1},{1,0},{2,3},{3,2},{4,5},{5,4},{6,7},{7,6},{8,9},{9,8},{10,11... | collective-permute-start | bytes 1544 | tf_op jit(solution)/shard_map/ppermute | solution.py:20
  406.9 7.7 %collective-permute-start.38 = (bf16[2,128,384]{2,1,0:T(8,128)(2,1)S(1)}, bf16[2,128,384]{2,1,0:T(8,128)(2,1)S(1)}, u32[]{:S(2)}, u32[]{:S(2)}) collective-permute-start(bf16[2,128,384]{2,1,0:T(8,128)(2,1)S(1)} %copy-done.37), channel_id=1, source_target_pairs={{0,24},{8,16},{16,8},{24,0},{1,25},{9,17},{17,9},{25,1},{2,26},{10... | collective-permute-start | bytes 589832 | tf_op jit(solution)/shard_map/ppermute | solution.py:901
  407.2 9.5 %collective-permute-start.41 = (bf16[2,128,384]{2,1,0:T(8,128)(2,1)S(1)}, bf16[2,128,384]{2,1,0:T(8,128)(2,1)S(1)}, u32[]{:S(2)}, u32[]{:S(2)}) collective-permute-start(bf16[2,128,384]{2,1,0:T(8,128)(2,1)S(1)} %get-tuple-element.314.refs_1_), channel_id=1, source_target_pairs={{0,1},{1,0},{2,3},{3,2},{4,5},{5,4},{6,7},{7,6},{8,9},{9,8},{10,11... | collective-permute-start | bytes 589832 | tf_op jit(solution)/shard_map/ppermute | solution.py:20
  408.4 10.8 %collective-permute-start.42 = (bf16[2,128,384]{2,1,0:T(8,128)(2,1)S(1)}, bf16[2,128,384]{2,1,0:T(8,128)(2,1)S(1)}, u32[]{:S(2)}, u32[]{:S(2)}) collective-permute-start(bf16[2,128,384]{2,1,0:T(8,128)(2,1)S(1)} %collective-permute-done.36.refs_2_), channel_id=1, source_target_pairs={{0,1},{1,0},{2,3},{3,2},{4,5},{5,4},{6,7},{7,6},{8,9},{9,8},{10,11... | collective-permute-start | bytes 589832 | tf_op jit(solution)/shard_map/ppermute | solution.py:20
  409.3 14.0 %collective-permute-start.43 = (bf16[2,128,384]{2,1,0:T(8,128)(2,1)S(1)}, bf16[2,128,384]{2,1,0:T(8,128)(2,1)S(1)}, u32[]{:S(2)}, u32[]{:S(2)}) collective-permute-start(bf16[2,128,384]{2,1,0:T(8,128)(2,1)S(1)} %collective-permute-done.37.refs_3_), channel_id=1, source_target_pairs={{0,1},{1,0},{2,3},{3,2},{4,5},{5,4},{6,7},{7,6},{8,9},{9,8},{10,11... | collective-permute-start | bytes 589832 | tf_op jit(solution)/shard_map/ppermute | solution.py:20
  414.6 10.8 %collective-permute-start.44 = (bf16[2,128,384]{2,1,0:T(8,128)(2,1)S(1)}, bf16[2,128,384]{2,1,0:T(8,128)(2,1)S(1)}, u32[]{:S(2)}, u32[]{:S(2)}) collective-permute-start(bf16[2,128,384]{2,1,0:T(8,128)(2,1)S(1)} %collective-permute-done.38.refs_4_), channel_id=1, source_target_pairs={{0,1},{1,0},{2,3},{3,2},{4,5},{5,4},{6,7},{7,6},{8,9},{9,8},{10,11... | collective-permute-start | bytes 589832 | tf_op jit(solution)/shard_map/ppermute | solution.py:20
  (48 other events, 303.4 us)
Sparse Core Ops, SparseCore 0:
  38.8 46.2 all-gather.3
  110.9 49.1 reduce-scatter.3
  166.4 31.2 all-gather.5
  217.8 50.6 reduce-scatter.5
  275.9 30.2 all-gather.7
  347.7 60.2 reduce-scatter.7

commit v7 on v6

--- a/solution.py
+++ b/solution.py
@@ -825,8 +825,8 @@
     if pair:
         gate_up = last_swaps(gate_up)
         down = last_swaps(first_sums(down))
-        d_mixed, *gate_up = lax.optimization_barrier((d_mixed, *gate_up))
-        d_mixed, *down = lax.optimization_barrier((d_mixed, *down))
+        glu_grad = last_sums(*gate_up, *down)
+        d_mixed, glu_grad = lax.optimization_barrier((d_mixed, glu_grad))
 
     mixed_in, d_gate_raw, adjoint, passed, first = call(
         mixer_back_kernel,
@@ -852,10 +852,9 @@
             )
         ).astype(BF)
     if pair:
-        glu_grad = last_sums(*after((*gate_up, *down), first))
+        glu_grad = after(glu_grad, first)
     else:
         glu_grad = jnp.concatenate([total_blocks(gate_up), total_blocks(down)], axis=1)
-    raw = after(raw, glu_grad)
     glu_grad = spread(glu_grad)
     *d_raw, part_bound = call(
         functools.partial(d_mixer_kernel, crowd, parts, count),

time: 451 us -> 449 us (level)
    all_gather x3, waiting for transfers between devices: 46.7 us -> 37.1 us  [gather_rows(): return lax.all_gather(own, ('z', 'c'), axis=0, tiled=True)]
    ppermute x38, waiting for transfers between devices: 119 us -> 127 us  [swap(): return lax.ppermute(value, axis, [(0, 1), (1, 0)])]
  transfers between devices with their start and end apart: 56 -> 56, of which waited for: 31 -> 27; matrix products, arithmetic and copies ran while one was open for 8% -> 8% of each run, Pallas kernels for 20% -> 20%
where the time goes in v7:
time: 449 us; the launch traced here: 442 us
  waiting for transfers between devices  197 us (44%)
  Pallas kernels  122 us (27%)
  starting transfers between devices  68.9 us (15%)
  local copies, waits for them, and re-layouts  22.7 us (5%)
  other arithmetic  16.8 us (4%)
  between operations  15.4 us (3%)
    ppermute x38, waiting for transfers between devices, swap(): return lax.ppermute(value, axis, [(0, 1), (1, 0)])  127 us
    pallas_call x25, Pallas kernels, call(): pl.pallas_call(body, out_shape=shapes, in_specs=[pl.BlockSpec(memory_spac...  122 us
    ppermute x38, starting transfers between devices, swap(): return lax.ppermute(value, axis, [(0, 1), (1, 0)])  39.1 us
    all_gather x3, waiting for transfers between devices, gather_rows(): return lax.all_gather(own, ('z', 'c'), axis=0, tiled=True)  37.1 us
    all_to_all x1, waiting for transfers between devices, per_device(): lax.all_to_all(jnp.broadcast_to(after(grad_y, glu)[None], (Z, rows, width...  13.4 us
    all_to_all x3, starting transfers between devices, spread(): return lax.all_to_all(value, ('z', 'c'), 0, 0, tiled=True)  12.7 us
    all_to_all x3, waiting for transfers between devices, spread(): return lax.all_to_all(value, ('z', 'c'), 0, 0, tiled=True)  11.7 us
  transfers between devices with their start and end apart: 56, of which 27 were waited for; matrix products, arithmetic and copies ran while one was open for 8% of the time, Pallas kernels for 20%

profile of v7, /device:TPU:0, one launch (start us, length us, event | category | flops | bytes accessed | tf_op | source)
XLA Modules:
  0.0 442.3 jit_solution(8815901760091802826)
XLA Ops:
  7.2 3.0 collective-permute-start.1
  10.2 2.5 shard_map.238
  12.8 4.9 %all-to-all-start = ((bf16[8,128,384]{2,1,0:T(8,128)(2,1)}), bf16[8,128,384]{2,1,0:T(8,128)(2,1)S(1)}, u32[]{:S(2)}, u32[]{:S(2)}) async-start(bf16[8,128,384]{2,1,0:T(8,128)(2,1)} %shard_map.238), calls=%async_computation | async-start | bytes 1572864 | tf_op jit(solution)/shard_map/all_to_all | solution.py:647
  18.4 4.0 shard_map.239
  25.9 2.4 shard_map.240.refs_9_.refs_1_
  28.3 10.4 %all-to-all-done = bf16[8,128,384]{2,1,0:T(8,128)(2,1)S(1)} async-done(((bf16[8,128,384]{2,1,0:T(8,128)(2,1)}), bf16[8,128,384]{2,1,0:T(8,128)(2,1)S(1)}, u32[]{:S(2)}, u32[]{:S(2)}) %all-to-all-start) | async-done | bytes 786464 | tf_op jit(solution)/shard_map/all_to_all | solution.py:647
  38.7 3.7 all-to-all-start.1
  47.9 37.1 %all-gather.4.cloned.1.call-done.refs_2_ = bf16[512,2176]{1,0:T(8,128)(2,1)} async-done(((bf16[64,2176]{1,0:T(8,128)(2,1)}), bf16[512,2176]{1,0:T(8,128)(2,1)}) %all-gather.4.cloned.1.call-update) | async-done | bytes 2228240 | tf_op jit(solution)/shard_map/all_gather | solution.py:590
  86.4 9.4 %shard_map.241 = (bf16[512,2048]{1,0:T(8,128)(2,1)}, f32[512,768]{1,0:T(8,128)}, f32[2,512,128]{2,1,0:T(8,128)}, f32[2,512,128]{2,1,0:T(8,128)}, f32[2,512,128]{2,1,0:T(8,128)}, /*index=5*/f32[16,256]{1,0:T(8,128)}) custom-call(s32[1]{0:T(128)} %bitcast.2.refs_0_.refs_1_, f32[1,2048]{1,0:T(1,128)} %pad_maximum_fusion.5.refs_1_.refs_3_, ...), custom_call_target="tpu_custom_call" | custom-call | bytes 1024 | tf_op jit(solution)/shard_map/pallas_call | solution.py:87
  101.3 2.6 collective-permute-done.7.refs_4_.refs_5_
  104.5 4.9 %shard_map.242 = (f32[2,512,128]{2,1,0:T(8,128)}, f32[8,256]{1,0:T(8,128)}, bf16[512,2176]{1,0:T(8,128)(2,1)}) custom-call(s32[34]{0:T(128)} %pad_add_fusion.refs_0_.refs_1_, f32[16,256]{1,0:T(8,128)} %get-tuple-element.168.refs_1_.refs_2_, f32[16,256]{1,0:T(8,128)} %copy-done.24, f32[16,256]{1,0:T(8,128)} %copy-done.25, f32[16,256]{1,0:T(8,128)} %copy-done.26, ...), custom_call_target="tpu_custom_call" | custom-call | bytes 1024 | tf_op jit(solution)/shard_map/pallas_call | solution.py:87
  115.8 2.0 broadcast_in_dim.22
  117.9 5.4 %all-to-all-start.2 = ((bf16[4,64,2048]{2,1,0:T(8,128)(2,1)}), bf16[4,64,2048]{2,1,0:T(8,128)(2,1)S(1)}, u32[]{:S(2)}, u32[]{:S(2)}) async-start(bf16[4,64,2048]{2,1,0:T(8,128)(2,1)} %broadcast_in_dim.22), calls=%async_computation.3 | async-start | bytes 2097152 | tf_op jit(solution)/shard_map/all_to_all | solution.py:760
  124.2 21.2 %collective-permute-done.8 = bf16[8,704,128]{2,1,0:T(8,128)(2,1)} collective-permute-done((bf16[8,704,128]{2,1,0:T(8,128)(2,1)}, bf16[8,704,128]{2,1,0:T(8,128)(2,1)}, u32[]{:S(2)}, u32[]{:S(2)}) %collective-permute-start.8) | collective-permute-done | bytes 1441824 | tf_op jit(solution)/shard_map/ppermute | solution.py:20
  148.2 13.4 %all-to-all-done.2 = bf16[4,64,2048]{2,1,0:T(8,128)(2,1)S(1)} async-done(((bf16[4,64,2048]{2,1,0:T(8,128)(2,1)}), bf16[4,64,2048]{2,1,0:T(8,128)(2,1)S(1)}, u32[]{:S(2)}, u32[]{:S(2)}) %all-to-all-start.2) | async-done | bytes 1048608 | tf_op jit(solution)/shard_map/all_to_all | solution.py:760
  163.5 2.7 shard_map.244
  175.4 1.9 pad_maximum_fusion.refs_2_
  178.9 2.2 collective-permute-start.12
  182.2 5.3 %collective-permute-done.13 = bf16[8,352,128]{2,1,0:T(8,128)(2,1)S(1)} collective-permute-done((bf16[8,352,128]{2,1,0:T(8,128)(2,1)S(1)}, bf16[8,352,128]{2,1,0:T(8,128)(2,1)S(1)}, u32[]{:S(2)}, u32[]{:S(2)}) %collective-permute-start.13) | collective-permute-done | bytes 720928 | tf_op jit(solution)/shard_map/ppermute | solution.py:20
  198.0 19.7 %shard_map.245 = (bf16[512,352]{1,0:T(8,128)(2,1)}, bf16[512,352]{1,0:T(8,128)(2,1)}, bf16[512,352]{1,0:T(8,128)(2,1)}, bf16[512,352]{1,0:T(8,128)(2,1)}, bf16[5...) custom-call(bf16[512,2048]{1,0:T(8,128)(2,1)} %all-gather.6.cloned.1.call-done.refs_0_.refs_4_, ...), custom_call_target="tpu_custom_call" | custom-call | bytes 1024 | tf_op jit(solution)/shard_map/pallas_call | solution.py:87
  217.8 6.7 %shard_map.246 = (bf16[2,352,1024]{2,1,0:T(8,128)(2,1)}, bf16[2,352,1024]{2,1,0:T(8,128)(2,1)}, bf16[2,352,1024]{2,1,0:T(8,128)(2,1)}, bf16[2,352,1024]{2,1,0:T(8,128)(2,1)}) custom-call(bf16[512,352]{1,0:T(8,128)(2,1)} %get-tuple-element.184.refs_0_, bf16[512,352]{1,0:T(8,128)(2,1)} %get-tuple-element.185.refs_1_, ...), custom_call_target="tpu_custom_call" | custom-call | bytes 1024 | tf_op jit(solution)/shard_map/pallas_call | solution.py:87
  224.5 2.2 collective-permute-start.17
  228.3 5.0 %shard_map.249 = (bf16[2,176,1024]{2,1,0:T(8,128)(2,1)}, bf16[2,176,1024]{2,1,0:T(8,128)(2,1)}, bf16[2,176,1024]{2,1,0:T(8,128)(2,1)}, bf16[2,176,1024]{2,1,0:T(8,128)(2,1)}) custom-call(bf16[512,352]{1,0:T(8,128)(2,1)} %get-tuple-element.201.refs_0_, bf16[512,352]{1,0:T(8,128)(2,1)} %get-tuple-element.202.refs_1_, bf16[512,2048]{1,0:T(8,128)(2,1)} %bitcast.85), custom_call_target="tpu_custom_call" | custom-call | bytes 1024 | tf_op jit(solution)/shard_map/pallas_call | solution.py:87
  233.8 25.5 %collective-permute-done.17.refs_1_ = bf16[2,352,1024]{2,1,0:T(8,128)(2,1)S(1)} collective-permute-done((bf16[2,352,1024]{2,1,0:T(8,128)(2,1)}, bf16[2,352,1024]{2,1,0:T(8,128)(2,1)S(1)}, u32[]{:S(2)}, u32[]{:S(2)}) %collective-permute-start.17) | collective-permute-done | bytes 1441824 | tf_op jit(solution)/shard_map/ppermute | solution.py:20
  259.3 2.0 collective-permute-done.18.refs_3_
  262.5 5.0 %shard_map.247 = (f32[352,1024]{1,0:T(8,128)}, bf16[352,1024]{1,0:T(8,128)(2,1)}, f32[352,1024]{1,0:T(8,128)}, bf16[352,1024]{1,0:T(8,128)(2,1)}) custom-call(bf16[2,352,1024]{2,1,0:T(8,128)(2,1)} %get-tuple-element.188.refs_0_, bf16[2,352,1024]{2,1,0:T(8,128)(2,1)} %copy-done.4, bf16[2,352,1024]{2,1,0:T(8,128)(2,1)} %get-tuple-element.190.refs_2_, ...), custom_call_target="tpu_custom_call" | custom-call | bytes 1024 | tf_op jit(solution)/shard_map/pallas_call | solution.py:87
  268.6 3.7 shard_map.248
  272.3 2.4 collective-permute-done.19.refs_1_
  278.0 3.2 shard_map.250
  283.2 17.5 %collective-permute-done.23.refs_5_ = bf16[176,1024]{1,0:T(8,128)(2,1)S(1)} collective-permute-done((bf16[176,1024]{1,0:T(8,128)(2,1)}, bf16[176,1024]{1,0:T(8,128)(2,1)S(1)}, u32[]{:S(2)}, u32[]{:S(2)}) %collective-permute-start.23) | collective-permute-done | bytes 360480 | tf_op jit(solution)/shard_map/ppermute | solution.py:20
  303.1 4.8 %shard_map.251 = bf16[8,1056,128]{2,1,0:T(8,128)(2,1)} custom-call(f32[352,1024]{1,0:T(8,128)} %get-tuple-element.208.refs_0_, bf16[352,1024]{1,0:T(8,128)(2,1)} %copy-done.9, f32[352,1024]{1,0:T(8,128)} %get-tuple-element.210.refs_2_, bf16[352,1024]{1,0:T(8,128)(2,1)} %copy-done.10, f32[176,1024]{1,0:T(8,128)} %get-tuple-element.216.refs_4_, ...), custom_call_target="tpu_custom_call" | custom-call | bytes 1024 | tf_op jit(solution)/shard_map/pallas_call | solution.py:87
  307.9 5.7 %shard_map.252 = (bf16[512,256]{1,0:T(8,128)(2,1)}, bf16[512,256]{1,0:T(8,128)(2,1)}, f32[2,512,128]{2,1,0:T(8,128)}, f32[2,512,128]{2,1,0:T(8,128)}, f32[8,256]{1,0:T(8,128)}) custom-call(bf16[512,2176]{1,0:T(8,128)(2,1)} %all-gather.8.cloned.1.call-done.refs_0_.refs_3_, bf16[256,2048]{1,0:T(8,128)(2,1)} %shard_map.240.refs_9_.refs_1_, ...), custom_call_target="tpu_custom_call" | custom-call | bytes 1024 | tf_op jit(solution)/shard_map/pallas_call | solution.py:87
  317.1 3.5 shard_map.254
  324.2 4.1 all-to-all-start.3
  328.6 4.4 shard_map.253
  333.0 5.1 %shard_map.255 = (bf16[1024,384]{1,0:T(8,128)(2,1)}, bf16[1024,384]{1,0:T(8,128)(2,1)}, bf16[1024,384]{1,0:T(8,128)(2,1)}, bf16[1024,384]{1,0:T(8,128)(2,1)}) custom-call(bf16[512,2048]{1,0:T(8,128)(2,1)} %get-tuple-element.239.refs_0_, bf16[512,384]{1,0:T(8,128)(2,1)} %get-tuple-element.244.refs_1_.refs_0_, bf16[512,384]{1,0:T(8,128)(2,1)} %get-tuple-element.245.refs_2_.refs_1_), custom_call_target="tpu_custom_call" | custom-call | bytes 1024 | tf_op jit(solution)/shard_map/pallas_call | solution.py:87
  338.3 5.6 %shard_map.256 = bf16[512,2048]{1,0:T(8,128)(2,1)} custom-call(bf16[512,384]{1,0:T(8,128)(2,1)} %get-tuple-element.244.refs_1_.refs_0_, bf16[512,384]{1,0:T(8,128)(2,1)} %get-tuple-element.245.refs_2_.refs_1_, bf16[1024,384]{1,0:T(8,128)(2,1)} %bitcast.90, bf16[1024,384]{1,0:T(8,128)(2,1)} %collective-permute-done.2.refs_6_.refs_3_, ...), custom_call_target="tpu_custom_call" | custom-call | bytes 1024 | tf_op jit(solution)/shard_map/pallas_call | solution.py:87
  350.4 31.7 %collective-permute-done.34 = f32[128]{0:T(128)S(1)} collective-permute-done((f32[128]{0:T(128)S(1)}, f32[128]{0:T(128)S(1)}, u32[]{:S(2)}, u32[]{:S(2)}) %collective-permute-start.34) | collective-permute-done | bytes 544 | tf_op jit(solution)/shard_map/ppermute | solution.py:20
  383.0 3.8 shard_map.259
  390.5 2.4 collective-permute-start.37
  395.4 6.2 %shard_map.260 = (f32[128,2816]{1,0:T(8,128)}, f32[128,2816]{1,0:T(8,128)}, f32[2816,128]{1,0:T(8,128)}, f32[128,128]{1,0:T(8,128)}) custom-call(bf16[8,1056,128]{2,1,0:T(8,128)(2,1)} %copy-done, bf16[128,2816]{1,0:T(8,128)(2,1)} %refs_1_.9, bf16[128,2816]{1,0:T(8,128)(2,1)} %refs_2_.7), custom_call_target="tpu_custom_call" | custom-call | bytes 1024 | tf_op jit(solution)/shard_map/pallas_call | solution.py:87
  407.8 3.9 collective-permute-done.38.refs_4_
  413.0 3.6 collective-permute-done.42.refs_6_
  416.6 4.0 collective-permute-done.43.refs_7_
  420.6 2.1 collective-permute-done.44.refs_8_
  423.4 5.1 %shard_map.261 = (f32[128,2048]{1,0:T(8,128)}, f32[128,2048]{1,0:T(8,128)}, f32[128,2048]{1,0:T(8,128)}, f32[128,128]{1,0:T(8,128)}) custom-call(s32[3]{0:T(128)} %pad_add_fusion.1.refs_0_, bf16[2,128,384]{2,1,0:T(8,128)(2,1)} %copy-done.21, bf16[2,128,384]{2,1,0:T(8,128)(2,1)} %copy-done.14, bf16[2,128,384]{2,1,0:T(8,128)(2,1)} %copy-done.15, ...), custom_call_target="tpu_custom_call" | custom-call | bytes 1024 | tf_op jit(solution)/shard_map/pallas_call | solution.py:87
  430.0 2.9 shard_map.257.refs_2_
  432.9 2.1 shard_map.258
  (245 shorter events, 94.2 us)
Async XLA Ops:
  7.2 17.6 %collective-permute-start.1 = (bf16[128,2048]{1,0:T(8,128)(2,1)}, bf16[128,2048]{1,0:T(8,128)(2,1)S(1)}, u32[]{:S(2)}, u32[]{:S(2)}) collective-permute-start(bf16[128,2048]{1,0:T(8,128)(2,1)} %param.27), channel_id=1, source_target_pairs={{0,4},{4,0},{1,5},{5,1},{2,6},{6,2},{3,7},{7,3},{8,12},{12,8},{9,1... | collective-permute-start | bytes 1572872 | tf_op jit(solution)/shard_map/ppermute | solution.py:20
  12.8 25.9 %all-to-all-start = ((bf16[8,128,384]{2,1,0:T(8,128)(2,1)}), bf16[8,128,384]{2,1,0:T(8,128)(2,1)S(1)}, u32[]{:S(2)}, u32[]{:S(2)}) async-start(bf16[8,128,384]{2,1,0:T(8,128)(2,1)} %shard_map.238), calls=%async_computation | async-start | bytes 1572864 | tf_op jit(solution)/shard_map/all_to_all | solution.py:647
  17.6 67.4 %all-gather.4.cloned.1.call-start = ((), (), s32[]{:S(2)}) async-start(), calls=%async_computation.7 | async-start | bytes 2506752 | tf_op jit(solution)/shard_map/all_gather | solution.py:590
  38.7 72.1 %all-to-all-start.1 = ((bf16[8,1056,128]{2,1,0:T(8,128)(2,1)}), bf16[8,1056,128]{2,1,0:T(8,128)(2,1)S(1)}, u32[]{:S(2)}, u32[]{:S(2)}) async-start(bf16[8,1056,128]{2,1,0:T(8,128)(2,1)} %shard_map.239), calls=%async_computation.1 | async-start | bytes 4325376 | tf_op jit(solution)/shard_map/all_to_all | solution.py:647
  42.4 121.1 %reduce-scatter.4.cloned.1.call-start = ((), (), s32[]{:S(2)}) async-start(), calls=%async_computation.8 | async-start | bytes 2506752 | tf_op jit(solution)/shard_map/reduce_scatter | solution.py:594
  43.8 42.6 %collective-permute-start.2 = (bf16[1024,384]{1,0:T(8,128)(2,1)S(1)}, bf16[1024,384]{1,0:T(8,128)(2,1)}, u32[]{:S(2)}, u32[]{:S(2)}) collective-permute-start(bf16[1024,384]{1,0:T(8,128)(2,1)S(1)} %bitcast.86), channel_id=1, source_target_pairs={{0,1},{1,0},{2,3},{3,2},{4,5},{5,4},{6,7},{7,6},{8,9},{9,8},{10,11... | collective-permute-start | bytes 2359304 | tf_op jit(solution)/shard_map/ppermute | solution.py:20
  45.3 41.1 %collective-permute-start.3 = (bf16[1024,384]{1,0:T(8,128)(2,1)S(1)}, bf16[1024,384]{1,0:T(8,128)(2,1)}, u32[]{:S(2)}, u32[]{:S(2)}) collective-permute-start(bf16[1024,384]{1,0:T(8,128)(2,1)S(1)} %bitcast.87), channel_id=1, source_target_pairs={{0,4},{4,0},{1,5},{5,1},{2,6},{6,2},{3,7},{7,3},{8,12},{12,8},{9,1... | collective-permute-start | bytes 2359304 | tf_op jit(solution)/shard_map/ppermute | solution.py:20
  45.8 40.5 %collective-permute-start.4 = (bf16[1024,384]{1,0:T(8,128)(2,1)S(1)}, bf16[1024,384]{1,0:T(8,128)(2,1)}, u32[]{:S(2)}, u32[]{:S(2)}) collective-permute-start(bf16[1024,384]{1,0:T(8,128)(2,1)S(1)} %bitcast.88), channel_id=1, source_target_pairs={{0,5},{1,4},{4,1},{5,0},{2,7},{3,6},{6,3},{7,2},{8,13},{9,12},{12,... | collective-permute-start | bytes 2359304 | tf_op jit(solution)/shard_map/ppermute | solution.py:656
  111.9 33.4 %collective-permute-start.8 = (bf16[8,704,128]{2,1,0:T(8,128)(2,1)}, bf16[8,704,128]{2,1,0:T(8,128)(2,1)}, u32[]{:S(2)}, u32[]{:S(2)}) collective-permute-start(bf16[8,704,128]{2,1,0:T(8,128)(2,1)} %slice.180), channel_id=1, source_target_pairs={{0,1},{1,0},{2,3},{3,2},{4,5},{5,4},{6,7},{7,6},{8,9},{9,8},{10,11... | collective-permute-start | bytes 4325384 | tf_op jit(solution)/shard_map/ppermute | solution.py:20
  113.4 33.2 %collective-permute-start.9 = (bf16[8,704,128]{2,1,0:T(8,128)(2,1)}, bf16[8,704,128]{2,1,0:T(8,128)(2,1)}, u32[]{:S(2)}, u32[]{:S(2)}) collective-permute-start(bf16[8,704,128]{2,1,0:T(8,128)(2,1)} %slice.180), channel_id=1, source_target_pairs={{0,4},{4,0},{1,5},{5,1},{2,6},{6,2},{3,7},{7,3},{8,12},{12,8},{9,1... | collective-permute-start | bytes 4325384 | tf_op jit(solution)/shard_map/ppermute | solution.py:20
  117.9 43.8 %all-to-all-start.2 = ((bf16[4,64,2048]{2,1,0:T(8,128)(2,1)}), bf16[4,64,2048]{2,1,0:T(8,128)(2,1)S(1)}, u32[]{:S(2)}, u32[]{:S(2)}) async-start(bf16[4,64,2048]{2,1,0:T(8,128)(2,1)} %broadcast_in_dim.22), calls=%async_computation.3 | async-start | bytes 2097152 | tf_op jit(solution)/shard_map/all_to_all | solution.py:760
  123.3 74.8 %all-gather.6.cloned.1.call-start = ((), (), s32[]{:S(2)}) async-start(), calls=%async_computation.9 | async-start | bytes 2359296 | tf_op jit(solution)/shard_map/all_gather | solution.py:590
  146.6 16.7 %collective-permute-start.11 = (bf16[8,352,128]{2,1,0:T(8,128)(2,1)}, bf16[8,352,128]{2,1,0:T(8,128)(2,1)S(1)}, u32[]{:S(2)}, u32[]{:S(2)}) collective-permute-start(bf16[8,352,128]{2,1,0:T(8,128)(2,1)} %slice.181), channel_id=1, source_target_pairs={{0,4},{4,0},{1,5},{5,1},{2,6},{6,2},{3,7},{7,3},{8,12},{12,8},{9,1... | collective-permute-start | bytes 2162696 | tf_op jit(solution)/shard_map/ppermute | solution.py:20
  147.1 16.4 %collective-permute-start.10 = (bf16[8,352,128]{2,1,0:T(8,128)(2,1)}, bf16[8,352,128]{2,1,0:T(8,128)(2,1)S(1)}, u32[]{:S(2)}, u32[]{:S(2)}) collective-permute-start(bf16[8,352,128]{2,1,0:T(8,128)(2,1)} %slice.181), channel_id=1, source_target_pairs={{0,1},{1,0},{2,3},{3,2},{4,5},{5,4},{6,7},{7,6},{8,9},{9,8},{10,11... | collective-permute-start | bytes 2162696 | tf_op jit(solution)/shard_map/ppermute | solution.py:20
  166.2 102.3 %reduce-scatter.6.cloned.1.call-start = ((), (), s32[]{:S(2)}) async-start(), calls=%async_computation.10 | async-start | bytes 4718592 | tf_op jit(solution)/shard_map/reduce_scatter | solution.py:594
  169.2 18.4 %collective-permute-start.13 = (bf16[8,352,128]{2,1,0:T(8,128)(2,1)S(1)}, bf16[8,352,128]{2,1,0:T(8,128)(2,1)S(1)}, u32[]{:S(2)}, u32[]{:S(2)}) collective-permute-start(bf16[8,352,128]{2,1,0:T(8,128)(2,1)S(1)} %slice.184), channel_id=1, source_target_pairs={{0,1},{1,0},{2,3},{3,2},{4,5},{5,4},{6,7},{7,6},{8,9},{9,8},{10,11... | collective-permute-start | bytes 2162696 | tf_op jit(solution)/shard_map/ppermute | solution.py:20
  171.0 18.0 %collective-permute-start.14 = (bf16[8,352,128]{2,1,0:T(8,128)(2,1)S(1)}, bf16[8,352,128]{2,1,0:T(8,128)(2,1)S(1)}, u32[]{:S(2)}, u32[]{:S(2)}) collective-permute-start(bf16[8,352,128]{2,1,0:T(8,128)(2,1)S(1)} %slice.185), channel_id=1, source_target_pairs={{0,4},{4,0},{1,5},{5,1},{2,6},{6,2},{3,7},{7,3},{8,12},{12,8},{9,1... | collective-permute-start | bytes 2162696 | tf_op jit(solution)/shard_map/ppermute | solution.py:20
  178.9 13.6 %collective-permute-start.12 = (bf16[4,64,2048]{2,1,0:T(8,128)(2,1)S(1)}, bf16[4,64,2048]{2,1,0:T(8,128)(2,1)S(1)}, u32[]{:S(2)}, u32[]{:S(2)}) collective-permute-start(bf16[4,64,2048]{2,1,0:T(8,128)(2,1)S(1)} %all-to-all-done.2), channel_id=1, source_target_pairs={{0,2},{2,0},{1,3},{3,1},{4,6},{6,4},{5,7},{7,5},{8,10},{10,8},{9,1... | collective-permute-start | bytes 3145736 | tf_op jit(solution)/shard_map/ppermute | solution.py:20
  181.1 14.2 %collective-permute-start.15 = (bf16[8,176,128]{2,1,0:T(8,128)(2,1)S(1)}, bf16[8,176,128]{2,1,0:T(8,128)(2,1)S(1)}, u32[]{:S(2)}, u32[]{:S(2)}) collective-permute-start(bf16[8,176,128]{2,1,0:T(8,128)(2,1)S(1)} %slice.186), channel_id=1, source_target_pairs={{0,1},{1,0},{2,3},{3,2},{4,5},{5,4},{6,7},{7,6},{8,9},{9,8},{10,11... | collective-permute-start | bytes 1081352 | tf_op jit(solution)/shard_map/ppermute | solution.py:20
  181.6 15.2 %collective-permute-start.16 = (bf16[8,176,128]{2,1,0:T(8,128)(2,1)S(1)}, bf16[8,176,128]{2,1,0:T(8,128)(2,1)S(1)}, u32[]{:S(2)}, u32[]{:S(2)}) collective-permute-start(bf16[8,176,128]{2,1,0:T(8,128)(2,1)S(1)} %slice.187), channel_id=1, source_target_pairs={{0,4},{4,0},{1,5},{5,1},{2,6},{6,2},{3,7},{7,3},{8,12},{12,8},{9,1... | collective-permute-start | bytes 1081352 | tf_op jit(solution)/shard_map/ppermute | solution.py:20
  217.8 90.1 %all-gather.8.cloned.1.call-start = ((), (), s32[]{:S(2)}) async-start(), calls=%async_computation.11 | async-start | bytes 2506752 | tf_op jit(solution)/shard_map/all_gather | solution.py:590
  224.5 34.8 %collective-permute-start.17 = (bf16[2,352,1024]{2,1,0:T(8,128)(2,1)}, bf16[2,352,1024]{2,1,0:T(8,128)(2,1)S(1)}, u32[]{:S(2)}, u32[]{:S(2)}) collective-permute-start(bf16[2,352,1024]{2,1,0:T(8,128)(2,1)} %get-tuple-element.189), channel_id=1, source_target_pairs={{0,1},{1,0},{2,3},{3,2},{4,5},{5,4},{6,7},{7,6},{8,9},{9,8},{10,11... | collective-permute-start | bytes 4325384 | tf_op jit(solution)/shard_map/ppermute | solution.py:20
  226.7 34.7 %collective-permute-start.18 = (bf16[2,352,1024]{2,1,0:T(8,128)(2,1)}, bf16[2,352,1024]{2,1,0:T(8,128)(2,1)S(1)}, u32[]{:S(2)}, u32[]{:S(2)}) collective-permute-start(bf16[2,352,1024]{2,1,0:T(8,128)(2,1)} %get-tuple-element.191), channel_id=1, source_target_pairs={{0,4},{4,0},{1,5},{5,1},{2,6},{6,2},{3,7},{7,3},{8,12},{12,8},{9,1... | collective-permute-start | bytes 4325384 | tf_op jit(solution)/shard_map/ppermute | solution.py:20
  233.3 41.3 %collective-permute-start.19 = (bf16[2,176,1024]{2,1,0:T(8,128)(2,1)}, bf16[2,176,1024]{2,1,0:T(8,128)(2,1)S(1)}, u32[]{:S(2)}, u32[]{:S(2)}) collective-permute-start(bf16[2,176,1024]{2,1,0:T(8,128)(2,1)} %get-tuple-element.204), channel_id=1, source_target_pairs={{0,1},{1,0},{2,3},{3,2},{4,5},{5,4},{6,7},{7,6},{8,9},{9,8},{10,11... | collective-permute-start | bytes 2162696 | tf_op jit(solution)/shard_map/ppermute | solution.py:20
  233.4 42.4 %collective-permute-start.20 = (bf16[2,176,1024]{2,1,0:T(8,128)(2,1)}, bf16[2,176,1024]{2,1,0:T(8,128)(2,1)S(1)}, u32[]{:S(2)}, u32[]{:S(2)}) collective-permute-start(bf16[2,176,1024]{2,1,0:T(8,128)(2,1)} %get-tuple-element.206), channel_id=1, source_target_pairs={{0,4},{4,0},{1,5},{5,1},{2,6},{6,2},{3,7},{7,3},{8,12},{12,8},{9,1... | collective-permute-start | bytes 2162696 | tf_op jit(solution)/shard_map/ppermute | solution.py:20
  275.8 26.0 %collective-permute-start.21 = (bf16[352,1024]{1,0:T(8,128)(2,1)S(1)}, bf16[352,1024]{1,0:T(8,128)(2,1)S(1)}, u32[]{:S(2)}, u32[]{:S(2)}) collective-permute-start(bf16[352,1024]{1,0:T(8,128)(2,1)S(1)} %copy-done.34), channel_id=1, source_target_pairs={{0,4},{4,0},{1,5},{5,1},{2,6},{6,2},{3,7},{7,3},{8,12},{12,8},{9,1... | collective-permute-start | bytes 2162696 | tf_op jit(solution)/shard_map/ppermute | solution.py:20
  277.4 24.5 %collective-permute-start.22 = (bf16[352,1024]{1,0:T(8,128)(2,1)S(1)}, bf16[352,1024]{1,0:T(8,128)(2,1)S(1)}, u32[]{:S(2)}, u32[]{:S(2)}) collective-permute-start(bf16[352,1024]{1,0:T(8,128)(2,1)S(1)} %copy-done.33), channel_id=1, source_target_pairs={{0,1},{1,0},{2,3},{3,2},{4,5},{5,4},{6,7},{7,6},{8,9},{9,8},{10,11... | collective-permute-start | bytes 2162696 | tf_op jit(solution)/shard_map/ppermute | solution.py:20
  281.2 19.5 %collective-permute-start.23 = (bf16[176,1024]{1,0:T(8,128)(2,1)}, bf16[176,1024]{1,0:T(8,128)(2,1)S(1)}, u32[]{:S(2)}, u32[]{:S(2)}) collective-permute-start(bf16[176,1024]{1,0:T(8,128)(2,1)} %get-tuple-element.217), channel_id=1, source_target_pairs={{0,4},{4,0},{1,5},{5,1},{2,6},{6,2},{3,7},{7,3},{8,12},{12,8},{9,1... | collective-permute-start | bytes 1081352 | tf_op jit(solution)/shard_map/ppermute | solution.py:20
  281.8 20.0 %collective-permute-start.24 = (bf16[176,1024]{1,0:T(8,128)(2,1)}, bf16[176,1024]{1,0:T(8,128)(2,1)S(1)}, u32[]{:S(2)}, u32[]{:S(2)}) collective-permute-start(bf16[176,1024]{1,0:T(8,128)(2,1)} %get-tuple-element.219), channel_id=1, source_target_pairs={{0,1},{1,0},{2,3},{3,2},{4,5},{5,4},{6,7},{7,6},{8,9},{9,8},{10,11... | collective-permute-start | bytes 1081352 | tf_op jit(solution)/shard_map/ppermute | solution.py:20
  313.6 7.0 %collective-permute-start.25 = (f32[8,256]{1,0:T(8,128)}, f32[8,256]{1,0:T(8,128)S(1)}, u32[]{:S(2)}, u32[]{:S(2)}) collective-permute-start(f32[8,256]{1,0:T(8,128)} %get-tuple-element.223.refs_6_), channel_id=1, source_target_pairs={{0,1},{1,0},{2,3},{3,2},{4,5},{5,4},{6,7},{7,6},{8,9},{9,8},{10,11... | collective-permute-start | bytes 24584 | tf_op jit(solution)/shard_map/ppermute | solution.py:20
  320.7 17.5 %collective-permute-start.28 = (bf16[128,1024]{1,0:T(8,128)(2,1)}, bf16[128,1024]{1,0:T(8,128)(2,1)S(1)}, u32[]{:S(2)}, u32[]{:S(2)}) collective-permute-start(bf16[128,1024]{1,0:T(8,128)(2,1)} %get-tuple-element.236), channel_id=1, source_target_pairs={{0,1},{1,0},{2,3},{3,2},{4,5},{5,4},{6,7},{7,6},{8,9},{9,8},{10,11... | collective-permute-start | bytes 786440 | tf_op jit(solution)/shard_map/ppermute | solution.py:20
  321.9 16.2 %collective-permute-start.29 = (bf16[128,1024]{1,0:T(8,128)(2,1)}, bf16[128,1024]{1,0:T(8,128)(2,1)S(1)}, u32[]{:S(2)}, u32[]{:S(2)}) collective-permute-start(bf16[128,1024]{1,0:T(8,128)(2,1)} %get-tuple-element.237), channel_id=1, source_target_pairs={{0,4},{4,0},{1,5},{5,1},{2,6},{6,2},{3,7},{7,3},{8,12},{12,8},{9,1... | collective-permute-start | bytes 786440 | tf_op jit(solution)/shard_map/ppermute | solution.py:20
  322.5 15.6 %collective-permute-start.30 = (bf16[128,1024]{1,0:T(8,128)(2,1)}, bf16[128,1024]{1,0:T(8,128)(2,1)S(1)}, u32[]{:S(2)}, u32[]{:S(2)}) collective-permute-start(bf16[128,1024]{1,0:T(8,128)(2,1)} %get-tuple-element.238), channel_id=1, source_target_pairs={{0,5},{1,4},{4,1},{5,0},{2,7},{3,6},{6,3},{7,2},{8,13},{9,12},{12,... | collective-permute-start | bytes 786440 | tf_op jit(solution)/shard_map/ppermute | solution.py:851
  324.2 69.8 %all-to-all-start.3 = ((bf16[8,1056,128]{2,1,0:T(8,128)(2,1)}), bf16[8,1056,128]{2,1,0:T(8,128)(2,1)S(1)}, u32[]{:S(2)}, u32[]{:S(2)}) async-start(bf16[8,1056,128]{2,1,0:T(8,128)(2,1)} %shard_map.251), calls=%async_computation.6 | async-start | bytes 4325376 | tf_op jit(solution)/shard_map/all_to_all | solution.py:647
  328.3 101.7 %reduce-scatter.8.cloned.1.call-start = ((), (), s32[]{:S(2)}) async-start(), calls=%async_computation.12 | async-start | bytes 2359296 | tf_op jit(solution)/shard_map/reduce_scatter | solution.py:594
  343.9 38.2 %collective-permute-start.31 = (bf16[1024,384]{1,0:T(8,128)(2,1)}, bf16[1024,384]{1,0:T(8,128)(2,1)S(1)}, u32[]{:S(2)}, u32[]{:S(2)}) collective-permute-start(bf16[1024,384]{1,0:T(8,128)(2,1)} %get-tuple-element.241), channel_id=1, source_target_pairs={{0,1},{1,0},{2,3},{3,2},{4,5},{5,4},{6,7},{7,6},{8,9},{9,8},{10,11... | collective-permute-start | bytes 2359304 | tf_op jit(solution)/shard_map/ppermute | solution.py:20
  345.3 36.8 %collective-permute-start.32 = (bf16[1024,384]{1,0:T(8,128)(2,1)}, bf16[1024,384]{1,0:T(8,128)(2,1)}, u32[]{:S(2)}, u32[]{:S(2)}) collective-permute-start(bf16[1024,384]{1,0:T(8,128)(2,1)} %get-tuple-element.242), channel_id=1, source_target_pairs={{0,4},{4,0},{1,5},{5,1},{2,6},{6,2},{3,7},{7,3},{8,12},{12,8},{9,1... | collective-permute-start | bytes 2359304 | tf_op jit(solution)/shard_map/ppermute | solution.py:20
  345.8 36.4 %collective-permute-start.33 = (bf16[1024,384]{1,0:T(8,128)(2,1)}, bf16[1024,384]{1,0:T(8,128)(2,1)}, u32[]{:S(2)}, u32[]{:S(2)}) collective-permute-start(bf16[1024,384]{1,0:T(8,128)(2,1)} %get-tuple-element.243), channel_id=1, source_target_pairs={{0,5},{1,4},{4,1},{5,0},{2,7},{3,6},{6,3},{7,2},{8,13},{9,12},{12,... | collective-permute-start | bytes 2359304 | tf_op jit(solution)/shard_map/ppermute | solution.py:888
  348.7 33.5 %collective-permute-start.34 = (f32[128]{0:T(128)S(1)}, f32[128]{0:T(128)S(1)}, u32[]{:S(2)}, u32[]{:S(2)}) collective-permute-start(f32[128]{0:T(128)S(1)} %fusion.9), channel_id=1, source_target_pairs={{0,4},{4,0},{1,5},{5,1},{2,6},{6,2},{3,7},{7,3},{8,12},{12,8},{9,1... | collective-permute-start | bytes 1544 | tf_op jit(solution)/shard_map/ppermute | solution.py:20
  349.7 37.3 %collective-permute-start.45 = (bf16[128,1024]{1,0:T(8,128)(2,1)S(1)}, bf16[128,1024]{1,0:T(8,128)(2,1)S(1)}, u32[]{:S(2)}, u32[]{:S(2)}) collective-permute-start(bf16[128,1024]{1,0:T(8,128)(2,1)S(1)} %add_convert_fusion), channel_id=1, source_target_pairs={{0,1},{1,0},{2,3},{3,2},{4,5},{5,4},{6,7},{7,6},{8,9},{9,8},{10,11... | collective-permute-start | bytes 786440 | tf_op jit(solution)/shard_map/ppermute | solution.py:20
  389.0 16.2 %collective-permute-start.36 = (bf16[2,128,384]{2,1,0:T(8,128)(2,1)S(1)}, bf16[2,128,384]{2,1,0:T(8,128)(2,1)S(1)}, u32[]{:S(2)}, u32[]{:S(2)}) collective-permute-start(bf16[2,128,384]{2,1,0:T(8,128)(2,1)S(1)} %get-tuple-element.281), channel_id=1, source_target_pairs={{0,8},{8,0},{16,24},{24,16},{1,9},{9,1},{17,25},{25,17},{2,10},{10... | collective-permute-start | bytes 589832 | tf_op jit(solution)/shard_map/ppermute | solution.py:900
  390.5 16.2 %collective-permute-start.37 = (bf16[2,128,384]{2,1,0:T(8,128)(2,1)S(1)}, bf16[2,128,384]{2,1,0:T(8,128)(2,1)S(1)}, u32[]{:S(2)}, u32[]{:S(2)}) collective-permute-start(bf16[2,128,384]{2,1,0:T(8,128)(2,1)S(1)} %get-tuple-element.280), channel_id=1, source_target_pairs={{0,16},{8,24},{16,0},{24,8},{1,17},{9,25},{17,1},{25,9},{2,18},{10... | collective-permute-start | bytes 589832 | tf_op jit(solution)/shard_map/ppermute | solution.py:900
  393.4 11.2 %collective-permute-start.39 = (f32[128]{0:T(128)S(1)}, f32[128]{0:T(128)S(1)}, u32[]{:S(2)}, u32[]{:S(2)}) collective-permute-start(f32[128]{0:T(128)S(1)} %fusion.8), channel_id=1, source_target_pairs={{0,1},{1,0},{2,3},{3,2},{4,5},{5,4},{6,7},{7,6},{8,9},{9,8},{10,11... | collective-permute-start | bytes 1544 | tf_op jit(solution)/shard_map/ppermute | solution.py:20
  404.2 7.5 %collective-permute-start.38 = (bf16[2,128,384]{2,1,0:T(8,128)(2,1)S(1)}, bf16[2,128,384]{2,1,0:T(8,128)(2,1)S(1)}, u32[]{:S(2)}, u32[]{:S(2)}) collective-permute-start(bf16[2,128,384]{2,1,0:T(8,128)(2,1)S(1)} %copy-done.39), channel_id=1, source_target_pairs={{0,24},{8,16},{16,8},{24,0},{1,25},{9,17},{17,9},{25,1},{2,26},{10... | collective-permute-start | bytes 589832 | tf_op jit(solution)/shard_map/ppermute | solution.py:900
  404.5 8.5 %collective-permute-start.41 = (bf16[2,128,384]{2,1,0:T(8,128)(2,1)S(1)}, bf16[2,128,384]{2,1,0:T(8,128)(2,1)S(1)}, u32[]{:S(2)}, u32[]{:S(2)}) collective-permute-start(bf16[2,128,384]{2,1,0:T(8,128)(2,1)S(1)} %get-tuple-element.282.refs_1_), channel_id=1, source_target_pairs={{0,1},{1,0},{2,3},{3,2},{4,5},{5,4},{6,7},{7,6},{8,9},{9,8},{10,11... | collective-permute-start | bytes 589832 | tf_op jit(solution)/shard_map/ppermute | solution.py:20
  405.2 11.4 %collective-permute-start.42 = (bf16[2,128,384]{2,1,0:T(8,128)(2,1)S(1)}, bf16[2,128,384]{2,1,0:T(8,128)(2,1)S(1)}, u32[]{:S(2)}, u32[]{:S(2)}) collective-permute-start(bf16[2,128,384]{2,1,0:T(8,128)(2,1)S(1)} %collective-permute-done.36.refs_2_), channel_id=1, source_target_pairs={{0,1},{1,0},{2,3},{3,2},{4,5},{5,4},{6,7},{7,6},{8,9},{9,8},{10,11... | collective-permute-start | bytes 589832 | tf_op jit(solution)/shard_map/ppermute | solution.py:20
  406.6 14.0 %collective-permute-start.43 = (bf16[2,128,384]{2,1,0:T(8,128)(2,1)S(1)}, bf16[2,128,384]{2,1,0:T(8,128)(2,1)S(1)}, u32[]{:S(2)}, u32[]{:S(2)}) collective-permute-start(bf16[2,128,384]{2,1,0:T(8,128)(2,1)S(1)} %collective-permute-done.37.refs_3_), channel_id=1, source_target_pairs={{0,1},{1,0},{2,3},{3,2},{4,5},{5,4},{6,7},{7,6},{8,9},{9,8},{10,11... | collective-permute-start | bytes 589832 | tf_op jit(solution)/shard_map/ppermute | solution.py:20
  411.8 11.0 %collective-permute-start.44 = (bf16[2,128,384]{2,1,0:T(8,128)(2,1)S(1)}, bf16[2,128,384]{2,1,0:T(8,128)(2,1)S(1)}, u32[]{:S(2)}, u32[]{:S(2)}) collective-permute-start(bf16[2,128,384]{2,1,0:T(8,128)(2,1)S(1)} %collective-permute-done.38.refs_4_), channel_id=1, source_target_pairs={{0,1},{1,0},{2,3},{3,2},{4,5},{5,4},{6,7},{7,6},{8,9},{9,8},{10,11... | collective-permute-start | bytes 589832 | tf_op jit(solution)/shard_map/ppermute | solution.py:20
  (50 other events, 268.8 us)
Sparse Core Ops, SparseCore 0:
  38.8 46.2 all-gather.3
  110.9 49.1 reduce-scatter.3
  166.4 31.2 all-gather.5
  217.9 50.6 reduce-scatter.5
  275.9 30.2 all-gather.7
  344.1 59.9 reduce-scatter.7

commit v8 on v7

--- a/solution.py
+++ b/solution.py
@@ -173,7 +173,7 @@
                 mine[k][1] = jnp.zeros(theirs.shape[1:], BF)
 
 
-def mixer_grads_kernel(at_ref, *refs):
+def mixer_grads_kernel(copies, at_ref, *refs):
     mine, theirs, refs = refs[:Z], refs[Z : 2 * Z], refs[2 * Z :]
     w_in, w_forget, w_gate, grad_in, grad_forget, grad_gate, along_ref = refs
     x, z, c = at_ref[0], at_ref[1], at_ref[2]
@@ -195,6 +195,7 @@
                     g_ref[:, to] = piece
                     weight = w_ref[:, to].astype(F32)
                     total = total + jnp.sum(piece * weight, axis=1, keepdims=True)
+        copies.flush(m)
     along_ref[...] = jnp.broadcast_to(total, along_ref.shape)
 
 
@@ -387,7 +388,7 @@
         copies.flush(3 * k, 3 * k + 1, 3 * k + 2)
 
 
-def glu_weights_kernel(parts, terms, *refs):
+def glu_weights_kernel(parts, terms, copies, *refs):
     count = len(terms)
     lefts, rights, outs = refs[: 2 * count], refs[2 * count : 2 * count + max(terms) + 1], None
     outs = refs[2 * count + max(terms) + 1 :]
@@ -406,6 +407,8 @@
                 upper, lower = outs[k], outs[2 + d]
                 if begin < cut:
                     upper[d, begin : min(end, cut)] = value[: min(end, cut) - begin]
+                if d == parts - 1 and cut <= end and begin < cut:
+                    copies.flush(k)
                 if end > cut:
                     lower[k, max(begin, cut) - cut : end - cut] = value[max(begin, cut) - begin :]
 
@@ -493,12 +496,13 @@
         first[:, j * LANES : (j + 1) * LANES] = last[2 * j]
 
 
-def mixer_weights_kernel(parts, normed, *refs):
+def mixer_weights_kernel(parts, copies, normed, *refs):
     d_raw, outs = refs[:parts], refs[parts:]
     deep = normed.shape[1] // parts
     for d in range(parts):
         for k in range(parts):
             outs[d * parts + k][...] = contract_rows(normed[:, d * deep : (d + 1) * deep], d_raw[k][...]).astype(BF)
+            copies.flush(d * parts + k)
 
 
 def out_weights_kernel(y_ref, x_ref, mixed, d_mixed, *refs):
@@ -782,6 +786,7 @@
             shapes = [((2, height // 2, width // 2), BF)] * 4
         return call(
             functools.partial(glu_weights_kernel, parts, terms), shapes, *lefts, *rights,
+            late=len(lefts) + len(rights),
         )
 
     def first_swaps(pieces):
@@ -867,7 +872,7 @@
     pieces = call(
         functools.partial(mixer_weights_kernel, parts),
         [((width // parts, 3 * feats // parts), BF)] * parts**2,
-        normed, *d_raw,
+        normed, *d_raw, late=1 + parts,
     )
     (partial,) = call(
         functools.partial(d_normed_kernel, parts), [((group, width), BF)],
@@ -934,7 +939,7 @@
     if pair:
         grad_in, grad_forget, grad_gate, grad_attn = call(
             mixer_grads_kernel, [square] * 3 + [((sub, LANES), F32)],
-            jnp.concatenate([near_x, z_c]), *mixer_grad, w_in, w_forget, w_gate, smem=1,
+            jnp.concatenate([near_x, z_c]), *mixer_grad, w_in, w_forget, w_gate, smem=1, late=2 * Z + 3,
         )
         grad_attn = grad_attn[:, 0]
     else:

time: 449 us -> 449 us (level)
  no operation moved by 1% of the time
where the time goes in v8:
time: 449 us; the launch traced here: 442 us
  waiting for transfers between devices  197 us (44%)
  Pallas kernels  122 us (27%)
  starting transfers between devices  68.9 us (15%)
  local copies, waits for them, and re-layouts  22.7 us (5%)
  other arithmetic  16.8 us (4%)
  between operations  15.4 us (3%)
    ppermute x38, waiting for transfers between devices, swap(): return lax.ppermute(value, axis, [(0, 1), (1, 0)])  127 us
    pallas_call x25, Pallas kernels, call(): pl.pallas_call(body, out_shape=shapes, in_specs=[pl.BlockSpec(memory_spac...  122 us
    ppermute x38, starting transfers between devices, swap(): return lax.ppermute(value, axis, [(0, 1), (1, 0)])  39.1 us
    all_gather x3, waiting for transfers between devices, gather_rows(): return lax.all_gather(own, ('z', 'c'), axis=0, tiled=True)  37.1 us
    all_to_all x1, waiting for transfers between devices, per_device(): lax.all_to_all(jnp.broadcast_to(after(grad_y, glu)[None], (Z, rows, width...  13.4 us
    all_to_all x3, starting transfers between devices, spread(): return lax.all_to_all(value, ('z', 'c'), 0, 0, tiled=True)  12.7 us
    all_to_all x3, waiting for transfers between devices, spread(): return lax.all_to_all(value, ('z', 'c'), 0, 0, tiled=True)  11.7 us
  transfers between devices with their start and end apart: 56, of which 27 were waited for; matrix products, arithmetic and copies ran while one was open for 8% of the time, Pallas kernels for 20%

profile of v8, /device:TPU:0, one launch (start us, length us, event | category | flops | bytes accessed | tf_op | source)
XLA Modules:
  0.0 442.3 jit_solution(8815901760091802826)
XLA Ops:
  7.2 3.0 collective-permute-start.1
  10.2 2.5 shard_map.238
  12.8 4.9 %all-to-all-start = ((bf16[8,128,384]{2,1,0:T(8,128)(2,1)}), bf16[8,128,384]{2,1,0:T(8,128)(2,1)S(1)}, u32[]{:S(2)}, u32[]{:S(2)}) async-start(bf16[8,128,384]{2,1,0:T(8,128)(2,1)} %shard_map.238), calls=%async_computation | async-start | bytes 1572864 | tf_op jit(solution)/shard_map/all_to_all | solution.py:651
  18.4 4.0 shard_map.239
  25.9 2.4 shard_map.240.refs_9_.refs_1_
  28.3 10.4 %all-to-all-done = bf16[8,128,384]{2,1,0:T(8,128)(2,1)S(1)} async-done(((bf16[8,128,384]{2,1,0:T(8,128)(2,1)}), bf16[8,128,384]{2,1,0:T(8,128)(2,1)S(1)}, u32[]{:S(2)}, u32[]{:S(2)}) %all-to-all-start) | async-done | bytes 786464 | tf_op jit(solution)/shard_map/all_to_all | solution.py:651
  38.7 3.7 all-to-all-start.1
  47.9 37.1 %all-gather.4.cloned.1.call-done.refs_2_ = bf16[512,2176]{1,0:T(8,128)(2,1)} async-done(((bf16[64,2176]{1,0:T(8,128)(2,1)}), bf16[512,2176]{1,0:T(8,128)(2,1)}) %all-gather.4.cloned.1.call-update) | async-done | bytes 2228240 | tf_op jit(solution)/shard_map/all_gather | solution.py:594
  86.4 9.4 %shard_map.241 = (bf16[512,2048]{1,0:T(8,128)(2,1)}, f32[512,768]{1,0:T(8,128)}, f32[2,512,128]{2,1,0:T(8,128)}, f32[2,512,128]{2,1,0:T(8,128)}, f32[2,512,128]{2,1,0:T(8,128)}, /*index=5*/f32[16,256]{1,0:T(8,128)}) custom-call(s32[1]{0:T(128)} %bitcast.2.refs_0_.refs_1_, f32[1,2048]{1,0:T(1,128)} %pad_maximum_fusion.5.refs_1_.refs_3_, ...), custom_call_target="tpu_custom_call" | custom-call | bytes 1024 | tf_op jit(solution)/shard_map/pallas_call | solution.py:87
  101.3 2.6 collective-permute-done.7.refs_4_.refs_5_
  104.5 4.9 %shard_map.242 = (f32[2,512,128]{2,1,0:T(8,128)}, f32[8,256]{1,0:T(8,128)}, bf16[512,2176]{1,0:T(8,128)(2,1)}) custom-call(s32[34]{0:T(128)} %pad_add_fusion.refs_0_.refs_1_, f32[16,256]{1,0:T(8,128)} %get-tuple-element.168.refs_1_.refs_2_, f32[16,256]{1,0:T(8,128)} %copy-done.24, f32[16,256]{1,0:T(8,128)} %copy-done.25, f32[16,256]{1,0:T(8,128)} %copy-done.26, ...), custom_call_target="tpu_custom_call" | custom-call | bytes 1024 | tf_op jit(solution)/shard_map/pallas_call | solution.py:87
  115.8 2.0 broadcast_in_dim.22
  117.9 5.4 %all-to-all-start.2 = ((bf16[4,64,2048]{2,1,0:T(8,128)(2,1)}), bf16[4,64,2048]{2,1,0:T(8,128)(2,1)S(1)}, u32[]{:S(2)}, u32[]{:S(2)}) async-start(bf16[4,64,2048]{2,1,0:T(8,128)(2,1)} %broadcast_in_dim.22), calls=%async_computation.3 | async-start | bytes 2097152 | tf_op jit(solution)/shard_map/all_to_all | solution.py:764
  124.2 21.2 %collective-permute-done.8 = bf16[8,704,128]{2,1,0:T(8,128)(2,1)} collective-permute-done((bf16[8,704,128]{2,1,0:T(8,128)(2,1)}, bf16[8,704,128]{2,1,0:T(8,128)(2,1)}, u32[]{:S(2)}, u32[]{:S(2)}) %collective-permute-start.8) | collective-permute-done | bytes 1441824 | tf_op jit(solution)/shard_map/ppermute | solution.py:20
  148.2 13.4 %all-to-all-done.2 = bf16[4,64,2048]{2,1,0:T(8,128)(2,1)S(1)} async-done(((bf16[4,64,2048]{2,1,0:T(8,128)(2,1)}), bf16[4,64,2048]{2,1,0:T(8,128)(2,1)S(1)}, u32[]{:S(2)}, u32[]{:S(2)}) %all-to-all-start.2) | async-done | bytes 1048608 | tf_op jit(solution)/shard_map/all_to_all | solution.py:764
  163.5 2.7 shard_map.244
  175.4 1.9 pad_maximum_fusion.refs_2_
  178.9 2.2 collective-permute-start.12
  182.2 5.3 %collective-permute-done.13 = bf16[8,352,128]{2,1,0:T(8,128)(2,1)S(1)} collective-permute-done((bf16[8,352,128]{2,1,0:T(8,128)(2,1)S(1)}, bf16[8,352,128]{2,1,0:T(8,128)(2,1)S(1)}, u32[]{:S(2)}, u32[]{:S(2)}) %collective-permute-start.13) | collective-permute-done | bytes 720928 | tf_op jit(solution)/shard_map/ppermute | solution.py:20
  198.0 19.7 %shard_map.245 = (bf16[512,352]{1,0:T(8,128)(2,1)}, bf16[512,352]{1,0:T(8,128)(2,1)}, bf16[512,352]{1,0:T(8,128)(2,1)}, bf16[512,352]{1,0:T(8,128)(2,1)}, bf16[5...) custom-call(bf16[512,2048]{1,0:T(8,128)(2,1)} %all-gather.6.cloned.1.call-done.refs_0_.refs_4_, ...), custom_call_target="tpu_custom_call" | custom-call | bytes 1024 | tf_op jit(solution)/shard_map/pallas_call | solution.py:87
  217.8 6.7 %shard_map.246 = (bf16[2,352,1024]{2,1,0:T(8,128)(2,1)}, bf16[2,352,1024]{2,1,0:T(8,128)(2,1)}, bf16[2,352,1024]{2,1,0:T(8,128)(2,1)}, bf16[2,352,1024]{2,1,0:T(8,128)(2,1)}) custom-call(bf16[512,352]{1,0:T(8,128)(2,1)} %get-tuple-element.184.refs_0_, bf16[512,352]{1,0:T(8,128)(2,1)} %get-tuple-element.185.refs_1_, ...), custom_call_target="tpu_custom_call" | custom-call | bytes 1024 | tf_op jit(solution)/shard_map/pallas_call | solution.py:87
  224.5 2.2 collective-permute-start.17
  228.3 5.0 %shard_map.249 = (bf16[2,176,1024]{2,1,0:T(8,128)(2,1)}, bf16[2,176,1024]{2,1,0:T(8,128)(2,1)}, bf16[2,176,1024]{2,1,0:T(8,128)(2,1)}, bf16[2,176,1024]{2,1,0:T(8,128)(2,1)}) custom-call(bf16[512,352]{1,0:T(8,128)(2,1)} %get-tuple-element.201.refs_0_, bf16[512,352]{1,0:T(8,128)(2,1)} %get-tuple-element.202.refs_1_, bf16[512,2048]{1,0:T(8,128)(2,1)} %bitcast.85), custom_call_target="tpu_custom_call" | custom-call | bytes 1024 | tf_op jit(solution)/shard_map/pallas_call | solution.py:87
  233.8 25.5 %collective-permute-done.17.refs_1_ = bf16[2,352,1024]{2,1,0:T(8,128)(2,1)S(1)} collective-permute-done((bf16[2,352,1024]{2,1,0:T(8,128)(2,1)}, bf16[2,352,1024]{2,1,0:T(8,128)(2,1)S(1)}, u32[]{:S(2)}, u32[]{:S(2)}) %collective-permute-start.17) | collective-permute-done | bytes 1441824 | tf_op jit(solution)/shard_map/ppermute | solution.py:20
  259.3 2.0 collective-permute-done.18.refs_3_
  262.5 5.0 %shard_map.247 = (f32[352,1024]{1,0:T(8,128)}, bf16[352,1024]{1,0:T(8,128)(2,1)}, f32[352,1024]{1,0:T(8,128)}, bf16[352,1024]{1,0:T(8,128)(2,1)}) custom-call(bf16[2,352,1024]{2,1,0:T(8,128)(2,1)} %get-tuple-element.188.refs_0_, bf16[2,352,1024]{2,1,0:T(8,128)(2,1)} %copy-done.4, bf16[2,352,1024]{2,1,0:T(8,128)(2,1)} %get-tuple-element.190.refs_2_, ...), custom_call_target="tpu_custom_call" | custom-call | bytes 1024 | tf_op jit(solution)/shard_map/pallas_call | solution.py:87
  268.6 3.7 shard_map.248
  272.3 2.4 collective-permute-done.19.refs_1_
  278.0 3.2 shard_map.250
  283.2 17.5 %collective-permute-done.23.refs_5_ = bf16[176,1024]{1,0:T(8,128)(2,1)S(1)} collective-permute-done((bf16[176,1024]{1,0:T(8,128)(2,1)}, bf16[176,1024]{1,0:T(8,128)(2,1)S(1)}, u32[]{:S(2)}, u32[]{:S(2)}) %collective-permute-start.23) | collective-permute-done | bytes 360480 | tf_op jit(solution)/shard_map/ppermute | solution.py:20
  303.1 4.8 %shard_map.251 = bf16[8,1056,128]{2,1,0:T(8,128)(2,1)} custom-call(f32[352,1024]{1,0:T(8,128)} %get-tuple-element.208.refs_0_, bf16[352,1024]{1,0:T(8,128)(2,1)} %copy-done.9, f32[352,1024]{1,0:T(8,128)} %get-tuple-element.210.refs_2_, bf16[352,1024]{1,0:T(8,128)(2,1)} %copy-done.10, f32[176,1024]{1,0:T(8,128)} %get-tuple-element.216.refs_4_, ...), custom_call_target="tpu_custom_call" | custom-call | bytes 1024 | tf_op jit(solution)/shard_map/pallas_call | solution.py:87
  307.9 5.7 %shard_map.252 = (bf16[512,256]{1,0:T(8,128)(2,1)}, bf16[512,256]{1,0:T(8,128)(2,1)}, f32[2,512,128]{2,1,0:T(8,128)}, f32[2,512,128]{2,1,0:T(8,128)}, f32[8,256]{1,0:T(8,128)}) custom-call(bf16[512,2176]{1,0:T(8,128)(2,1)} %all-gather.8.cloned.1.call-done.refs_0_.refs_3_, bf16[256,2048]{1,0:T(8,128)(2,1)} %shard_map.240.refs_9_.refs_1_, ...), custom_call_target="tpu_custom_call" | custom-call | bytes 1024 | tf_op jit(solution)/shard_map/pallas_call | solution.py:87
  317.1 3.5 shard_map.254
  324.2 4.1 all-to-all-start.3
  328.6 4.4 shard_map.253
  333.0 5.1 %shard_map.255 = (bf16[1024,384]{1,0:T(8,128)(2,1)}, bf16[1024,384]{1,0:T(8,128)(2,1)}, bf16[1024,384]{1,0:T(8,128)(2,1)}, bf16[1024,384]{1,0:T(8,128)(2,1)}) custom-call(bf16[512,2048]{1,0:T(8,128)(2,1)} %get-tuple-element.239.refs_0_, bf16[512,384]{1,0:T(8,128)(2,1)} %get-tuple-element.244.refs_1_.refs_0_, bf16[512,384]{1,0:T(8,128)(2,1)} %get-tuple-element.245.refs_2_.refs_1_), custom_call_target="tpu_custom_call" | custom-call | bytes 1024 | tf_op jit(solution)/shard_map/pallas_call | solution.py:87
  338.3 5.6 %shard_map.256 = bf16[512,2048]{1,0:T(8,128)(2,1)} custom-call(bf16[512,384]{1,0:T(8,128)(2,1)} %get-tuple-element.244.refs_1_.refs_0_, bf16[512,384]{1,0:T(8,128)(2,1)} %get-tuple-element.245.refs_2_.refs_1_, bf16[1024,384]{1,0:T(8,128)(2,1)} %bitcast.90, bf16[1024,384]{1,0:T(8,128)(2,1)} %collective-permute-done.2.refs_6_.refs_3_, ...), custom_call_target="tpu_custom_call" | custom-call | bytes 1024 | tf_op jit(solution)/shard_map/pallas_call | solution.py:87
  350.4 31.7 %collective-permute-done.34 = f32[128]{0:T(128)S(1)} collective-permute-done((f32[128]{0:T(128)S(1)}, f32[128]{0:T(128)S(1)}, u32[]{:S(2)}, u32[]{:S(2)}) %collective-permute-start.34) | collective-permute-done | bytes 544 | tf_op jit(solution)/shard_map/ppermute | solution.py:20
  383.0 3.8 shard_map.259
  390.5 2.4 collective-permute-start.37
  395.4 6.2 %shard_map.260 = (f32[128,2816]{1,0:T(8,128)}, f32[128,2816]{1,0:T(8,128)}, f32[2816,128]{1,0:T(8,128)}, f32[128,128]{1,0:T(8,128)}) custom-call(bf16[8,1056,128]{2,1,0:T(8,128)(2,1)} %copy-done, bf16[128,2816]{1,0:T(8,128)(2,1)} %refs_1_.9, bf16[128,2816]{1,0:T(8,128)(2,1)} %refs_2_.7), custom_call_target="tpu_custom_call" | custom-call | bytes 1024 | tf_op jit(solution)/shard_map/pallas_call | solution.py:87
  407.8 3.9 collective-permute-done.38.refs_4_
  413.0 3.6 collective-permute-done.42.refs_6_
  416.6 4.0 collective-permute-done.43.refs_7_
  420.6 2.1 collective-permute-done.44.refs_8_
  423.4 5.1 %shard_map.261 = (f32[128,2048]{1,0:T(8,128)}, f32[128,2048]{1,0:T(8,128)}, f32[128,2048]{1,0:T(8,128)}, f32[128,128]{1,0:T(8,128)}) custom-call(s32[3]{0:T(128)} %pad_add_fusion.1.refs_0_, bf16[2,128,384]{2,1,0:T(8,128)(2,1)} %copy-done.21, bf16[2,128,384]{2,1,0:T(8,128)(2,1)} %copy-done.14, bf16[2,128,384]{2,1,0:T(8,128)(2,1)} %copy-done.15, ...), custom_call_target="tpu_custom_call" | custom-call | bytes 1024 | tf_op jit(solution)/shard_map/pallas_call | solution.py:87
  430.0 2.9 shard_map.257.refs_2_
  432.9 2.1 shard_map.258
  (245 shorter events, 94.2 us)
Async XLA Ops:
  7.2 17.6 %collective-permute-start.1 = (bf16[128,2048]{1,0:T(8,128)(2,1)}, bf16[128,2048]{1,0:T(8,128)(2,1)S(1)}, u32[]{:S(2)}, u32[]{:S(2)}) collective-permute-start(bf16[128,2048]{1,0:T(8,128)(2,1)} %param.27), channel_id=1, source_target_pairs={{0,4},{4,0},{1,5},{5,1},{2,6},{6,2},{3,7},{7,3},{8,12},{12,8},{9,1... | collective-permute-start | bytes 1572872 | tf_op jit(solution)/shard_map/ppermute | solution.py:20
  12.8 25.9 %all-to-all-start = ((bf16[8,128,384]{2,1,0:T(8,128)(2,1)}), bf16[8,128,384]{2,1,0:T(8,128)(2,1)S(1)}, u32[]{:S(2)}, u32[]{:S(2)}) async-start(bf16[8,128,384]{2,1,0:T(8,128)(2,1)} %shard_map.238), calls=%async_computation | async-start | bytes 1572864 | tf_op jit(solution)/shard_map/all_to_all | solution.py:651
  17.6 67.4 %all-gather.4.cloned.1.call-start = ((), (), s32[]{:S(2)}) async-start(), calls=%async_computation.7 | async-start | bytes 2506752 | tf_op jit(solution)/shard_map/all_gather | solution.py:594
  38.7 72.1 %all-to-all-start.1 = ((bf16[8,1056,128]{2,1,0:T(8,128)(2,1)}), bf16[8,1056,128]{2,1,0:T(8,128)(2,1)S(1)}, u32[]{:S(2)}, u32[]{:S(2)}) async-start(bf16[8,1056,128]{2,1,0:T(8,128)(2,1)} %shard_map.239), calls=%async_computation.1 | async-start | bytes 4325376 | tf_op jit(solution)/shard_map/all_to_all | solution.py:651
  42.4 121.1 %reduce-scatter.4.cloned.1.call-start = ((), (), s32[]{:S(2)}) async-start(), calls=%async_computation.8 | async-start | bytes 2506752 | tf_op jit(solution)/shard_map/reduce_scatter | solution.py:598
  43.8 42.6 %collective-permute-start.2 = (bf16[1024,384]{1,0:T(8,128)(2,1)S(1)}, bf16[1024,384]{1,0:T(8,128)(2,1)}, u32[]{:S(2)}, u32[]{:S(2)}) collective-permute-start(bf16[1024,384]{1,0:T(8,128)(2,1)S(1)} %bitcast.86), channel_id=1, source_target_pairs={{0,1},{1,0},{2,3},{3,2},{4,5},{5,4},{6,7},{7,6},{8,9},{9,8},{10,11... | collective-permute-start | bytes 2359304 | tf_op jit(solution)/shard_map/ppermute | solution.py:20
  45.3 41.1 %collective-permute-start.3 = (bf16[1024,384]{1,0:T(8,128)(2,1)S(1)}, bf16[1024,384]{1,0:T(8,128)(2,1)}, u32[]{:S(2)}, u32[]{:S(2)}) collective-permute-start(bf16[1024,384]{1,0:T(8,128)(2,1)S(1)} %bitcast.87), channel_id=1, source_target_pairs={{0,4},{4,0},{1,5},{5,1},{2,6},{6,2},{3,7},{7,3},{8,12},{12,8},{9,1... | collective-permute-start | bytes 2359304 | tf_op jit(solution)/shard_map/ppermute | solution.py:20
  45.8 40.5 %collective-permute-start.4 = (bf16[1024,384]{1,0:T(8,128)(2,1)S(1)}, bf16[1024,384]{1,0:T(8,128)(2,1)}, u32[]{:S(2)}, u32[]{:S(2)}) collective-permute-start(bf16[1024,384]{1,0:T(8,128)(2,1)S(1)} %bitcast.88), channel_id=1, source_target_pairs={{0,5},{1,4},{4,1},{5,0},{2,7},{3,6},{6,3},{7,2},{8,13},{9,12},{12,... | collective-permute-start | bytes 2359304 | tf_op jit(solution)/shard_map/ppermute | solution.py:660
  111.9 33.4 %collective-permute-start.8 = (bf16[8,704,128]{2,1,0:T(8,128)(2,1)}, bf16[8,704,128]{2,1,0:T(8,128)(2,1)}, u32[]{:S(2)}, u32[]{:S(2)}) collective-permute-start(bf16[8,704,128]{2,1,0:T(8,128)(2,1)} %slice.180), channel_id=1, source_target_pairs={{0,1},{1,0},{2,3},{3,2},{4,5},{5,4},{6,7},{7,6},{8,9},{9,8},{10,11... | collective-permute-start | bytes 4325384 | tf_op jit(solution)/shard_map/ppermute | solution.py:20
  113.4 33.2 %collective-permute-start.9 = (bf16[8,704,128]{2,1,0:T(8,128)(2,1)}, bf16[8,704,128]{2,1,0:T(8,128)(2,1)}, u32[]{:S(2)}, u32[]{:S(2)}) collective-permute-start(bf16[8,704,128]{2,1,0:T(8,128)(2,1)} %slice.180), channel_id=1, source_target_pairs={{0,4},{4,0},{1,5},{5,1},{2,6},{6,2},{3,7},{7,3},{8,12},{12,8},{9,1... | collective-permute-start | bytes 4325384 | tf_op jit(solution)/shard_map/ppermute | solution.py:20
  117.9 43.8 %all-to-all-start.2 = ((bf16[4,64,2048]{2,1,0:T(8,128)(2,1)}), bf16[4,64,2048]{2,1,0:T(8,128)(2,1)S(1)}, u32[]{:S(2)}, u32[]{:S(2)}) async-start(bf16[4,64,2048]{2,1,0:T(8,128)(2,1)} %broadcast_in_dim.22), calls=%async_computation.3 | async-start | bytes 2097152 | tf_op jit(solution)/shard_map/all_to_all | solution.py:764
  123.3 74.8 %all-gather.6.cloned.1.call-start = ((), (), s32[]{:S(2)}) async-start(), calls=%async_computation.9 | async-start | bytes 2359296 | tf_op jit(solution)/shard_map/all_gather | solution.py:594
  146.6 16.7 %collective-permute-start.11 = (bf16[8,352,128]{2,1,0:T(8,128)(2,1)}, bf16[8,352,128]{2,1,0:T(8,128)(2,1)S(1)}, u32[]{:S(2)}, u32[]{:S(2)}) collective-permute-start(bf16[8,352,128]{2,1,0:T(8,128)(2,1)} %slice.181), channel_id=1, source_target_pairs={{0,4},{4,0},{1,5},{5,1},{2,6},{6,2},{3,7},{7,3},{8,12},{12,8},{9,1... | collective-permute-start | bytes 2162696 | tf_op jit(solution)/shard_map/ppermute | solution.py:20
  147.1 16.4 %collective-permute-start.10 = (bf16[8,352,128]{2,1,0:T(8,128)(2,1)}, bf16[8,352,128]{2,1,0:T(8,128)(2,1)S(1)}, u32[]{:S(2)}, u32[]{:S(2)}) collective-permute-start(bf16[8,352,128]{2,1,0:T(8,128)(2,1)} %slice.181), channel_id=1, source_target_pairs={{0,1},{1,0},{2,3},{3,2},{4,5},{5,4},{6,7},{7,6},{8,9},{9,8},{10,11... | collective-permute-start | bytes 2162696 | tf_op jit(solution)/shard_map/ppermute | solution.py:20
  166.2 102.3 %reduce-scatter.6.cloned.1.call-start = ((), (), s32[]{:S(2)}) async-start(), calls=%async_computation.10 | async-start | bytes 4718592 | tf_op jit(solution)/shard_map/reduce_scatter | solution.py:598
  169.2 18.4 %collective-permute-start.13 = (bf16[8,352,128]{2,1,0:T(8,128)(2,1)S(1)}, bf16[8,352,128]{2,1,0:T(8,128)(2,1)S(1)}, u32[]{:S(2)}, u32[]{:S(2)}) collective-permute-start(bf16[8,352,128]{2,1,0:T(8,128)(2,1)S(1)} %slice.184), channel_id=1, source_target_pairs={{0,1},{1,0},{2,3},{3,2},{4,5},{5,4},{6,7},{7,6},{8,9},{9,8},{10,11... | collective-permute-start | bytes 2162696 | tf_op jit(solution)/shard_map/ppermute | solution.py:20
  171.0 18.0 %collective-permute-start.14 = (bf16[8,352,128]{2,1,0:T(8,128)(2,1)S(1)}, bf16[8,352,128]{2,1,0:T(8,128)(2,1)S(1)}, u32[]{:S(2)}, u32[]{:S(2)}) collective-permute-start(bf16[8,352,128]{2,1,0:T(8,128)(2,1)S(1)} %slice.185), channel_id=1, source_target_pairs={{0,4},{4,0},{1,5},{5,1},{2,6},{6,2},{3,7},{7,3},{8,12},{12,8},{9,1... | collective-permute-start | bytes 2162696 | tf_op jit(solution)/shard_map/ppermute | solution.py:20
  178.9 13.6 %collective-permute-start.12 = (bf16[4,64,2048]{2,1,0:T(8,128)(2,1)S(1)}, bf16[4,64,2048]{2,1,0:T(8,128)(2,1)S(1)}, u32[]{:S(2)}, u32[]{:S(2)}) collective-permute-start(bf16[4,64,2048]{2,1,0:T(8,128)(2,1)S(1)} %all-to-all-done.2), channel_id=1, source_target_pairs={{0,2},{2,0},{1,3},{3,1},{4,6},{6,4},{5,7},{7,5},{8,10},{10,8},{9,1... | collective-permute-start | bytes 3145736 | tf_op jit(solution)/shard_map/ppermute | solution.py:20
  181.1 14.2 %collective-permute-start.15 = (bf16[8,176,128]{2,1,0:T(8,128)(2,1)S(1)}, bf16[8,176,128]{2,1,0:T(8,128)(2,1)S(1)}, u32[]{:S(2)}, u32[]{:S(2)}) collective-permute-start(bf16[8,176,128]{2,1,0:T(8,128)(2,1)S(1)} %slice.186), channel_id=1, source_target_pairs={{0,1},{1,0},{2,3},{3,2},{4,5},{5,4},{6,7},{7,6},{8,9},{9,8},{10,11... | collective-permute-start | bytes 1081352 | tf_op jit(solution)/shard_map/ppermute | solution.py:20
  181.6 15.2 %collective-permute-start.16 = (bf16[8,176,128]{2,1,0:T(8,128)(2,1)S(1)}, bf16[8,176,128]{2,1,0:T(8,128)(2,1)S(1)}, u32[]{:S(2)}, u32[]{:S(2)}) collective-permute-start(bf16[8,176,128]{2,1,0:T(8,128)(2,1)S(1)} %slice.187), channel_id=1, source_target_pairs={{0,4},{4,0},{1,5},{5,1},{2,6},{6,2},{3,7},{7,3},{8,12},{12,8},{9,1... | collective-permute-start | bytes 1081352 | tf_op jit(solution)/shard_map/ppermute | solution.py:20
  217.8 90.1 %all-gather.8.cloned.1.call-start = ((), (), s32[]{:S(2)}) async-start(), calls=%async_computation.11 | async-start | bytes 2506752 | tf_op jit(solution)/shard_map/all_gather | solution.py:594
  224.5 34.8 %collective-permute-start.17 = (bf16[2,352,1024]{2,1,0:T(8,128)(2,1)}, bf16[2,352,1024]{2,1,0:T(8,128)(2,1)S(1)}, u32[]{:S(2)}, u32[]{:S(2)}) collective-permute-start(bf16[2,352,1024]{2,1,0:T(8,128)(2,1)} %get-tuple-element.189), channel_id=1, source_target_pairs={{0,1},{1,0},{2,3},{3,2},{4,5},{5,4},{6,7},{7,6},{8,9},{9,8},{10,11... | collective-permute-start | bytes 4325384 | tf_op jit(solution)/shard_map/ppermute | solution.py:20
  226.7 34.7 %collective-permute-start.18 = (bf16[2,352,1024]{2,1,0:T(8,128)(2,1)}, bf16[2,352,1024]{2,1,0:T(8,128)(2,1)S(1)}, u32[]{:S(2)}, u32[]{:S(2)}) collective-permute-start(bf16[2,352,1024]{2,1,0:T(8,128)(2,1)} %get-tuple-element.191), channel_id=1, source_target_pairs={{0,4},{4,0},{1,5},{5,1},{2,6},{6,2},{3,7},{7,3},{8,12},{12,8},{9,1... | collective-permute-start | bytes 4325384 | tf_op jit(solution)/shard_map/ppermute | solution.py:20
  233.3 41.3 %collective-permute-start.19 = (bf16[2,176,1024]{2,1,0:T(8,128)(2,1)}, bf16[2,176,1024]{2,1,0:T(8,128)(2,1)S(1)}, u32[]{:S(2)}, u32[]{:S(2)}) collective-permute-start(bf16[2,176,1024]{2,1,0:T(8,128)(2,1)} %get-tuple-element.204), channel_id=1, source_target_pairs={{0,1},{1,0},{2,3},{3,2},{4,5},{5,4},{6,7},{7,6},{8,9},{9,8},{10,11... | collective-permute-start | bytes 2162696 | tf_op jit(solution)/shard_map/ppermute | solution.py:20
  233.4 42.4 %collective-permute-start.20 = (bf16[2,176,1024]{2,1,0:T(8,128)(2,1)}, bf16[2,176,1024]{2,1,0:T(8,128)(2,1)S(1)}, u32[]{:S(2)}, u32[]{:S(2)}) collective-permute-start(bf16[2,176,1024]{2,1,0:T(8,128)(2,1)} %get-tuple-element.206), channel_id=1, source_target_pairs={{0,4},{4,0},{1,5},{5,1},{2,6},{6,2},{3,7},{7,3},{8,12},{12,8},{9,1... | collective-permute-start | bytes 2162696 | tf_op jit(solution)/shard_map/ppermute | solution.py:20
  275.8 26.0 %collective-permute-start.21 = (bf16[352,1024]{1,0:T(8,128)(2,1)S(1)}, bf16[352,1024]{1,0:T(8,128)(2,1)S(1)}, u32[]{:S(2)}, u32[]{:S(2)}) collective-permute-start(bf16[352,1024]{1,0:T(8,128)(2,1)S(1)} %copy-done.34), channel_id=1, source_target_pairs={{0,4},{4,0},{1,5},{5,1},{2,6},{6,2},{3,7},{7,3},{8,12},{12,8},{9,1... | collective-permute-start | bytes 2162696 | tf_op jit(solution)/shard_map/ppermute | solution.py:20
  277.4 24.5 %collective-permute-start.22 = (bf16[352,1024]{1,0:T(8,128)(2,1)S(1)}, bf16[352,1024]{1,0:T(8,128)(2,1)S(1)}, u32[]{:S(2)}, u32[]{:S(2)}) collective-permute-start(bf16[352,1024]{1,0:T(8,128)(2,1)S(1)} %copy-done.33), channel_id=1, source_target_pairs={{0,1},{1,0},{2,3},{3,2},{4,5},{5,4},{6,7},{7,6},{8,9},{9,8},{10,11... | collective-permute-start | bytes 2162696 | tf_op jit(solution)/shard_map/ppermute | solution.py:20
  281.2 19.5 %collective-permute-start.23 = (bf16[176,1024]{1,0:T(8,128)(2,1)}, bf16[176,1024]{1,0:T(8,128)(2,1)S(1)}, u32[]{:S(2)}, u32[]{:S(2)}) collective-permute-start(bf16[176,1024]{1,0:T(8,128)(2,1)} %get-tuple-element.217), channel_id=1, source_target_pairs={{0,4},{4,0},{1,5},{5,1},{2,6},{6,2},{3,7},{7,3},{8,12},{12,8},{9,1... | collective-permute-start | bytes 1081352 | tf_op jit(solution)/shard_map/ppermute | solution.py:20
  281.8 20.0 %collective-permute-start.24 = (bf16[176,1024]{1,0:T(8,128)(2,1)}, bf16[176,1024]{1,0:T(8,128)(2,1)S(1)}, u32[]{:S(2)}, u32[]{:S(2)}) collective-permute-start(bf16[176,1024]{1,0:T(8,128)(2,1)} %get-tuple-element.219), channel_id=1, source_target_pairs={{0,1},{1,0},{2,3},{3,2},{4,5},{5,4},{6,7},{7,6},{8,9},{9,8},{10,11... | collective-permute-start | bytes 1081352 | tf_op jit(solution)/shard_map/ppermute | solution.py:20
  313.6 7.0 %collective-permute-start.25 = (f32[8,256]{1,0:T(8,128)}, f32[8,256]{1,0:T(8,128)S(1)}, u32[]{:S(2)}, u32[]{:S(2)}) collective-permute-start(f32[8,256]{1,0:T(8,128)} %get-tuple-element.223.refs_6_), channel_id=1, source_target_pairs={{0,1},{1,0},{2,3},{3,2},{4,5},{5,4},{6,7},{7,6},{8,9},{9,8},{10,11... | collective-permute-start | bytes 24584 | tf_op jit(solution)/shard_map/ppermute | solution.py:20
  320.7 17.5 %collective-permute-start.28 = (bf16[128,1024]{1,0:T(8,128)(2,1)}, bf16[128,1024]{1,0:T(8,128)(2,1)S(1)}, u32[]{:S(2)}, u32[]{:S(2)}) collective-permute-start(bf16[128,1024]{1,0:T(8,128)(2,1)} %get-tuple-element.236), channel_id=1, source_target_pairs={{0,1},{1,0},{2,3},{3,2},{4,5},{5,4},{6,7},{7,6},{8,9},{9,8},{10,11... | collective-permute-start | bytes 786440 | tf_op jit(solution)/shard_map/ppermute | solution.py:20
  321.9 16.2 %collective-permute-start.29 = (bf16[128,1024]{1,0:T(8,128)(2,1)}, bf16[128,1024]{1,0:T(8,128)(2,1)S(1)}, u32[]{:S(2)}, u32[]{:S(2)}) collective-permute-start(bf16[128,1024]{1,0:T(8,128)(2,1)} %get-tuple-element.237), channel_id=1, source_target_pairs={{0,4},{4,0},{1,5},{5,1},{2,6},{6,2},{3,7},{7,3},{8,12},{12,8},{9,1... | collective-permute-start | bytes 786440 | tf_op jit(solution)/shard_map/ppermute | solution.py:20
  322.5 15.6 %collective-permute-start.30 = (bf16[128,1024]{1,0:T(8,128)(2,1)}, bf16[128,1024]{1,0:T(8,128)(2,1)S(1)}, u32[]{:S(2)}, u32[]{:S(2)}) collective-permute-start(bf16[128,1024]{1,0:T(8,128)(2,1)} %get-tuple-element.238), channel_id=1, source_target_pairs={{0,5},{1,4},{4,1},{5,0},{2,7},{3,6},{6,3},{7,2},{8,13},{9,12},{12,... | collective-permute-start | bytes 786440 | tf_op jit(solution)/shard_map/ppermute | solution.py:856
  324.2 69.8 %all-to-all-start.3 = ((bf16[8,1056,128]{2,1,0:T(8,128)(2,1)}), bf16[8,1056,128]{2,1,0:T(8,128)(2,1)S(1)}, u32[]{:S(2)}, u32[]{:S(2)}) async-start(bf16[8,1056,128]{2,1,0:T(8,128)(2,1)} %shard_map.251), calls=%async_computation.6 | async-start | bytes 4325376 | tf_op jit(solution)/shard_map/all_to_all | solution.py:651
  328.3 101.7 %reduce-scatter.8.cloned.1.call-start = ((), (), s32[]{:S(2)}) async-start(), calls=%async_computation.12 | async-start | bytes 2359296 | tf_op jit(solution)/shard_map/reduce_scatter | solution.py:598
  343.9 38.2 %collective-permute-start.31 = (bf16[1024,384]{1,0:T(8,128)(2,1)}, bf16[1024,384]{1,0:T(8,128)(2,1)S(1)}, u32[]{:S(2)}, u32[]{:S(2)}) collective-permute-start(bf16[1024,384]{1,0:T(8,128)(2,1)} %get-tuple-element.241), channel_id=1, source_target_pairs={{0,1},{1,0},{2,3},{3,2},{4,5},{5,4},{6,7},{7,6},{8,9},{9,8},{10,11... | collective-permute-start | bytes 2359304 | tf_op jit(solution)/shard_map/ppermute | solution.py:20
  345.3 36.8 %collective-permute-start.32 = (bf16[1024,384]{1,0:T(8,128)(2,1)}, bf16[1024,384]{1,0:T(8,128)(2,1)}, u32[]{:S(2)}, u32[]{:S(2)}) collective-permute-start(bf16[1024,384]{1,0:T(8,128)(2,1)} %get-tuple-element.242), channel_id=1, source_target_pairs={{0,4},{4,0},{1,5},{5,1},{2,6},{6,2},{3,7},{7,3},{8,12},{12,8},{9,1... | collective-permute-start | bytes 2359304 | tf_op jit(solution)/shard_map/ppermute | solution.py:20
  345.8 36.4 %collective-permute-start.33 = (bf16[1024,384]{1,0:T(8,128)(2,1)}, bf16[1024,384]{1,0:T(8,128)(2,1)}, u32[]{:S(2)}, u32[]{:S(2)}) collective-permute-start(bf16[1024,384]{1,0:T(8,128)(2,1)} %get-tuple-element.243), channel_id=1, source_target_pairs={{0,5},{1,4},{4,1},{5,0},{2,7},{3,6},{6,3},{7,2},{8,13},{9,12},{12,... | collective-permute-start | bytes 2359304 | tf_op jit(solution)/shard_map/ppermute | solution.py:893
  348.7 33.5 %collective-permute-start.34 = (f32[128]{0:T(128)S(1)}, f32[128]{0:T(128)S(1)}, u32[]{:S(2)}, u32[]{:S(2)}) collective-permute-start(f32[128]{0:T(128)S(1)} %fusion.9), channel_id=1, source_target_pairs={{0,4},{4,0},{1,5},{5,1},{2,6},{6,2},{3,7},{7,3},{8,12},{12,8},{9,1... | collective-permute-start | bytes 1544 | tf_op jit(solution)/shard_map/ppermute | solution.py:20
  349.7 37.3 %collective-permute-start.45 = (bf16[128,1024]{1,0:T(8,128)(2,1)S(1)}, bf16[128,1024]{1,0:T(8,128)(2,1)S(1)}, u32[]{:S(2)}, u32[]{:S(2)}) collective-permute-start(bf16[128,1024]{1,0:T(8,128)(2,1)S(1)} %add_convert_fusion), channel_id=1, source_target_pairs={{0,1},{1,0},{2,3},{3,2},{4,5},{5,4},{6,7},{7,6},{8,9},{9,8},{10,11... | collective-permute-start | bytes 786440 | tf_op jit(solution)/shard_map/ppermute | solution.py:20
  389.0 16.2 %collective-permute-start.36 = (bf16[2,128,384]{2,1,0:T(8,128)(2,1)S(1)}, bf16[2,128,384]{2,1,0:T(8,128)(2,1)S(1)}, u32[]{:S(2)}, u32[]{:S(2)}) collective-permute-start(bf16[2,128,384]{2,1,0:T(8,128)(2,1)S(1)} %get-tuple-element.281), channel_id=1, source_target_pairs={{0,8},{8,0},{16,24},{24,16},{1,9},{9,1},{17,25},{25,17},{2,10},{10... | collective-permute-start | bytes 589832 | tf_op jit(solution)/shard_map/ppermute | solution.py:905
  390.5 16.2 %collective-permute-start.37 = (bf16[2,128,384]{2,1,0:T(8,128)(2,1)S(1)}, bf16[2,128,384]{2,1,0:T(8,128)(2,1)S(1)}, u32[]{:S(2)}, u32[]{:S(2)}) collective-permute-start(bf16[2,128,384]{2,1,0:T(8,128)(2,1)S(1)} %get-tuple-element.280), channel_id=1, source_target_pairs={{0,16},{8,24},{16,0},{24,8},{1,17},{9,25},{17,1},{25,9},{2,18},{10... | collective-permute-start | bytes 589832 | tf_op jit(solution)/shard_map/ppermute | solution.py:905
  393.4 11.2 %collective-permute-start.39 = (f32[128]{0:T(128)S(1)}, f32[128]{0:T(128)S(1)}, u32[]{:S(2)}, u32[]{:S(2)}) collective-permute-start(f32[128]{0:T(128)S(1)} %fusion.8), channel_id=1, source_target_pairs={{0,1},{1,0},{2,3},{3,2},{4,5},{5,4},{6,7},{7,6},{8,9},{9,8},{10,11... | collective-permute-start | bytes 1544 | tf_op jit(solution)/shard_map/ppermute | solution.py:20
  404.2 7.5 %collective-permute-start.38 = (bf16[2,128,384]{2,1,0:T(8,128)(2,1)S(1)}, bf16[2,128,384]{2,1,0:T(8,128)(2,1)S(1)}, u32[]{:S(2)}, u32[]{:S(2)}) collective-permute-start(bf16[2,128,384]{2,1,0:T(8,128)(2,1)S(1)} %copy-done.39), channel_id=1, source_target_pairs={{0,24},{8,16},{16,8},{24,0},{1,25},{9,17},{17,9},{25,1},{2,26},{10... | collective-permute-start | bytes 589832 | tf_op jit(solution)/shard_map/ppermute | solution.py:905
  404.5 8.5 %collective-permute-start.41 = (bf16[2,128,384]{2,1,0:T(8,128)(2,1)S(1)}, bf16[2,128,384]{2,1,0:T(8,128)(2,1)S(1)}, u32[]{:S(2)}, u32[]{:S(2)}) collective-permute-start(bf16[2,128,384]{2,1,0:T(8,128)(2,1)S(1)} %get-tuple-element.282.refs_1_), channel_id=1, source_target_pairs={{0,1},{1,0},{2,3},{3,2},{4,5},{5,4},{6,7},{7,6},{8,9},{9,8},{10,11... | collective-permute-start | bytes 589832 | tf_op jit(solution)/shard_map/ppermute | solution.py:20
  405.2 11.4 %collective-permute-start.42 = (bf16[2,128,384]{2,1,0:T(8,128)(2,1)S(1)}, bf16[2,128,384]{2,1,0:T(8,128)(2,1)S(1)}, u32[]{:S(2)}, u32[]{:S(2)}) collective-permute-start(bf16[2,128,384]{2,1,0:T(8,128)(2,1)S(1)} %collective-permute-done.36.refs_2_), channel_id=1, source_target_pairs={{0,1},{1,0},{2,3},{3,2},{4,5},{5,4},{6,7},{7,6},{8,9},{9,8},{10,11... | collective-permute-start | bytes 589832 | tf_op jit(solution)/shard_map/ppermute | solution.py:20
  406.6 14.0 %collective-permute-start.43 = (bf16[2,128,384]{2,1,0:T(8,128)(2,1)S(1)}, bf16[2,128,384]{2,1,0:T(8,128)(2,1)S(1)}, u32[]{:S(2)}, u32[]{:S(2)}) collective-permute-start(bf16[2,128,384]{2,1,0:T(8,128)(2,1)S(1)} %collective-permute-done.37.refs_3_), channel_id=1, source_target_pairs={{0,1},{1,0},{2,3},{3,2},{4,5},{5,4},{6,7},{7,6},{8,9},{9,8},{10,11... | collective-permute-start | bytes 589832 | tf_op jit(solution)/shard_map/ppermute | solution.py:20
  411.8 11.0 %collective-permute-start.44 = (bf16[2,128,384]{2,1,0:T(8,128)(2,1)S(1)}, bf16[2,128,384]{2,1,0:T(8,128)(2,1)S(1)}, u32[]{:S(2)}, u32[]{:S(2)}) collective-permute-start(bf16[2,128,384]{2,1,0:T(8,128)(2,1)S(1)} %collective-permute-done.38.refs_4_), channel_id=1, source_target_pairs={{0,1},{1,0},{2,3},{3,2},{4,5},{5,4},{6,7},{7,6},{8,9},{9,8},{10,11... | collective-permute-start | bytes 589832 | tf_op jit(solution)/shard_map/ppermute | solution.py:20
  (50 other events, 268.8 us)
Sparse Core Ops, SparseCore 0:
  38.8 46.2 all-gather.3
  110.9 49.1 reduce-scatter.3
  166.4 31.2 all-gather.5
  217.9 50.6 reduce-scatter.5
  275.9 30.2 all-gather.7
  344.1 59.9 reduce-scatter.7
